TPU v7x, 512 devices: a whole 4x4x16 slice. The times are simulated.
512 devices in a mesh: dp: 16 (over y, x_hi, core), loop: 32 (over x_lo, z).
Axes of the slice: x: 4 (x_hi: 2, x_lo: 2; x = x_hi * 2 + x_lo), y: 4, z: 16, core: 2. Of those that a mesh axis runs over, the one named last changes fastest.
Arguments:
- netlist: bfloat16 [16, 16384, 512], P('dp', 'loop'), may hold values from -9 to 9
- rtl: bfloat16 [16, 16384, 512], P('dp', 'loop'), may hold values from -9 to 9
- hard_target: int32 [16, 32, 16, 1], P('dp', 'loop'), may hold values from 0 to 15; in each aligned block of 16 rows (0 to 15, 16 to 31, ..., all dimensions but the last counted through in order) at most 2 rows name the same one
- hard_block: int32 [16, 32, 16], P('dp', 'loop'), may hold values from 0 to 3
Outputs:
- row_loss: float32 [16, 16384], P('dp', 'loop')
- netlist_grad: float32 [16, 16384, 512], P('dp', 'loop')
- rtl_grad: float32 [16, 16384, 512], P('dp', 'loop')
Inputs may be any that keep to these rules, and one draw needn't show every extreme that they name: `hard_target`: among the 16 entries of one tile, no group is named more than 2 times, a bound that some block reaches.
All inputs are finite; a program needn't handle non-finite values.
Results may differ from a plain program's by a relative error of at most 0.0018.
Values may be sent and summed in bfloat16 or wider, within the bound.
No kernel may reach another device: no remote copies, remote signals or barrier semaphores. Data moves between devices by JAX's collectives and lax.ppermute only.
A program may use at most 64 MiB of HBM per device.

v0:
```python
import math

import jax
import jax.numpy as jnp
from jax import lax
from jax.sharding import PartitionSpec as P

BLOCK = 128
STEPS = 2
CAP = 2


def passed_along(block, axis, distance):
    devices = range(lax.axis_size(axis))
    route = [((i - distance) % len(devices), i) for i in devices]
    return lax.ppermute(block, axis, route)


def slot_ranks(targets):
    count = targets.shape[-1]
    same = targets[..., :, None] == targets[..., None, :]
    earlier = jnp.arange(count)[None, :] < jnp.arange(count)[:, None]
    return jnp.sum((same & earlier).astype(jnp.int32), axis=-1)


def body(netlist, rtl, hard_target, hard_block):
    queries = netlist[0]
    own_keys = rtl[0]
    row_count, feature = queries.shape
    logit_scale = 3.0 / math.sqrt(feature)
    groups = lax.axis_size("dp")
    slot_ids = jnp.arange(CAP, dtype=jnp.int32)
    tile_list = [own_keys]
    moving = own_keys
    for offset in range(STEPS):
        moving = passed_along(moving, "loop", 1)
        tile_list.append(moving)
    cycle_keys = jnp.concatenate(tile_list, axis=0)
    targets = hard_target[0, 0, :, 0]
    picks = hard_block[0, 0]
    slot_rank = slot_ranks(targets)
    group_ids = jnp.arange(groups, dtype=jnp.int32)
    select = (
        (targets[None, None, :] == group_ids[:, None, None])
        & (slot_rank[None, None, :] == slot_ids[None, :, None])
    ).astype(jnp.int32)
    chosen = jnp.sum(select * picks[None, None, :], axis=-1)
    slot_live = jnp.sum(select, axis=-1).astype(jnp.bfloat16)
    packed = jnp.take(own_keys.reshape(-1, BLOCK, feature), chosen, axis=0)
    arrived, arrived_live = (
        lax.all_to_all(packed, "dp", split_axis=0, concat_axis=0, tiled=True),
        lax.all_to_all(slot_live, "dp", split_axis=0, concat_axis=0, tiled=True),
    )
    hard_keys = arrived.reshape(-1, feature)
    hard_live = jnp.broadcast_to(
        arrived_live.astype(jnp.float32)[:, :, None] > 0.5, arrived.shape[:3]
    ).reshape(-1)
    cycle_scores = (
        jnp.einsum("qe,ke->qk", queries, cycle_keys, preferred_element_type=jnp.float32)
        * logit_scale
    )
    hard_scores = (
        jnp.einsum("qe,ke->qk", queries, hard_keys, preferred_element_type=jnp.float32)
        * logit_scale
    )
    hard_scores = jnp.where(hard_live[None, :], hard_scores, -jnp.inf)
    row_max = jnp.maximum(jnp.max(cycle_scores, axis=1), jnp.max(hard_scores, axis=1))
    cycle_exp = jnp.exp(cycle_scores - row_max[:, None])
    hard_exp = jnp.exp(hard_scores - row_max[:, None])
    row_total = jnp.sum(cycle_exp, axis=1) + jnp.sum(hard_exp, axis=1)
    positive = (
        jnp.sum(queries.astype(jnp.float32) * own_keys.astype(jnp.float32), axis=1) * logit_scale
    )
    row_loss = row_max + jnp.log(row_total) - positive
    cycle_weight = cycle_exp / row_total[:, None]
    cycle_weight = cycle_weight.at[:, :row_count].add(-jnp.eye(row_count, dtype=jnp.float32))
    cycle_weight = cycle_weight.astype(jnp.bfloat16)
    hard_weight = (hard_exp / row_total[:, None]).astype(jnp.bfloat16)
    netlist_grad = (
        jnp.einsum("qk,ke->qe", cycle_weight, cycle_keys, preferred_element_type=jnp.float32)
        + jnp.einsum("qk,ke->qe", hard_weight, hard_keys, preferred_element_type=jnp.float32)
    ) * logit_scale
    key_grads = (
        jnp.einsum("qk,qe->ke", cycle_weight, queries, preferred_element_type=jnp.float32)
        * logit_scale
    )
    grad_tiles = [
        key_grads[offset * row_count : (offset + 1) * row_count] for offset in range(STEPS + 1)
    ]
    carried = grad_tiles[STEPS]
    for offset in range(STEPS - 1, -1, -1):
        carried = passed_along(carried, "loop", -1) + grad_tiles[offset]
    return (row_loss[None], netlist_grad[None], carried[None])


def solution(mesh):
    return jax.shard_map(
        body,
        mesh=mesh,
        in_specs=(
            P("dp", "loop", None),
            P("dp", "loop", None),
            P("dp", "loop", None, None),
            P("dp", "loop", None),
        ),
        out_specs=(P("dp", "loop"), P("dp", "loop", None), P("dp", "loop", None)),
        check_vma=False,
    )
```

profile of v0, /device:TPU:1, one launch (start us, length us, event | category | flops | bytes accessed | tf_op | source)
XLA Modules:
  0.0 167.1 jit_solution(10513311926960830396)
XLA Ops:
  0.6 0.9 convert_reduce_fusion
  1.5 0.7 iota_compare_fusion.2
  2.2 0.8 fusion.14
  3.0 0.7 copy.23
  3.7 10.1 %all-to-all-start = ((bf16[16,1,2]{2,1,0:T(2,128)(2,1)}), bf16[16,1,2]{2,1,0:T(2,128)(2,1)S(1)}, u32[]{:S(2)}, u32[]{:S(2)}) async-start(bf16[16,1,2]{2,1,0:T(2,128)(2,1)} %copy.23), calls=%async_computation | async-start | bytes 16384 | tf_op jit(solution)/shard_map/all_to_all | solution.py:52
  13.9 0.1 copy.27
  14.0 0.1 reshape.183
  14.1 0.1 copy.26
  14.2 3.8 %gather_fusion = bf16[32,128,512]{2,1,0:T(8,128)(2,1)} fusion(bf16[4,128,512]{2,1,0:T(8,128)(2,1)} %bitcast.36, s32[1024]{0:T(1024)S(1)} %pad_clamp_fusion), kind=kCustom, calls=%fused_computation | custom fusion | bytes 8388736 | tf_op jit(solution)/shard_map/jit(_take)/gather | solution.py:49
  18.0 4.6 %broadcast_select_fusion = bf16[16,2,128,512]{3,2,1,0:T(8,128)(2,1)} fusion(bf16[16,2,128,512]{3,2,1,0:T(8,128)(2,1)} %bitcast.40, pred[16,2]{1,0:T(8,128)(4,1)S(1)} %copy.26), kind=kLoop, calls=%fused_computation.6 | loop fusion | flops 2097152 | bytes 8388640 | tf_op jit(solution)/shard_map/jit(_take)/select_n | solution.py:49
  22.6 0.0 copy-start
  22.6 0.0 copy-start.2
  22.6 0.0 all-to-all-done
  22.6 7.4 %all-to-all-start.1 = ((bf16[16,2,128,512]{3,2,1,0:T(8,128)(2,1)}), bf16[16,2,128,512]{3,2,1,0:T(8,128)(2,1)}, u32[]{:S(2)}, u32[]{:S(2)}) async-start(bf16[16,2,128,512]{3,2,1,0:T(8,128)(2,1)} %broadcast_select_fusion), calls=%async_computation.1 | async-start | bytes 8388608 | tf_op jit(solution)/shard_map/all_to_all | solution.py:51
  30.0 0.0 copy-done
  30.0 1.9 %collective-permute-start = (bf16[512,512]{1,0:T(8,128)(2,1)S(1)}, bf16[512,512]{1,0:T(8,128)(2,1)S(1)}, u32[]{:S(2)}, u32[]{:S(2)}) collective-permute-start(bf16[512,512]{1,0:T(8,128)(2,1)S(1)} %bitcast.37), channel_id=1, source_target_pairs={{31,0},{0,1},{1,2},{2,3},{3,4},{4,5},{5,6},{6,7},{7,8},{8,9},{9,10... | collective-permute-start | bytes 1572872 | tf_op jit(solution)/shard_map/ppermute | solution.py:16
  31.9 19.8 %collective-permute-done = bf16[512,512]{1,0:T(8,128)(2,1)S(1)} collective-permute-done((bf16[512,512]{1,0:T(8,128)(2,1)S(1)}, bf16[512,512]{1,0:T(8,128)(2,1)S(1)}, u32[]{:S(2)}, u32[]{:S(2)}) %collective-permute-start) | collective-permute-done | bytes 524320 | tf_op jit(solution)/shard_map/ppermute | solution.py:16
  51.7 1.9 %collective-permute-start.1 = (bf16[512,512]{1,0:T(8,128)(2,1)S(1)}, bf16[512,512]{1,0:T(8,128)(2,1)S(1)}, u32[]{:S(2)}, u32[]{:S(2)}) collective-permute-start(bf16[512,512]{1,0:T(8,128)(2,1)S(1)} %collective-permute-done), channel_id=1, source_target_pairs={{31,0},{0,1},{1,2},{2,3},{3,4},{4,5},{5,6},{6,7},{7,8},{8,9},{9,10... | collective-permute-start | bytes 1572872 | tf_op jit(solution)/shard_map/ppermute | solution.py:16
  53.6 0.6 compare_reduce_fusion
  54.3 0.0 copy-done.2
  54.3 0.2 multiply_reduce_fusion
  54.5 0.1 copy.24
  54.6 0.1 copy.25
  54.7 0.1 broadcast_in_dim.46
  54.8 13.8 %collective-permute-done.1 = bf16[512,512]{1,0:T(8,128)(2,1)S(1)} collective-permute-done((bf16[512,512]{1,0:T(8,128)(2,1)S(1)}, bf16[512,512]{1,0:T(8,128)(2,1)S(1)}, u32[]{:S(2)}, u32[]{:S(2)}) %collective-permute-start.1) | collective-permute-done | bytes 524320 | tf_op jit(solution)/shard_map/ppermute | solution.py:16
  68.6 2.8 %fusion.21 = (f32[512]{0:T(512)S(1)}, f32[1536,512]{1,0:T(8,128)}) fusion(bf16[1,512,512]{2,1,0:T(8,128)(2,1)S(1)} %copy-done.2, bf16[512,512]{1,0:T(8,128)(2,1)S(1)} %collective-permute-done.1, bf16[512,512]{1,0:T(8,128)(2,1)S(1)} %collective-permute-done, bf16[512,512]{1,0:T(8,128)(2,1)S(1)} %bitcast.38), kind=kOutput, calls=%fused_computation.51 | convolution fusion | flops 811597312 | bytes 5244928 | tf_op jit(solution)/shard_map/qe,ke->qk/dot_general | solution.py:59
  71.4 32.1 %all-to-all-done.1 = bf16[16,2,128,512]{3,2,1,0:T(8,128)(2,1)} async-done(((bf16[16,2,128,512]{3,2,1,0:T(8,128)(2,1)}), bf16[16,2,128,512]{3,2,1,0:T(8,128)(2,1)}, u32[]{:S(2)}, u32[]{:S(2)}) %all-to-all-start.1) | async-done | bytes 4194336 | tf_op jit(solution)/shard_map/all_to_all | solution.py:51
  103.5 0.0 copy-start.1
  103.5 5.0 %fusion = (f32[512]{0:T(512)S(1)}, f32[4096,512]{1,0:T(8,128)S(1)}) fusion(pred[4096]{0:T(1024)(128)(4,1)S(1)} %broadcast_in_dim.47, bf16[4096,512]{1,0:T(8,128)(2,1)} %bitcast.9, bf16[1,512,512]{2,1,0:T(8,128)(2,1)S(1)} %copy-done.2), kind=kOutput, calls=%fused_computation.4 | convolution fusion | flops 2153774592 | bytes 13113344 | tf_op jit(solution)/shard_map/qe,ke->qk/dot_general | solution.py:63
  108.5 0.0 copy-done.1
  108.5 0.5 fusion.3
  109.0 2.7 %fusion.1 = f32[512]{0:T(512)S(1)} fusion(f32[4096,512]{1,0:T(8,128)S(1)} %get-tuple-element.22, f32[512]{0:T(512)S(1)} %max.15, pred[4096]{0:T(1024)(128)(4,1)S(1)} %broadcast_in_dim.47), kind=kLoop, calls=%fused_computation.5 | loop fusion | flops 8388096 | bytes 8396800 | tf_op jit(solution)/shard_map/reduce_sum | solution.py:70
  111.7 0.6 multiply_subtract_fusion
  112.3 0.4 divide_bitcast_fusion
  112.7 0.9 fusion.6
  113.6 1.0 convolution_multiply_fusion
  114.6 0.1 slice.35
  114.7 1.9 %collective-permute-start.2 = (f32[512,512]{1,0:T(8,128)S(1)}, f32[512,512]{1,0:T(8,128)S(1)}, u32[]{:S(2)}, u32[]{:S(2)}) collective-permute-start(f32[512,512]{1,0:T(8,128)S(1)} %slice.35), channel_id=1, source_target_pairs={{1,0},{2,1},{3,2},{4,3},{5,4},{6,5},{7,6},{8,7},{9,8},{10,9},{11,1... | collective-permute-start | bytes 3145736 | tf_op jit(solution)/shard_map/ppermute | solution.py:16
  116.6 23.8 %collective-permute-done.2 = f32[512,512]{1,0:T(8,128)S(1)} collective-permute-done((f32[512,512]{1,0:T(8,128)S(1)}, f32[512,512]{1,0:T(8,128)S(1)}, u32[]{:S(2)}, u32[]{:S(2)}) %collective-permute-start.2) | collective-permute-done | bytes 1048608 | tf_op jit(solution)/shard_map/ppermute | solution.py:16
  140.4 0.2 slice_add_fusion.1
  140.6 4.3 %collective-permute-start.3 = (f32[512,512]{1,0:T(8,128)S(1)}, f32[512,512]{1,0:T(8,128)S(1)}, u32[]{:S(2)}, u32[]{:S(2)}) collective-permute-start(f32[512,512]{1,0:T(8,128)S(1)} %slice_add_fusion.1), channel_id=1, source_target_pairs={{1,0},{2,1},{3,2},{4,3},{5,4},{6,5},{7,6},{8,7},{9,8},{10,9},{11,1... | collective-permute-start | bytes 3145736 | tf_op jit(solution)/shard_map/ppermute | solution.py:16
  144.9 6.2 %fusion.2 = f32[512,512]{1,0:T(8,128)S(1)} fusion(bf16[4096,512]{1,0:T(8,128)(2,1)} %bitcast.9, f32[4096,512]{1,0:T(8,128)S(1)} %get-tuple-element.22, f32[512]{0:T(512)S(1)} %get-tuple-element.18, f32[512]{0:T(512)S(1)} %max.15, pred[4096]{0:T(1024)(128)(4,1)S(1)} %broadcast_in_dim.47), kind=kOutput, calls=%fused_computation.7 | convolution fusion | flops 2157969408 | bytes 13639680 | tf_op jit(solution)/shard_map/qk,ke->qe/dot_general | solution.py:81
  151.2 2.0 %fusion.5 = f32[1,512,512]{2,1,0:T(8,128)} fusion(f32[512,512]{1,0:T(8,128)S(1)} %fusion.2, f32[512,1536]{0,1:T(8,128)S(1)} %fusion.6, bf16[512,512]{1,0:T(8,128)(2,1)S(1)} %collective-permute-done.1, bf16[512,512]{1,0:T(8,128)(2,1)S(1)} %collective-permute-done, bf16[512,512]{1,0:T(8,128)(2,1)S(1)} %bitcast.39), kind=kOutput, calls=%fused_computation.17 | convolution fusion | flops 811335680 | bytes 6815744 | tf_op jit(solution)/shard_map/qk,ke->qe/dot_general | solution.py:80
  153.2 12.7 %collective-permute-done.3 = f32[512,512]{1,0:T(8,128)S(1)} collective-permute-done((f32[512,512]{1,0:T(8,128)S(1)}, f32[512,512]{1,0:T(8,128)S(1)}, u32[]{:S(2)}, u32[]{:S(2)}) %collective-permute-start.3) | collective-permute-done | bytes 1048608 | tf_op jit(solution)/shard_map/ppermute | solution.py:16
  165.9 1.2 fusion.7
  (8 shorter events, 0.1 us)
Async XLA Ops:
  3.7 18.9 %all-to-all-start = ((bf16[16,1,2]{2,1,0:T(2,128)(2,1)}), bf16[16,1,2]{2,1,0:T(2,128)(2,1)S(1)}, u32[]{:S(2)}, u32[]{:S(2)}) async-start(bf16[16,1,2]{2,1,0:T(2,128)(2,1)} %copy.23), calls=%async_computation | async-start | bytes 16384 | tf_op jit(solution)/shard_map/all_to_all | solution.py:52
  22.6 7.4 %copy-start = (bf16[1,512,512]{2,1,0:T(8,128)(2,1)S(1)}, bf16[1,512,512]{2,1,0:T(8,128)(2,1)}, u32[]{:S(2)}) copy-start(bf16[1,512,512]{2,1,0:T(8,128)(2,1)} %param.7) | copy-start | bytes 1572868
  22.6 31.7 %copy-start.2 = (bf16[1,512,512]{2,1,0:T(8,128)(2,1)S(1)}, bf16[1,512,512]{2,1,0:T(8,128)(2,1)}, u32[]{:S(2)}) copy-start(bf16[1,512,512]{2,1,0:T(8,128)(2,1)} %param.6) | copy-start | bytes 1572868
  22.6 80.9 %all-to-all-start.1 = ((bf16[16,2,128,512]{3,2,1,0:T(8,128)(2,1)}), bf16[16,2,128,512]{3,2,1,0:T(8,128)(2,1)}, u32[]{:S(2)}, u32[]{:S(2)}) async-start(bf16[16,2,128,512]{3,2,1,0:T(8,128)(2,1)} %broadcast_select_fusion), calls=%async_computation.1 | async-start | bytes 8388608 | tf_op jit(solution)/shard_map/all_to_all | solution.py:51
  30.0 21.7 %collective-permute-start = (bf16[512,512]{1,0:T(8,128)(2,1)S(1)}, bf16[512,512]{1,0:T(8,128)(2,1)S(1)}, u32[]{:S(2)}, u32[]{:S(2)}) collective-permute-start(bf16[512,512]{1,0:T(8,128)(2,1)S(1)} %bitcast.37), channel_id=1, source_target_pairs={{31,0},{0,1},{1,2},{2,3},{3,4},{4,5},{5,6},{6,7},{7,8},{8,9},{9,10... | collective-permute-start | bytes 1572872 | tf_op jit(solution)/shard_map/ppermute | solution.py:16
  51.7 16.9 %collective-permute-start.1 = (bf16[512,512]{1,0:T(8,128)(2,1)S(1)}, bf16[512,512]{1,0:T(8,128)(2,1)S(1)}, u32[]{:S(2)}, u32[]{:S(2)}) collective-permute-start(bf16[512,512]{1,0:T(8,128)(2,1)S(1)} %collective-permute-done), channel_id=1, source_target_pairs={{31,0},{0,1},{1,2},{2,3},{3,4},{4,5},{5,6},{6,7},{7,8},{8,9},{9,10... | collective-permute-start | bytes 1572872 | tf_op jit(solution)/shard_map/ppermute | solution.py:16
  103.5 5.0 %copy-start.1 = (f32[1536,512]{1,0:T(8,128)S(1)}, f32[1536,512]{1,0:T(8,128)}, u32[]{:S(2)}) copy-start(f32[1536,512]{1,0:T(8,128)} %get-tuple-element.20) | copy-start | bytes 9437188
  114.7 25.7 %collective-permute-start.2 = (f32[512,512]{1,0:T(8,128)S(1)}, f32[512,512]{1,0:T(8,128)S(1)}, u32[]{:S(2)}, u32[]{:S(2)}) collective-permute-start(f32[512,512]{1,0:T(8,128)S(1)} %slice.35), channel_id=1, source_target_pairs={{1,0},{2,1},{3,2},{4,3},{5,4},{6,5},{7,6},{8,7},{9,8},{10,9},{11,1... | collective-permute-start | bytes 3145736 | tf_op jit(solution)/shard_map/ppermute | solution.py:16
  140.6 25.3 %collective-permute-start.3 = (f32[512,512]{1,0:T(8,128)S(1)}, f32[512,512]{1,0:T(8,128)S(1)}, u32[]{:S(2)}, u32[]{:S(2)}) collective-permute-start(f32[512,512]{1,0:T(8,128)S(1)} %slice_add_fusion.1), channel_id=1, source_target_pairs={{1,0},{2,1},{3,2},{4,3},{5,4},{6,5},{7,6},{8,7},{9,8},{10,9},{11,1... | collective-permute-start | bytes 3145736 | tf_op jit(solution)/shard_map/ppermute | solution.py:16
where the time goes:
time: 168 us; the launch traced here: 167 us
  waiting for transfers between devices  102 us (61%)
  starting transfers between devices  27.7 us (16%)
  matrix products  16.9 us (10%)
  other arithmetic  14.4 us (9%)
  local copies, waits for them, and re-layouts  5.13 us (3%)
    ppermute x4, waiting for transfers between devices, passed_along(): return lax.ppermute(block, axis, route)  70.1 us
    all_to_all x1, waiting for transfers between devices, body(): lax.all_to_all(packed, 'dp', split_axis=0, concat_axis=0, tiled=True)  32.1 us
    all_to_all x1, starting transfers between devices, body(): lax.all_to_all(slot_live, 'dp', split_axis=0, concat_axis=0, tiled=True)  10.1 us
    ppermute x4, starting transfers between devices, passed_along(): return lax.ppermute(block, axis, route)  10.1 us
    all_to_all x1, starting transfers between devices, body(): lax.all_to_all(packed, 'dp', split_axis=0, concat_axis=0, tiled=True)  7.42 us
    dot_general x1, matrix products, body(): jnp.einsum('qk,ke->qe', hard_weight, hard_keys, preferred_element_type=jn...  6.25 us
    dot_general x1, matrix products, body(): jnp.einsum('qe,ke->qk', queries, hard_keys, preferred_element_type=jnp.fl...  4.95 us
    select_n x2, other arithmetic, body(): packed = jnp.take(own_keys.reshape(-1, BLOCK, feature), chosen, axis=0)  4.63 us
  transfers between devices with their start and end apart: 6, of which 5 were waited for; matrix products, arithmetic and copies ran while one was open for 12% of the time, Pallas kernels for 0%

commit v1 on v0

v1 whole, which is shorter than its diff:
```python
import functools
import math

import jax
import jax.numpy as jnp
from jax import lax
from jax.experimental import pallas as pl
from jax.experimental.pallas import tpu as pltpu
from jax.sharding import PartitionSpec as P

BLOCK = 128
CAP = 2
CHUNK = 256
VMEM_LIMIT = 56 * 1024 * 1024


def passed_along(block, axis, distance):
    devices = range(lax.axis_size(axis))
    route = [((i - distance) % len(devices), i) for i in devices]
    return lax.ppermute(block, axis, route)


def nt_dot(a, b):
    return lax.dot_general(a, b, (((1,), (1,)), ((), ())), preferred_element_type=jnp.float32)


def whole(space=pltpu.VMEM):
    return pl.BlockSpec(memory_space=space)


def pack_kernel(entries, targets, picks, tile, out, rank_of, sems):
    for j in range(entries):
        t = targets[j]
        rank = jnp.int32(0)
        for j2 in range(j):
            rank += (targets[j2] == t).astype(jnp.int32)
        rank_of[j] = t * CAP + jnp.minimum(rank, CAP - 1)
        pltpu.make_async_copy(tile.at[picks[j]], out.at[rank_of[j]], sems.at[j]).start()
    for j in range(entries):
        pltpu.make_async_copy(tile.at[picks[j]], out.at[rank_of[j]], sems.at[j]).wait()


def pack(targets, picks, tile, groups):
    entries = targets.shape[0]
    blocks, rows, feature = tile.shape
    return pl.pallas_call(
        functools.partial(pack_kernel, entries),
        out_shape=jax.ShapeDtypeStruct((groups * CAP, rows, feature), tile.dtype),
        in_specs=[whole(pltpu.SMEM), whole(pltpu.SMEM), whole()],
        out_specs=whole(pl.ANY),
        scratch_shapes=[pltpu.SMEM((entries,), jnp.int32), pltpu.SemaphoreType.DMA((entries,))],
        name="pack",
    )(targets, picks, tile)


def cycle_kernel(scale, q_ref, k0_ref, k1_ref, k2_ref, m_ref, l_ref, pos_ref, num_ref):
    q = q_ref[...]
    rows = q.shape[0]
    first = pl.multiple_of(pl.program_id(0) * rows, rows)
    keys = [k0_ref[...], k1_ref[...], k2_ref[...]]
    scores = [nt_dot(q, k) * scale for k in keys]
    m = jnp.max(jnp.maximum(jnp.maximum(scores[0], scores[1]), scores[2]), axis=1, keepdims=True)
    exps = [jnp.exp(s - m) for s in scores]
    m_ref[...] = m
    l_ref[...] = jnp.sum(exps[0] + exps[1] + exps[2], axis=1, keepdims=True)
    num = jnp.zeros((rows, q.shape[1]), jnp.float32)
    for e, k in zip(exps, keys):
        num += jnp.dot(e.astype(jnp.bfloat16), k, preferred_element_type=jnp.float32)
    num_ref[...] = num
    own = k0_ref[pl.ds(first, rows), :].astype(jnp.float32)
    pos_ref[...] = jnp.sum(q.astype(jnp.float32) * own, axis=1, keepdims=True) * scale


def cycle_part(scale, q, k0, k1, k2, rows=256):
    n, feature = q.shape
    block = pl.BlockSpec((rows, feature), lambda i: (i, 0))
    column = pl.BlockSpec((rows, 1), lambda i: (i, 0))
    full = pl.BlockSpec((n, feature), lambda i: (0, 0))
    col = jax.ShapeDtypeStruct((n, 1), jnp.float32)
    return pl.pallas_call(
        functools.partial(cycle_kernel, scale),
        grid=(n // rows,),
        out_shape=(col, col, col, jax.ShapeDtypeStruct((n, feature), jnp.float32)),
        in_specs=[block, full, full, full],
        out_specs=(column, column, column, block),
        compiler_params=pltpu.CompilerParams(vmem_limit_bytes=VMEM_LIMIT),
        cost_estimate=pl.CostEstimate(flops=4 * n * 3 * n * feature, bytes_accessed=4 * n * feature * 2 + n * feature * 4, transcendentals=3 * n * n),
        name="cycle",
    )(q, k0, k1, k2)


def hard_kernel(scale, sources, slots, counts, q_ref, k0_ref, m_ref, l_ref, pos_ref, num_ref, blocks,
                grad_ref, loss_ref, stats_ref, keys, scores, where, sems):
    n, feature = q_ref.shape
    live = jnp.int32(0)
    per = CHUNK // BLOCK
    for g in range(sources):
        for c in range(slots):
            @pl.when(counts[g] > c)
            def _(live=live, g=g, c=c):
                pltpu.make_async_copy(blocks.at[g * slots + c], keys.at[pl.ds(live * BLOCK, BLOCK)], sems.at[live]).start()
            live += (counts[g] > c).astype(jnp.int32)
    chunks = (live + per - 1) // per

    @pl.when(live < chunks * per)
    def _():
        keys[pl.ds(pl.multiple_of(live * BLOCK, BLOCK), BLOCK), :] = jnp.zeros((BLOCK, feature), keys.dtype)

    q = q_ref[...]

    def score(i, m):
        for p in range(per):
            @pl.when(i * per + p < live)
            def _(p=p):
                pltpu.make_async_copy(blocks.at[0], keys.at[pl.ds((i * per + p) * BLOCK, BLOCK)], sems.at[i * per + p]).wait()
        k = keys[pl.ds(pl.multiple_of(i * CHUNK, CHUNK), CHUNK), :]
        s = nt_dot(q, k) * scale
        lane = lax.broadcasted_iota(jnp.int32, (n, CHUNK), 1) + i * CHUNK
        s = jnp.where(lane < live * BLOCK, s, -jnp.inf)
        scores[i] = s
        return jnp.maximum(m, jnp.maximum(s[:, :BLOCK], s[:, BLOCK:]))

    old = m_ref[...]
    wide = lax.fori_loop(0, chunks, score, jnp.broadcast_to(old, (n, BLOCK)))
    m = jnp.max(wide, axis=1, keepdims=True)
    shrink = jnp.exp(old - m)
    grad_ref[...] = num_ref[...] * shrink

    def weigh(i, l):
        e = jnp.exp(scores[i] - m)
        k = keys[pl.ds(pl.multiple_of(i * CHUNK, CHUNK), CHUNK), :]
        grad_ref[...] += jnp.dot(e.astype(jnp.bfloat16), k, preferred_element_type=jnp.float32)
        return l + (e[:, :BLOCK] + e[:, BLOCK:])

    l = lax.fori_loop(0, chunks, weigh, jnp.zeros((n, BLOCK), jnp.float32))
    total = jnp.sum(l, axis=1, keepdims=True) + l_ref[...] * shrink
    inverse = 1.0 / total
    grad_ref[...] = (grad_ref[...] * inverse - k0_ref[...].astype(jnp.float32)) * scale
    loss = m + jnp.log(total) - pos_ref[...]
    lane = lax.broadcasted_iota(jnp.int32, (n, BLOCK), 1)
    table = jnp.where(lane == 0, m, jnp.where(lane == 1, inverse, loss))
    flipped = table.T
    stats_ref[...] = flipped[:8]
    loss_ref[...] = flipped[2:3]


def hard_part(scale, counts, q, k0, m, l, pos, num, blocks):
    n, feature = q.shape
    sources = counts.shape[0]
    total = sources * CAP
    f32 = jnp.float32
    return pl.pallas_call(
        functools.partial(hard_kernel, scale, sources, CAP),
        out_shape=(jax.ShapeDtypeStruct((n, feature), f32), jax.ShapeDtypeStruct((1, n), f32), jax.ShapeDtypeStruct((8, n), f32)),
        in_specs=[whole(pltpu.SMEM)] + [whole()] * 6 + [whole(pl.ANY)],
        out_specs=(whole(), whole(), whole()),
        scratch_shapes=[
            pltpu.VMEM((total * BLOCK, feature), jnp.bfloat16),
            pltpu.VMEM((total * BLOCK // CHUNK, n, CHUNK), f32),
            pltpu.SMEM((total,), jnp.int32),
            pltpu.SemaphoreType.DMA((total,)),
        ],
        compiler_params=pltpu.CompilerParams(vmem_limit_bytes=VMEM_LIMIT),
        cost_estimate=pl.CostEstimate(flops=2 * n * total * BLOCK * feature, bytes_accessed=total * BLOCK * feature, transcendentals=n * total * BLOCK // 2),
        name="hard",
    )(counts, q, k0, m, l, pos, num, blocks)


def rtl_kernel(scale, k_ref, n0_ref, n1_ref, n2_ref, s0_ref, s1_ref, s2_ref, out_ref):
    k = k_ref[...]
    total = jnp.zeros(out_ref.shape, jnp.float32)
    for n_ref, s_ref in ((n0_ref, s0_ref), (n1_ref, s1_ref), (n2_ref, s2_ref)):
        rows = n_ref[...]
        s = nt_dot(k, rows) * scale
        w = jnp.exp(s - s_ref[0:1, :]) * s_ref[1:2, :]
        total += jnp.dot(w.astype(jnp.bfloat16), rows, preferred_element_type=jnp.float32)
    first = pl.multiple_of(pl.program_id(0) * k.shape[0], k.shape[0])
    own = n0_ref[pl.ds(first, k.shape[0]), :].astype(jnp.float32)
    out_ref[...] = (total - own) * scale


def rtl_part(scale, k, n0, n1, n2, s0, s1, s2, rows=256):
    n, feature = k.shape
    block = pl.BlockSpec((rows, feature), lambda i: (i, 0))
    full = pl.BlockSpec((n, feature), lambda i: (0, 0))
    stat = pl.BlockSpec((8, n), lambda i: (0, 0))
    return pl.pallas_call(
        functools.partial(rtl_kernel, scale),
        grid=(n // rows,),
        out_shape=jax.ShapeDtypeStruct((n, feature), jnp.float32),
        in_specs=[block, full, full, full, stat, stat, stat],
        out_specs=block,
        compiler_params=pltpu.CompilerParams(vmem_limit_bytes=VMEM_LIMIT),
        cost_estimate=pl.CostEstimate(flops=4 * n * 3 * n * feature, bytes_accessed=4 * n * feature * 2 + n * feature * 4, transcendentals=3 * n * n),
        name="rtl",
    )(k, n0, n1, n2, s0, s1, s2)


def body(netlist, rtl, hard_target, hard_block):
    queries = netlist[0]
    own_keys = rtl[0]
    row_count, feature = queries.shape
    scale = 3.0 / math.sqrt(feature)
    groups = lax.axis_size("dp")
    targets = hard_target[0, 0, :, 0]
    picks = hard_block[0, 0]

    packed = pack(targets, picks, own_keys.reshape(-1, BLOCK, feature), groups)
    arrived = lax.all_to_all(packed, "dp", split_axis=0, concat_axis=0, tiled=True)
    named = jnp.sum((targets[None, :] == jnp.arange(groups, dtype=jnp.int32)[:, None]).astype(jnp.int32), axis=1)
    counts = lax.all_to_all(named, "dp", split_axis=0, concat_axis=0, tiled=True)

    rtl1 = passed_along(own_keys, "loop", 1)
    net1 = passed_along(queries, "loop", -1)
    rtl2 = passed_along(rtl1, "loop", 1)
    net2 = passed_along(net1, "loop", -1)

    m, l, pos, num = cycle_part(scale, queries, own_keys, rtl1, rtl2)
    grad, loss, stats = hard_part(scale, counts, queries, own_keys, m, l, pos, num, arrived)
    stats1 = passed_along(stats, "loop", -1)
    stats2 = passed_along(stats, "loop", -2)
    rtl_grad = rtl_part(scale, own_keys, queries, net1, net2, stats, stats1, stats2)
    return (loss, grad[None], rtl_grad[None])


def solution(mesh):
    return jax.shard_map(
        body,
        mesh=mesh,
        in_specs=(
            P("dp", "loop", None),
            P("dp", "loop", None),
            P("dp", "loop", None, None),
            P("dp", "loop", None),
        ),
        out_specs=(P("dp", "loop"), P("dp", "loop", None), P("dp", "loop", None)),
        check_vma=False,
    )
```

time: 168 us -> 133 us (0.79)
  the two profiles are of different devices: /device:TPU:1 before, /device:TPU:8 now
where the time goes in v1:
time: 133 us
  waiting for transfers between devices  54.5 us (41%)
  starting transfers between devices  46.1 us (35%)
  Pallas kernels  27.7 us (21%)
  local copies, waits for them, and re-layouts  2.14 us (2%)
  other arithmetic  1.73 us (1%)
    ppermute x6, starting transfers between devices, passed_along(): return lax.ppermute(block, axis, route)  31.2 us
    all_to_all x1, waiting for transfers between devices, body(): lax.all_to_all(packed, 'dp', split_axis=0, concat_axis=0, tiled=True)  27 us
    ppermute x6, waiting for transfers between devices, passed_along(): return lax.ppermute(block, axis, route)  23.8 us
    pallas_call x1, Pallas kernels, hard_part(): pl.pallas_call(functools.partial(hard_kernel, scale, sources, CAP), out_s...  15.4 us
    all_to_all x1, starting transfers between devices, body(): lax.all_to_all(named, 'dp', split_axis=0, concat_axis=0, tiled=True)  9.1 us
    all_to_all x1, starting transfers between devices, body(): lax.all_to_all(packed, 'dp', split_axis=0, concat_axis=0, tiled=True)  5.73 us
    pallas_call x1, Pallas kernels, cycle_part(): pl.pallas_call(functools.partial(cycle_kernel, scale), grid=(n // rows,),...  5.03 us
    pallas_call x1, Pallas kernels, rtl_part(): pl.pallas_call(functools.partial(rtl_kernel, scale), grid=(n // rows,), o...  4.73 us
  transfers between devices with their start and end apart: 8, of which 5 were waited for; matrix products, arithmetic and copies ran while one was open for 1% of the time, Pallas kernels for 17%

profile of v1, /device:TPU:8, one launch (start us, length us, event | category | flops | bytes accessed | tf_op | source)
XLA Modules:
  0.0 132.9 jit_solution(16042283008435507163)
XLA Ops:
  0.6 0.8 convert_reduce_fusion
  1.4 0.7 copy.9
  2.1 9.1 %all-to-all-start = ((s32[16,1,1]{2,1,0:T(1,128)}), s32[16,1,1]{2,1,0:T(1,128)S(1)}, u32[]{:S(2)}, u32[]{:S(2)}) async-start(s32[16,1,1]{2,1,0:T(1,128)} %copy.9), calls=%async_computation | async-start | bytes 16384 | tf_op jit(solution)/shard_map/all_to_all | solution.py:211
  11.2 2.5 %pack.1 = bf16[32,128,512]{2,1,0:T(8,128)(2,1)} custom-call(s32[16]{0:T(128)} %bitcast.14, s32[16]{0:T(128)} %bitcast.15, bf16[4,128,512]{2,1,0:T(8,128)(2,1)} %bitcast.8), custom_call_target="tpu_custom_call" | custom-call | tf_op jit(solution)/shard_map/pack/pallas_call | solution.py:46
  13.7 0.0 copy-start
  13.7 0.0 copy-start.1
  13.7 3.6 %all-to-all-done = s32[16,1,1]{2,1,0:T(1,128)S(1)} async-done(((s32[16,1,1]{2,1,0:T(1,128)}), s32[16,1,1]{2,1,0:T(1,128)S(1)}, u32[]{:S(2)}, u32[]{:S(2)}) %all-to-all-start) | async-done | bytes 96 | tf_op jit(solution)/shard_map/all_to_all | solution.py:211
  17.4 5.7 %all-to-all-start.1 = ((bf16[32,128,512]{2,1,0:T(8,128)(2,1)}), bf16[32,128,512]{2,1,0:T(8,128)(2,1)}, u32[]{:S(2)}, u32[]{:S(2)}) async-start(bf16[32,128,512]{2,1,0:T(8,128)(2,1)} %pack.1), calls=%async_computation.1 | async-start | bytes 8388608 | tf_op jit(solution)/shard_map/all_to_all | solution.py:209
  23.1 0.0 copy-done
  23.1 2.1 %collective-permute-start = (bf16[512,512]{1,0:T(8,128)(2,1)S(1)}, bf16[512,512]{1,0:T(8,128)(2,1)S(1)}, u32[]{:S(2)}, u32[]{:S(2)}) collective-permute-start(bf16[512,512]{1,0:T(8,128)(2,1)S(1)} %bitcast.12), channel_id=1, source_target_pairs={{31,0},{0,1},{1,2},{2,3},{3,4},{4,5},{5,6},{6,7},{7,8},{8,9},{9,10... | collective-permute-start | bytes 1572872 | tf_op jit(solution)/shard_map/ppermute | solution.py:20
  25.2 0.0 copy-done.1
  25.2 9.5 %collective-permute-start.2 = (bf16[512,512]{1,0:T(8,128)(2,1)S(1)}, bf16[512,512]{1,0:T(8,128)(2,1)S(1)}, u32[]{:S(2)}, u32[]{:S(2)}) collective-permute-start(bf16[512,512]{1,0:T(8,128)(2,1)S(1)} %bitcast.20), channel_id=1, source_target_pairs={{1,0},{2,1},{3,2},{4,3},{5,4},{6,5},{7,6},{8,7},{9,8},{10,9},{11,1... | collective-permute-start | bytes 1572872 | tf_op jit(solution)/shard_map/ppermute | solution.py:20
  34.7 10.4 %collective-permute-done.k1_ref = bf16[512,512]{1,0:T(8,128)(2,1)S(1)} collective-permute-done((bf16[512,512]{1,0:T(8,128)(2,1)S(1)}, bf16[512,512]{1,0:T(8,128)(2,1)S(1)}, u32[]{:S(2)}, u32[]{:S(2)}) %collective-permute-start) | collective-permute-done | bytes 524320 | tf_op jit(solution)/shard_map/ppermute | solution.py:20
  45.1 0.0 copy-start.4
  45.1 1.9 %collective-permute-start.1 = (bf16[512,512]{1,0:T(8,128)(2,1)S(1)}, bf16[512,512]{1,0:T(8,128)(2,1)S(1)}, u32[]{:S(2)}, u32[]{:S(2)}) collective-permute-start(bf16[512,512]{1,0:T(8,128)(2,1)S(1)} %collective-permute-done.k1_ref), channel_id=1, source_target_pairs={{31,0},{0,1},{1,2},{2,3},{3,4},{4,5},{5,6},{6,7},{7,8},{8,9},{9,10... | collective-permute-start | bytes 1572872 | tf_op jit(solution)/shard_map/ppermute | solution.py:20
  47.0 0.0 collective-permute-done.2.n1_ref
  47.1 0.0 copy-start.2
  47.1 6.0 %collective-permute-start.3 = (bf16[512,512]{1,0:T(8,128)(2,1)S(1)}, bf16[512,512]{1,0:T(8,128)(2,1)S(1)}, u32[]{:S(2)}, u32[]{:S(2)}) collective-permute-start(bf16[512,512]{1,0:T(8,128)(2,1)S(1)} %collective-permute-done.2.n1_ref), channel_id=1, source_target_pairs={{1,0},{2,1},{3,2},{4,3},{5,4},{6,5},{7,6},{8,7},{9,8},{10,9},{11,1... | collective-permute-start | bytes 1572872 | tf_op jit(solution)/shard_map/ppermute | solution.py:20
  53.1 1.0 reduce.counts
  54.1 8.7 %collective-permute-done.1.k2_ref = bf16[512,512]{1,0:T(8,128)(2,1)S(1)} collective-permute-done((bf16[512,512]{1,0:T(8,128)(2,1)S(1)}, bf16[512,512]{1,0:T(8,128)(2,1)S(1)}, u32[]{:S(2)}, u32[]{:S(2)}) %collective-permute-start.1) | collective-permute-done | bytes 524320 | tf_op jit(solution)/shard_map/ppermute | solution.py:20
  62.7 0.0 copy-done.4
  62.7 0.0 copy-start.5
  62.7 0.8 copy-done.5
  63.6 5.0 %cycle.1 = (f32[512,1]{1,0:T(8,128)}, f32[512,1]{1,0:T(8,128)}, f32[512,1]{1,0:T(8,128)}, f32[512,512]{1,0:T(8,128)}) custom-call(bf16[512,512]{1,0:T(8,128)(2,1)} %bitcast.17, bf16[512,512]{1,0:T(8,128)(2,1)} %bitcast.9, bf16[512,512]{1,0:T(8,128)(2,1)} %copy-done.4, bf16[512,512]{1,0:T(8,128)(2,1)} %copy-done.5), custom_call_target="tpu_custom_call" | custom-call | flops 1610612736 | bytes 3145728 | tf_op jit(solution)/shard_map/cycle/pallas_call | solution.py:80
  68.6 27.0 %all-to-all-done.1.blocks = bf16[32,128,512]{2,1,0:T(8,128)(2,1)} async-done(((bf16[32,128,512]{2,1,0:T(8,128)(2,1)}), bf16[32,128,512]{2,1,0:T(8,128)(2,1)}, u32[]{:S(2)}, u32[]{:S(2)}) %all-to-all-start.1) | async-done | bytes 4194336 | tf_op jit(solution)/shard_map/all_to_all | solution.py:209
  95.6 15.4 %hard.1 = (f32[512,512]{1,0:T(8,128)}, f32[1,512]{1,0:T(1,128)}, f32[8,512]{1,0:T(8,128)}) custom-call(s32[16]{0:T(128)} %reduce.counts, bf16[512,512]{1,0:T(8,128)(2,1)} %bitcast.18, bf16[512,512]{1,0:T(8,128)(2,1)} %bitcast.10, f32[512,1]{1,0:T(8,128)} %get-tuple-element.10.m_ref, f32[512,1]{1,0:T(8,128)} %get-tuple-element.11.l_ref, ...), custom_call_target="tpu_custom_call" | custom-call | flops 2147483648 | bytes 2097152 | tf_op jit(solution)/shard_map/hard/pallas_call | solution.py:152
  111.0 0.0 copy-done.2
  111.1 9.8 %collective-permute-start.4 = (f32[8,512]{1,0:T(8,128)}, f32[8,512]{1,0:T(8,128)S(1)}, u32[]{:S(2)}, u32[]{:S(2)}) collective-permute-start(f32[8,512]{1,0:T(8,128)} %get-tuple-element.16.s0_ref), channel_id=1, source_target_pairs={{1,0},{2,1},{3,2},{4,3},{5,4},{6,5},{7,6},{8,7},{9,8},{10,9},{11,1... | collective-permute-start | bytes 49160 | tf_op jit(solution)/shard_map/ppermute | solution.py:20
  120.8 1.9 %collective-permute-start.5 = (f32[8,512]{1,0:T(8,128)}, f32[8,512]{1,0:T(8,128)S(1)}, u32[]{:S(2)}, u32[]{:S(2)}) collective-permute-start(f32[8,512]{1,0:T(8,128)} %get-tuple-element.16.s0_ref), channel_id=1, source_target_pairs={{2,0},{3,1},{4,2},{5,3},{6,4},{7,5},{8,6},{9,7},{10,8},{11,9},{12,... | collective-permute-start | bytes 49160 | tf_op jit(solution)/shard_map/ppermute | solution.py:20
  122.8 0.0 collective-permute-done.3.n2_ref
  122.8 0.0 copy-start.3
  122.8 0.0 collective-permute-done.4.s1_ref
  122.8 0.0 copy-start.6
  122.8 4.8 %collective-permute-done.5.s2_ref = f32[8,512]{1,0:T(8,128)S(1)} collective-permute-done((f32[8,512]{1,0:T(8,128)}, f32[8,512]{1,0:T(8,128)S(1)}, u32[]{:S(2)}, u32[]{:S(2)}) %collective-permute-start.5) | collective-permute-done | bytes 16416 | tf_op jit(solution)/shard_map/ppermute | solution.py:20
  127.6 0.0 copy-done.3
  127.6 0.0 copy-done.6
  127.6 0.0 copy-start.7
  127.6 0.6 copy-done.7
  128.2 4.7 %rtl.1 = f32[512,512]{1,0:T(8,128)} custom-call(bf16[512,512]{1,0:T(8,128)(2,1)} %bitcast.11, bf16[512,512]{1,0:T(8,128)(2,1)} %bitcast.19, bf16[512,512]{1,0:T(8,128)(2,1)} %copy-done.2, bf16[512,512]{1,0:T(8,128)(2,1)} %copy-done.3, f32[8,512]{1,0:T(8,128)} %get-tuple-element.16.s0_ref, f32[8,512]{1,0:T(8,128)} %copy-done.6, f32[8,512]{1,0:T(8,128)} %copy-done.7), custom_call_target="tpu_custom_call" | custom-call | flops 1610612736 | bytes 3145728 | tf_op jit(solution)/shard_map/rtl/pallas_call | solution.py:187
Async XLA Ops:
  2.1 15.3 %all-to-all-start = ((s32[16,1,1]{2,1,0:T(1,128)}), s32[16,1,1]{2,1,0:T(1,128)S(1)}, u32[]{:S(2)}, u32[]{:S(2)}) async-start(s32[16,1,1]{2,1,0:T(1,128)} %copy.9), calls=%async_computation | async-start | bytes 16384 | tf_op jit(solution)/shard_map/all_to_all | solution.py:211
  13.7 9.4 %copy-start = (bf16[1,512,512]{2,1,0:T(8,128)(2,1)S(1)}, bf16[1,512,512]{2,1,0:T(8,128)(2,1)}, u32[]{:S(2)}) copy-start(bf16[1,512,512]{2,1,0:T(8,128)(2,1)} %param.5) | copy-start | bytes 1572868
  13.7 11.5 %copy-start.1 = (bf16[1,512,512]{2,1,0:T(8,128)(2,1)S(1)}, bf16[1,512,512]{2,1,0:T(8,128)(2,1)}, u32[]{:S(2)}) copy-start(bf16[1,512,512]{2,1,0:T(8,128)(2,1)} %param.4) | copy-start | bytes 1572868
  17.4 78.3 %all-to-all-start.1 = ((bf16[32,128,512]{2,1,0:T(8,128)(2,1)}), bf16[32,128,512]{2,1,0:T(8,128)(2,1)}, u32[]{:S(2)}, u32[]{:S(2)}) async-start(bf16[32,128,512]{2,1,0:T(8,128)(2,1)} %pack.1), calls=%async_computation.1 | async-start | bytes 8388608 | tf_op jit(solution)/shard_map/all_to_all | solution.py:209
  23.1 22.0 %collective-permute-start = (bf16[512,512]{1,0:T(8,128)(2,1)S(1)}, bf16[512,512]{1,0:T(8,128)(2,1)S(1)}, u32[]{:S(2)}, u32[]{:S(2)}) collective-permute-start(bf16[512,512]{1,0:T(8,128)(2,1)S(1)} %bitcast.12), channel_id=1, source_target_pairs={{31,0},{0,1},{1,2},{2,3},{3,4},{4,5},{5,6},{6,7},{7,8},{8,9},{9,10... | collective-permute-start | bytes 1572872 | tf_op jit(solution)/shard_map/ppermute | solution.py:20
  25.2 21.8 %collective-permute-start.2 = (bf16[512,512]{1,0:T(8,128)(2,1)S(1)}, bf16[512,512]{1,0:T(8,128)(2,1)S(1)}, u32[]{:S(2)}, u32[]{:S(2)}) collective-permute-start(bf16[512,512]{1,0:T(8,128)(2,1)S(1)} %bitcast.20), channel_id=1, source_target_pairs={{1,0},{2,1},{3,2},{4,3},{5,4},{6,5},{7,6},{8,7},{9,8},{10,9},{11,1... | collective-permute-start | bytes 1572872 | tf_op jit(solution)/shard_map/ppermute | solution.py:20
  45.1 17.6 %copy-start.4 = (bf16[512,512]{1,0:T(8,128)(2,1)}, bf16[512,512]{1,0:T(8,128)(2,1)S(1)}, u32[]{:S(2)}) copy-start(bf16[512,512]{1,0:T(8,128)(2,1)S(1)} %collective-permute-done.k1_ref) | copy-start | bytes 1572868
  45.1 17.6 %collective-permute-start.1 = (bf16[512,512]{1,0:T(8,128)(2,1)S(1)}, bf16[512,512]{1,0:T(8,128)(2,1)S(1)}, u32[]{:S(2)}, u32[]{:S(2)}) collective-permute-start(bf16[512,512]{1,0:T(8,128)(2,1)S(1)} %collective-permute-done.k1_ref), channel_id=1, source_target_pairs={{31,0},{0,1},{1,2},{2,3},{3,4},{4,5},{5,6},{6,7},{7,8},{8,9},{9,10... | collective-permute-start | bytes 1572872 | tf_op jit(solution)/shard_map/ppermute | solution.py:20
  47.1 64.0 %copy-start.2 = (bf16[512,512]{1,0:T(8,128)(2,1)}, bf16[512,512]{1,0:T(8,128)(2,1)S(1)}, u32[]{:S(2)}) copy-start(bf16[512,512]{1,0:T(8,128)(2,1)S(1)} %collective-permute-done.2.n1_ref) | copy-start | bytes 1572868
  47.1 75.7 %collective-permute-start.3 = (bf16[512,512]{1,0:T(8,128)(2,1)S(1)}, bf16[512,512]{1,0:T(8,128)(2,1)S(1)}, u32[]{:S(2)}, u32[]{:S(2)}) collective-permute-start(bf16[512,512]{1,0:T(8,128)(2,1)S(1)} %collective-permute-done.2.n1_ref), channel_id=1, source_target_pairs={{1,0},{2,1},{3,2},{4,3},{5,4},{6,5},{7,6},{8,7},{9,8},{10,9},{11,1... | collective-permute-start | bytes 1572872 | tf_op jit(solution)/shard_map/ppermute | solution.py:20
  62.7 0.8 copy-start.5
  111.1 11.7 %collective-permute-start.4 = (f32[8,512]{1,0:T(8,128)}, f32[8,512]{1,0:T(8,128)S(1)}, u32[]{:S(2)}, u32[]{:S(2)}) collective-permute-start(f32[8,512]{1,0:T(8,128)} %get-tuple-element.16.s0_ref), channel_id=1, source_target_pairs={{1,0},{2,1},{3,2},{4,3},{5,4},{6,5},{7,6},{8,7},{9,8},{10,9},{11,1... | collective-permute-start | bytes 49160 | tf_op jit(solution)/shard_map/ppermute | solution.py:20
  120.8 6.7 %collective-permute-start.5 = (f32[8,512]{1,0:T(8,128)}, f32[8,512]{1,0:T(8,128)S(1)}, u32[]{:S(2)}, u32[]{:S(2)}) collective-permute-start(f32[8,512]{1,0:T(8,128)} %get-tuple-element.16.s0_ref), channel_id=1, source_target_pairs={{2,0},{3,1},{4,2},{5,3},{6,4},{7,5},{8,6},{9,7},{10,8},{11,9},{12,... | collective-permute-start | bytes 49160 | tf_op jit(solution)/shard_map/ppermute | solution.py:20
  122.8 4.8 %copy-start.3 = (bf16[512,512]{1,0:T(8,128)(2,1)}, bf16[512,512]{1,0:T(8,128)(2,1)S(1)}, u32[]{:S(2)}) copy-start(bf16[512,512]{1,0:T(8,128)(2,1)S(1)} %collective-permute-done.3.n2_ref) | copy-start | bytes 1572868
  122.8 4.8 %copy-start.6 = (f32[8,512]{1,0:T(8,128)}, f32[8,512]{1,0:T(8,128)S(1)}, u32[]{:S(2)}) copy-start(f32[8,512]{1,0:T(8,128)S(1)} %collective-permute-done.4.s1_ref) | copy-start | bytes 49156
  127.6 0.6 copy-start.7

commit v2 on v1

v2 whole, which is shorter than its diff:
```python
import functools
import math

import jax
import jax.numpy as jnp
from jax import lax
from jax.experimental import pallas as pl
from jax.experimental.pallas import tpu as pltpu
from jax.sharding import PartitionSpec as P

BLOCK = 128
CAP = 2
CHUNK = 256
VMEM_LIMIT = 28 * 1024 * 1024
ABSENT = 1024.0


def passed_along(block, axis, distance):
    devices = range(lax.axis_size(axis))
    route = [((i - distance) % len(devices), i) for i in devices]
    return lax.ppermute(block, axis, route)


def nt_dot(a, b):
    return lax.dot_general(a, b, (((1,), (1,)), ((), ())), preferred_element_type=jnp.float32)


def whole(space=pltpu.VMEM):
    return pl.BlockSpec(memory_space=space)


def pack_kernel(entries, me, targets, picks, tile, out, place, used, mark, sems, mark_sems):
    column = (me[0] >> 1) & 1
    slots = out.shape[0]
    mark[...] = jnp.full(mark.shape, ABSENT, mark.dtype)
    for s in range(slots):
        used[s] = 0
    for j in range(entries):
        t = targets[j]
        rank = jnp.int32(0)
        for j2 in range(j):
            rank += (targets[j2] == t).astype(jnp.int32)
        slot = ((t >> 2) * 2 + (t & 1)) * CAP + jnp.minimum(rank, CAP - 1)
        place[j] = jnp.where(((t >> 1) & 1) == column, slot, -1)

        @pl.when(place[j] >= 0)
        def _(j=j):
            used[place[j]] = 1
            pltpu.make_async_copy(tile.at[picks[j]], out.at[place[j]], sems.at[j]).start()

    rows, lanes = mark.shape
    for s in range(slots):
        @pl.when(used[s] == 0)
        def _(s=s):
            pltpu.make_async_copy(mark, out.at[s, pl.ds(0, rows), pl.ds(0, lanes)], mark_sems.at[s]).start()

    for j in range(entries):
        @pl.when(place[j] >= 0)
        def _(j=j):
            pltpu.make_async_copy(tile.at[picks[j]], out.at[place[j]], sems.at[j]).wait()

    for s in range(slots):
        @pl.when(used[s] == 0)
        def _(s=s):
            pltpu.make_async_copy(mark, out.at[s, pl.ds(0, rows), pl.ds(0, lanes)], mark_sems.at[s]).wait()


def pack(me, targets, picks, tile, places):
    entries = targets.shape[0]
    blocks, rows, feature = tile.shape
    slots = places * CAP
    return pl.pallas_call(
        functools.partial(pack_kernel, entries),
        out_shape=jax.ShapeDtypeStruct((slots, rows, feature), tile.dtype),
        in_specs=[whole(pltpu.SMEM)] * 3 + [whole()],
        out_specs=whole(pl.ANY),
        scratch_shapes=[
            pltpu.SMEM((entries,), jnp.int32),
            pltpu.SMEM((slots,), jnp.int32),
            pltpu.VMEM((16, 128), tile.dtype),
            pltpu.SemaphoreType.DMA((entries,)),
            pltpu.SemaphoreType.DMA((slots,)),
        ],
        compiler_params=pltpu.CompilerParams(vmem_limit_bytes=4 * 1024 * 1024),
        name="pack",
    )(me, targets, picks, tile)


def cycle_kernel(rate, q_ref, k0_ref, k1_ref, k2_ref, m_ref, l_ref, num_ref):
    q = q_ref[...]
    rows = q.shape[0]
    keys = [k0_ref[...], k1_ref[...], k2_ref[...]]
    scores = [nt_dot(q, k) for k in keys]
    m = jnp.max(jnp.maximum(jnp.maximum(scores[0], scores[1]), scores[2]), axis=1, keepdims=True)
    exps = [jnp.exp2((s - m) * rate) for s in scores]
    m_ref[...] = m
    l_ref[...] = jnp.sum(exps[0] + exps[1] + exps[2], axis=1, keepdims=True)
    num = jnp.zeros((rows, q.shape[1]), jnp.float32)
    for e, k in zip(exps, keys):
        num += jnp.dot(e.astype(jnp.bfloat16), k, preferred_element_type=jnp.float32)
    num_ref[...] = num


def cycle_part(rate, q, k0, k1, k2, rows=256):
    n, feature = q.shape
    block = pl.BlockSpec((rows, feature), lambda i: (i, 0))
    column = pl.BlockSpec((rows, 1), lambda i: (i, 0))
    full = pl.BlockSpec((n, feature), lambda i: (0, 0))
    col = jax.ShapeDtypeStruct((n, 1), jnp.float32)
    return pl.pallas_call(
        functools.partial(cycle_kernel, rate),
        grid=(n // rows,),
        out_shape=(col, col, jax.ShapeDtypeStruct((n, feature), jnp.float32)),
        in_specs=[block, full, full, full],
        out_specs=(column, column, block),
        compiler_params=pltpu.CompilerParams(vmem_limit_bytes=VMEM_LIMIT),
        cost_estimate=pl.CostEstimate(flops=4 * n * 3 * n * feature, bytes_accessed=4 * n * feature * 2 + n * feature * 4, transcendentals=3 * n * n),
        name="cycle",
    )(q, k0, k1, k2)


def hard_kernel(rate, scale, last, q_ref, k0_ref, m_ref, l_ref, num_ref, blocks, *rest):
    if last:
        num_out, loss_ref, stats_ref, scores, order = rest
    else:
        num_out, m_out, l_out, scores, order = rest
    n, feature = q_ref.shape
    slots = blocks.shape[0]
    per = CHUNK // BLOCK
    order[0] = 0
    live = jnp.int32(0)
    for s in range(slots):
        there = jnp.max(blocks[s, :16, :128].astype(jnp.float32)) < ABSENT / 2
        order[live] = s
        live += there.astype(jnp.int32)
    odd = (live & 1) == 1
    chunks = (live + 1) >> 1

    @pl.when(odd)
    def _():
        order[live] = order[live - 1]

    q = q_ref[...]

    def chunk_keys(i):
        return jnp.concatenate([blocks[order[i * per + p]] for p in range(per)], axis=0)

    def score(i, m):
        s = nt_dot(q, chunk_keys(i))
        scores[i] = s
        return jnp.maximum(m, jnp.maximum(s[:, :BLOCK], s[:, BLOCK:]))

    old = m_ref[...]
    wide = lax.fori_loop(0, chunks, score, jnp.broadcast_to(old, (n, BLOCK)))
    m = jnp.max(wide, axis=1, keepdims=True)
    shrink = jnp.exp2((old - m) * rate)
    num_out[...] = num_ref[...] * shrink

    @pl.when(odd)
    def _():
        scores[chunks - 1, :, BLOCK:] = jnp.full((n, BLOCK), -jnp.inf, jnp.float32)

    def weigh(i, l):
        e = jnp.exp2((scores[i] - m) * rate)
        num_out[...] += jnp.dot(e.astype(jnp.bfloat16), chunk_keys(i), preferred_element_type=jnp.float32)
        return l + (e[:, :BLOCK] + e[:, BLOCK:])

    l = lax.fori_loop(0, chunks, weigh, jnp.zeros((n, BLOCK), jnp.float32))
    total = jnp.sum(l, axis=1, keepdims=True) + l_ref[...] * shrink
    if not last:
        m_out[...] = m
        l_out[...] = total
        return
    inverse = 1.0 / total
    own = k0_ref[...].astype(jnp.float32)
    num_out[...] = (num_out[...] * inverse - own) * scale
    positive = jnp.sum(q.astype(jnp.float32) * own, axis=1, keepdims=True)
    loss = (m - positive) * scale + jnp.log(total)
    lane = lax.broadcasted_iota(jnp.int32, (n, BLOCK), 1)
    table = jnp.where(lane == 0, m, jnp.where(lane == 1, inverse, loss))
    flipped = table.T
    stats_ref[...] = flipped[:8]
    loss_ref[...] = flipped[2:3]


def hard_part(rate, scale, last, q, k0, m, l, num, blocks):
    n, feature = q.shape
    slots = blocks.shape[0]
    f32 = jnp.float32
    col = jax.ShapeDtypeStruct((n, 1), f32)
    ends = (jax.ShapeDtypeStruct((1, n), f32), jax.ShapeDtypeStruct((8, n), f32)) if last else (col, col)
    keys = slots * BLOCK
    return pl.pallas_call(
        functools.partial(hard_kernel, rate, scale, last),
        out_shape=(jax.ShapeDtypeStruct((n, feature), f32),) + ends,
        in_specs=[whole()] * 6,
        out_specs=(whole(), whole(), whole()),
        scratch_shapes=[pltpu.VMEM((keys // CHUNK, n, CHUNK), f32), pltpu.SMEM((slots + 1,), jnp.int32)],
        compiler_params=pltpu.CompilerParams(vmem_limit_bytes=VMEM_LIMIT),
        cost_estimate=pl.CostEstimate(flops=2 * n * keys * feature, bytes_accessed=2 * keys * feature, transcendentals=n * keys // 2),
        name="hard_last" if last else "hard_first",
    )(q, k0, m, l, num, blocks)


def rtl_kernel(rate, scale, k_ref, n0_ref, n1_ref, n2_ref, s0_ref, s1_ref, s2_ref, out_ref):
    k = k_ref[...]
    total = jnp.zeros(out_ref.shape, jnp.float32)
    for n_ref, s_ref in ((n0_ref, s0_ref), (n1_ref, s1_ref), (n2_ref, s2_ref)):
        rows = n_ref[...]
        s = nt_dot(k, rows)
        w = jnp.exp2((s - s_ref[0:1, :]) * rate) * s_ref[1:2, :]
        total += jnp.dot(w.astype(jnp.bfloat16), rows, preferred_element_type=jnp.float32)
    first = pl.multiple_of(pl.program_id(0) * k.shape[0], k.shape[0])
    own = n0_ref[pl.ds(first, k.shape[0]), :].astype(jnp.float32)
    out_ref[...] = (total - own) * scale


def rtl_part(rate, scale, k, n0, n1, n2, s0, s1, s2, rows=256):
    n, feature = k.shape
    block = pl.BlockSpec((rows, feature), lambda i: (i, 0))
    full = pl.BlockSpec((n, feature), lambda i: (0, 0))
    stat = pl.BlockSpec((8, n), lambda i: (0, 0))
    return pl.pallas_call(
        functools.partial(rtl_kernel, rate, scale),
        grid=(n // rows,),
        out_shape=jax.ShapeDtypeStruct((n, feature), jnp.float32),
        in_specs=[block, full, full, full, stat, stat, stat],
        out_specs=block,
        compiler_params=pltpu.CompilerParams(vmem_limit_bytes=VMEM_LIMIT),
        cost_estimate=pl.CostEstimate(flops=4 * n * 3 * n * feature, bytes_accessed=4 * n * feature * 2 + n * feature * 4, transcendentals=3 * n * n),
        name="rtl",
    )(k, n0, n1, n2, s0, s1, s2)


def body(netlist, rtl, hard_target, hard_block):
    queries = netlist[0]
    own_keys = rtl[0]
    row_count, feature = queries.shape
    scale = 3.0 / math.sqrt(feature)
    rate = scale * math.log2(math.e)
    groups = lax.axis_size("dp")
    me = lax.axis_index("dp")
    targets = hard_target[0, 0, :, 0]
    picks = hard_block[0, 0]
    entries = targets.shape[0]
    columns = [[g for g in range(groups) if (g // 2) % 2 == x] for x in range(2)]
    places = groups // 2

    def spread(packed):
        return lax.all_to_all(packed, "dp", split_axis=0, concat_axis=0, axis_index_groups=columns, tiled=True)

    at = jnp.full((1,), me, jnp.int32)
    swap = [(g, g ^ 2) for g in range(groups)]
    packed = pack(at, targets, picks, own_keys.reshape(-1, BLOCK, feature), places)
    first = spread(packed)
    partner = lax.ppermute(own_keys, "dp", swap)
    theirs = lax.ppermute(jnp.concatenate([targets, picks]), "dp", swap)
    rtl1 = passed_along(own_keys, "loop", 1)
    net1 = passed_along(queries, "loop", -1)
    partner, theirs, rtl1, net1 = lax.optimization_barrier((partner, theirs, rtl1, net1))
    second = spread(pack(at, theirs[:entries], theirs[entries:], partner.reshape(-1, BLOCK, feature), places))
    rtl2 = passed_along(rtl1, "loop", 1)
    net2 = passed_along(net1, "loop", -1)

    m, l, num = cycle_part(rate, queries, own_keys, rtl1, rtl2)
    num, m, l = hard_part(rate, scale, False, queries, own_keys, m, l, num, first)
    grad, loss, stats = hard_part(rate, scale, True, queries, own_keys, m, l, num, second)
    stats1 = passed_along(stats, "loop", -1)
    stats2 = passed_along(stats, "loop", -2)
    rtl_grad = rtl_part(rate, scale, own_keys, queries, net1, net2, stats, stats1, stats2)
    return (loss, grad[None], rtl_grad[None])


def solution(mesh):
    return jax.shard_map(
        body,
        mesh=mesh,
        in_specs=(
            P("dp", "loop", None),
            P("dp", "loop", None),
            P("dp", "loop", None, None),
            P("dp", "loop", None),
        ),
        out_specs=(P("dp", "loop"), P("dp", "loop", None), P("dp", "loop", None)),
        check_vma=False,
    )
```

time: 133 us -> 111 us (0.83)
  the two profiles are of different devices: /device:TPU:8 before, /device:TPU:9 now
where the time goes in v2:
time: 111 us; the launch traced here: 110 us
  starting transfers between devices  46.7 us (42%)
  Pallas kernels  27.3 us (25%)
  waiting for transfers between devices  24.7 us (22%)
  local copies, waits for them, and re-layouts  10.7 us (10%)
    ppermute x6, starting transfers between devices, passed_along(): return lax.ppermute(block, axis, route)  25.8 us
    all_to_all x2, starting transfers between devices, spread(): lax.all_to_all(packed, 'dp', split_axis=0, concat_axis=0, axis_index_grou...  15.5 us
    pallas_call x2, Pallas kernels, hard_part(): pl.pallas_call(functools.partial(hard_kernel, rate, scale, last), out_sha...  14.7 us
    ppermute x6, waiting for transfers between devices, passed_along(): return lax.ppermute(block, axis, route)  13.8 us
    ppermute x1, waiting for transfers between devices, body(): theirs = lax.ppermute(jnp.concatenate([targets, picks]), 'dp', swap)  10.9 us
    unnamed x30, local copies, waits for them, and re-layouts  10.7 us
    pallas_call x2, Pallas kernels, pack(): pl.pallas_call(functools.partial(pack_kernel, entries), out_shape=jax.Sha...  5.51 us
    pallas_call x1, Pallas kernels, rtl_part(): pl.pallas_call(functools.partial(rtl_kernel, rate, scale), grid=(n // row...  4.42 us
  transfers between devices with their start and end apart: 10, of which 3 were waited for; matrix products, arithmetic and copies ran while one was open for 0% of the time, Pallas kernels for 18%

profile of v2, /device:TPU:9, one launch (start us, length us, event | category | flops | bytes accessed | tf_op | source)
XLA Modules:
  0.0 110.3 jit_solution(4868727620134398353)
XLA Ops:
  0.6 0.0 copy-start.2
  0.6 1.0 copy-done.2
  1.7 0.0 copy-start.9
  1.7 0.7 copy-done.9
  2.3 0.7 copy-done.11
  3.0 2.8 %pack.2 = bf16[16,128,512]{2,1,0:T(8,128)(2,1)S(1)} custom-call(s32[1]{0:T(128)} %bitcast.4.me, s32[16]{0:T(128)S(1)} %bitcast.22, s32[16]{0:T(128)S(1)} %bitcast.24, bf16[4,128,512]{2,1,0:T(8,128)(2,1)S(1)} %bitcast.9), custom_call_target="tpu_custom_call" | custom-call | tf_op jit(solution)/shard_map/pack/pallas_call | solution.py:72
  5.8 0.0 copy-start
  5.8 1.3 %copy-done = bf16[16,128,512]{2,1,0:T(8,128)(2,1)} copy-done((bf16[16,128,512]{2,1,0:T(8,128)(2,1)}, bf16[16,128,512]{2,1,0:T(8,128)(2,1)S(1)}, u32[]{:S(2)}) %copy-start) | copy-done | bytes 2097176
  7.1 9.8 %all-to-all-start = ((bf16[16,128,512]{2,1,0:T(8,128)(2,1)}), bf16[16,128,512]{2,1,0:T(8,128)(2,1)S(1)}, u32[]{:S(2)}, u32[]{:S(2)}) async-start(bf16[16,128,512]{2,1,0:T(8,128)(2,1)} %copy-done), calls=%async_computation | async-start | bytes 4194304 | tf_op jit(solution)/shard_map/all_to_all | solution.py:250
  16.9 0.0 copy-done.3
  16.9 1.9 %collective-permute-start = (bf16[512,512]{1,0:T(8,128)(2,1)S(1)}, bf16[512,512]{1,0:T(8,128)(2,1)S(1)}, u32[]{:S(2)}, u32[]{:S(2)}) collective-permute-start(bf16[512,512]{1,0:T(8,128)(2,1)S(1)} %bitcast.10), channel_id=1, source_target_pairs={{0,64},{32,96},{64,0},{96,32},{128,192},{160,224},{192,128},{224,1... | collective-permute-start | bytes 1572872 | tf_op jit(solution)/shard_map/ppermute | solution.py:256
  18.8 2.0 %collective-permute-start.2 = (bf16[512,512]{1,0:T(8,128)(2,1)S(1)}, bf16[512,512]{1,0:T(8,128)(2,1)S(1)}, u32[]{:S(2)}, u32[]{:S(2)}) collective-permute-start(bf16[512,512]{1,0:T(8,128)(2,1)S(1)} %bitcast.11), channel_id=1, source_target_pairs={{31,0},{0,1},{1,2},{2,3},{3,4},{4,5},{5,6},{6,7},{7,8},{8,9},{9,10... | collective-permute-start | bytes 1572872 | tf_op jit(solution)/shard_map/ppermute | solution.py:21
  20.8 0.0 copy-done.4
  20.8 9.4 %collective-permute-start.3 = (bf16[512,512]{1,0:T(8,128)(2,1)S(1)}, bf16[512,512]{1,0:T(8,128)(2,1)}, u32[]{:S(2)}, u32[]{:S(2)}) collective-permute-start(bf16[512,512]{1,0:T(8,128)(2,1)S(1)} %bitcast.16), channel_id=1, source_target_pairs={{1,0},{2,1},{3,2},{4,3},{5,4},{6,5},{7,6},{8,7},{9,8},{10,9},{11,1... | collective-permute-start | bytes 1572872 | tf_op jit(solution)/shard_map/ppermute | solution.py:21
  30.2 0.0 copy-done.10
  30.2 0.0 copy-done.12
  30.2 0.1 pad_add_fusion
  30.3 3.5 %collective-permute-start.1 = (s32[32]{0:T(128)S(1)}, s32[32]{0:T(128)S(1)}, u32[]{:S(2)}, u32[]{:S(2)}) collective-permute-start(s32[32]{0:T(128)S(1)} %pad_add_fusion), channel_id=1, source_target_pairs={{0,64},{32,96},{64,0},{96,32},{128,192},{160,224},{192,128},{224,1... | collective-permute-start | bytes 392 | tf_op jit(solution)/shard_map/ppermute | solution.py:257
  33.7 10.9 %collective-permute-done.1 = s32[32]{0:T(128)S(1)} collective-permute-done((s32[32]{0:T(128)S(1)}, s32[32]{0:T(128)S(1)}, u32[]{:S(2)}, u32[]{:S(2)}) %collective-permute-start.1) | collective-permute-done | bytes 160 | tf_op jit(solution)/shard_map/ppermute | solution.py:257
  44.6 0.0 collective-permute-done
  44.6 0.0 collective-permute-done.2.k1_ref
  44.6 0.8 copy-done.13
  45.4 0.0 collective-permute-done.3.n1_ref
  45.4 0.1 fusion
  45.5 2.8 %pack.3 = bf16[16,128,512]{2,1,0:T(8,128)(2,1)S(1)} custom-call(s32[1]{0:T(128)} %bitcast.4.me, s32[16]{0:T(128)S(1)} %get-tuple-element.30.targets, s32[16]{0:T(128)S(1)} %get-tuple-element.29.picks, bf16[4,128,512]{2,1,0:T(8,128)(2,1)S(1)} %bitcast.21), custom_call_target="tpu_custom_call" | custom-call | tf_op jit(solution)/shard_map/pack/pallas_call | solution.py:72
  48.3 0.0 copy-start.1
  48.3 1.3 %copy-done.1 = bf16[16,128,512]{2,1,0:T(8,128)(2,1)} copy-done((bf16[16,128,512]{2,1,0:T(8,128)(2,1)}, bf16[16,128,512]{2,1,0:T(8,128)(2,1)S(1)}, u32[]{:S(2)}) %copy-start.1) | copy-done | bytes 2097176
  49.6 0.0 all-to-all-done.blocks
  49.6 5.7 %all-to-all-start.1 = ((bf16[16,128,512]{2,1,0:T(8,128)(2,1)}), bf16[16,128,512]{2,1,0:T(8,128)(2,1)}, u32[]{:S(2)}, u32[]{:S(2)}) async-start(bf16[16,128,512]{2,1,0:T(8,128)(2,1)} %copy-done.1), calls=%async_computation.1 | async-start | bytes 4194304 | tf_op jit(solution)/shard_map/all_to_all | solution.py:250
  55.3 1.9 %collective-permute-start.4 = (bf16[512,512]{1,0:T(8,128)(2,1)}, bf16[512,512]{1,0:T(8,128)(2,1)S(1)}, u32[]{:S(2)}, u32[]{:S(2)}) collective-permute-start(bf16[512,512]{1,0:T(8,128)(2,1)} %copy-done.13), channel_id=1, source_target_pairs={{31,0},{0,1},{1,2},{2,3},{3,4},{4,5},{5,6},{6,7},{7,8},{8,9},{9,10... | collective-permute-start | bytes 1572872 | tf_op jit(solution)/shard_map/ppermute | solution.py:21
  57.3 7.5 %collective-permute-start.5 = (bf16[512,512]{1,0:T(8,128)(2,1)}, bf16[512,512]{1,0:T(8,128)(2,1)}, u32[]{:S(2)}, u32[]{:S(2)}) collective-permute-start(bf16[512,512]{1,0:T(8,128)(2,1)} %collective-permute-done.3.n1_ref), channel_id=1, source_target_pairs={{1,0},{2,1},{3,2},{4,3},{5,4},{6,5},{7,6},{8,7},{9,8},{10,9},{11,1... | collective-permute-start | bytes 1572872 | tf_op jit(solution)/shard_map/ppermute | solution.py:21
  64.7 10.3 %collective-permute-done.4.k2_ref = bf16[512,512]{1,0:T(8,128)(2,1)S(1)} collective-permute-done((bf16[512,512]{1,0:T(8,128)(2,1)}, bf16[512,512]{1,0:T(8,128)(2,1)S(1)}, u32[]{:S(2)}, u32[]{:S(2)}) %collective-permute-start.4) | collective-permute-done | bytes 524320 | tf_op jit(solution)/shard_map/ppermute | solution.py:21
  75.0 1.0 copy-done.14
  76.0 2.6 %cycle.1 = (f32[512,1]{1,0:T(8,128)S(1)}, f32[512,1]{1,0:T(8,128)S(1)}, f32[512,512]{1,0:T(8,128)S(1)}) custom-call(bf16[512,512]{1,0:T(8,128)(2,1)S(1)} %bitcast.17, bf16[512,512]{1,0:T(8,128)(2,1)S(1)} %bitcast.12, bf16[512,512]{1,0:T(8,128)(2,1)S(1)} %copy-done.14, bf16[512,512]{1,0:T(8,128)(2,1)S(1)} %collective-permute-done.4.k2_ref), custom_call_target="tpu_custom_call" | custom-call | flops 1610612736 | bytes 3145728 | tf_op jit(solution)/shard_map/cycle/pallas_call | solution.py:110
  78.6 5.9 %hard_first.1 = (f32[512,512]{1,0:T(8,128)S(1)}, f32[512,1]{1,0:T(8,128)S(1)}, f32[512,1]{1,0:T(8,128)S(1)}) custom-call(bf16[512,512]{1,0:T(8,128)(2,1)S(1)} %bitcast.18, bf16[512,512]{1,0:T(8,128)(2,1)S(1)} %bitcast.13, f32[512,1]{1,0:T(8,128)S(1)} %get-tuple-element.17.m_ref, f32[512,1]{1,0:T(8,128)S(1)} %get-tuple-element.18.l_ref, ...), custom_call_target="tpu_custom_call" | custom-call | flops 1073741824 | bytes 2097152 | tf_op jit(solution)/shard_map/hard_first/pallas_call | solution.py:193
  84.6 0.0 copy-start.5
  84.6 1.0 copy-done.5
  85.5 0.7 copy-done.7
  86.2 0.0 all-to-all-done.1.blocks
  86.3 1.2 %copy-done.6 = f32[512,512]{1,0:T(8,128)S(1)} copy-done((f32[512,512]{1,0:T(8,128)S(1)}, f32[512,512]{1,0:T(8,128)}, u32[]{:S(2)}) %copy-start.6) | copy-done | bytes 1048600
  87.5 0.9 copy-done.8
  88.4 8.8 %hard_last.1 = (f32[512,512]{1,0:T(8,128)}, f32[1,512]{1,0:T(1,128)}, f32[8,512]{1,0:T(8,128)S(1)}) custom-call(bf16[512,512]{1,0:T(8,128)(2,1)S(1)} %bitcast.19, bf16[512,512]{1,0:T(8,128)(2,1)S(1)} %bitcast.14, f32[512,1]{1,0:T(8,128)S(1)} %get-tuple-element.20.m_ref, f32[512,1]{1,0:T(8,128)S(1)} %copy-done.8, f32[512,512]{1,0:T(8,128)S(1)} %copy-done.6, ...), custom_call_target="tpu_custom_call" | custom-call | flops 1073741824 | bytes 2097152 | tf_op jit(solution)/shard_map/hard_last/pallas_call | solution.py:193
  97.2 3.1 %collective-permute-start.6 = (f32[8,512]{1,0:T(8,128)S(1)}, f32[8,512]{1,0:T(8,128)S(1)}, u32[]{:S(2)}, u32[]{:S(2)}) collective-permute-start(f32[8,512]{1,0:T(8,128)S(1)} %get-tuple-element.28.s0_ref), channel_id=1, source_target_pairs={{1,0},{2,1},{3,2},{4,3},{5,4},{6,5},{7,6},{8,7},{9,8},{10,9},{11,1... | collective-permute-start | bytes 49160 | tf_op jit(solution)/shard_map/ppermute | solution.py:21
  100.4 1.9 %collective-permute-start.7 = (f32[8,512]{1,0:T(8,128)S(1)}, f32[8,512]{1,0:T(8,128)S(1)}, u32[]{:S(2)}, u32[]{:S(2)}) collective-permute-start(f32[8,512]{1,0:T(8,128)S(1)} %get-tuple-element.28.s0_ref), channel_id=1, source_target_pairs={{2,0},{3,1},{4,2},{5,3},{6,4},{7,5},{8,6},{9,7},{10,8},{11,9},{12,... | collective-permute-start | bytes 49160 | tf_op jit(solution)/shard_map/ppermute | solution.py:21
  102.3 0.0 collective-permute-done.5.n2_ref
  102.3 0.0 collective-permute-done.6.s1_ref
  102.3 3.6 %collective-permute-done.7.s2_ref = f32[8,512]{1,0:T(8,128)S(1)} collective-permute-done((f32[8,512]{1,0:T(8,128)S(1)}, f32[8,512]{1,0:T(8,128)S(1)}, u32[]{:S(2)}, u32[]{:S(2)}) %collective-permute-start.7) | collective-permute-done | bytes 16416 | tf_op jit(solution)/shard_map/ppermute | solution.py:21
  105.9 4.4 %rtl.1 = f32[512,512]{1,0:T(8,128)} custom-call(bf16[512,512]{1,0:T(8,128)(2,1)S(1)} %bitcast.15, bf16[512,512]{1,0:T(8,128)(2,1)S(1)} %bitcast.20, bf16[512,512]{1,0:T(8,128)(2,1)} %collective-permute-done.3.n1_ref, bf16[512,512]{1,0:T(8,128)(2,1)} %collective-permute-done.5.n2_ref, f32[8,512]{1,0:T(8,128)S(1)} %get-tuple-element.28.s0_ref, ...), custom_call_target="tpu_custom_call" | custom-call | flops 1610612736 | bytes 3145728 | tf_op jit(solution)/shard_map/rtl/pallas_call | solution.py:223
  (10 shorter events, 0.0 us)
Async XLA Ops:
  0.6 1.0 copy-start.2
  1.7 0.7 copy-start.9
  2.3 0.7 copy-start.11
  5.8 1.3 %copy-start = (bf16[16,128,512]{2,1,0:T(8,128)(2,1)}, bf16[16,128,512]{2,1,0:T(8,128)(2,1)S(1)}, u32[]{:S(2)}) copy-start(bf16[16,128,512]{2,1,0:T(8,128)(2,1)S(1)} %pack.2) | copy-start | bytes 6291460
  7.1 9.8 %copy-start.3 = (bf16[1,512,512]{2,1,0:T(8,128)(2,1)S(1)}, bf16[1,512,512]{2,1,0:T(8,128)(2,1)}, u32[]{:S(2)}) copy-start(bf16[1,512,512]{2,1,0:T(8,128)(2,1)} %param.5) | copy-start | bytes 1572868
  7.1 13.8 %copy-start.4 = (bf16[1,512,512]{2,1,0:T(8,128)(2,1)S(1)}, bf16[1,512,512]{2,1,0:T(8,128)(2,1)}, u32[]{:S(2)}) copy-start(bf16[1,512,512]{2,1,0:T(8,128)(2,1)} %param.4) | copy-start | bytes 1572868
  7.1 23.1 %copy-start.10 = (s32[1,1,16,1]{2,3,1,0:T(1,128)S(1)}, s32[1,1,16,1]{2,3,1,0:T(1,128)}, u32[]{:S(2)}) copy-start(s32[1,1,16,1]{2,3,1,0:T(1,128)} %param.6) | copy-start | bytes 196
  7.1 23.1 %copy-start.12 = (s32[1,1,16]{2,1,0:T(1,128)S(1)}, s32[1,1,16]{2,1,0:T(1,128)}, u32[]{:S(2)}) copy-start(s32[1,1,16]{2,1,0:T(1,128)} %param.7) | copy-start | bytes 196
  7.1 42.6 %all-to-all-start = ((bf16[16,128,512]{2,1,0:T(8,128)(2,1)}), bf16[16,128,512]{2,1,0:T(8,128)(2,1)S(1)}, u32[]{:S(2)}, u32[]{:S(2)}) async-start(bf16[16,128,512]{2,1,0:T(8,128)(2,1)} %copy-done), calls=%async_computation | async-start | bytes 4194304 | tf_op jit(solution)/shard_map/all_to_all | solution.py:250
  16.9 27.8 %collective-permute-start = (bf16[512,512]{1,0:T(8,128)(2,1)S(1)}, bf16[512,512]{1,0:T(8,128)(2,1)S(1)}, u32[]{:S(2)}, u32[]{:S(2)}) collective-permute-start(bf16[512,512]{1,0:T(8,128)(2,1)S(1)} %bitcast.10), channel_id=1, source_target_pairs={{0,64},{32,96},{64,0},{96,32},{128,192},{160,224},{192,128},{224,1... | collective-permute-start | bytes 1572872 | tf_op jit(solution)/shard_map/ppermute | solution.py:256
  18.8 25.9 %collective-permute-start.2 = (bf16[512,512]{1,0:T(8,128)(2,1)S(1)}, bf16[512,512]{1,0:T(8,128)(2,1)S(1)}, u32[]{:S(2)}, u32[]{:S(2)}) collective-permute-start(bf16[512,512]{1,0:T(8,128)(2,1)S(1)} %bitcast.11), channel_id=1, source_target_pairs={{31,0},{0,1},{1,2},{2,3},{3,4},{4,5},{5,6},{6,7},{7,8},{8,9},{9,10... | collective-permute-start | bytes 1572872 | tf_op jit(solution)/shard_map/ppermute | solution.py:21
  20.8 24.6 %collective-permute-start.3 = (bf16[512,512]{1,0:T(8,128)(2,1)S(1)}, bf16[512,512]{1,0:T(8,128)(2,1)}, u32[]{:S(2)}, u32[]{:S(2)}) collective-permute-start(bf16[512,512]{1,0:T(8,128)(2,1)S(1)} %bitcast.16), channel_id=1, source_target_pairs={{1,0},{2,1},{3,2},{4,3},{5,4},{6,5},{7,6},{8,7},{9,8},{10,9},{11,1... | collective-permute-start | bytes 1572872 | tf_op jit(solution)/shard_map/ppermute | solution.py:21
  30.3 14.3 %collective-permute-start.1 = (s32[32]{0:T(128)S(1)}, s32[32]{0:T(128)S(1)}, u32[]{:S(2)}, u32[]{:S(2)}) collective-permute-start(s32[32]{0:T(128)S(1)} %pad_add_fusion), channel_id=1, source_target_pairs={{0,64},{32,96},{64,0},{96,32},{128,192},{160,224},{192,128},{224,1... | collective-permute-start | bytes 392 | tf_op jit(solution)/shard_map/ppermute | solution.py:257
  44.6 0.8 copy-start.13
  48.3 1.4 %copy-start.1 = (bf16[16,128,512]{2,1,0:T(8,128)(2,1)}, bf16[16,128,512]{2,1,0:T(8,128)(2,1)S(1)}, u32[]{:S(2)}) copy-start(bf16[16,128,512]{2,1,0:T(8,128)(2,1)S(1)} %pack.3) | copy-start | bytes 6291460
  49.6 36.6 %all-to-all-start.1 = ((bf16[16,128,512]{2,1,0:T(8,128)(2,1)}), bf16[16,128,512]{2,1,0:T(8,128)(2,1)}, u32[]{:S(2)}, u32[]{:S(2)}) async-start(bf16[16,128,512]{2,1,0:T(8,128)(2,1)} %copy-done.1), calls=%async_computation.1 | async-start | bytes 4194304 | tf_op jit(solution)/shard_map/all_to_all | solution.py:250
  55.3 19.6 %collective-permute-start.4 = (bf16[512,512]{1,0:T(8,128)(2,1)}, bf16[512,512]{1,0:T(8,128)(2,1)S(1)}, u32[]{:S(2)}, u32[]{:S(2)}) collective-permute-start(bf16[512,512]{1,0:T(8,128)(2,1)} %copy-done.13), channel_id=1, source_target_pairs={{31,0},{0,1},{1,2},{2,3},{3,4},{4,5},{5,6},{6,7},{7,8},{8,9},{9,10... | collective-permute-start | bytes 1572872 | tf_op jit(solution)/shard_map/ppermute | solution.py:21
  57.3 45.0 %collective-permute-start.5 = (bf16[512,512]{1,0:T(8,128)(2,1)}, bf16[512,512]{1,0:T(8,128)(2,1)}, u32[]{:S(2)}, u32[]{:S(2)}) collective-permute-start(bf16[512,512]{1,0:T(8,128)(2,1)} %collective-permute-done.3.n1_ref), channel_id=1, source_target_pairs={{1,0},{2,1},{3,2},{4,3},{5,4},{6,5},{7,6},{8,7},{9,8},{10,9},{11,1... | collective-permute-start | bytes 1572872 | tf_op jit(solution)/shard_map/ppermute | solution.py:21
  75.0 1.0 copy-start.14
  84.6 1.0 copy-start.5
  85.5 0.7 copy-start.7
  86.3 1.2 %copy-start.6 = (f32[512,512]{1,0:T(8,128)S(1)}, f32[512,512]{1,0:T(8,128)}, u32[]{:S(2)}) copy-start(f32[512,512]{1,0:T(8,128)} %copy-done.5) | copy-start | bytes 3145732
  87.5 0.9 copy-start.8
  97.2 5.1 %collective-permute-start.6 = (f32[8,512]{1,0:T(8,128)S(1)}, f32[8,512]{1,0:T(8,128)S(1)}, u32[]{:S(2)}, u32[]{:S(2)}) collective-permute-start(f32[8,512]{1,0:T(8,128)S(1)} %get-tuple-element.28.s0_ref), channel_id=1, source_target_pairs={{1,0},{2,1},{3,2},{4,3},{5,4},{6,5},{7,6},{8,7},{9,8},{10,9},{11,1... | collective-permute-start | bytes 49160 | tf_op jit(solution)/shard_map/ppermute | solution.py:21
  100.4 5.5 %collective-permute-start.7 = (f32[8,512]{1,0:T(8,128)S(1)}, f32[8,512]{1,0:T(8,128)S(1)}, u32[]{:S(2)}, u32[]{:S(2)}) collective-permute-start(f32[8,512]{1,0:T(8,128)S(1)} %get-tuple-element.28.s0_ref), channel_id=1, source_target_pairs={{2,0},{3,1},{4,2},{5,3},{6,4},{7,5},{8,6},{9,7},{10,8},{11,9},{12,... | collective-permute-start | bytes 49160 | tf_op jit(solution)/shard_map/ppermute | solution.py:21

commit v3 on v2

v3 whole, which is shorter than its diff:
```python
import functools
import math

import jax
import jax.numpy as jnp
from jax import lax
from jax.experimental import pallas as pl
from jax.experimental.pallas import tpu as pltpu
from jax.sharding import PartitionSpec as P

BLOCK = 128
CAP = 2
CHUNK = 256
VMEM_LIMIT = 28 * 1024 * 1024
BIG_GRANT = 60 * 1024 * 1024
ABSENT = 1024.0
LANES = 128


def passed_along(block, axis, distance):
    devices = range(lax.axis_size(axis))
    route = [((i - distance) % len(devices), i) for i in devices]
    return lax.ppermute(block, axis, route)


def nt_dot(a, b):
    return lax.dot_general(a, b, (((1,), (1,)), ((), ())), preferred_element_type=jnp.float32)


def whole(space=pltpu.VMEM):
    return pl.BlockSpec(memory_space=space)


def shared(slots, entries, out, tile, place, used, seen, mark, sems, mark_sems, column, target_of, pick_of):
    mark[...] = jnp.full(mark.shape, ABSENT, mark.dtype)
    for s in range(slots):
        used[s] = 0
        seen[s] = 0
    for j in range(entries):
        t = target_of(j)
        rank = seen[t]
        seen[t] = rank + 1
        slot = ((t >> 2) * 2 + (t & 1)) * CAP + jnp.minimum(rank, CAP - 1)
        place[j] = jnp.where(((t >> 1) & 1) == column, slot, -1)

        @pl.when(place[j] >= 0)
        def _(j=j):
            used[place[j]] = 1
            pltpu.make_async_copy(tile.at[pick_of(j)], out.at[place[j]], sems.at[j]).start()

    rows, lanes = mark.shape
    for s in range(slots):
        @pl.when(used[s] == 0)
        def _(s=s):
            pltpu.make_async_copy(mark, out.at[s, pl.ds(0, rows), pl.ds(0, lanes)], mark_sems.at[s]).start()

    def finish():
        for j in range(entries):
            @pl.when(place[j] >= 0)
            def _(j=j):
                pltpu.make_async_copy(tile.at[pick_of(j)], out.at[place[j]], sems.at[j]).wait()

        for s in range(slots):
            @pl.when(used[s] == 0)
            def _(s=s):
                pltpu.make_async_copy(mark, out.at[s, pl.ds(0, rows), pl.ds(0, lanes)], mark_sems.at[s]).wait()

    return finish


def own_kernel(entries, me, targets, picks, rtl, out, mail, target_s, pick_s, tile, head, place, used, seen, mark, sems, mark_sems, in_sems):
    lists = [pltpu.make_async_copy(targets, target_s, in_sems.at[0]), pltpu.make_async_copy(picks, pick_s, in_sems.at[1])]
    load = pltpu.make_async_copy(rtl, tile, in_sems.at[2])
    for copy in lists + [load]:
        copy.start()
    for copy in lists:
        copy.wait()
    load.wait()
    blocks = tile.shape[0]
    store = pltpu.make_async_copy(tile, mail.at[pl.ds(0, blocks)], in_sems.at[3])
    store.start()
    column = (me[0] >> 1) & 1
    finish = shared(out.shape[0], entries, out, tile, place, used, seen, mark, sems, mark_sems, column, lambda j: target_s[j], lambda j: pick_s[j])
    lane = lax.broadcasted_iota(jnp.int32, head.shape, 1)
    line = jnp.zeros(head.shape, jnp.int32)
    for j in range(entries):
        line = jnp.where(lane == j, target_s[j], line)
        line = jnp.where(lane == entries + j, pick_s[j], line)
    head[...] = line.astype(jnp.float32).astype(head.dtype)
    rows, lanes = head.shape
    note = pltpu.make_async_copy(head, mail.at[blocks, pl.ds(0, rows), pl.ds(0, lanes)], in_sems.at[4])
    note.start()
    finish()
    store.wait()
    note.wait()


def pack_own(me, targets, picks, tile, places):
    entries = targets.shape[0]
    blocks, rows, feature = tile.shape
    slots = places * CAP
    hbm = whole(pltpu.HBM)
    return pl.pallas_call(
        functools.partial(own_kernel, entries),
        out_shape=(jax.ShapeDtypeStruct((slots, rows, feature), tile.dtype), jax.ShapeDtypeStruct((blocks + 1, rows, feature), tile.dtype)),
        in_specs=[whole(pltpu.SMEM), hbm, hbm, hbm],
        out_specs=(hbm, hbm),
        scratch_shapes=[
            pltpu.SMEM((entries,), jnp.int32),
            pltpu.SMEM((entries,), jnp.int32),
            pltpu.VMEM(tile.shape, tile.dtype),
            pltpu.VMEM((16, 128), tile.dtype),
            pltpu.SMEM((entries,), jnp.int32),
            pltpu.SMEM((slots,), jnp.int32),
            pltpu.SMEM((slots,), jnp.int32),
            pltpu.VMEM((16, 128), tile.dtype),
            pltpu.SemaphoreType.DMA((entries,)),
            pltpu.SemaphoreType.DMA((slots,)),
            pltpu.SemaphoreType.DMA((5,)),
        ],
        compiler_params=pltpu.CompilerParams(vmem_limit_bytes=BIG_GRANT),
        name="pack_own",
    )(me, targets, picks, tile)


def far_kernel(entries, me, mail, out, list_v, list_s, tile, head, place, used, seen, mark, sems, mark_sems, in_sems):
    blocks = tile.shape[0]
    rows, lanes = head.shape
    note = pltpu.make_async_copy(mail.at[blocks, pl.ds(0, rows), pl.ds(0, lanes)], head, in_sems.at[0])
    load = pltpu.make_async_copy(mail.at[pl.ds(0, blocks)], tile, in_sems.at[1])
    note.start()
    load.start()
    note.wait()
    list_v[...] = head[...].astype(jnp.float32)[:8].astype(jnp.int32)
    down = pltpu.make_async_copy(list_v, list_s, in_sems.at[2])
    down.start()
    down.wait()
    load.wait()
    column = (me[0] >> 1) & 1
    shared(out.shape[0], entries, out, tile, place, used, seen, mark, sems, mark_sems, column, lambda j: list_s[0, j], lambda j: list_s[0, entries + j])()


def pack_far(me, mail, places, entries):
    blocks, rows, feature = mail.shape
    slots = places * CAP
    hbm = whole(pltpu.HBM)
    return pl.pallas_call(
        functools.partial(far_kernel, entries),
        out_shape=jax.ShapeDtypeStruct((slots, rows, feature), mail.dtype),
        in_specs=[whole(pltpu.SMEM), hbm],
        out_specs=hbm,
        scratch_shapes=[
            pltpu.VMEM((8, 128), jnp.int32),
            pltpu.SMEM((8, 128), jnp.int32),
            pltpu.VMEM((blocks - 1, rows, feature), mail.dtype),
            pltpu.VMEM((16, 128), mail.dtype),
            pltpu.SMEM((entries,), jnp.int32),
            pltpu.SMEM((slots,), jnp.int32),
            pltpu.SMEM((slots,), jnp.int32),
            pltpu.VMEM((16, 128), mail.dtype),
            pltpu.SemaphoreType.DMA((entries,)),
            pltpu.SemaphoreType.DMA((slots,)),
            pltpu.SemaphoreType.DMA((3,)),
        ],
        compiler_params=pltpu.CompilerParams(vmem_limit_bytes=BIG_GRANT),
        name="pack_far",
    )(me, mail)


def cycle_kernel(rate, tiles, q_ref, *refs):
    q = q_ref[...]
    rows, feature = q.shape
    keys = [ref[...] for ref in refs[:tiles]]
    state_in, state_ref = (None, refs[tiles]) if len(refs) == tiles + 1 else refs[tiles:]
    scores = [nt_dot(q, k) for k in keys]
    m = jnp.max(functools.reduce(jnp.maximum, scores), axis=1, keepdims=True)
    if state_in is not None:
        old = state_in[:, feature : feature + 1]
        m = jnp.maximum(m, old)
    exps = [jnp.exp2((s - m) * rate) for s in scores]
    l = jnp.sum(functools.reduce(jnp.add, exps), axis=1, keepdims=True)
    num = jnp.zeros((rows, feature), jnp.float32)
    if state_in is not None:
        shrink = jnp.exp2((old - m) * rate)
        l += state_in[:, feature + 1 : feature + 2] * shrink
        num = state_in[:, :feature] * shrink
    for e, k in zip(exps, keys):
        num += jnp.dot(e.astype(jnp.bfloat16), k, preferred_element_type=jnp.float32)
    state_ref[:, :feature] = num
    lane = lax.broadcasted_iota(jnp.int32, (rows, LANES), 1)
    state_ref[:, feature:] = jnp.where(lane == 0, m, l)


def cycle_part(rate, q, keys, states, rows=256):
    n, feature = q.shape
    tiles = len(keys)
    block = pl.BlockSpec((rows, feature), lambda i: (i, 0))
    wide = pl.BlockSpec((rows, feature + LANES), lambda i: (i, 0))
    full = pl.BlockSpec((n, feature), lambda i: (0, 0))
    return pl.pallas_call(
        functools.partial(cycle_kernel, rate, tiles),
        grid=(n // rows,),
        out_shape=jax.ShapeDtypeStruct((n, feature + LANES), jnp.float32),
        in_specs=[block] + [full] * tiles + [wide] * len(states),
        out_specs=wide,
        compiler_params=pltpu.CompilerParams(vmem_limit_bytes=VMEM_LIMIT),
        cost_estimate=pl.CostEstimate(flops=4 * n * tiles * n * feature, bytes_accessed=(tiles + 3) * n * feature * 2, transcendentals=tiles * n * n),
        name="cycle_more" if states else "cycle",
    )(q, *keys, *states)


def hard_kernel(rate, scale, last, q_ref, k0_ref, state_in, blocks, *rest):
    if last:
        num, loss_ref, stats_ref, state, keys, scores, order, sems, state_sem = rest
    else:
        state_out, state, keys, scores, order, sems, state_sem = rest
    n, feature = q_ref.shape
    slots = blocks.shape[0]
    loads = [pltpu.make_async_copy(blocks.at[s], keys.at[s], sems.at[s]) for s in range(slots)]
    for load in loads:
        load.start()
    restore = pltpu.make_async_copy(state_in, state, state_sem.at[0])
    restore.start()
    live = jnp.int32(0)
    for s in range(slots):
        loads[s].wait()
        there = jnp.max(keys[s, :16, :128].astype(jnp.float32)) < ABSENT / 2
        order[live] = s
        live += there.astype(jnp.int32)
    odd = (live & 1) == 1
    pairs = (live + 1) >> 1
    fours = pairs >> 1
    single = (pairs & 1) == 1

    @pl.when(odd)
    def _():
        order[live] = order[live - 1]

    q = q_ref[...]

    def some_keys(pair, count):
        return jnp.concatenate([keys[order[pair * 2 + p]] for p in range(2 * count)], axis=0)

    def score(pair, count, m):
        s = nt_dot(q, some_keys(pair, count))
        for c in range(count):
            scores[pair + c] = s[:, c * CHUNK : (c + 1) * CHUNK]
        for c in range(2 * count):
            m = jnp.maximum(m, s[:, c * BLOCK : (c + 1) * BLOCK])
        return m

    wide = lax.fori_loop(0, fours, lambda i, m: score(2 * i, 2, m), jnp.full((n, BLOCK), -jnp.inf, jnp.float32))
    wide = lax.fori_loop(2 * fours, pairs, lambda i, m: score(i, 1, m), wide)
    restore.wait()
    old = state[:, feature : feature + 1]
    m = jnp.maximum(jnp.max(wide, axis=1, keepdims=True), old)
    shrink = jnp.exp2((old - m) * rate)
    kept = state[:, feature + 1 : feature + 2] * shrink
    if not last:
        num = state.at[:, pl.ds(0, feature)]
    num[...] = state[:, :feature] * shrink

    @pl.when(odd)
    def _():
        scores[pairs - 1, :, BLOCK:] = jnp.full((n, BLOCK), -jnp.inf, jnp.float32)

    def weigh(pair, count, l):
        parts = [jnp.exp2((scores[pair + c] - m) * rate) for c in range(count)]
        e = parts[0] if count == 1 else jnp.concatenate(parts, axis=1)
        num[...] += jnp.dot(e.astype(jnp.bfloat16), some_keys(pair, count), preferred_element_type=jnp.float32)
        for part in parts:
            l = l + (part[:, :BLOCK] + part[:, BLOCK:])
        return l

    l = lax.fori_loop(0, fours, lambda i, l: weigh(2 * i, 2, l), jnp.zeros((n, BLOCK), jnp.float32))
    l = lax.fori_loop(2 * fours, pairs, lambda i, l: weigh(i, 1, l), l)
    total = jnp.sum(l, axis=1, keepdims=True) + kept
    lane = lax.broadcasted_iota(jnp.int32, (n, LANES), 1)
    if not last:
        state[:, feature:] = jnp.where(lane == 0, m, total)
        save = pltpu.make_async_copy(state, state_out, state_sem.at[0])
        save.start()
        save.wait()
        return
    inverse = 1.0 / total
    own = k0_ref[...].astype(jnp.float32)
    num[...] = (num[...] * inverse - own) * scale
    positive = jnp.sum(q.astype(jnp.float32) * own, axis=1, keepdims=True)
    loss = (m - positive) * scale + jnp.log(total)
    table = jnp.where(lane == 0, m, jnp.where(lane == 1, inverse, loss))
    flipped = table.T
    stats_ref[...] = flipped[:8]
    loss_ref[...] = flipped[2:3]


def hard_part(rate, scale, last, q, k0, state, blocks):
    n, feature = q.shape
    slots = blocks.shape[0]
    f32 = jnp.float32
    shapes = [jax.ShapeDtypeStruct(state.shape, f32)]
    specs = [whole(pltpu.HBM)]
    if last:
        shapes = [jax.ShapeDtypeStruct((n, feature), f32), jax.ShapeDtypeStruct((1, n), f32), jax.ShapeDtypeStruct((8, n), f32)]
        specs = [whole()] * 3
    keys = slots * BLOCK
    return pl.pallas_call(
        functools.partial(hard_kernel, rate, scale, last),
        out_shape=shapes,
        in_specs=[whole(), whole(), whole(pl.ANY), whole(pl.ANY)],
        out_specs=specs,
        scratch_shapes=[
            pltpu.VMEM(state.shape, f32),
            pltpu.VMEM(blocks.shape, blocks.dtype),
            pltpu.VMEM((keys // CHUNK, n, CHUNK), f32),
            pltpu.SMEM((slots + 1,), jnp.int32),
            pltpu.SemaphoreType.DMA((slots,)),
            pltpu.SemaphoreType.DMA((1,)),
        ],
        compiler_params=pltpu.CompilerParams(vmem_limit_bytes=BIG_GRANT),
        cost_estimate=pl.CostEstimate(flops=2 * n * keys * feature, bytes_accessed=2 * keys * feature, transcendentals=n * keys // 2),
        name="hard_last" if last else "hard_first",
    )(q, k0, state, blocks)


def rtl_kernel(rate, scale, tiles, k_ref, *refs):
    n_refs, s_refs = refs[:tiles], refs[tiles : 2 * tiles]
    base_ref, out_ref = refs[2 * tiles :]
    k = k_ref[...]
    total = -base_ref[...].astype(jnp.float32) if tiles == 1 else base_ref[...]
    for n_ref, s_ref in zip(n_refs, s_refs):
        rows = n_ref[...]
        s = nt_dot(k, rows)
        w = jnp.exp2((s - s_ref[0:1, :]) * rate) * s_ref[1:2, :]
        total += jnp.dot(w.astype(jnp.bfloat16), rows, preferred_element_type=jnp.float32)
    out_ref[...] = total if tiles == 1 else total * scale


def rtl_part(rate, scale, k, nets, stats, base, rows=256):
    n, feature = k.shape
    tiles = len(nets)
    block = pl.BlockSpec((rows, feature), lambda i: (i, 0))
    full = pl.BlockSpec((n, feature), lambda i: (0, 0))
    stat = pl.BlockSpec((8, n), lambda i: (0, 0))
    return pl.pallas_call(
        functools.partial(rtl_kernel, rate, scale, tiles),
        grid=(n // rows,),
        out_shape=jax.ShapeDtypeStruct((n, feature), jnp.float32),
        in_specs=[block] + [full] * tiles + [stat] * tiles + [block],
        out_specs=block,
        compiler_params=pltpu.CompilerParams(vmem_limit_bytes=VMEM_LIMIT),
        cost_estimate=pl.CostEstimate(flops=4 * n * tiles * n * feature, bytes_accessed=(tiles + 3) * n * feature * 2, transcendentals=tiles * n * n),
        name="rtl_own" if tiles == 1 else "rtl_others",
    )(k, *nets, *stats, base)


def body(netlist, rtl, hard_target, hard_block):
    queries = netlist[0]
    own_keys = rtl[0]
    feature = queries.shape[1]
    scale = 3.0 / math.sqrt(feature)
    rate = scale * math.log2(math.e)
    groups = lax.axis_size("dp")
    targets = hard_target[0, 0, :, 0]
    picks = hard_block[0, 0]
    columns = [[g for g in range(groups) if (g // 2) % 2 == x] for x in range(2)]
    places = groups // 2

    def spread(packed):
        return lax.all_to_all(packed, "dp", split_axis=0, concat_axis=0, axis_index_groups=columns, tiled=True)

    at = jnp.full((1,), lax.axis_index("dp"), jnp.int32)
    packed, mail = pack_own(at, targets, picks, own_keys.reshape(-1, BLOCK, feature), places)
    first = spread(packed)
    mail = lax.ppermute(mail, "dp", [(g, g ^ 2) for g in range(groups)])
    rtl1 = passed_along(own_keys, "loop", 1)
    net1 = passed_along(queries, "loop", -1)
    rtl2 = passed_along(own_keys, "loop", 2)
    net2 = passed_along(queries, "loop", -2)
    mail, rtl1, net1 = lax.optimization_barrier((mail, rtl1, net1))
    second = spread(pack_far(at, mail, places, targets.shape[0]))

    state = cycle_part(rate, queries, [own_keys, rtl1], [])
    (state,) = hard_part(rate, scale, False, queries, own_keys, state, first)
    state = cycle_part(rate, queries, [rtl2], [state])
    grad, loss, stats = hard_part(rate, scale, True, queries, own_keys, state, second)
    stats1 = passed_along(stats, "loop", -1)
    stats2 = passed_along(stats, "loop", -2)
    begun = rtl_part(rate, scale, own_keys, [queries], [stats], queries)
    rtl_grad = rtl_part(rate, scale, own_keys, [net1, net2], [stats1, stats2], begun)
    return (loss, grad[None], rtl_grad[None])


def solution(mesh):
    return jax.shard_map(
        body,
        mesh=mesh,
        in_specs=(
            P("dp", "loop", None),
            P("dp", "loop", None),
            P("dp", "loop", None, None),
            P("dp", "loop", None),
        ),
        out_specs=(P("dp", "loop"), P("dp", "loop", None), P("dp", "loop", None)),
        check_vma=False,
    )
```

time: 111 us -> 109 us (0.982)
  the two profiles are of different devices: /device:TPU:9 before, /device:TPU:1 now
where the time goes in v3:
time: 109 us; the launch traced here: 107 us
  starting transfers between devices  41.5 us (38%)
  Pallas kernels  31.5 us (29%)
  waiting for transfers between devices  28.3 us (26%)
  local copies, waits for them, and re-layouts  5.02 us (5%)
    ppermute x6, starting transfers between devices, passed_along(): return lax.ppermute(block, axis, route)  22.8 us
    ppermute x6, waiting for transfers between devices, passed_along(): return lax.ppermute(block, axis, route)  21.5 us
    all_to_all x2, starting transfers between devices, spread(): lax.all_to_all(packed, 'dp', split_axis=0, concat_axis=0, axis_index_grou...  16.7 us
    pallas_call x2, Pallas kernels, hard_part(): pl.pallas_call(functools.partial(hard_kernel, rate, scale, last), out_sha...  16 us
    ppermute x1, waiting for transfers between devices, body(): mail = lax.ppermute(mail, 'dp', [(g, g ^ 2) for g in range(groups)])  6.81 us
    pallas_call x2, Pallas kernels, cycle_part(): pl.pallas_call(functools.partial(cycle_kernel, rate, tiles), grid=(n // r...  5.42 us
    unnamed x16, local copies, waits for them, and re-layouts  5.02 us
    pallas_call x2, Pallas kernels, rtl_part(): pl.pallas_call(functools.partial(rtl_kernel, rate, scale, tiles), grid=(n...  4.96 us
  transfers between devices with their start and end apart: 9, of which 5 were waited for; matrix products, arithmetic and copies ran while one was open for 0% of the time, Pallas kernels for 25%

profile of v3, /device:TPU:1, one launch (start us, length us, event | category | flops | bytes accessed | tf_op | source)
XLA Modules:
  0.0 107.2 jit_solution(8963149647983076548)
XLA Ops:
  0.6 2.5 %pack_own.1 = (bf16[16,128,512]{2,1,0:T(8,128)(2,1)}, bf16[5,128,512]{2,1,0:T(8,128)(2,1)}) custom-call(s32[1]{0:T(128)} %bitcast.2.me, s32[16]{0:T(128)} %bitcast.16, s32[16]{0:T(128)} %bitcast.17, bf16[4,128,512]{2,1,0:T(8,128)(2,1)} %bitcast.8), custom_call_target="tpu_custom_call" | custom-call | tf_op jit(solution)/shard_map/pack_own/pallas_call | solution.py:103
  3.2 0.0 copy-start.7
  3.2 0.0 copy-start
  3.2 11.3 %all-to-all-start = ((bf16[16,128,512]{2,1,0:T(8,128)(2,1)}), bf16[16,128,512]{2,1,0:T(8,128)(2,1)}, u32[]{:S(2)}, u32[]{:S(2)}) async-start(bf16[16,128,512]{2,1,0:T(8,128)(2,1)} %get-tuple-element.13), calls=%async_computation | async-start | bytes 4194304 | tf_op jit(solution)/shard_map/all_to_all | solution.py:369
  14.5 0.0 copy-done.7
  14.5 1.9 %collective-permute-start.1 = (bf16[5,128,512]{2,1,0:T(8,128)(2,1)S(1)}, bf16[5,128,512]{2,1,0:T(8,128)(2,1)S(1)}, u32[]{:S(2)}, u32[]{:S(2)}) collective-permute-start(bf16[5,128,512]{2,1,0:T(8,128)(2,1)S(1)} %copy-done.7), channel_id=1, source_target_pairs={{0,64},{32,96},{64,0},{96,32},{128,192},{160,224},{192,128},{224,1... | collective-permute-start | bytes 1966088 | tf_op jit(solution)/shard_map/ppermute | solution.py:374
  16.4 0.0 copy-done
  16.4 1.9 %collective-permute-start.2 = (bf16[512,512]{1,0:T(8,128)(2,1)S(1)}, bf16[512,512]{1,0:T(8,128)(2,1)S(1)}, u32[]{:S(2)}, u32[]{:S(2)}) collective-permute-start(bf16[512,512]{1,0:T(8,128)(2,1)S(1)} %bitcast.11), channel_id=1, source_target_pairs={{31,0},{0,1},{1,2},{2,3},{3,4},{4,5},{5,6},{6,7},{7,8},{8,9},{9,10... | collective-permute-start | bytes 1572872 | tf_op jit(solution)/shard_map/ppermute | solution.py:23
  18.3 8.8 %collective-permute-start.3 = (bf16[512,512]{1,0:T(8,128)(2,1)}, bf16[512,512]{1,0:T(8,128)(2,1)S(1)}, u32[]{:S(2)}, u32[]{:S(2)}) collective-permute-start(bf16[512,512]{1,0:T(8,128)(2,1)} %bitcast.q_ref.refs_0_.refs_2_), channel_id=1, source_target_pairs={{1,0},{2,1},{3,2},{4,3},{5,4},{6,5},{7,6},{8,7},{9,8},{10,9},{11,1... | collective-permute-start | bytes 1572872 | tf_op jit(solution)/shard_map/ppermute | solution.py:23
  27.1 10.3 %collective-permute-done.2.refs_1_ = bf16[512,512]{1,0:T(8,128)(2,1)S(1)} collective-permute-done((bf16[512,512]{1,0:T(8,128)(2,1)S(1)}, bf16[512,512]{1,0:T(8,128)(2,1)S(1)}, u32[]{:S(2)}, u32[]{:S(2)}) %collective-permute-start.2) | collective-permute-done | bytes 524320 | tf_op jit(solution)/shard_map/ppermute | solution.py:23
  37.4 1.1 %collective-permute-done.3.refs_0_ = bf16[512,512]{1,0:T(8,128)(2,1)S(1)} collective-permute-done((bf16[512,512]{1,0:T(8,128)(2,1)}, bf16[512,512]{1,0:T(8,128)(2,1)S(1)}, u32[]{:S(2)}, u32[]{:S(2)}) %collective-permute-start.3) | collective-permute-done | bytes 524320 | tf_op jit(solution)/shard_map/ppermute | solution.py:23
  38.5 6.8 %collective-permute-done.1.mail = bf16[5,128,512]{2,1,0:T(8,128)(2,1)S(1)} collective-permute-done((bf16[5,128,512]{2,1,0:T(8,128)(2,1)S(1)}, bf16[5,128,512]{2,1,0:T(8,128)(2,1)S(1)}, u32[]{:S(2)}, u32[]{:S(2)}) %collective-permute-start.1) | collective-permute-done | bytes 655392 | tf_op jit(solution)/shard_map/ppermute | solution.py:374
  45.3 0.0 copy-start.6
  45.3 0.8 copy-done.6
  46.1 2.6 %pack_far.1 = bf16[16,128,512]{2,1,0:T(8,128)(2,1)} custom-call(s32[1]{0:T(128)} %bitcast.2.me, bf16[5,128,512]{2,1,0:T(8,128)(2,1)} %copy-done.6), custom_call_target="tpu_custom_call" | custom-call | tf_op jit(solution)/shard_map/pack_far/pallas_call | solution.py:147
  48.7 0.0 all-to-all-done.blocks
  48.7 5.5 %all-to-all-start.1 = ((bf16[16,128,512]{2,1,0:T(8,128)(2,1)}), bf16[16,128,512]{2,1,0:T(8,128)(2,1)}, u32[]{:S(2)}, u32[]{:S(2)}) async-start(bf16[16,128,512]{2,1,0:T(8,128)(2,1)} %pack_far.1), calls=%async_computation.1 | async-start | bytes 4194304 | tf_op jit(solution)/shard_map/all_to_all | solution.py:369
  54.2 1.9 %collective-permute-start = (bf16[512,512]{1,0:T(8,128)(2,1)S(1)}, bf16[512,512]{1,0:T(8,128)(2,1)S(1)}, u32[]{:S(2)}, u32[]{:S(2)}) collective-permute-start(bf16[512,512]{1,0:T(8,128)(2,1)S(1)} %bitcast.12), channel_id=1, source_target_pairs={{30,0},{31,1},{0,2},{1,3},{2,4},{3,5},{4,6},{5,7},{6,8},{7,9},{8,1... | collective-permute-start | bytes 1572872 | tf_op jit(solution)/shard_map/ppermute | solution.py:23
  56.1 6.4 %collective-permute-start.4 = (bf16[512,512]{1,0:T(8,128)(2,1)}, bf16[512,512]{1,0:T(8,128)(2,1)S(1)}, u32[]{:S(2)}, u32[]{:S(2)}) collective-permute-start(bf16[512,512]{1,0:T(8,128)(2,1)} %bitcast.q_ref.refs_0_.refs_2_), channel_id=1, source_target_pairs={{2,0},{3,1},{4,2},{5,3},{6,4},{7,5},{8,6},{9,7},{10,8},{11,9},{12,... | collective-permute-start | bytes 1572872 | tf_op jit(solution)/shard_map/ppermute | solution.py:23
  62.5 2.9 %cycle.1.state_in = f32[512,640]{1,0:T(8,128)S(1)} custom-call(bf16[512,512]{1,0:T(8,128)(2,1)} %bitcast.q_ref.refs_0_.refs_2_, bf16[512,512]{1,0:T(8,128)(2,1)S(1)} %bitcast.13, bf16[512,512]{1,0:T(8,128)(2,1)S(1)} %collective-permute-done.2.refs_1_), custom_call_target="tpu_custom_call" | custom-call | flops 1073741824 | bytes 2621440 | tf_op jit(solution)/shard_map/cycle/pallas_call | solution.py:200
  65.4 0.0 copy-start.4
  65.4 1.0 copy-done.4
  66.4 7.9 %hard_first.1.refs_1_ = f32[512,640]{1,0:T(8,128)} custom-call(bf16[512,512]{1,0:T(8,128)(2,1)} %bitcast.q_ref.refs_0_.refs_2_, bf16[512,512]{1,0:T(8,128)(2,1)} %bitcast.9, f32[512,640]{1,0:T(8,128)} %copy-done.4, bf16[16,128,512]{2,1,0:T(8,128)(2,1)} %all-to-all-done.blocks), custom_call_target="tpu_custom_call" | custom-call | flops 1073741824 | bytes 2097152 | tf_op jit(solution)/shard_map/hard_first/pallas_call | solution.py:306
  74.3 9.6 %collective-permute-done.refs_0_ = bf16[512,512]{1,0:T(8,128)(2,1)S(1)} collective-permute-done((bf16[512,512]{1,0:T(8,128)(2,1)S(1)}, bf16[512,512]{1,0:T(8,128)(2,1)S(1)}, u32[]{:S(2)}, u32[]{:S(2)}) %collective-permute-start) | collective-permute-done | bytes 524320 | tf_op jit(solution)/shard_map/ppermute | solution.py:23
  83.9 0.0 copy-start.3
  83.9 1.3 %copy-done.3 = f32[512,640]{1,0:T(8,128)S(1)} copy-done((f32[512,640]{1,0:T(8,128)S(1)}, f32[512,640]{1,0:T(8,128)}, u32[]{:S(2)}) %copy-start.3) | copy-done | bytes 1310744
  85.2 2.5 %cycle_more.1.state_in = f32[512,640]{1,0:T(8,128)S(1)} custom-call(bf16[512,512]{1,0:T(8,128)(2,1)} %bitcast.q_ref.refs_0_.refs_2_, bf16[512,512]{1,0:T(8,128)(2,1)S(1)} %collective-permute-done.refs_0_, f32[512,640]{1,0:T(8,128)S(1)} %copy-done.3), custom_call_target="tpu_custom_call" | custom-call | flops 536870912 | bytes 2097152 | tf_op jit(solution)/shard_map/cycle_more/pallas_call | solution.py:200
  87.7 0.0 copy-start.2
  87.8 1.1 %copy-done.2 = f32[512,640]{1,0:T(8,128)} copy-done((f32[512,640]{1,0:T(8,128)}, f32[512,640]{1,0:T(8,128)S(1)}, u32[]{:S(2)}) %copy-start.2) | copy-done | bytes 1310744
  88.8 0.0 copy-start.1
  88.9 0.0 all-to-all-done.1.blocks
  88.9 8.1 %hard_last.1 = (f32[512,512]{1,0:T(8,128)}, f32[1,512]{1,0:T(1,128)}, f32[8,512]{1,0:T(8,128)}) custom-call(bf16[512,512]{1,0:T(8,128)(2,1)} %bitcast.q_ref.refs_0_.refs_2_, bf16[512,512]{1,0:T(8,128)(2,1)} %bitcast.10, f32[512,640]{1,0:T(8,128)} %copy-done.2, bf16[16,128,512]{2,1,0:T(8,128)(2,1)} %all-to-all-done.1.blocks), custom_call_target="tpu_custom_call" | custom-call | flops 1073741824 | bytes 2097152 | tf_op jit(solution)/shard_map/hard_last/pallas_call | solution.py:306
  97.0 1.9 %collective-permute-start.5 = (f32[8,512]{1,0:T(8,128)}, f32[8,512]{1,0:T(8,128)S(1)}, u32[]{:S(2)}, u32[]{:S(2)}) collective-permute-start(f32[8,512]{1,0:T(8,128)} %get-tuple-element.18.refs_1_), channel_id=1, source_target_pairs={{1,0},{2,1},{3,2},{4,3},{5,4},{6,5},{7,6},{8,7},{9,8},{10,9},{11,1... | collective-permute-start | bytes 49160 | tf_op jit(solution)/shard_map/ppermute | solution.py:23
  98.9 1.9 %collective-permute-start.6 = (f32[8,512]{1,0:T(8,128)}, f32[8,512]{1,0:T(8,128)S(1)}, u32[]{:S(2)}, u32[]{:S(2)}) collective-permute-start(f32[8,512]{1,0:T(8,128)} %get-tuple-element.18.refs_1_), channel_id=1, source_target_pairs={{2,0},{3,1},{4,2},{5,3},{6,4},{7,5},{8,6},{9,7},{10,8},{11,9},{12,... | collective-permute-start | bytes 49160 | tf_op jit(solution)/shard_map/ppermute | solution.py:23
  100.8 0.0 copy-done.1
  100.9 0.0 copy-start.5
  100.9 0.7 copy-done.5
  101.6 2.3 %rtl_own.1.refs_4_ = f32[512,512]{1,0:T(8,128)S(1)} custom-call(bf16[512,512]{1,0:T(8,128)(2,1)S(1)} %bitcast.14, bf16[512,512]{1,0:T(8,128)(2,1)} %bitcast.q_ref.refs_0_.refs_2_, f32[8,512]{1,0:T(8,128)S(1)} %copy-done.5, bf16[512,512]{1,0:T(8,128)(2,1)} %bitcast.q_ref.refs_0_.refs_2_), custom_call_target="tpu_custom_call" | custom-call | flops 536870912 | bytes 2097152 | tf_op jit(solution)/shard_map/rtl_own/pallas_call | solution.py:344
  103.9 0.0 collective-permute-done.4.refs_1_
  103.9 0.0 collective-permute-done.5.refs_2_
  103.9 0.6 collective-permute-done.6.refs_3_
  104.5 2.6 %rtl_others.1 = f32[512,512]{1,0:T(8,128)} custom-call(bf16[512,512]{1,0:T(8,128)(2,1)S(1)} %bitcast.15, bf16[512,512]{1,0:T(8,128)(2,1)S(1)} %collective-permute-done.3.refs_0_, bf16[512,512]{1,0:T(8,128)(2,1)S(1)} %collective-permute-done.4.refs_1_, f32[8,512]{1,0:T(8,128)S(1)} %collective-permute-done.5.refs_2_, ...), custom_call_target="tpu_custom_call" | custom-call | flops 1073741824 | bytes 2621440 | tf_op jit(solution)/shard_map/rtl_others/pallas_call | solution.py:344
Async XLA Ops:
  3.2 11.3 %copy-start.7 = (bf16[5,128,512]{2,1,0:T(8,128)(2,1)S(1)}, bf16[5,128,512]{2,1,0:T(8,128)(2,1)}, u32[]{:S(2)}) copy-start(bf16[5,128,512]{2,1,0:T(8,128)(2,1)} %get-tuple-element.11) | copy-start | bytes 1966084
  3.2 13.2 %copy-start = (bf16[1,512,512]{2,1,0:T(8,128)(2,1)S(1)}, bf16[1,512,512]{2,1,0:T(8,128)(2,1)}, u32[]{:S(2)}) copy-start(bf16[1,512,512]{2,1,0:T(8,128)(2,1)} %param.5) | copy-start | bytes 1572868
  3.2 45.5 %all-to-all-start = ((bf16[16,128,512]{2,1,0:T(8,128)(2,1)}), bf16[16,128,512]{2,1,0:T(8,128)(2,1)}, u32[]{:S(2)}, u32[]{:S(2)}) async-start(bf16[16,128,512]{2,1,0:T(8,128)(2,1)} %get-tuple-element.13), calls=%async_computation | async-start | bytes 4194304 | tf_op jit(solution)/shard_map/all_to_all | solution.py:369
  14.5 30.8 %collective-permute-start.1 = (bf16[5,128,512]{2,1,0:T(8,128)(2,1)S(1)}, bf16[5,128,512]{2,1,0:T(8,128)(2,1)S(1)}, u32[]{:S(2)}, u32[]{:S(2)}) collective-permute-start(bf16[5,128,512]{2,1,0:T(8,128)(2,1)S(1)} %copy-done.7), channel_id=1, source_target_pairs={{0,64},{32,96},{64,0},{96,32},{128,192},{160,224},{192,128},{224,1... | collective-permute-start | bytes 1966088 | tf_op jit(solution)/shard_map/ppermute | solution.py:374
  16.4 21.0 %collective-permute-start.2 = (bf16[512,512]{1,0:T(8,128)(2,1)S(1)}, bf16[512,512]{1,0:T(8,128)(2,1)S(1)}, u32[]{:S(2)}, u32[]{:S(2)}) collective-permute-start(bf16[512,512]{1,0:T(8,128)(2,1)S(1)} %bitcast.11), channel_id=1, source_target_pairs={{31,0},{0,1},{1,2},{2,3},{3,4},{4,5},{5,6},{6,7},{7,8},{8,9},{9,10... | collective-permute-start | bytes 1572872 | tf_op jit(solution)/shard_map/ppermute | solution.py:23
  18.3 20.1 %collective-permute-start.3 = (bf16[512,512]{1,0:T(8,128)(2,1)}, bf16[512,512]{1,0:T(8,128)(2,1)S(1)}, u32[]{:S(2)}, u32[]{:S(2)}) collective-permute-start(bf16[512,512]{1,0:T(8,128)(2,1)} %bitcast.q_ref.refs_0_.refs_2_), channel_id=1, source_target_pairs={{1,0},{2,1},{3,2},{4,3},{5,4},{6,5},{7,6},{8,7},{9,8},{10,9},{11,1... | collective-permute-start | bytes 1572872 | tf_op jit(solution)/shard_map/ppermute | solution.py:23
  45.3 0.8 copy-start.6
  48.7 40.1 %all-to-all-start.1 = ((bf16[16,128,512]{2,1,0:T(8,128)(2,1)}), bf16[16,128,512]{2,1,0:T(8,128)(2,1)}, u32[]{:S(2)}, u32[]{:S(2)}) async-start(bf16[16,128,512]{2,1,0:T(8,128)(2,1)} %pack_far.1), calls=%async_computation.1 | async-start | bytes 4194304 | tf_op jit(solution)/shard_map/all_to_all | solution.py:369
  54.2 29.7 %collective-permute-start = (bf16[512,512]{1,0:T(8,128)(2,1)S(1)}, bf16[512,512]{1,0:T(8,128)(2,1)S(1)}, u32[]{:S(2)}, u32[]{:S(2)}) collective-permute-start(bf16[512,512]{1,0:T(8,128)(2,1)S(1)} %bitcast.12), channel_id=1, source_target_pairs={{30,0},{31,1},{0,2},{1,3},{2,4},{3,5},{4,6},{5,7},{6,8},{7,9},{8,1... | collective-permute-start | bytes 1572872 | tf_op jit(solution)/shard_map/ppermute | solution.py:23
  56.1 47.8 %collective-permute-start.4 = (bf16[512,512]{1,0:T(8,128)(2,1)}, bf16[512,512]{1,0:T(8,128)(2,1)S(1)}, u32[]{:S(2)}, u32[]{:S(2)}) collective-permute-start(bf16[512,512]{1,0:T(8,128)(2,1)} %bitcast.q_ref.refs_0_.refs_2_), channel_id=1, source_target_pairs={{2,0},{3,1},{4,2},{5,3},{6,4},{7,5},{8,6},{9,7},{10,8},{11,9},{12,... | collective-permute-start | bytes 1572872 | tf_op jit(solution)/shard_map/ppermute | solution.py:23
  65.4 1.0 copy-start.4
  83.9 1.3 %copy-start.3 = (f32[512,640]{1,0:T(8,128)S(1)}, f32[512,640]{1,0:T(8,128)}, u32[]{:S(2)}) copy-start(f32[512,640]{1,0:T(8,128)} %hard_first.1.refs_1_) | copy-start | bytes 3932164
  87.7 1.1 %copy-start.2 = (f32[512,640]{1,0:T(8,128)}, f32[512,640]{1,0:T(8,128)S(1)}, u32[]{:S(2)}) copy-start(f32[512,640]{1,0:T(8,128)S(1)} %cycle_more.1.state_in) | copy-start | bytes 3932164
  88.8 12.0 %copy-start.1 = (bf16[1,512,512]{2,1,0:T(8,128)(2,1)S(1)}, bf16[1,512,512]{2,1,0:T(8,128)(2,1)}, u32[]{:S(2)}) copy-start(bf16[1,512,512]{2,1,0:T(8,128)(2,1)} %param.5) | copy-start | bytes 1572868
  97.0 6.9 %collective-permute-start.5 = (f32[8,512]{1,0:T(8,128)}, f32[8,512]{1,0:T(8,128)S(1)}, u32[]{:S(2)}, u32[]{:S(2)}) collective-permute-start(f32[8,512]{1,0:T(8,128)} %get-tuple-element.18.refs_1_), channel_id=1, source_target_pairs={{1,0},{2,1},{3,2},{4,3},{5,4},{6,5},{7,6},{8,7},{9,8},{10,9},{11,1... | collective-permute-start | bytes 49160 | tf_op jit(solution)/shard_map/ppermute | solution.py:23
  98.9 5.6 %collective-permute-start.6 = (f32[8,512]{1,0:T(8,128)}, f32[8,512]{1,0:T(8,128)S(1)}, u32[]{:S(2)}, u32[]{:S(2)}) collective-permute-start(f32[8,512]{1,0:T(8,128)} %get-tuple-element.18.refs_1_), channel_id=1, source_target_pairs={{2,0},{3,1},{4,2},{5,3},{6,4},{7,5},{8,6},{9,7},{10,8},{11,9},{12,... | collective-permute-start | bytes 49160 | tf_op jit(solution)/shard_map/ppermute | solution.py:23
  100.9 0.7 copy-start.5

commit v4 on v3

--- a/solution.py
+++ b/solution.py
@@ -10,7 +10,7 @@
 
 BLOCK = 128
 CAP = 2
-CHUNK = 256
+CHUNK = 512
 VMEM_LIMIT = 28 * 1024 * 1024
 BIG_GRANT = 60 * 1024 * 1024
 ABSENT = 1024.0
@@ -188,7 +188,13 @@
         num += jnp.dot(e.astype(jnp.bfloat16), k, preferred_element_type=jnp.float32)
     state_ref[:, :feature] = num
     lane = lax.broadcasted_iota(jnp.int32, (rows, LANES), 1)
-    state_ref[:, feature:] = jnp.where(lane == 0, m, l)
+    if state_in is not None:
+        positive = state_in[:, feature + 2 : feature + 3]
+    else:
+        first = pl.multiple_of(pl.program_id(0) * rows, rows)
+        own = refs[0][pl.ds(first, rows), :]
+        positive = jnp.sum(q.astype(jnp.float32) * own.astype(jnp.float32), axis=1, keepdims=True)
+    state_ref[:, feature:] = jnp.where(lane == 0, m, jnp.where(lane == 1, l, positive))
 
 
 def cycle_part(rate, q, keys, states, rows=256):
@@ -209,148 +215,154 @@
     )(q, *keys, *states)
 
 
-def hard_kernel(rate, scale, last, q_ref, k0_ref, state_in, blocks, *rest):
+def hard_kernel(rate, scale, last, q_hbm, k_hbm, state_in, blocks, *rest):
     if last:
-        num, loss_ref, stats_ref, state, keys, scores, order, sems, state_sem = rest
+        grad, loss_ref, stats_ref, q_ref, k_ref, state, keys, scores, order, sems, out_sems = rest
     else:
-        state_out, state, keys, scores, order, sems, state_sem = rest
+        state_out, q_ref, state, keys, scores, order, sems, out_sems = rest
     n, feature = q_ref.shape
     slots = blocks.shape[0]
-    loads = [pltpu.make_async_copy(blocks.at[s], keys.at[s], sems.at[s]) for s in range(slots)]
-    for load in loads:
-        load.start()
-    restore = pltpu.make_async_copy(state_in, state, state_sem.at[0])
-    restore.start()
+    per = CHUNK // BLOCK
+    load_keys = pltpu.make_async_copy(blocks, keys, sems.at[0])
+    load_q = pltpu.make_async_copy(q_hbm, q_ref, sems.at[1])
+    load_state = pltpu.make_async_copy(state_in, state, sems.at[2])
+    load_keys.start()
+    load_q.start()
+    load_state.start()
+    if last:
+        load_own = pltpu.make_async_copy(k_hbm, k_ref, sems.at[3])
+        load_own.start()
+    load_keys.wait()
+    there = [(jnp.max(keys[s, :16, :128].astype(jnp.float32)) < ABSENT / 2).astype(jnp.int32) for s in range(slots)]
     live = jnp.int32(0)
     for s in range(slots):
-        loads[s].wait()
-        there = jnp.max(keys[s, :16, :128].astype(jnp.float32)) < ABSENT / 2
         order[live] = s
-        live += there.astype(jnp.int32)
-    odd = (live & 1) == 1
-    pairs = (live + 1) >> 1
-    fours = pairs >> 1
-    single = (pairs & 1) == 1
-
-    @pl.when(odd)
-    def _():
-        order[live] = order[live - 1]
-
+        live += there[s]
+    chunks = (live + per - 1) // per
+    tail = order[jnp.maximum(live - 1, 0)]
+    for p in range(per - 1):
+        order[live + p] = tail
+
+    def chunk_keys(i):
+        return jnp.concatenate([keys[order[i * per + p]] for p in range(per)], axis=0)
+
+    load_q.wait()
     q = q_ref[...]
 
-    def some_keys(pair, count):
-        return jnp.concatenate([keys[order[pair * 2 + p]] for p in range(2 * count)], axis=0)
-
-    def score(pair, count, m):
-        s = nt_dot(q, some_keys(pair, count))
-        for c in range(count):
-            scores[pair + c] = s[:, c * CHUNK : (c + 1) * CHUNK]
-        for c in range(2 * count):
+    def score(i, m):
+        s = nt_dot(q, chunk_keys(i))
+        scores[i] = s
+        for c in range(per):
             m = jnp.maximum(m, s[:, c * BLOCK : (c + 1) * BLOCK])
         return m
 
-    wide = lax.fori_loop(0, fours, lambda i, m: score(2 * i, 2, m), jnp.full((n, BLOCK), -jnp.inf, jnp.float32))
-    wide = lax.fori_loop(2 * fours, pairs, lambda i, m: score(i, 1, m), wide)
-    restore.wait()
+    wide = lax.fori_loop(0, chunks, score, jnp.full((n, BLOCK), -jnp.inf, jnp.float32))
+    load_state.wait()
     old = state[:, feature : feature + 1]
     m = jnp.maximum(jnp.max(wide, axis=1, keepdims=True), old)
     shrink = jnp.exp2((old - m) * rate)
     kept = state[:, feature + 1 : feature + 2] * shrink
-    if not last:
-        num = state.at[:, pl.ds(0, feature)]
-    num[...] = state[:, :feature] * shrink
-
-    @pl.when(odd)
-    def _():
-        scores[pairs - 1, :, BLOCK:] = jnp.full((n, BLOCK), -jnp.inf, jnp.float32)
-
-    def weigh(pair, count, l):
-        parts = [jnp.exp2((scores[pair + c] - m) * rate) for c in range(count)]
-        e = parts[0] if count == 1 else jnp.concatenate(parts, axis=1)
-        num[...] += jnp.dot(e.astype(jnp.bfloat16), some_keys(pair, count), preferred_element_type=jnp.float32)
-        for part in parts:
-            l = l + (part[:, :BLOCK] + part[:, BLOCK:])
+    state[:, :feature] = state[:, :feature] * shrink
+    for p in range(1, per):
+        @pl.when(((chunks - 1) * per + p >= live) & (chunks > 0))
+        def _(p=p):
+            scores[chunks - 1, :, p * BLOCK : (p + 1) * BLOCK] = jnp.full((n, BLOCK), -jnp.inf, jnp.float32)
+
+    def weigh(i, l):
+        e = jnp.exp2((scores[i] - m) * rate)
+        state[:, :feature] += jnp.dot(e.astype(jnp.bfloat16), chunk_keys(i), preferred_element_type=jnp.float32)
+        for c in range(per):
+            l = l + e[:, c * BLOCK : (c + 1) * BLOCK]
         return l
 
-    l = lax.fori_loop(0, fours, lambda i, l: weigh(2 * i, 2, l), jnp.zeros((n, BLOCK), jnp.float32))
-    l = lax.fori_loop(2 * fours, pairs, lambda i, l: weigh(i, 1, l), l)
+    l = lax.fori_loop(0, chunks, weigh, jnp.zeros((n, BLOCK), jnp.float32))
     total = jnp.sum(l, axis=1, keepdims=True) + kept
     lane = lax.broadcasted_iota(jnp.int32, (n, LANES), 1)
     if not last:
-        state[:, feature:] = jnp.where(lane == 0, m, total)
-        save = pltpu.make_async_copy(state, state_out, state_sem.at[0])
+        state[:, feature:] = jnp.where(lane == 0, m, jnp.where(lane == 1, total, state[:, feature:]))
+        save = pltpu.make_async_copy(state, state_out, out_sems.at[0])
         save.start()
         save.wait()
         return
+    load_own.wait()
     inverse = 1.0 / total
-    own = k0_ref[...].astype(jnp.float32)
-    num[...] = (num[...] * inverse - own) * scale
-    positive = jnp.sum(q.astype(jnp.float32) * own, axis=1, keepdims=True)
+    piece = n // out_sems.shape[0]
+    saves = []
+    for r in range(out_sems.shape[0]):
+        part = pl.ds(r * piece, piece)
+        gain = inverse[r * piece : (r + 1) * piece] * scale
+        state[part, :feature] = state[part, :feature] * gain - k_ref[part, :].astype(jnp.float32) * scale
+        saves.append(pltpu.make_async_copy(state.at[part, pl.ds(0, feature)], grad.at[part], out_sems.at[r]))
+        saves[-1].start()
+    positive = state[:, feature + 2 : feature + 3]
     loss = (m - positive) * scale + jnp.log(total)
     table = jnp.where(lane == 0, m, jnp.where(lane == 1, inverse, loss))
     flipped = table.T
     stats_ref[...] = flipped[:8]
     loss_ref[...] = flipped[2:3]
+    for save in saves:
+        save.wait()
 
 
 def hard_part(rate, scale, last, q, k0, state, blocks):
     n, feature = q.shape
     slots = blocks.shape[0]
     f32 = jnp.float32
+    keys = slots * BLOCK
+    scratch = [pltpu.VMEM(q.shape, q.dtype)]
     shapes = [jax.ShapeDtypeStruct(state.shape, f32)]
-    specs = [whole(pltpu.HBM)]
+    specs = [whole(pl.ANY)]
     if last:
+        scratch += [pltpu.VMEM(k0.shape, k0.dtype)]
         shapes = [jax.ShapeDtypeStruct((n, feature), f32), jax.ShapeDtypeStruct((1, n), f32), jax.ShapeDtypeStruct((8, n), f32)]
-        specs = [whole()] * 3
-    keys = slots * BLOCK
+        specs = [whole(pl.ANY), whole(), whole()]
+    scratch += [
+        pltpu.VMEM(state.shape, f32),
+        pltpu.VMEM(blocks.shape, blocks.dtype),
+        pltpu.VMEM((keys // CHUNK, n, CHUNK), f32),
+        pltpu.SMEM((slots + CHUNK // BLOCK,), jnp.int32),
+        pltpu.SemaphoreType.DMA((4,)),
+        pltpu.SemaphoreType.DMA((4 if last else 1,)),
+    ]
     return pl.pallas_call(
         functools.partial(hard_kernel, rate, scale, last),
         out_shape=shapes,
-        in_specs=[whole(), whole(), whole(pl.ANY), whole(pl.ANY)],
+        in_specs=[whole(pl.ANY)] * 4,
         out_specs=specs,
-        scratch_shapes=[
-            pltpu.VMEM(state.shape, f32),
-            pltpu.VMEM(blocks.shape, blocks.dtype),
-            pltpu.VMEM((keys // CHUNK, n, CHUNK), f32),
-            pltpu.SMEM((slots + 1,), jnp.int32),
-            pltpu.SemaphoreType.DMA((slots,)),
-            pltpu.SemaphoreType.DMA((1,)),
-        ],
+        scratch_shapes=scratch,
         compiler_params=pltpu.CompilerParams(vmem_limit_bytes=BIG_GRANT),
         cost_estimate=pl.CostEstimate(flops=2 * n * keys * feature, bytes_accessed=2 * keys * feature, transcendentals=n * keys // 2),
         name="hard_last" if last else "hard_first",
     )(q, k0, state, blocks)
 
 
-def rtl_kernel(rate, scale, tiles, k_ref, *refs):
-    n_refs, s_refs = refs[:tiles], refs[tiles : 2 * tiles]
-    base_ref, out_ref = refs[2 * tiles :]
+def rtl_kernel(rate, scale, k_ref, n0_ref, n1_ref, n2_ref, s0_ref, s1_ref, s2_ref, out_ref):
     k = k_ref[...]
-    total = -base_ref[...].astype(jnp.float32) if tiles == 1 else base_ref[...]
-    for n_ref, s_ref in zip(n_refs, s_refs):
+    first = pl.multiple_of(pl.program_id(0) * k.shape[0], k.shape[0])
+    total = -n0_ref[pl.ds(first, k.shape[0]), :].astype(jnp.float32)
+    for n_ref, s_ref in ((n0_ref, s0_ref), (n1_ref, s1_ref), (n2_ref, s2_ref)):
         rows = n_ref[...]
         s = nt_dot(k, rows)
         w = jnp.exp2((s - s_ref[0:1, :]) * rate) * s_ref[1:2, :]
         total += jnp.dot(w.astype(jnp.bfloat16), rows, preferred_element_type=jnp.float32)
-    out_ref[...] = total if tiles == 1 else total * scale
-
-
-def rtl_part(rate, scale, k, nets, stats, base, rows=256):
+    out_ref[...] = total * scale
+
+
+def rtl_part(rate, scale, k, n0, n1, n2, s0, s1, s2, rows=256):
     n, feature = k.shape
-    tiles = len(nets)
     block = pl.BlockSpec((rows, feature), lambda i: (i, 0))
-    full = pl.BlockSpec((n, feature), lambda i: (0, 0))
-    stat = pl.BlockSpec((8, n), lambda i: (0, 0))
+    full = pl.BlockSpec((n, feature), lambda i: (0, 0), pipeline_mode=pl.Buffered(1))
+    stat = pl.BlockSpec((8, n), lambda i: (0, 0), pipeline_mode=pl.Buffered(1))
     return pl.pallas_call(
-        functools.partial(rtl_kernel, rate, scale, tiles),
+        functools.partial(rtl_kernel, rate, scale),
         grid=(n // rows,),
         out_shape=jax.ShapeDtypeStruct((n, feature), jnp.float32),
-        in_specs=[block] + [full] * tiles + [stat] * tiles + [block],
+        in_specs=[block, full, full, full, stat, stat, stat],
         out_specs=block,
         compiler_params=pltpu.CompilerParams(vmem_limit_bytes=VMEM_LIMIT),
-        cost_estimate=pl.CostEstimate(flops=4 * n * tiles * n * feature, bytes_accessed=(tiles + 3) * n * feature * 2, transcendentals=tiles * n * n),
-        name="rtl_own" if tiles == 1 else "rtl_others",
-    )(k, *nets, *stats, base)
+        cost_estimate=pl.CostEstimate(flops=4 * n * 3 * n * feature, bytes_accessed=6 * n * feature * 2, transcendentals=3 * n * n),
+        name="rtl",
+    )(k, n0, n1, n2, s0, s1, s2)
 
 
 def body(netlist, rtl, hard_target, hard_block):
@@ -372,12 +384,14 @@
     packed, mail = pack_own(at, targets, picks, own_keys.reshape(-1, BLOCK, feature), places)
     first = spread(packed)
     mail = lax.ppermute(mail, "dp", [(g, g ^ 2) for g in range(groups)])
-    rtl1 = passed_along(own_keys, "loop", 1)
-    net1 = passed_along(queries, "loop", -1)
-    rtl2 = passed_along(own_keys, "loop", 2)
-    net2 = passed_along(queries, "loop", -2)
-    mail, rtl1, net1 = lax.optimization_barrier((mail, rtl1, net1))
-    second = spread(pack_far(at, mail, places, targets.shape[0]))
+    mail, onward, back = lax.optimization_barrier((mail, own_keys, queries))
+    rtl1 = passed_along(onward, "loop", 1)
+    net1 = passed_along(back, "loop", -1)
+    packed = pack_far(at, mail, places, targets.shape[0])
+    packed, rtl1, net1 = lax.optimization_barrier((packed, rtl1, net1))
+    second = spread(packed)
+    rtl2 = passed_along(rtl1, "loop", 1)
+    net2 = passed_along(net1, "loop", -1)
 
     state = cycle_part(rate, queries, [own_keys, rtl1], [])
     (state,) = hard_part(rate, scale, False, queries, own_keys, state, first)
@@ -385,8 +399,7 @@
     grad, loss, stats = hard_part(rate, scale, True, queries, own_keys, state, second)
     stats1 = passed_along(stats, "loop", -1)
     stats2 = passed_along(stats, "loop", -2)
-    begun = rtl_part(rate, scale, own_keys, [queries], [stats], queries)
-    rtl_grad = rtl_part(rate, scale, own_keys, [net1, net2], [stats1, stats2], begun)
+    rtl_grad = rtl_part(rate, scale, own_keys, queries, net1, net2, stats, stats1, stats2)
     return (loss, grad[None], rtl_grad[None])
 
 

time: 109 us -> 109 us (level); the launches traced: 107 us -> 109 us
  Pallas kernels: 31.5 us -> 28.2 us
  waiting for transfers between devices: 28.3 us -> 31.3 us
  starting transfers between devices: 41.5 us -> 44.4 us
    ppermute x6, waiting for transfers between devices: 21.5 us -> 10.3 us  [passed_along(): return lax.ppermute(block, axis, route)]
    ppermute x1, waiting for transfers between devices: 6.81 us -> 17.6 us  [body(): mail = lax.ppermute(mail, 'dp', [(g, g ^ 2) for g in range(groups)])]
    all_to_all x2, waiting for transfers between devices: 0.01 us -> 3.3 us  [spread(): lax.all_to_all(packed, 'dp', split_axis=0, concat_axis=0, axis_index_grou...]
    ppermute x6, starting transfers between devices: 22.8 us -> 25.4 us  [passed_along(): return lax.ppermute(block, axis, route)]
    pallas_call x2, Pallas kernels: 5.42 us -> 3.59 us  [cycle_part(): pl.pallas_call(functools.partial(cycle_kernel, rate, tiles), grid=(n // r...]
    pallas_call x2 -> x1, Pallas kernels: 4.96 us -> 3.37 us  [rtl_part(): pl.pallas_call(functools.partial(rtl_kernel, rate, scale), grid=(n // row...]
    unnamed x16 -> x22, local copies, waits for them, and re-layouts: 5.02 us -> 4.18 us
  transfers between devices with their start and end apart: 9 -> 9, of which waited for: 5 -> 5; matrix products, arithmetic and copies ran while one was open for 0% -> 0% of each run, Pallas kernels for 25% -> 20%
where the time goes in v4:
time: 109 us
  starting transfers between devices  44.4 us (41%)
  waiting for transfers between devices  31.3 us (29%)
  Pallas kernels  28.2 us (26%)
  local copies, waits for them, and re-layouts  4.18 us (4%)
    ppermute x6, starting transfers between devices, passed_along(): return lax.ppermute(block, axis, route)  25.4 us
    ppermute x1, waiting for transfers between devices, body(): mail = lax.ppermute(mail, 'dp', [(g, g ^ 2) for g in range(groups)])  17.6 us
    all_to_all x2, starting transfers between devices, spread(): lax.all_to_all(packed, 'dp', split_axis=0, concat_axis=0, axis_index_grou...  17.1 us
    pallas_call x2, Pallas kernels, hard_part(): pl.pallas_call(functools.partial(hard_kernel, rate, scale, last), out_sha...  16.1 us
    ppermute x6, waiting for transfers between devices, passed_along(): return lax.ppermute(block, axis, route)  10.3 us
    unnamed x22, local copies, waits for them, and re-layouts  4.18 us
    pallas_call x2, Pallas kernels, cycle_part(): pl.pallas_call(functools.partial(cycle_kernel, rate, tiles), grid=(n // r...  3.59 us
    pallas_call x1, Pallas kernels, rtl_part(): pl.pallas_call(functools.partial(rtl_kernel, rate, scale), grid=(n // row...  3.37 us
  transfers between devices with their start and end apart: 9, of which 5 were waited for; matrix products, arithmetic and copies ran while one was open for 0% of the time, Pallas kernels for 20%

profile of v4, /device:TPU:1, one launch (start us, length us, event | category | flops | bytes accessed | tf_op | source)
XLA Modules:
  0.0 108.9 jit_solution(14359754615838129406)
XLA Ops:
  0.6 2.5 %pack_own.1 = (bf16[16,128,512]{2,1,0:T(8,128)(2,1)}, bf16[5,128,512]{2,1,0:T(8,128)(2,1)}) custom-call(s32[1]{0:T(128)} %bitcast.2.me, s32[16]{0:T(128)} %bitcast.20, s32[16]{0:T(128)} %bitcast.21, bf16[4,128,512]{2,1,0:T(8,128)(2,1)} %bitcast.14), custom_call_target="tpu_custom_call" | custom-call | tf_op jit(solution)/shard_map/pack_own/pallas_call | solution.py:103
  3.1 0.0 copy-start.10
  3.2 0.0 copy-start.5
  3.2 0.0 copy-start.2
  3.2 11.3 %all-to-all-start = ((bf16[16,128,512]{2,1,0:T(8,128)(2,1)}), bf16[16,128,512]{2,1,0:T(8,128)(2,1)}, u32[]{:S(2)}, u32[]{:S(2)}) async-start(bf16[16,128,512]{2,1,0:T(8,128)(2,1)} %get-tuple-element.19), calls=%async_computation | async-start | bytes 4194304 | tf_op jit(solution)/shard_map/all_to_all | solution.py:381
  14.5 0.0 copy-done.10
  14.5 1.9 %collective-permute-start = (bf16[5,128,512]{2,1,0:T(8,128)(2,1)S(1)}, bf16[5,128,512]{2,1,0:T(8,128)(2,1)S(1)}, u32[]{:S(2)}, u32[]{:S(2)}) collective-permute-start(bf16[5,128,512]{2,1,0:T(8,128)(2,1)S(1)} %copy-done.10), channel_id=1, source_target_pairs={{0,64},{32,96},{64,0},{96,32},{128,192},{160,224},{192,128},{224,1... | collective-permute-start | bytes 1966088 | tf_op jit(solution)/shard_map/ppermute | solution.py:386
  16.4 17.6 %collective-permute-done.mail = bf16[5,128,512]{2,1,0:T(8,128)(2,1)S(1)} collective-permute-done((bf16[5,128,512]{2,1,0:T(8,128)(2,1)S(1)}, bf16[5,128,512]{2,1,0:T(8,128)(2,1)S(1)}, u32[]{:S(2)}, u32[]{:S(2)}) %collective-permute-start) | collective-permute-done | bytes 655392 | tf_op jit(solution)/shard_map/ppermute | solution.py:386
  34.0 0.0 copy-start.9
  34.0 0.0 copy-done.5
  34.0 1.9 %collective-permute-start.1 = (bf16[512,512]{1,0:T(8,128)(2,1)S(1)}, bf16[512,512]{1,0:T(8,128)(2,1)S(1)}, u32[]{:S(2)}, u32[]{:S(2)}) collective-permute-start(bf16[512,512]{1,0:T(8,128)(2,1)S(1)} %bitcast.17), channel_id=1, source_target_pairs={{31,0},{0,1},{1,2},{2,3},{3,4},{4,5},{5,6},{6,7},{7,8},{8,9},{9,10... | collective-permute-start | bytes 1572872 | tf_op jit(solution)/shard_map/ppermute | solution.py:23
  36.0 0.0 copy-done.2
  36.0 7.2 %collective-permute-start.2 = (bf16[512,512]{1,0:T(8,128)(2,1)S(1)}, bf16[512,512]{1,0:T(8,128)(2,1)S(1)}, u32[]{:S(2)}, u32[]{:S(2)}) collective-permute-start(bf16[512,512]{1,0:T(8,128)(2,1)S(1)} %bitcast.10), channel_id=1, source_target_pairs={{1,0},{2,1},{3,2},{4,3},{5,4},{6,5},{7,6},{8,7},{9,8},{10,9},{11,1... | collective-permute-start | bytes 1572872 | tf_op jit(solution)/shard_map/ppermute | solution.py:23
  43.2 0.0 copy-done.9
  43.2 2.7 %pack_far.1 = bf16[16,128,512]{2,1,0:T(8,128)(2,1)} custom-call(s32[1]{0:T(128)} %bitcast.2.me, bf16[5,128,512]{2,1,0:T(8,128)(2,1)} %copy-done.9), custom_call_target="tpu_custom_call" | custom-call | tf_op jit(solution)/shard_map/pack_far/pallas_call | solution.py:147
  45.8 7.0 %collective-permute-done.1.refs_1_ = bf16[512,512]{1,0:T(8,128)(2,1)S(1)} collective-permute-done((bf16[512,512]{1,0:T(8,128)(2,1)S(1)}, bf16[512,512]{1,0:T(8,128)(2,1)S(1)}, u32[]{:S(2)}, u32[]{:S(2)}) %collective-permute-start.1) | collective-permute-done | bytes 524320 | tf_op jit(solution)/shard_map/ppermute | solution.py:23
  52.8 0.9 collective-permute-done.2.n1_ref
  53.7 0.0 all-to-all-done.blocks
  53.7 5.8 %all-to-all-start.1 = ((bf16[16,128,512]{2,1,0:T(8,128)(2,1)}), bf16[16,128,512]{2,1,0:T(8,128)(2,1)}, u32[]{:S(2)}, u32[]{:S(2)}) async-start(bf16[16,128,512]{2,1,0:T(8,128)(2,1)} %pack_far.1), calls=%async_computation.1 | async-start | bytes 4194304 | tf_op jit(solution)/shard_map/all_to_all | solution.py:381
  59.5 1.9 %collective-permute-start.3 = (bf16[512,512]{1,0:T(8,128)(2,1)S(1)}, bf16[512,512]{1,0:T(8,128)(2,1)S(1)}, u32[]{:S(2)}, u32[]{:S(2)}) collective-permute-start(bf16[512,512]{1,0:T(8,128)(2,1)S(1)} %collective-permute-done.1.refs_1_), channel_id=1, source_target_pairs={{31,0},{0,1},{1,2},{2,3},{3,4},{4,5},{5,6},{6,7},{7,8},{8,9},{9,10... | collective-permute-start | bytes 1572872 | tf_op jit(solution)/shard_map/ppermute | solution.py:23
  61.4 6.2 %collective-permute-start.4 = (bf16[512,512]{1,0:T(8,128)(2,1)S(1)}, bf16[512,512]{1,0:T(8,128)(2,1)S(1)}, u32[]{:S(2)}, u32[]{:S(2)}) collective-permute-start(bf16[512,512]{1,0:T(8,128)(2,1)S(1)} %collective-permute-done.2.n1_ref), channel_id=1, source_target_pairs={{1,0},{2,1},{3,2},{4,3},{5,4},{6,5},{7,6},{8,7},{9,8},{10,9},{11,1... | collective-permute-start | bytes 1572872 | tf_op jit(solution)/shard_map/ppermute | solution.py:23
  67.7 2.0 %cycle.1.state_in = f32[512,640]{1,0:T(8,128)S(1)} custom-call(bf16[512,512]{1,0:T(8,128)(2,1)S(1)} %bitcast.11, bf16[512,512]{1,0:T(8,128)(2,1)S(1)} %bitcast.18, bf16[512,512]{1,0:T(8,128)(2,1)S(1)} %collective-permute-done.1.refs_1_), custom_call_target="tpu_custom_call" | custom-call | flops 1073741824 | bytes 2621440 | tf_op jit(solution)/shard_map/cycle/pallas_call | solution.py:206
  69.6 0.0 copy-start.7
  69.6 1.0 copy-done.7
  70.7 0.0 copy-start.3
  70.7 7.9 %hard_first.1.refs_1_ = f32[512,640]{1,0:T(8,128)} custom-call(bf16[512,512]{1,0:T(8,128)(2,1)} %bitcast.8, bf16[512,512]{1,0:T(8,128)(2,1)} %bitcast.15, f32[512,640]{1,0:T(8,128)} %copy-done.7, bf16[16,128,512]{2,1,0:T(8,128)(2,1)} %all-to-all-done.blocks), custom_call_target="tpu_custom_call" | custom-call | flops 1073741824 | bytes 2097152 | tf_op jit(solution)/shard_map/hard_first/pallas_call | solution.py:327
  78.6 0.0 collective-permute-done.3.refs_0_
  78.6 0.0 copy-done.3
  78.6 0.0 copy-start.1
  78.6 1.3 %copy-done.1 = f32[512,640]{1,0:T(8,128)S(1)} copy-done((f32[512,640]{1,0:T(8,128)S(1)}, f32[512,640]{1,0:T(8,128)}, u32[]{:S(2)}) %copy-start.1) | copy-done | bytes 1310744
  80.0 1.6 %cycle_more.1.state_in = f32[512,640]{1,0:T(8,128)S(1)} custom-call(bf16[512,512]{1,0:T(8,128)(2,1)S(1)} %bitcast.12, bf16[512,512]{1,0:T(8,128)(2,1)S(1)} %collective-permute-done.3.refs_0_, f32[512,640]{1,0:T(8,128)S(1)} %copy-done.1), custom_call_target="tpu_custom_call" | custom-call | flops 536870912 | bytes 2097152 | tf_op jit(solution)/shard_map/cycle_more/pallas_call | solution.py:206
  81.6 0.0 copy-start
  81.6 1.1 copy-done
  82.7 0.0 copy-start.4
  82.7 0.0 copy-start.6
  82.7 3.3 %all-to-all-done.1.blocks = bf16[16,128,512]{2,1,0:T(8,128)(2,1)} async-done(((bf16[16,128,512]{2,1,0:T(8,128)(2,1)}), bf16[16,128,512]{2,1,0:T(8,128)(2,1)}, u32[]{:S(2)}, u32[]{:S(2)}) %all-to-all-start.1) | async-done | bytes 2097184 | tf_op jit(solution)/shard_map/all_to_all | solution.py:381
  86.0 8.2 %hard_last.1 = (f32[512,512]{1,0:T(8,128)}, f32[1,512]{1,0:T(1,128)}, f32[8,512]{1,0:T(8,128)}) custom-call(bf16[512,512]{1,0:T(8,128)(2,1)} %bitcast.9, bf16[512,512]{1,0:T(8,128)(2,1)} %bitcast.16, f32[512,640]{1,0:T(8,128)} %copy-done, bf16[16,128,512]{2,1,0:T(8,128)(2,1)} %all-to-all-done.1.blocks), custom_call_target="tpu_custom_call" | custom-call | flops 1073741824 | bytes 2097152 | tf_op jit(solution)/shard_map/hard_last/pallas_call | solution.py:327
  94.1 5.3 %collective-permute-start.6 = (f32[8,512]{1,0:T(8,128)}, f32[8,512]{1,0:T(8,128)S(1)}, u32[]{:S(2)}, u32[]{:S(2)}) collective-permute-start(f32[8,512]{1,0:T(8,128)} %get-tuple-element.24.s0_ref), channel_id=1, source_target_pairs={{2,0},{3,1},{4,2},{5,3},{6,4},{7,5},{8,6},{9,7},{10,8},{11,9},{12,... | collective-permute-start | bytes 49160 | tf_op jit(solution)/shard_map/ppermute | solution.py:23
  99.4 2.9 %collective-permute-start.5 = (f32[8,512]{1,0:T(8,128)}, f32[8,512]{1,0:T(8,128)S(1)}, u32[]{:S(2)}, u32[]{:S(2)}) collective-permute-start(f32[8,512]{1,0:T(8,128)} %get-tuple-element.24.s0_ref), channel_id=1, source_target_pairs={{1,0},{2,1},{3,2},{4,3},{5,4},{6,5},{7,6},{8,7},{9,8},{10,9},{11,1... | collective-permute-start | bytes 49160 | tf_op jit(solution)/shard_map/ppermute | solution.py:23
  102.3 0.0 collective-permute-done.4.n2_ref
  102.3 0.0 collective-permute-done.6.s2_ref
  102.3 2.5 %collective-permute-done.5.s1_ref = f32[8,512]{1,0:T(8,128)S(1)} collective-permute-done((f32[8,512]{1,0:T(8,128)}, f32[8,512]{1,0:T(8,128)S(1)}, u32[]{:S(2)}, u32[]{:S(2)}) %collective-permute-start.5) | collective-permute-done | bytes 16416 | tf_op jit(solution)/shard_map/ppermute | solution.py:23
  104.8 0.0 copy-done.4
  104.8 0.0 copy-done.6
  104.8 0.0 copy-start.8
  104.8 0.7 copy-done.8
  105.5 3.4 %rtl.1 = f32[512,512]{1,0:T(8,128)} custom-call(bf16[512,512]{1,0:T(8,128)(2,1)S(1)} %bitcast.19, bf16[512,512]{1,0:T(8,128)(2,1)S(1)} %bitcast.13, bf16[512,512]{1,0:T(8,128)(2,1)S(1)} %collective-permute-done.2.n1_ref, bf16[512,512]{1,0:T(8,128)(2,1)S(1)} %collective-permute-done.4.n2_ref, f32[8,512]{1,0:T(8,128)S(1)} %copy-done.8, ...), custom_call_target="tpu_custom_call" | custom-call | flops 1610612736 | bytes 3145728 | tf_op jit(solution)/shard_map/rtl/pallas_call | solution.py:356
Async XLA Ops:
  3.1 11.3 %copy-start.10 = (bf16[5,128,512]{2,1,0:T(8,128)(2,1)S(1)}, bf16[5,128,512]{2,1,0:T(8,128)(2,1)}, u32[]{:S(2)}) copy-start(bf16[5,128,512]{2,1,0:T(8,128)(2,1)} %get-tuple-element.14) | copy-start | bytes 1966084
  3.2 30.9 %copy-start.5 = (bf16[1,512,512]{2,1,0:T(8,128)(2,1)S(1)}, bf16[1,512,512]{2,1,0:T(8,128)(2,1)}, u32[]{:S(2)}) copy-start(bf16[1,512,512]{2,1,0:T(8,128)(2,1)} %param.5) | copy-start | bytes 1572868
  3.2 32.8 %copy-start.2 = (bf16[1,512,512]{2,1,0:T(8,128)(2,1)S(1)}, bf16[1,512,512]{2,1,0:T(8,128)(2,1)}, u32[]{:S(2)}) copy-start(bf16[1,512,512]{2,1,0:T(8,128)(2,1)} %param.4) | copy-start | bytes 1572868
  3.2 50.5 %all-to-all-start = ((bf16[16,128,512]{2,1,0:T(8,128)(2,1)}), bf16[16,128,512]{2,1,0:T(8,128)(2,1)}, u32[]{:S(2)}, u32[]{:S(2)}) async-start(bf16[16,128,512]{2,1,0:T(8,128)(2,1)} %get-tuple-element.19), calls=%async_computation | async-start | bytes 4194304 | tf_op jit(solution)/shard_map/all_to_all | solution.py:381
  14.5 19.6 %collective-permute-start = (bf16[5,128,512]{2,1,0:T(8,128)(2,1)S(1)}, bf16[5,128,512]{2,1,0:T(8,128)(2,1)S(1)}, u32[]{:S(2)}, u32[]{:S(2)}) collective-permute-start(bf16[5,128,512]{2,1,0:T(8,128)(2,1)S(1)} %copy-done.10), channel_id=1, source_target_pairs={{0,64},{32,96},{64,0},{96,32},{128,192},{160,224},{192,128},{224,1... | collective-permute-start | bytes 1966088 | tf_op jit(solution)/shard_map/ppermute | solution.py:386
  34.0 9.1 %copy-start.9 = (bf16[5,128,512]{2,1,0:T(8,128)(2,1)}, bf16[5,128,512]{2,1,0:T(8,128)(2,1)S(1)}, u32[]{:S(2)}) copy-start(bf16[5,128,512]{2,1,0:T(8,128)(2,1)S(1)} %collective-permute-done.mail) | copy-start | bytes 1966084
  34.0 18.8 %collective-permute-start.1 = (bf16[512,512]{1,0:T(8,128)(2,1)S(1)}, bf16[512,512]{1,0:T(8,128)(2,1)S(1)}, u32[]{:S(2)}, u32[]{:S(2)}) collective-permute-start(bf16[512,512]{1,0:T(8,128)(2,1)S(1)} %bitcast.17), channel_id=1, source_target_pairs={{31,0},{0,1},{1,2},{2,3},{3,4},{4,5},{5,6},{6,7},{7,8},{8,9},{9,10... | collective-permute-start | bytes 1572872 | tf_op jit(solution)/shard_map/ppermute | solution.py:23
  36.0 17.7 %collective-permute-start.2 = (bf16[512,512]{1,0:T(8,128)(2,1)S(1)}, bf16[512,512]{1,0:T(8,128)(2,1)S(1)}, u32[]{:S(2)}, u32[]{:S(2)}) collective-permute-start(bf16[512,512]{1,0:T(8,128)(2,1)S(1)} %bitcast.10), channel_id=1, source_target_pairs={{1,0},{2,1},{3,2},{4,3},{5,4},{6,5},{7,6},{8,7},{9,8},{10,9},{11,1... | collective-permute-start | bytes 1572872 | tf_op jit(solution)/shard_map/ppermute | solution.py:23
  53.7 32.3 %all-to-all-start.1 = ((bf16[16,128,512]{2,1,0:T(8,128)(2,1)}), bf16[16,128,512]{2,1,0:T(8,128)(2,1)}, u32[]{:S(2)}, u32[]{:S(2)}) async-start(bf16[16,128,512]{2,1,0:T(8,128)(2,1)} %pack_far.1), calls=%async_computation.1 | async-start | bytes 4194304 | tf_op jit(solution)/shard_map/all_to_all | solution.py:381
  59.5 19.1 %collective-permute-start.3 = (bf16[512,512]{1,0:T(8,128)(2,1)S(1)}, bf16[512,512]{1,0:T(8,128)(2,1)S(1)}, u32[]{:S(2)}, u32[]{:S(2)}) collective-permute-start(bf16[512,512]{1,0:T(8,128)(2,1)S(1)} %collective-permute-done.1.refs_1_), channel_id=1, source_target_pairs={{31,0},{0,1},{1,2},{2,3},{3,4},{4,5},{5,6},{6,7},{7,8},{8,9},{9,10... | collective-permute-start | bytes 1572872 | tf_op jit(solution)/shard_map/ppermute | solution.py:23
  61.4 40.9 %collective-permute-start.4 = (bf16[512,512]{1,0:T(8,128)(2,1)S(1)}, bf16[512,512]{1,0:T(8,128)(2,1)S(1)}, u32[]{:S(2)}, u32[]{:S(2)}) collective-permute-start(bf16[512,512]{1,0:T(8,128)(2,1)S(1)} %collective-permute-done.2.n1_ref), channel_id=1, source_target_pairs={{1,0},{2,1},{3,2},{4,3},{5,4},{6,5},{7,6},{8,7},{9,8},{10,9},{11,1... | collective-permute-start | bytes 1572872 | tf_op jit(solution)/shard_map/ppermute | solution.py:23
  69.6 1.0 copy-start.7
  70.7 7.9 %copy-start.3 = (bf16[1,512,512]{2,1,0:T(8,128)(2,1)S(1)}, bf16[1,512,512]{2,1,0:T(8,128)(2,1)}, u32[]{:S(2)}) copy-start(bf16[1,512,512]{2,1,0:T(8,128)(2,1)} %param.4) | copy-start | bytes 1572868
  78.6 1.3 %copy-start.1 = (f32[512,640]{1,0:T(8,128)S(1)}, f32[512,640]{1,0:T(8,128)}, u32[]{:S(2)}) copy-start(f32[512,640]{1,0:T(8,128)} %hard_first.1.refs_1_) | copy-start | bytes 3932164
  81.6 1.1 %copy-start = (f32[512,640]{1,0:T(8,128)}, f32[512,640]{1,0:T(8,128)S(1)}, u32[]{:S(2)}) copy-start(f32[512,640]{1,0:T(8,128)S(1)} %cycle_more.1.state_in) | copy-start | bytes 3932164
  82.7 22.1 %copy-start.4 = (bf16[1,512,512]{2,1,0:T(8,128)(2,1)S(1)}, bf16[1,512,512]{2,1,0:T(8,128)(2,1)}, u32[]{:S(2)}) copy-start(bf16[1,512,512]{2,1,0:T(8,128)(2,1)} %param.4) | copy-start | bytes 1572868
  82.7 22.1 %copy-start.6 = (bf16[1,512,512]{2,1,0:T(8,128)(2,1)S(1)}, bf16[1,512,512]{2,1,0:T(8,128)(2,1)}, u32[]{:S(2)}) copy-start(bf16[1,512,512]{2,1,0:T(8,128)(2,1)} %param.5) | copy-start | bytes 1572868
  94.1 8.2 %collective-permute-start.6 = (f32[8,512]{1,0:T(8,128)}, f32[8,512]{1,0:T(8,128)S(1)}, u32[]{:S(2)}, u32[]{:S(2)}) collective-permute-start(f32[8,512]{1,0:T(8,128)} %get-tuple-element.24.s0_ref), channel_id=1, source_target_pairs={{2,0},{3,1},{4,2},{5,3},{6,4},{7,5},{8,6},{9,7},{10,8},{11,9},{12,... | collective-permute-start | bytes 49160 | tf_op jit(solution)/shard_map/ppermute | solution.py:23
  99.4 5.4 %collective-permute-start.5 = (f32[8,512]{1,0:T(8,128)}, f32[8,512]{1,0:T(8,128)S(1)}, u32[]{:S(2)}, u32[]{:S(2)}) collective-permute-start(f32[8,512]{1,0:T(8,128)} %get-tuple-element.24.s0_ref), channel_id=1, source_target_pairs={{1,0},{2,1},{3,2},{4,3},{5,4},{6,5},{7,6},{8,7},{9,8},{10,9},{11,1... | collective-permute-start | bytes 49160 | tf_op jit(solution)/shard_map/ppermute | solution.py:23
  104.8 0.7 copy-start.8

commit v5 on v4

--- a/solution.py
+++ b/solution.py
@@ -46,7 +46,7 @@
         @pl.when(place[j] >= 0)
         def _(j=j):
             used[place[j]] = 1
-            pltpu.make_async_copy(tile.at[pick_of(j)], out.at[place[j]], sems.at[j]).start()
+            pltpu.make_async_copy(tile.at[pl.ds(pl.multiple_of(pick_of(j) * BLOCK, BLOCK), BLOCK)], out.at[place[j]], sems.at[j]).start()
 
     rows, lanes = mark.shape
     for s in range(slots):
@@ -58,7 +58,7 @@
         for j in range(entries):
             @pl.when(place[j] >= 0)
             def _(j=j):
-                pltpu.make_async_copy(tile.at[pick_of(j)], out.at[place[j]], sems.at[j]).wait()
+                pltpu.make_async_copy(tile.at[pl.ds(pl.multiple_of(pick_of(j) * BLOCK, BLOCK), BLOCK)], out.at[place[j]], sems.at[j]).wait()
 
         for s in range(slots):
             @pl.when(used[s] == 0)
@@ -76,8 +76,8 @@
     for copy in lists:
         copy.wait()
     load.wait()
-    blocks = tile.shape[0]
-    store = pltpu.make_async_copy(tile, mail.at[pl.ds(0, blocks)], in_sems.at[3])
+    size = tile.shape[0]
+    store = pltpu.make_async_copy(tile, mail.at[pl.ds(0, size)], in_sems.at[3])
     store.start()
     column = (me[0] >> 1) & 1
     finish = shared(out.shape[0], entries, out, tile, place, used, seen, mark, sems, mark_sems, column, lambda j: target_s[j], lambda j: pick_s[j])
@@ -88,7 +88,7 @@
         line = jnp.where(lane == entries + j, pick_s[j], line)
     head[...] = line.astype(jnp.float32).astype(head.dtype)
     rows, lanes = head.shape
-    note = pltpu.make_async_copy(head, mail.at[blocks, pl.ds(0, rows), pl.ds(0, lanes)], in_sems.at[4])
+    note = pltpu.make_async_copy(head, mail.at[pl.ds(size, rows), pl.ds(0, lanes)], in_sems.at[4])
     note.start()
     finish()
     store.wait()
@@ -97,12 +97,12 @@
 
 def pack_own(me, targets, picks, tile, places):
     entries = targets.shape[0]
-    blocks, rows, feature = tile.shape
+    rows, feature = tile.shape
     slots = places * CAP
     hbm = whole(pltpu.HBM)
     return pl.pallas_call(
         functools.partial(own_kernel, entries),
-        out_shape=(jax.ShapeDtypeStruct((slots, rows, feature), tile.dtype), jax.ShapeDtypeStruct((blocks + 1, rows, feature), tile.dtype)),
+        out_shape=(jax.ShapeDtypeStruct((slots, BLOCK, feature), tile.dtype), jax.ShapeDtypeStruct((rows + 16, feature), tile.dtype)),
         in_specs=[whole(pltpu.SMEM), hbm, hbm, hbm],
         out_specs=(hbm, hbm),
         scratch_shapes=[
@@ -124,10 +124,10 @@
 
 
 def far_kernel(entries, me, mail, out, list_v, list_s, tile, head, place, used, seen, mark, sems, mark_sems, in_sems):
-    blocks = tile.shape[0]
+    size = tile.shape[0]
     rows, lanes = head.shape
-    note = pltpu.make_async_copy(mail.at[blocks, pl.ds(0, rows), pl.ds(0, lanes)], head, in_sems.at[0])
-    load = pltpu.make_async_copy(mail.at[pl.ds(0, blocks)], tile, in_sems.at[1])
+    note = pltpu.make_async_copy(mail.at[pl.ds(size, rows), pl.ds(0, lanes)], head, in_sems.at[0])
+    load = pltpu.make_async_copy(mail.at[pl.ds(0, size)], tile, in_sems.at[1])
     note.start()
     load.start()
     note.wait()
@@ -141,18 +141,18 @@
 
 
 def pack_far(me, mail, places, entries):
-    blocks, rows, feature = mail.shape
+    rows, feature = mail.shape
     slots = places * CAP
     hbm = whole(pltpu.HBM)
     return pl.pallas_call(
         functools.partial(far_kernel, entries),
-        out_shape=jax.ShapeDtypeStruct((slots, rows, feature), mail.dtype),
+        out_shape=jax.ShapeDtypeStruct((slots, BLOCK, feature), mail.dtype),
         in_specs=[whole(pltpu.SMEM), hbm],
         out_specs=hbm,
         scratch_shapes=[
             pltpu.VMEM((8, 128), jnp.int32),
             pltpu.SMEM((8, 128), jnp.int32),
-            pltpu.VMEM((blocks - 1, rows, feature), mail.dtype),
+            pltpu.VMEM((rows - 16, feature), mail.dtype),
             pltpu.VMEM((16, 128), mail.dtype),
             pltpu.SMEM((entries,), jnp.int32),
             pltpu.SMEM((slots,), jnp.int32),
@@ -381,20 +381,19 @@
         return lax.all_to_all(packed, "dp", split_axis=0, concat_axis=0, axis_index_groups=columns, tiled=True)
 
     at = jnp.full((1,), lax.axis_index("dp"), jnp.int32)
-    packed, mail = pack_own(at, targets, picks, own_keys.reshape(-1, BLOCK, feature), places)
+    packed, mail = pack_own(at, targets, picks, own_keys, places)
     first = spread(packed)
     mail = lax.ppermute(mail, "dp", [(g, g ^ 2) for g in range(groups)])
-    mail, onward, back = lax.optimization_barrier((mail, own_keys, queries))
-    rtl1 = passed_along(onward, "loop", 1)
+    rtl1 = passed_along(own_keys, "loop", 1)
+    mail, rtl1, back = lax.optimization_barrier((mail, rtl1, queries))
+    second = spread(pack_far(at, mail, places, targets.shape[0]))
+    rtl2 = passed_along(rtl1, "loop", 1)
     net1 = passed_along(back, "loop", -1)
-    packed = pack_far(at, mail, places, targets.shape[0])
-    packed, rtl1, net1 = lax.optimization_barrier((packed, rtl1, net1))
-    second = spread(packed)
-    rtl2 = passed_along(rtl1, "loop", 1)
-    net2 = passed_along(net1, "loop", -1)
 
     state = cycle_part(rate, queries, [own_keys, rtl1], [])
     (state,) = hard_part(rate, scale, False, queries, own_keys, state, first)
+    net1, state = lax.optimization_barrier((net1, state))
+    net2 = passed_along(net1, "loop", -1)
     state = cycle_part(rate, queries, [rtl2], [state])
     grad, loss, stats = hard_part(rate, scale, True, queries, own_keys, state, second)
     stats1 = passed_along(stats, "loop", -1)

time: 109 us -> 97.8 us (0.90); the launches traced: 109 us -> 96.4 us
  starting transfers between devices: 44.4 us -> 33.8 us
  waiting for transfers between devices: 31.3 us -> 29.8 us
  Pallas kernels: 28.2 us -> 27 us
    ppermute x6, waiting for transfers between devices: 10.3 us -> 22.7 us  [passed_along(): return lax.ppermute(block, axis, route)]
    ppermute x1, waiting for transfers between devices: 17.6 us -> 5.54 us  [body(): mail = lax.ppermute(mail, 'dp', [(g, g ^ 2) for g in range(groups)])]
    ppermute x6, starting transfers between devices: 25.4 us -> 15.1 us  [passed_along(): return lax.ppermute(block, axis, route)]
    pallas_call x2, Pallas kernels: 16.1 us -> 11.9 us  [hard_part(): pl.pallas_call(functools.partial(hard_kernel, rate, scale, last), out_sha...]
    pallas_call x2, Pallas kernels: 3.59 us -> 5.5 us  [cycle_part(): pl.pallas_call(functools.partial(cycle_kernel, rate, tiles), grid=(n // r...]
    all_to_all x2, waiting for transfers between devices: 3.3 us -> 1.55 us  [spread(): lax.all_to_all(packed, 'dp', split_axis=0, concat_axis=0, axis_index_grou...]
    unnamed x22 -> x16, local copies, waits for them, and re-layouts: 4.18 us -> 4.98 us
  transfers between devices with their start and end apart: 9 -> 9, of which waited for: 5 -> 6; matrix products, arithmetic and copies ran while one was open for 0% -> 0% of each run, Pallas kernels for 20% -> 21%
where the time goes in v5:
time: 97.8 us; the launch traced here: 96.4 us
  starting transfers between devices  33.8 us (35%)
  waiting for transfers between devices  29.8 us (30%)
  Pallas kernels  27 us (28%)
  local copies, waits for them, and re-layouts  4.98 us (5%)
    ppermute x6, waiting for transfers between devices, passed_along(): return lax.ppermute(block, axis, route)  22.7 us
    all_to_all x2, starting transfers between devices, spread(): lax.all_to_all(packed, 'dp', split_axis=0, concat_axis=0, axis_index_grou...  16.7 us
    ppermute x6, starting transfers between devices, passed_along(): return lax.ppermute(block, axis, route)  15.1 us
    pallas_call x2, Pallas kernels, hard_part(): pl.pallas_call(functools.partial(hard_kernel, rate, scale, last), out_sha...  11.9 us
    ppermute x1, waiting for transfers between devices, body(): mail = lax.ppermute(mail, 'dp', [(g, g ^ 2) for g in range(groups)])  5.54 us
    pallas_call x2, Pallas kernels, cycle_part(): pl.pallas_call(functools.partial(cycle_kernel, rate, tiles), grid=(n // r...  5.5 us
    unnamed x16, local copies, waits for them, and re-layouts  4.98 us
    pallas_call x1, Pallas kernels, rtl_part(): pl.pallas_call(functools.partial(rtl_kernel, rate, scale), grid=(n // row...  4.42 us
  transfers between devices with their start and end apart: 9, of which 6 were waited for; matrix products, arithmetic and copies ran while one was open for 0% of the time, Pallas kernels for 21%

profile of v5, /device:TPU:1, one launch (start us, length us, event | category | flops | bytes accessed | tf_op | source)
XLA Modules:
  0.0 96.4 jit_solution(18215543793499363607)
XLA Ops:
  0.6 2.5 %pack_own.1 = (bf16[16,128,512]{2,1,0:T(8,128)(2,1)}, bf16[528,512]{1,0:T(8,128)(2,1)}) custom-call(s32[1]{0:T(128)} %bitcast.2.me, s32[16]{0:T(128)} %bitcast.13, s32[16]{0:T(128)} %bitcast.14, bf16[512,512]{1,0:T(8,128)(2,1)} %bitcast.7), custom_call_target="tpu_custom_call" | custom-call | tf_op jit(solution)/shard_map/pack_own/pallas_call | solution.py:103
  3.2 0.0 copy-start.7
  3.2 0.0 copy-start.2
  3.2 11.3 %all-to-all-start = ((bf16[16,128,512]{2,1,0:T(8,128)(2,1)}), bf16[16,128,512]{2,1,0:T(8,128)(2,1)}, u32[]{:S(2)}, u32[]{:S(2)}) async-start(bf16[16,128,512]{2,1,0:T(8,128)(2,1)} %get-tuple-element.16), calls=%async_computation | async-start | bytes 4194304 | tf_op jit(solution)/shard_map/all_to_all | solution.py:381
  14.5 0.0 copy-done.7
  14.5 1.9 %collective-permute-start = (bf16[528,512]{1,0:T(8,128)(2,1)S(1)}, bf16[528,512]{1,0:T(8,128)(2,1)S(1)}, u32[]{:S(2)}, u32[]{:S(2)}) collective-permute-start(bf16[528,512]{1,0:T(8,128)(2,1)S(1)} %copy-done.7), channel_id=1, source_target_pairs={{0,64},{32,96},{64,0},{96,32},{128,192},{160,224},{192,128},{224,1... | collective-permute-start | bytes 1622024 | tf_op jit(solution)/shard_map/ppermute | solution.py:386
  16.4 0.0 copy-done.2
  16.4 1.9 %collective-permute-start.1 = (bf16[512,512]{1,0:T(8,128)(2,1)S(1)}, bf16[512,512]{1,0:T(8,128)(2,1)S(1)}, u32[]{:S(2)}, u32[]{:S(2)}) collective-permute-start(bf16[512,512]{1,0:T(8,128)(2,1)S(1)} %bitcast.10), channel_id=1, source_target_pairs={{31,0},{0,1},{1,2},{2,3},{3,4},{4,5},{5,6},{6,7},{7,8},{8,9},{9,10... | collective-permute-start | bytes 1572872 | tf_op jit(solution)/shard_map/ppermute | solution.py:23
  18.4 18.9 %collective-permute-done.1.refs_1_ = bf16[512,512]{1,0:T(8,128)(2,1)S(1)} collective-permute-done((bf16[512,512]{1,0:T(8,128)(2,1)S(1)}, bf16[512,512]{1,0:T(8,128)(2,1)S(1)}, u32[]{:S(2)}, u32[]{:S(2)}) %collective-permute-start.1) | collective-permute-done | bytes 524320 | tf_op jit(solution)/shard_map/ppermute | solution.py:23
  37.3 5.5 %collective-permute-done.mail = bf16[528,512]{1,0:T(8,128)(2,1)S(1)} collective-permute-done((bf16[528,512]{1,0:T(8,128)(2,1)S(1)}, bf16[528,512]{1,0:T(8,128)(2,1)S(1)}, u32[]{:S(2)}, u32[]{:S(2)}) %collective-permute-start) | collective-permute-done | bytes 540704 | tf_op jit(solution)/shard_map/ppermute | solution.py:386
  42.9 0.0 copy-start.6
  42.9 0.8 copy-done.6
  43.7 2.7 %pack_far.1 = bf16[16,128,512]{2,1,0:T(8,128)(2,1)} custom-call(s32[1]{0:T(128)} %bitcast.2.me, bf16[528,512]{1,0:T(8,128)(2,1)} %copy-done.6), custom_call_target="tpu_custom_call" | custom-call | tf_op jit(solution)/shard_map/pack_far/pallas_call | solution.py:147
  46.3 0.0 all-to-all-done.blocks
  46.4 5.4 %all-to-all-start.1 = ((bf16[16,128,512]{2,1,0:T(8,128)(2,1)}), bf16[16,128,512]{2,1,0:T(8,128)(2,1)}, u32[]{:S(2)}, u32[]{:S(2)}) async-start(bf16[16,128,512]{2,1,0:T(8,128)(2,1)} %pack_far.1), calls=%async_computation.1 | async-start | bytes 4194304 | tf_op jit(solution)/shard_map/all_to_all | solution.py:381
  51.8 1.9 %collective-permute-start.3 = (bf16[512,512]{1,0:T(8,128)(2,1)}, bf16[512,512]{1,0:T(8,128)(2,1)S(1)}, u32[]{:S(2)}, u32[]{:S(2)}) collective-permute-start(bf16[512,512]{1,0:T(8,128)(2,1)} %bitcast.q_ref.q_hbm.n0_ref), channel_id=1, source_target_pairs={{1,0},{2,1},{3,2},{4,3},{5,4},{6,5},{7,6},{8,7},{9,8},{10,9},{11,1... | collective-permute-start | bytes 1572872 | tf_op jit(solution)/shard_map/ppermute | solution.py:23
  53.7 3.4 %collective-permute-start.2 = (bf16[512,512]{1,0:T(8,128)(2,1)S(1)}, bf16[512,512]{1,0:T(8,128)(2,1)S(1)}, u32[]{:S(2)}, u32[]{:S(2)}) collective-permute-start(bf16[512,512]{1,0:T(8,128)(2,1)S(1)} %collective-permute-done.1.refs_1_), channel_id=1, source_target_pairs={{31,0},{0,1},{1,2},{2,3},{3,4},{4,5},{5,6},{6,7},{7,8},{8,9},{9,10... | collective-permute-start | bytes 1572872 | tf_op jit(solution)/shard_map/ppermute | solution.py:23
  57.0 2.9 %cycle.1.state_in = f32[512,640]{1,0:T(8,128)S(1)} custom-call(bf16[512,512]{1,0:T(8,128)(2,1)} %bitcast.q_ref.q_hbm.n0_ref, bf16[512,512]{1,0:T(8,128)(2,1)S(1)} %bitcast.11, bf16[512,512]{1,0:T(8,128)(2,1)S(1)} %collective-permute-done.1.refs_1_), custom_call_target="tpu_custom_call" | custom-call | flops 1073741824 | bytes 2621440 | tf_op jit(solution)/shard_map/cycle/pallas_call | solution.py:206
  60.0 0.0 copy-start.4
  60.0 1.0 %copy-done.4 = f32[512,640]{1,0:T(8,128)} copy-done((f32[512,640]{1,0:T(8,128)}, f32[512,640]{1,0:T(8,128)S(1)}, u32[]{:S(2)}) %copy-start.4) | copy-done | bytes 1310744
  61.0 5.8 %hard_first.1.refs_1_ = f32[512,640]{1,0:T(8,128)} custom-call(bf16[512,512]{1,0:T(8,128)(2,1)} %bitcast.q_ref.q_hbm.n0_ref, bf16[512,512]{1,0:T(8,128)(2,1)} %bitcast.8, f32[512,640]{1,0:T(8,128)} %copy-done.4, bf16[16,128,512]{2,1,0:T(8,128)(2,1)} %all-to-all-done.blocks), custom_call_target="tpu_custom_call" | custom-call | flops 1073741824 | bytes 2097152 | tf_op jit(solution)/shard_map/hard_first/pallas_call | solution.py:327
  66.8 0.7 collective-permute-done.3.n1_ref
  67.5 4.1 %collective-permute-start.4 = (bf16[512,512]{1,0:T(8,128)(2,1)S(1)}, bf16[512,512]{1,0:T(8,128)(2,1)S(1)}, u32[]{:S(2)}, u32[]{:S(2)}) collective-permute-start(bf16[512,512]{1,0:T(8,128)(2,1)S(1)} %collective-permute-done.3.n1_ref), channel_id=1, source_target_pairs={{1,0},{2,1},{3,2},{4,3},{5,4},{6,5},{7,6},{8,7},{9,8},{10,9},{11,1... | collective-permute-start | bytes 1572872 | tf_op jit(solution)/shard_map/ppermute | solution.py:23
  71.6 0.0 collective-permute-done.2.refs_0_
  71.6 0.0 copy-start
  71.7 1.3 %copy-done = f32[512,640]{1,0:T(8,128)S(1)} copy-done((f32[512,640]{1,0:T(8,128)S(1)}, f32[512,640]{1,0:T(8,128)}, u32[]{:S(2)}) %copy-start) | copy-done | bytes 1310744
  73.0 2.6 %cycle_more.1.state_in = f32[512,640]{1,0:T(8,128)S(1)} custom-call(bf16[512,512]{1,0:T(8,128)(2,1)} %bitcast.q_ref.q_hbm.n0_ref, bf16[512,512]{1,0:T(8,128)(2,1)S(1)} %collective-permute-done.2.refs_0_, f32[512,640]{1,0:T(8,128)S(1)} %copy-done), custom_call_target="tpu_custom_call" | custom-call | flops 536870912 | bytes 2097152 | tf_op jit(solution)/shard_map/cycle_more/pallas_call | solution.py:206
  75.5 0.0 copy-start.1
  75.5 1.1 %copy-done.1 = f32[512,640]{1,0:T(8,128)} copy-done((f32[512,640]{1,0:T(8,128)}, f32[512,640]{1,0:T(8,128)S(1)}, u32[]{:S(2)}) %copy-start.1) | copy-done | bytes 1310744
  76.6 0.0 copy-start.3
  76.6 1.5 %all-to-all-done.1.blocks = bf16[16,128,512]{2,1,0:T(8,128)(2,1)} async-done(((bf16[16,128,512]{2,1,0:T(8,128)(2,1)}), bf16[16,128,512]{2,1,0:T(8,128)(2,1)}, u32[]{:S(2)}, u32[]{:S(2)}) %all-to-all-start.1) | async-done | bytes 2097184 | tf_op jit(solution)/shard_map/all_to_all | solution.py:381
  78.2 6.1 %hard_last.1 = (f32[512,512]{1,0:T(8,128)}, f32[1,512]{1,0:T(1,128)}, f32[8,512]{1,0:T(8,128)}) custom-call(bf16[512,512]{1,0:T(8,128)(2,1)} %bitcast.q_ref.q_hbm.n0_ref, bf16[512,512]{1,0:T(8,128)(2,1)} %bitcast.9, f32[512,640]{1,0:T(8,128)} %copy-done.1, bf16[16,128,512]{2,1,0:T(8,128)(2,1)} %all-to-all-done.1.blocks), custom_call_target="tpu_custom_call" | custom-call | flops 1073741824 | bytes 2097152 | tf_op jit(solution)/shard_map/hard_last/pallas_call | solution.py:327
  84.3 1.9 %collective-permute-start.6 = (f32[8,512]{1,0:T(8,128)}, f32[8,512]{1,0:T(8,128)S(1)}, u32[]{:S(2)}, u32[]{:S(2)}) collective-permute-start(f32[8,512]{1,0:T(8,128)} %get-tuple-element.22.s0_ref), channel_id=1, source_target_pairs={{2,0},{3,1},{4,2},{5,3},{6,4},{7,5},{8,6},{9,7},{10,8},{11,9},{12,... | collective-permute-start | bytes 49160 | tf_op jit(solution)/shard_map/ppermute | solution.py:23
  86.3 1.9 %collective-permute-start.5 = (f32[8,512]{1,0:T(8,128)}, f32[8,512]{1,0:T(8,128)S(1)}, u32[]{:S(2)}, u32[]{:S(2)}) collective-permute-start(f32[8,512]{1,0:T(8,128)} %get-tuple-element.22.s0_ref), channel_id=1, source_target_pairs={{1,0},{2,1},{3,2},{4,3},{5,4},{6,5},{7,6},{8,7},{9,8},{10,9},{11,1... | collective-permute-start | bytes 49160 | tf_op jit(solution)/shard_map/ppermute | solution.py:23
  88.2 0.0 collective-permute-done.4.n2_ref
  88.2 1.7 %collective-permute-done.6.s2_ref = f32[8,512]{1,0:T(8,128)S(1)} collective-permute-done((f32[8,512]{1,0:T(8,128)}, f32[8,512]{1,0:T(8,128)S(1)}, u32[]{:S(2)}, u32[]{:S(2)}) %collective-permute-start.6) | collective-permute-done | bytes 16416 | tf_op jit(solution)/shard_map/ppermute | solution.py:23
  89.9 1.3 %collective-permute-done.5.s1_ref = f32[8,512]{1,0:T(8,128)S(1)} collective-permute-done((f32[8,512]{1,0:T(8,128)}, f32[8,512]{1,0:T(8,128)S(1)}, u32[]{:S(2)}, u32[]{:S(2)}) %collective-permute-start.5) | collective-permute-done | bytes 16416 | tf_op jit(solution)/shard_map/ppermute | solution.py:23
  91.3 0.0 copy-done.3
  91.3 0.0 copy-start.5
  91.3 0.7 copy-done.5
  92.0 4.4 %rtl.1 = f32[512,512]{1,0:T(8,128)} custom-call(bf16[512,512]{1,0:T(8,128)(2,1)S(1)} %bitcast.12, bf16[512,512]{1,0:T(8,128)(2,1)} %bitcast.q_ref.q_hbm.n0_ref, bf16[512,512]{1,0:T(8,128)(2,1)S(1)} %collective-permute-done.3.n1_ref, bf16[512,512]{1,0:T(8,128)(2,1)S(1)} %collective-permute-done.4.n2_ref, f32[8,512]{1,0:T(8,128)S(1)} %copy-done.5, ...), custom_call_target="tpu_custom_call" | custom-call | flops 1610612736 | bytes 3145728 | tf_op jit(solution)/shard_map/rtl/pallas_call | solution.py:356
Async XLA Ops:
  3.2 11.3 %copy-start.7 = (bf16[528,512]{1,0:T(8,128)(2,1)S(1)}, bf16[528,512]{1,0:T(8,128)(2,1)}, u32[]{:S(2)}) copy-start(bf16[528,512]{1,0:T(8,128)(2,1)} %get-tuple-element.13) | copy-start | bytes 1622020
  3.2 13.2 %copy-start.2 = (bf16[1,512,512]{2,1,0:T(8,128)(2,1)S(1)}, bf16[1,512,512]{2,1,0:T(8,128)(2,1)}, u32[]{:S(2)}) copy-start(bf16[1,512,512]{2,1,0:T(8,128)(2,1)} %param.5) | copy-start | bytes 1572868
  3.2 43.1 %all-to-all-start = ((bf16[16,128,512]{2,1,0:T(8,128)(2,1)}), bf16[16,128,512]{2,1,0:T(8,128)(2,1)}, u32[]{:S(2)}, u32[]{:S(2)}) async-start(bf16[16,128,512]{2,1,0:T(8,128)(2,1)} %get-tuple-element.16), calls=%async_computation | async-start | bytes 4194304 | tf_op jit(solution)/shard_map/all_to_all | solution.py:381
  14.5 28.3 %collective-permute-start = (bf16[528,512]{1,0:T(8,128)(2,1)S(1)}, bf16[528,512]{1,0:T(8,128)(2,1)S(1)}, u32[]{:S(2)}, u32[]{:S(2)}) collective-permute-start(bf16[528,512]{1,0:T(8,128)(2,1)S(1)} %copy-done.7), channel_id=1, source_target_pairs={{0,64},{32,96},{64,0},{96,32},{128,192},{160,224},{192,128},{224,1... | collective-permute-start | bytes 1622024 | tf_op jit(solution)/shard_map/ppermute | solution.py:386
  16.4 20.9 %collective-permute-start.1 = (bf16[512,512]{1,0:T(8,128)(2,1)S(1)}, bf16[512,512]{1,0:T(8,128)(2,1)S(1)}, u32[]{:S(2)}, u32[]{:S(2)}) collective-permute-start(bf16[512,512]{1,0:T(8,128)(2,1)S(1)} %bitcast.10), channel_id=1, source_target_pairs={{31,0},{0,1},{1,2},{2,3},{3,4},{4,5},{5,6},{6,7},{7,8},{8,9},{9,10... | collective-permute-start | bytes 1572872 | tf_op jit(solution)/shard_map/ppermute | solution.py:23
  42.9 0.8 copy-start.6
  46.4 31.8 %all-to-all-start.1 = ((bf16[16,128,512]{2,1,0:T(8,128)(2,1)}), bf16[16,128,512]{2,1,0:T(8,128)(2,1)}, u32[]{:S(2)}, u32[]{:S(2)}) async-start(bf16[16,128,512]{2,1,0:T(8,128)(2,1)} %pack_far.1), calls=%async_computation.1 | async-start | bytes 4194304 | tf_op jit(solution)/shard_map/all_to_all | solution.py:381
  51.8 15.8 %collective-permute-start.3 = (bf16[512,512]{1,0:T(8,128)(2,1)}, bf16[512,512]{1,0:T(8,128)(2,1)S(1)}, u32[]{:S(2)}, u32[]{:S(2)}) collective-permute-start(bf16[512,512]{1,0:T(8,128)(2,1)} %bitcast.q_ref.q_hbm.n0_ref), channel_id=1, source_target_pairs={{1,0},{2,1},{3,2},{4,3},{5,4},{6,5},{7,6},{8,7},{9,8},{10,9},{11,1... | collective-permute-start | bytes 1572872 | tf_op jit(solution)/shard_map/ppermute | solution.py:23
  53.7 18.0 %collective-permute-start.2 = (bf16[512,512]{1,0:T(8,128)(2,1)S(1)}, bf16[512,512]{1,0:T(8,128)(2,1)S(1)}, u32[]{:S(2)}, u32[]{:S(2)}) collective-permute-start(bf16[512,512]{1,0:T(8,128)(2,1)S(1)} %collective-permute-done.1.refs_1_), channel_id=1, source_target_pairs={{31,0},{0,1},{1,2},{2,3},{3,4},{4,5},{5,6},{6,7},{7,8},{8,9},{9,10... | collective-permute-start | bytes 1572872 | tf_op jit(solution)/shard_map/ppermute | solution.py:23
  60.0 1.0 %copy-start.4 = (f32[512,640]{1,0:T(8,128)}, f32[512,640]{1,0:T(8,128)S(1)}, u32[]{:S(2)}) copy-start(f32[512,640]{1,0:T(8,128)S(1)} %cycle.1.state_in) | copy-start | bytes 3932164
  67.5 20.7 %collective-permute-start.4 = (bf16[512,512]{1,0:T(8,128)(2,1)S(1)}, bf16[512,512]{1,0:T(8,128)(2,1)S(1)}, u32[]{:S(2)}, u32[]{:S(2)}) collective-permute-start(bf16[512,512]{1,0:T(8,128)(2,1)S(1)} %collective-permute-done.3.n1_ref), channel_id=1, source_target_pairs={{1,0},{2,1},{3,2},{4,3},{5,4},{6,5},{7,6},{8,7},{9,8},{10,9},{11,1... | collective-permute-start | bytes 1572872 | tf_op jit(solution)/shard_map/ppermute | solution.py:23
  71.6 1.3 %copy-start = (f32[512,640]{1,0:T(8,128)S(1)}, f32[512,640]{1,0:T(8,128)}, u32[]{:S(2)}) copy-start(f32[512,640]{1,0:T(8,128)} %hard_first.1.refs_1_) | copy-start | bytes 3932164
  75.5 1.1 %copy-start.1 = (f32[512,640]{1,0:T(8,128)}, f32[512,640]{1,0:T(8,128)S(1)}, u32[]{:S(2)}) copy-start(f32[512,640]{1,0:T(8,128)S(1)} %cycle_more.1.state_in) | copy-start | bytes 3932164
  76.6 14.6 %copy-start.3 = (bf16[1,512,512]{2,1,0:T(8,128)(2,1)S(1)}, bf16[1,512,512]{2,1,0:T(8,128)(2,1)}, u32[]{:S(2)}) copy-start(bf16[1,512,512]{2,1,0:T(8,128)(2,1)} %param.5) | copy-start | bytes 1572868
  84.3 5.6 %collective-permute-start.6 = (f32[8,512]{1,0:T(8,128)}, f32[8,512]{1,0:T(8,128)S(1)}, u32[]{:S(2)}, u32[]{:S(2)}) collective-permute-start(f32[8,512]{1,0:T(8,128)} %get-tuple-element.22.s0_ref), channel_id=1, source_target_pairs={{2,0},{3,1},{4,2},{5,3},{6,4},{7,5},{8,6},{9,7},{10,8},{11,9},{12,... | collective-permute-start | bytes 49160 | tf_op jit(solution)/shard_map/ppermute | solution.py:23
  86.3 5.0 %collective-permute-start.5 = (f32[8,512]{1,0:T(8,128)}, f32[8,512]{1,0:T(8,128)S(1)}, u32[]{:S(2)}, u32[]{:S(2)}) collective-permute-start(f32[8,512]{1,0:T(8,128)} %get-tuple-element.22.s0_ref), channel_id=1, source_target_pairs={{1,0},{2,1},{3,2},{4,3},{5,4},{6,5},{7,6},{8,7},{9,8},{10,9},{11,1... | collective-permute-start | bytes 49160 | tf_op jit(solution)/shard_map/ppermute | solution.py:23
  91.3 0.7 copy-start.5

commit v6 on v5

--- a/solution.py
+++ b/solution.py
@@ -11,8 +11,10 @@
 BLOCK = 128
 CAP = 2
 CHUNK = 512
-VMEM_LIMIT = 28 * 1024 * 1024
+VMEM_LIMIT = 20 * 1024 * 1024
 BIG_GRANT = 60 * 1024 * 1024
+FAR_GRANT = 64_000_000
+HARD_GRANT = 32 * 1024 * 1024
 ABSENT = 1024.0
 LANES = 128
 
@@ -162,76 +164,97 @@
             pltpu.SemaphoreType.DMA((slots,)),
             pltpu.SemaphoreType.DMA((3,)),
         ],
-        compiler_params=pltpu.CompilerParams(vmem_limit_bytes=BIG_GRANT),
+        compiler_params=pltpu.CompilerParams(vmem_limit_bytes=FAR_GRANT),
         name="pack_far",
     )(me, mail)
 
 
-def cycle_kernel(rate, tiles, q_ref, *refs):
+def cycle_kernel(rate, scale, start, end, q_ref, k_ref, *refs):
     q = q_ref[...]
+    k = k_ref[...]
     rows, feature = q.shape
-    keys = [ref[...] for ref in refs[:tiles]]
-    state_in, state_ref = (None, refs[tiles]) if len(refs) == tiles + 1 else refs[tiles:]
-    scores = [nt_dot(q, k) for k in keys]
-    m = jnp.max(functools.reduce(jnp.maximum, scores), axis=1, keepdims=True)
-    if state_in is not None:
+    s = nt_dot(q, k)
+    m = jnp.max(s, axis=1, keepdims=True)
+    if start:
+        (state_ref,) = refs
+        first = pl.multiple_of(pl.program_id(0) * rows, rows)
+        own = k_ref[pl.ds(first, rows), :].astype(jnp.float32)
+        positive = jnp.sum(q.astype(jnp.float32) * own, axis=1, keepdims=True)
+    else:
+        state_in = refs[0]
         old = state_in[:, feature : feature + 1]
+        positive = state_in[:, feature + 2 : feature + 3]
         m = jnp.maximum(m, old)
-    exps = [jnp.exp2((s - m) * rate) for s in scores]
-    l = jnp.sum(functools.reduce(jnp.add, exps), axis=1, keepdims=True)
-    num = jnp.zeros((rows, feature), jnp.float32)
-    if state_in is not None:
+    if end:
+        others_ref = refs[1]
+        m = jnp.maximum(m, others_ref[:, feature : feature + 1])
+    e = jnp.exp2((s - m) * rate)
+    l = jnp.sum(e, axis=1, keepdims=True)
+    num = jnp.dot(e.astype(jnp.bfloat16), k, preferred_element_type=jnp.float32)
+    if not start:
         shrink = jnp.exp2((old - m) * rate)
         l += state_in[:, feature + 1 : feature + 2] * shrink
-        num = state_in[:, :feature] * shrink
-    for e, k in zip(exps, keys):
-        num += jnp.dot(e.astype(jnp.bfloat16), k, preferred_element_type=jnp.float32)
-    state_ref[:, :feature] = num
+        num += state_in[:, :feature] * shrink
+    if end:
+        shrink = jnp.exp2((others_ref[:, feature : feature + 1] - m) * rate)
+        l += others_ref[:, feature + 1 : feature + 2] * shrink
+        num += others_ref[:, :feature] * shrink
     lane = lax.broadcasted_iota(jnp.int32, (rows, LANES), 1)
-    if state_in is not None:
-        positive = state_in[:, feature + 2 : feature + 3]
-    else:
-        first = pl.multiple_of(pl.program_id(0) * rows, rows)
-        own = refs[0][pl.ds(first, rows), :]
-        positive = jnp.sum(q.astype(jnp.float32) * own.astype(jnp.float32), axis=1, keepdims=True)
-    state_ref[:, feature:] = jnp.where(lane == 0, m, jnp.where(lane == 1, l, positive))
-
-
-def cycle_part(rate, q, keys, states, rows=256):
+    if not end:
+        state_ref = refs[-1]
+        state_ref[:, :feature] = num
+        state_ref[:, feature:] = jnp.where(lane == 0, m, jnp.where(lane == 1, l, positive))
+        return
+    own_ref, grad_ref, loss_ref, stats_ref = refs[2:]
+    inverse = 1.0 / l
+    grad_ref[...] = (num * inverse - own_ref[...].astype(jnp.float32)) * scale
+    loss = (m - positive) * scale + jnp.log(l)
+    table = jnp.where(lane == 0, m, jnp.where(lane == 1, inverse, loss))
+    flipped = table.T
+    stats_ref[...] = flipped[:8]
+    loss_ref[...] = flipped[2:3]
+
+
+def cycle_part(rate, scale, q, k, state=None, rest=None, rows=256):
     n, feature = q.shape
-    tiles = len(keys)
+    f32 = jnp.float32
     block = pl.BlockSpec((rows, feature), lambda i: (i, 0))
     wide = pl.BlockSpec((rows, feature + LANES), lambda i: (i, 0))
-    full = pl.BlockSpec((n, feature), lambda i: (0, 0))
+    full = pl.BlockSpec((n, feature), lambda i: (0, 0), pipeline_mode=pl.Buffered(1))
+    start, end = state is None, rest is not None
+    args, specs = [q, k], [block, full]
+    if not start:
+        args, specs = args + [state], specs + [wide]
+    shapes, outs = jax.ShapeDtypeStruct((n, feature + LANES), f32), wide
+    if end:
+        args, specs = args + list(rest), specs + [wide, block]
+        shapes = (jax.ShapeDtypeStruct((n, feature), f32), jax.ShapeDtypeStruct((1, n), f32), jax.ShapeDtypeStruct((8, n), f32))
+        outs = (block, pl.BlockSpec((1, rows), lambda i: (0, i)), pl.BlockSpec((8, rows), lambda i: (0, i)))
     return pl.pallas_call(
-        functools.partial(cycle_kernel, rate, tiles),
+        functools.partial(cycle_kernel, rate, scale, start, end),
         grid=(n // rows,),
-        out_shape=jax.ShapeDtypeStruct((n, feature + LANES), jnp.float32),
-        in_specs=[block] + [full] * tiles + [wide] * len(states),
-        out_specs=wide,
+        out_shape=shapes,
+        in_specs=specs,
+        out_specs=outs,
         compiler_params=pltpu.CompilerParams(vmem_limit_bytes=VMEM_LIMIT),
-        cost_estimate=pl.CostEstimate(flops=4 * n * tiles * n * feature, bytes_accessed=(tiles + 3) * n * feature * 2, transcendentals=tiles * n * n),
-        name="cycle_more" if states else "cycle",
-    )(q, *keys, *states)
-
-
-def hard_kernel(rate, scale, last, q_hbm, k_hbm, state_in, blocks, *rest):
-    if last:
-        grad, loss_ref, stats_ref, q_ref, k_ref, state, keys, scores, order, sems, out_sems = rest
-    else:
-        state_out, q_ref, state, keys, scores, order, sems, out_sems = rest
+        cost_estimate=pl.CostEstimate(flops=4 * n * n * feature, bytes_accessed=8 * n * feature, transcendentals=n * n),
+        name="cycle_own" if start else "cycle_last" if end else "cycle_more",
+    )(*args)
+
+
+def hard_kernel(rate, fresh, q_hbm, *refs):
+    state_in = None if fresh else refs[0]
+    blocks, state, q_ref, keys, scores, order, sems = refs[-7:]
     n, feature = q_ref.shape
     slots = blocks.shape[0]
     per = CHUNK // BLOCK
     load_keys = pltpu.make_async_copy(blocks, keys, sems.at[0])
     load_q = pltpu.make_async_copy(q_hbm, q_ref, sems.at[1])
-    load_state = pltpu.make_async_copy(state_in, state, sems.at[2])
     load_keys.start()
     load_q.start()
-    load_state.start()
-    if last:
-        load_own = pltpu.make_async_copy(k_hbm, k_ref, sems.at[3])
-        load_own.start()
+    if not fresh:
+        load_state = pltpu.make_async_copy(state_in, state, sems.at[2])
+        load_state.start()
     load_keys.wait()
     there = [(jnp.max(keys[s, :16, :128].astype(jnp.float32)) < ABSENT / 2).astype(jnp.int32) for s in range(slots)]
     live = jnp.int32(0)
@@ -257,12 +280,17 @@
         return m
 
     wide = lax.fori_loop(0, chunks, score, jnp.full((n, BLOCK), -jnp.inf, jnp.float32))
-    load_state.wait()
-    old = state[:, feature : feature + 1]
-    m = jnp.maximum(jnp.max(wide, axis=1, keepdims=True), old)
-    shrink = jnp.exp2((old - m) * rate)
-    kept = state[:, feature + 1 : feature + 2] * shrink
-    state[:, :feature] = state[:, :feature] * shrink
+    m = jnp.max(wide, axis=1, keepdims=True)
+    if fresh:
+        state[...] = jnp.zeros(state.shape, jnp.float32)
+        kept = 0.0
+    else:
+        load_state.wait()
+        old = state[:, feature : feature + 1]
+        m = jnp.maximum(m, old)
+        shrink = jnp.exp2((old - m) * rate)
+        kept = state[:, feature + 1 : feature + 2] * shrink
+        state[:, :feature] = state[:, :feature] * shrink
     for p in range(1, per):
         @pl.when(((chunks - 1) * per + p >= live) & (chunks > 0))
         def _(p=p):
@@ -278,62 +306,30 @@
     l = lax.fori_loop(0, chunks, weigh, jnp.zeros((n, BLOCK), jnp.float32))
     total = jnp.sum(l, axis=1, keepdims=True) + kept
     lane = lax.broadcasted_iota(jnp.int32, (n, LANES), 1)
-    if not last:
-        state[:, feature:] = jnp.where(lane == 0, m, jnp.where(lane == 1, total, state[:, feature:]))
-        save = pltpu.make_async_copy(state, state_out, out_sems.at[0])
-        save.start()
-        save.wait()
-        return
-    load_own.wait()
-    inverse = 1.0 / total
-    piece = n // out_sems.shape[0]
-    saves = []
-    for r in range(out_sems.shape[0]):
-        part = pl.ds(r * piece, piece)
-        gain = inverse[r * piece : (r + 1) * piece] * scale
-        state[part, :feature] = state[part, :feature] * gain - k_ref[part, :].astype(jnp.float32) * scale
-        saves.append(pltpu.make_async_copy(state.at[part, pl.ds(0, feature)], grad.at[part], out_sems.at[r]))
-        saves[-1].start()
-    positive = state[:, feature + 2 : feature + 3]
-    loss = (m - positive) * scale + jnp.log(total)
-    table = jnp.where(lane == 0, m, jnp.where(lane == 1, inverse, loss))
-    flipped = table.T
-    stats_ref[...] = flipped[:8]
-    loss_ref[...] = flipped[2:3]
-    for save in saves:
-        save.wait()
-
-
-def hard_part(rate, scale, last, q, k0, state, blocks):
+    state[:, feature:] = jnp.where(lane == 0, m, jnp.where(lane == 1, total, state[:, feature:]))
+
+
+def hard_part(rate, q, states, blocks, name):
     n, feature = q.shape
     slots = blocks.shape[0]
     f32 = jnp.float32
     keys = slots * BLOCK
-    scratch = [pltpu.VMEM(q.shape, q.dtype)]
-    shapes = [jax.ShapeDtypeStruct(state.shape, f32)]
-    specs = [whole(pl.ANY)]
-    if last:
-        scratch += [pltpu.VMEM(k0.shape, k0.dtype)]
-        shapes = [jax.ShapeDtypeStruct((n, feature), f32), jax.ShapeDtypeStruct((1, n), f32), jax.ShapeDtypeStruct((8, n), f32)]
-        specs = [whole(pl.ANY), whole(), whole()]
-    scratch += [
-        pltpu.VMEM(state.shape, f32),
-        pltpu.VMEM(blocks.shape, blocks.dtype),
-        pltpu.VMEM((keys // CHUNK, n, CHUNK), f32),
-        pltpu.SMEM((slots + CHUNK // BLOCK,), jnp.int32),
-        pltpu.SemaphoreType.DMA((4,)),
-        pltpu.SemaphoreType.DMA((4 if last else 1,)),
-    ]
     return pl.pallas_call(
-        functools.partial(hard_kernel, rate, scale, last),
-        out_shape=shapes,
-        in_specs=[whole(pl.ANY)] * 4,
-        out_specs=specs,
-        scratch_shapes=scratch,
-        compiler_params=pltpu.CompilerParams(vmem_limit_bytes=BIG_GRANT),
+        functools.partial(hard_kernel, rate, not states),
+        out_shape=jax.ShapeDtypeStruct((n, feature + LANES), f32),
+        in_specs=[whole(pl.ANY)] * (2 + len(states)),
+        out_specs=whole(),
+        scratch_shapes=[
+            pltpu.VMEM(q.shape, q.dtype),
+            pltpu.VMEM(blocks.shape, blocks.dtype),
+            pltpu.VMEM((keys // CHUNK, n, CHUNK), f32),
+            pltpu.SMEM((slots + CHUNK // BLOCK,), jnp.int32),
+            pltpu.SemaphoreType.DMA((3,)),
+        ],
+        compiler_params=pltpu.CompilerParams(vmem_limit_bytes=HARD_GRANT),
         cost_estimate=pl.CostEstimate(flops=2 * n * keys * feature, bytes_accessed=2 * keys * feature, transcendentals=n * keys // 2),
-        name="hard_last" if last else "hard_first",
-    )(q, k0, state, blocks)
+        name=name,
+    )(q, *states, blocks)
 
 
 def rtl_kernel(rate, scale, k_ref, n0_ref, n1_ref, n2_ref, s0_ref, s1_ref, s2_ref, out_ref):
@@ -384,18 +380,19 @@
     packed, mail = pack_own(at, targets, picks, own_keys, places)
     first = spread(packed)
     mail = lax.ppermute(mail, "dp", [(g, g ^ 2) for g in range(groups)])
-    rtl1 = passed_along(own_keys, "loop", 1)
-    mail, rtl1, back = lax.optimization_barrier((mail, rtl1, queries))
+    mail, onward, back = lax.optimization_barrier((mail, own_keys, queries))
+    rtl1 = passed_along(onward, "loop", 1)
+    net1 = passed_along(back, "loop", -1)
     second = spread(pack_far(at, mail, places, targets.shape[0]))
+
+    state = cycle_part(rate, scale, queries, own_keys)
+    state = hard_part(rate, queries, [state], first, "hard_first")
+    rtl1, net1, state = lax.optimization_barrier((rtl1, net1, state))
     rtl2 = passed_along(rtl1, "loop", 1)
-    net1 = passed_along(back, "loop", -1)
-
-    state = cycle_part(rate, queries, [own_keys, rtl1], [])
-    (state,) = hard_part(rate, scale, False, queries, own_keys, state, first)
-    net1, state = lax.optimization_barrier((net1, state))
     net2 = passed_along(net1, "loop", -1)
-    state = cycle_part(rate, queries, [rtl2], [state])
-    grad, loss, stats = hard_part(rate, scale, True, queries, own_keys, state, second)
+    state = cycle_part(rate, scale, queries, rtl1, state)
+    others = hard_part(rate, queries, [], second, "hard_second")
+    grad, loss, stats = cycle_part(rate, scale, queries, rtl2, state, (others, own_keys))
     stats1 = passed_along(stats, "loop", -1)
     stats2 = passed_along(stats, "loop", -2)
     rtl_grad = rtl_part(rate, scale, own_keys, queries, net1, net2, stats, stats1, stats2)

time: 97.8 us -> 101 us (1.033)
  the two profiles are of different devices: /device:TPU:1 before, /device:TPU:8 now
where the time goes in v6:
time: 101 us
  starting transfers between devices  40.7 us (40%)
  waiting for transfers between devices  34.4 us (34%)
  Pallas kernels  23.8 us (24%)
  local copies, waits for them, and re-layouts  1.05 us (1%)
    ppermute x6, starting transfers between devices, passed_along(): return lax.ppermute(block, axis, route)  23.8 us
    ppermute x1, waiting for transfers between devices, body(): mail = lax.ppermute(mail, 'dp', [(g, g ^ 2) for g in range(groups)])  16.1 us
    all_to_all x2, starting transfers between devices, spread(): lax.all_to_all(packed, 'dp', split_axis=0, concat_axis=0, axis_index_grou...  15 us
    ppermute x6, waiting for transfers between devices, passed_along(): return lax.ppermute(block, axis, route)  13.3 us
    pallas_call x2, Pallas kernels, hard_part(): pl.pallas_call(functools.partial(hard_kernel, rate, not states), out_shap...  7.41 us
    pallas_call x3, Pallas kernels, cycle_part(): pl.pallas_call(functools.partial(cycle_kernel, rate, scale, start, end),...  6.73 us
    all_to_all x2, waiting for transfers between devices, spread(): lax.all_to_all(packed, 'dp', split_axis=0, concat_axis=0, axis_index_grou...  5.04 us
    pallas_call x1, Pallas kernels, rtl_part(): pl.pallas_call(functools.partial(rtl_kernel, rate, scale), grid=(n // row...  4.42 us
  transfers between devices with their start and end apart: 9, of which 6 were waited for; matrix products, arithmetic and copies ran while one was open for 0% of the time, Pallas kernels for 17%

profile of v6, /device:TPU:8, one launch (start us, length us, event | category | flops | bytes accessed | tf_op | source)
XLA Modules:
  0.0 100.8 jit_solution(7805712105146232816)
XLA Ops:
  0.6 2.6 %pack_own.1 = (bf16[16,128,512]{2,1,0:T(8,128)(2,1)}, bf16[528,512]{1,0:T(8,128)(2,1)}) custom-call(s32[1]{0:T(128)} %bitcast.1.me, s32[16]{0:T(128)} %bitcast.19, s32[16]{0:T(128)} %bitcast.20, bf16[512,512]{1,0:T(8,128)(2,1)} %bitcast.14), custom_call_target="tpu_custom_call" | custom-call | tf_op jit(solution)/shard_map/pack_own/pallas_call | solution.py:105
  3.2 9.3 %all-to-all-start = ((bf16[16,128,512]{2,1,0:T(8,128)(2,1)}), bf16[16,128,512]{2,1,0:T(8,128)(2,1)S(1)}, u32[]{:S(2)}, u32[]{:S(2)}) async-start(bf16[16,128,512]{2,1,0:T(8,128)(2,1)} %get-tuple-element.17), calls=%async_computation | async-start | bytes 4194304 | tf_op jit(solution)/shard_map/all_to_all | solution.py:377
  12.5 1.9 %collective-permute-start = (bf16[528,512]{1,0:T(8,128)(2,1)}, bf16[528,512]{1,0:T(8,128)(2,1)}, u32[]{:S(2)}, u32[]{:S(2)}) collective-permute-start(bf16[528,512]{1,0:T(8,128)(2,1)} %get-tuple-element.14), channel_id=1, source_target_pairs={{0,64},{32,96},{64,0},{96,32},{128,192},{160,224},{192,128},{224,1... | collective-permute-start | bytes 1622024 | tf_op jit(solution)/shard_map/ppermute | solution.py:382
  14.4 16.1 %collective-permute-done.mail = bf16[528,512]{1,0:T(8,128)(2,1)} collective-permute-done((bf16[528,512]{1,0:T(8,128)(2,1)}, bf16[528,512]{1,0:T(8,128)(2,1)}, u32[]{:S(2)}, u32[]{:S(2)}) %collective-permute-start) | collective-permute-done | bytes 540704 | tf_op jit(solution)/shard_map/ppermute | solution.py:382
  30.6 2.7 %pack_far.1 = bf16[16,128,512]{2,1,0:T(8,128)(2,1)} custom-call(s32[1]{0:T(128)} %bitcast.1.me, bf16[528,512]{1,0:T(8,128)(2,1)} %collective-permute-done.mail), custom_call_target="tpu_custom_call" | custom-call | tf_op jit(solution)/shard_map/pack_far/pallas_call | solution.py:149
  33.2 0.0 copy-start
  33.3 5.0 %all-to-all-done.refs_1_ = bf16[16,128,512]{2,1,0:T(8,128)(2,1)S(1)} async-done(((bf16[16,128,512]{2,1,0:T(8,128)(2,1)}), bf16[16,128,512]{2,1,0:T(8,128)(2,1)S(1)}, u32[]{:S(2)}, u32[]{:S(2)}) %all-to-all-start) | async-done | bytes 2097184 | tf_op jit(solution)/shard_map/all_to_all | solution.py:377
  38.3 5.7 %all-to-all-start.1 = ((bf16[16,128,512]{2,1,0:T(8,128)(2,1)}), bf16[16,128,512]{2,1,0:T(8,128)(2,1)}, u32[]{:S(2)}, u32[]{:S(2)}) async-start(bf16[16,128,512]{2,1,0:T(8,128)(2,1)} %pack_far.1), calls=%async_computation.1 | async-start | bytes 4194304 | tf_op jit(solution)/shard_map/all_to_all | solution.py:377
  44.0 1.9 %collective-permute-start.1 = (bf16[512,512]{1,0:T(8,128)(2,1)}, bf16[512,512]{1,0:T(8,128)(2,1)}, u32[]{:S(2)}, u32[]{:S(2)}) collective-permute-start(bf16[512,512]{1,0:T(8,128)(2,1)} %bitcast.15), channel_id=1, source_target_pairs={{31,0},{0,1},{1,2},{2,3},{3,4},{4,5},{5,6},{6,7},{7,8},{8,9},{9,10... | collective-permute-start | bytes 1572872 | tf_op jit(solution)/shard_map/ppermute | solution.py:25
  45.9 0.0 copy-done
  45.9 7.9 %collective-permute-start.2 = (bf16[512,512]{1,0:T(8,128)(2,1)S(1)}, bf16[512,512]{1,0:T(8,128)(2,1)}, u32[]{:S(2)}, u32[]{:S(2)}) collective-permute-start(bf16[512,512]{1,0:T(8,128)(2,1)S(1)} %bitcast.7), channel_id=1, source_target_pairs={{1,0},{2,1},{3,2},{4,3},{5,4},{6,5},{7,6},{8,7},{9,8},{10,9},{11,1... | collective-permute-start | bytes 1572872 | tf_op jit(solution)/shard_map/ppermute | solution.py:25
  53.8 0.0 copy-start.1
  53.8 1.0 %copy-done.1 = bf16[1,512,512]{2,1,0:T(8,128)(2,1)S(1)} copy-done((bf16[1,512,512]{2,1,0:T(8,128)(2,1)S(1)}, bf16[1,512,512]{2,1,0:T(8,128)(2,1)}, u32[]{:S(2)}) %copy-start.1) | copy-done | bytes 524312
  54.8 1.3 %cycle_own.1.refs_0_ = f32[512,640]{1,0:T(8,128)S(1)} custom-call(bf16[512,512]{1,0:T(8,128)(2,1)S(1)} %bitcast.8, bf16[512,512]{1,0:T(8,128)(2,1)S(1)} %bitcast.16), custom_call_target="tpu_custom_call" | custom-call | flops 536870912 | bytes 2097152 | tf_op jit(solution)/shard_map/cycle_own/pallas_call | solution.py:233
  56.1 3.3 %hard_first.1.refs_0_ = f32[512,640]{1,0:T(8,128)S(1)} custom-call(bf16[512,512]{1,0:T(8,128)(2,1)S(1)} %bitcast.9, f32[512,640]{1,0:T(8,128)S(1)} %cycle_own.1.refs_0_, bf16[16,128,512]{2,1,0:T(8,128)(2,1)S(1)} %all-to-all-done.refs_1_), custom_call_target="tpu_custom_call" | custom-call | flops 1073741824 | bytes 2097152 | tf_op jit(solution)/shard_map/hard_first/pallas_call | solution.py:317
  59.5 4.9 %collective-permute-done.1.k_ref = bf16[512,512]{1,0:T(8,128)(2,1)} collective-permute-done((bf16[512,512]{1,0:T(8,128)(2,1)}, bf16[512,512]{1,0:T(8,128)(2,1)}, u32[]{:S(2)}, u32[]{:S(2)}) %collective-permute-start.1) | collective-permute-done | bytes 524320 | tf_op jit(solution)/shard_map/ppermute | solution.py:25
  64.4 0.9 collective-permute-done.2.n1_ref
  65.2 1.9 %collective-permute-start.3 = (bf16[512,512]{1,0:T(8,128)(2,1)}, bf16[512,512]{1,0:T(8,128)(2,1)S(1)}, u32[]{:S(2)}, u32[]{:S(2)}) collective-permute-start(bf16[512,512]{1,0:T(8,128)(2,1)} %collective-permute-done.1.k_ref), channel_id=1, source_target_pairs={{31,0},{0,1},{1,2},{2,3},{3,4},{4,5},{5,6},{6,7},{7,8},{8,9},{9,10... | collective-permute-start | bytes 1572872 | tf_op jit(solution)/shard_map/ppermute | solution.py:25
  67.2 6.6 %collective-permute-start.4 = (bf16[512,512]{1,0:T(8,128)(2,1)}, bf16[512,512]{1,0:T(8,128)(2,1)S(1)}, u32[]{:S(2)}, u32[]{:S(2)}) collective-permute-start(bf16[512,512]{1,0:T(8,128)(2,1)} %collective-permute-done.2.n1_ref), channel_id=1, source_target_pairs={{1,0},{2,1},{3,2},{4,3},{5,4},{6,5},{7,6},{8,7},{9,8},{10,9},{11,1... | collective-permute-start | bytes 1572872 | tf_op jit(solution)/shard_map/ppermute | solution.py:25
  73.8 2.7 %cycle_more.1.refs_0_ = f32[512,640]{1,0:T(8,128)S(1)} custom-call(bf16[512,512]{1,0:T(8,128)(2,1)S(1)} %bitcast.10, bf16[512,512]{1,0:T(8,128)(2,1)} %collective-permute-done.1.k_ref, f32[512,640]{1,0:T(8,128)S(1)} %hard_first.1.refs_0_), custom_call_target="tpu_custom_call" | custom-call | flops 536870912 | bytes 2097152 | tf_op jit(solution)/shard_map/cycle_more/pallas_call | solution.py:233
  76.5 0.0 copy-start.2
  76.5 0.0 all-to-all-done.1.refs_0_
  76.5 4.1 %hard_second.1.refs_1_ = f32[512,640]{1,0:T(8,128)S(1)} custom-call(bf16[512,512]{1,0:T(8,128)(2,1)S(1)} %bitcast.11, bf16[16,128,512]{2,1,0:T(8,128)(2,1)} %all-to-all-done.1.refs_0_), custom_call_target="tpu_custom_call" | custom-call | flops 1073741824 | bytes 2097152 | tf_op jit(solution)/shard_map/hard_second/pallas_call | solution.py:317
  80.6 2.9 %collective-permute-done.3.k_ref = bf16[512,512]{1,0:T(8,128)(2,1)S(1)} collective-permute-done((bf16[512,512]{1,0:T(8,128)(2,1)}, bf16[512,512]{1,0:T(8,128)(2,1)S(1)}, u32[]{:S(2)}, u32[]{:S(2)}) %collective-permute-start.3) | collective-permute-done | bytes 524320 | tf_op jit(solution)/shard_map/ppermute | solution.py:25
  83.5 0.0 copy-done.2
  83.5 2.8 %cycle_last.1 = (f32[512,512]{1,0:T(8,128)}, f32[1,512]{1,0:T(1,128)}, f32[8,512]{1,0:T(8,128)S(1)}) custom-call(bf16[512,512]{1,0:T(8,128)(2,1)S(1)} %bitcast.12, bf16[512,512]{1,0:T(8,128)(2,1)S(1)} %collective-permute-done.3.k_ref, f32[512,640]{1,0:T(8,128)S(1)} %cycle_more.1.refs_0_, f32[512,640]{1,0:T(8,128)S(1)} %hard_second.1.refs_1_, ...), custom_call_target="tpu_custom_call" | custom-call | flops 536870912 | bytes 2097152 | tf_op jit(solution)/shard_map/cycle_last/pallas_call | solution.py:233
  86.2 3.6 %collective-permute-start.5 = (f32[8,512]{1,0:T(8,128)S(1)}, f32[8,512]{1,0:T(8,128)S(1)}, u32[]{:S(2)}, u32[]{:S(2)}) collective-permute-start(f32[8,512]{1,0:T(8,128)S(1)} %get-tuple-element.24.s0_ref), channel_id=1, source_target_pairs={{1,0},{2,1},{3,2},{4,3},{5,4},{6,5},{7,6},{8,7},{9,8},{10,9},{11,1... | collective-permute-start | bytes 49160 | tf_op jit(solution)/shard_map/ppermute | solution.py:25
  89.9 1.9 %collective-permute-start.6 = (f32[8,512]{1,0:T(8,128)S(1)}, f32[8,512]{1,0:T(8,128)S(1)}, u32[]{:S(2)}, u32[]{:S(2)}) collective-permute-start(f32[8,512]{1,0:T(8,128)S(1)} %get-tuple-element.24.s0_ref), channel_id=1, source_target_pairs={{2,0},{3,1},{4,2},{5,3},{6,4},{7,5},{8,6},{9,7},{10,8},{11,9},{12,... | collective-permute-start | bytes 49160 | tf_op jit(solution)/shard_map/ppermute | solution.py:25
  91.8 0.0 collective-permute-done.4.n2_ref
  91.8 0.0 collective-permute-done.5.s1_ref
  91.8 4.5 %collective-permute-done.6.s2_ref = f32[8,512]{1,0:T(8,128)S(1)} collective-permute-done((f32[8,512]{1,0:T(8,128)S(1)}, f32[8,512]{1,0:T(8,128)S(1)}, u32[]{:S(2)}, u32[]{:S(2)}) %collective-permute-start.6) | collective-permute-done | bytes 16416 | tf_op jit(solution)/shard_map/ppermute | solution.py:25
  96.4 4.4 %rtl.1 = f32[512,512]{1,0:T(8,128)} custom-call(bf16[512,512]{1,0:T(8,128)(2,1)S(1)} %bitcast.18, bf16[512,512]{1,0:T(8,128)(2,1)S(1)} %bitcast.13, bf16[512,512]{1,0:T(8,128)(2,1)} %collective-permute-done.2.n1_ref, bf16[512,512]{1,0:T(8,128)(2,1)S(1)} %collective-permute-done.4.n2_ref, f32[8,512]{1,0:T(8,128)S(1)} %get-tuple-element.24.s0_ref, ...), custom_call_target="tpu_custom_call" | custom-call | flops 1610612736 | bytes 3145728 | tf_op jit(solution)/shard_map/rtl/pallas_call | solution.py:352
Async XLA Ops:
  3.2 35.1 %all-to-all-start = ((bf16[16,128,512]{2,1,0:T(8,128)(2,1)}), bf16[16,128,512]{2,1,0:T(8,128)(2,1)S(1)}, u32[]{:S(2)}, u32[]{:S(2)}) async-start(bf16[16,128,512]{2,1,0:T(8,128)(2,1)} %get-tuple-element.17), calls=%async_computation | async-start | bytes 4194304 | tf_op jit(solution)/shard_map/all_to_all | solution.py:377
  12.5 18.0 %collective-permute-start = (bf16[528,512]{1,0:T(8,128)(2,1)}, bf16[528,512]{1,0:T(8,128)(2,1)}, u32[]{:S(2)}, u32[]{:S(2)}) collective-permute-start(bf16[528,512]{1,0:T(8,128)(2,1)} %get-tuple-element.14), channel_id=1, source_target_pairs={{0,64},{32,96},{64,0},{96,32},{128,192},{160,224},{192,128},{224,1... | collective-permute-start | bytes 1622024 | tf_op jit(solution)/shard_map/ppermute | solution.py:382
  33.2 12.6 %copy-start = (bf16[1,512,512]{2,1,0:T(8,128)(2,1)S(1)}, bf16[1,512,512]{2,1,0:T(8,128)(2,1)}, u32[]{:S(2)}) copy-start(bf16[1,512,512]{2,1,0:T(8,128)(2,1)} %param.4) | copy-start | bytes 1572868
  38.3 38.2 %all-to-all-start.1 = ((bf16[16,128,512]{2,1,0:T(8,128)(2,1)}), bf16[16,128,512]{2,1,0:T(8,128)(2,1)}, u32[]{:S(2)}, u32[]{:S(2)}) async-start(bf16[16,128,512]{2,1,0:T(8,128)(2,1)} %pack_far.1), calls=%async_computation.1 | async-start | bytes 4194304 | tf_op jit(solution)/shard_map/all_to_all | solution.py:377
  44.0 20.4 %collective-permute-start.1 = (bf16[512,512]{1,0:T(8,128)(2,1)}, bf16[512,512]{1,0:T(8,128)(2,1)}, u32[]{:S(2)}, u32[]{:S(2)}) collective-permute-start(bf16[512,512]{1,0:T(8,128)(2,1)} %bitcast.15), channel_id=1, source_target_pairs={{31,0},{0,1},{1,2},{2,3},{3,4},{4,5},{5,6},{6,7},{7,8},{8,9},{9,10... | collective-permute-start | bytes 1572872 | tf_op jit(solution)/shard_map/ppermute | solution.py:25
  45.9 19.3 %collective-permute-start.2 = (bf16[512,512]{1,0:T(8,128)(2,1)S(1)}, bf16[512,512]{1,0:T(8,128)(2,1)}, u32[]{:S(2)}, u32[]{:S(2)}) collective-permute-start(bf16[512,512]{1,0:T(8,128)(2,1)S(1)} %bitcast.7), channel_id=1, source_target_pairs={{1,0},{2,1},{3,2},{4,3},{5,4},{6,5},{7,6},{8,7},{9,8},{10,9},{11,1... | collective-permute-start | bytes 1572872 | tf_op jit(solution)/shard_map/ppermute | solution.py:25
  53.8 1.0 %copy-start.1 = (bf16[1,512,512]{2,1,0:T(8,128)(2,1)S(1)}, bf16[1,512,512]{2,1,0:T(8,128)(2,1)}, u32[]{:S(2)}) copy-start(bf16[1,512,512]{2,1,0:T(8,128)(2,1)} %param.5) | copy-start | bytes 1572868
  65.2 18.2 %collective-permute-start.3 = (bf16[512,512]{1,0:T(8,128)(2,1)}, bf16[512,512]{1,0:T(8,128)(2,1)S(1)}, u32[]{:S(2)}, u32[]{:S(2)}) collective-permute-start(bf16[512,512]{1,0:T(8,128)(2,1)} %collective-permute-done.1.k_ref), channel_id=1, source_target_pairs={{31,0},{0,1},{1,2},{2,3},{3,4},{4,5},{5,6},{6,7},{7,8},{8,9},{9,10... | collective-permute-start | bytes 1572872 | tf_op jit(solution)/shard_map/ppermute | solution.py:25
  67.2 24.6 %collective-permute-start.4 = (bf16[512,512]{1,0:T(8,128)(2,1)}, bf16[512,512]{1,0:T(8,128)(2,1)S(1)}, u32[]{:S(2)}, u32[]{:S(2)}) collective-permute-start(bf16[512,512]{1,0:T(8,128)(2,1)} %collective-permute-done.2.n1_ref), channel_id=1, source_target_pairs={{1,0},{2,1},{3,2},{4,3},{5,4},{6,5},{7,6},{8,7},{9,8},{10,9},{11,1... | collective-permute-start | bytes 1572872 | tf_op jit(solution)/shard_map/ppermute | solution.py:25
  76.5 7.0 %copy-start.2 = (bf16[1,512,512]{2,1,0:T(8,128)(2,1)S(1)}, bf16[1,512,512]{2,1,0:T(8,128)(2,1)}, u32[]{:S(2)}) copy-start(bf16[1,512,512]{2,1,0:T(8,128)(2,1)} %param.5) | copy-start | bytes 1572868
  86.2 5.6 %collective-permute-start.5 = (f32[8,512]{1,0:T(8,128)S(1)}, f32[8,512]{1,0:T(8,128)S(1)}, u32[]{:S(2)}, u32[]{:S(2)}) collective-permute-start(f32[8,512]{1,0:T(8,128)S(1)} %get-tuple-element.24.s0_ref), channel_id=1, source_target_pairs={{1,0},{2,1},{3,2},{4,3},{5,4},{6,5},{7,6},{8,7},{9,8},{10,9},{11,1... | collective-permute-start | bytes 49160 | tf_op jit(solution)/shard_map/ppermute | solution.py:25
  89.9 6.5 %collective-permute-start.6 = (f32[8,512]{1,0:T(8,128)S(1)}, f32[8,512]{1,0:T(8,128)S(1)}, u32[]{:S(2)}, u32[]{:S(2)}) collective-permute-start(f32[8,512]{1,0:T(8,128)S(1)} %get-tuple-element.24.s0_ref), channel_id=1, source_target_pairs={{2,0},{3,1},{4,2},{5,3},{6,4},{7,5},{8,6},{9,7},{10,8},{11,9},{12,... | collective-permute-start | bytes 49160 | tf_op jit(solution)/shard_map/ppermute | solution.py:25

commit v7 on v6

--- a/solution.py
+++ b/solution.py
@@ -169,43 +169,35 @@
     )(me, mail)
 
 
-def cycle_kernel(rate, scale, start, end, q_ref, k_ref, *refs):
+def cycle_kernel(rate, scale, tiles, end, q_ref, *refs):
     q = q_ref[...]
-    k = k_ref[...]
     rows, feature = q.shape
-    s = nt_dot(q, k)
-    m = jnp.max(s, axis=1, keepdims=True)
-    if start:
-        (state_ref,) = refs
-        first = pl.multiple_of(pl.program_id(0) * rows, rows)
-        own = k_ref[pl.ds(first, rows), :].astype(jnp.float32)
-        positive = jnp.sum(q.astype(jnp.float32) * own, axis=1, keepdims=True)
-    else:
-        state_in = refs[0]
-        old = state_in[:, feature : feature + 1]
-        positive = state_in[:, feature + 2 : feature + 3]
-        m = jnp.maximum(m, old)
-    if end:
-        others_ref = refs[1]
-        m = jnp.maximum(m, others_ref[:, feature : feature + 1])
-    e = jnp.exp2((s - m) * rate)
-    l = jnp.sum(e, axis=1, keepdims=True)
-    num = jnp.dot(e.astype(jnp.bfloat16), k, preferred_element_type=jnp.float32)
-    if not start:
-        shrink = jnp.exp2((old - m) * rate)
-        l += state_in[:, feature + 1 : feature + 2] * shrink
-        num += state_in[:, :feature] * shrink
-    if end:
-        shrink = jnp.exp2((others_ref[:, feature : feature + 1] - m) * rate)
-        l += others_ref[:, feature + 1 : feature + 2] * shrink
-        num += others_ref[:, :feature] * shrink
+    first = pl.multiple_of(pl.program_id(0) * rows, rows)
+    keys = [ref[...] for ref in refs[:tiles]]
+    scores = [nt_dot(q, k) for k in keys]
+    m = jnp.max(functools.reduce(jnp.maximum, scores), axis=1, keepdims=True)
+    states = refs[tiles : tiles + 2] if end else ()
+    for state in states:
+        m = jnp.maximum(m, state[:, feature : feature + 1])
+    exps = [jnp.exp2((s - m) * rate) for s in scores]
+    l = jnp.sum(functools.reduce(jnp.add, exps), axis=1, keepdims=True)
+    num = jnp.dot(exps[0].astype(jnp.bfloat16), keys[0], preferred_element_type=jnp.float32)
+    for e, k in zip(exps[1:], keys[1:]):
+        num += jnp.dot(e.astype(jnp.bfloat16), k, preferred_element_type=jnp.float32)
+    for state in states:
+        shrink = jnp.exp2((state[:, feature : feature + 1] - m) * rate)
+        l += state[:, feature + 1 : feature + 2] * shrink
+        num += state[:, :feature] * shrink
     lane = lax.broadcasted_iota(jnp.int32, (rows, LANES), 1)
     if not end:
         state_ref = refs[-1]
+        own = refs[0][pl.ds(first, rows), :].astype(jnp.float32)
+        positive = jnp.sum(q.astype(jnp.float32) * own, axis=1, keepdims=True)
         state_ref[:, :feature] = num
         state_ref[:, feature:] = jnp.where(lane == 0, m, jnp.where(lane == 1, l, positive))
         return
-    own_ref, grad_ref, loss_ref, stats_ref = refs[2:]
+    positive = states[0][:, feature + 2 : feature + 3]
+    own_ref, grad_ref, loss_ref, stats_ref = refs[tiles + 2 :]
     inverse = 1.0 / l
     grad_ref[...] = (num * inverse - own_ref[...].astype(jnp.float32)) * scale
     loss = (m - positive) * scale + jnp.log(l)
@@ -215,30 +207,29 @@
     loss_ref[...] = flipped[2:3]
 
 
-def cycle_part(rate, scale, q, k, state=None, rest=None, rows=256):
+def cycle_part(rate, scale, q, keys, states=(), own=None, rows=256):
     n, feature = q.shape
     f32 = jnp.float32
+    tiles = len(keys)
     block = pl.BlockSpec((rows, feature), lambda i: (i, 0))
     wide = pl.BlockSpec((rows, feature + LANES), lambda i: (i, 0))
     full = pl.BlockSpec((n, feature), lambda i: (0, 0), pipeline_mode=pl.Buffered(1))
-    start, end = state is None, rest is not None
-    args, specs = [q, k], [block, full]
-    if not start:
-        args, specs = args + [state], specs + [wide]
+    end = own is not None
+    args, specs = [q, *keys, *states], [block] + [full] * tiles + [wide] * len(states)
     shapes, outs = jax.ShapeDtypeStruct((n, feature + LANES), f32), wide
     if end:
-        args, specs = args + list(rest), specs + [wide, block]
+        args, specs = args + [own], specs + [block]
         shapes = (jax.ShapeDtypeStruct((n, feature), f32), jax.ShapeDtypeStruct((1, n), f32), jax.ShapeDtypeStruct((8, n), f32))
         outs = (block, pl.BlockSpec((1, rows), lambda i: (0, i)), pl.BlockSpec((8, rows), lambda i: (0, i)))
     return pl.pallas_call(
-        functools.partial(cycle_kernel, rate, scale, start, end),
+        functools.partial(cycle_kernel, rate, scale, tiles, end),
         grid=(n // rows,),
         out_shape=shapes,
         in_specs=specs,
         out_specs=outs,
         compiler_params=pltpu.CompilerParams(vmem_limit_bytes=VMEM_LIMIT),
-        cost_estimate=pl.CostEstimate(flops=4 * n * n * feature, bytes_accessed=8 * n * feature, transcendentals=n * n),
-        name="cycle_own" if start else "cycle_last" if end else "cycle_more",
+        cost_estimate=pl.CostEstimate(flops=4 * n * tiles * n * feature, bytes_accessed=8 * n * feature, transcendentals=tiles * n * n),
+        name="cycle_last" if end else "cycle_own",
     )(*args)
 
 
@@ -380,19 +371,28 @@
     packed, mail = pack_own(at, targets, picks, own_keys, places)
     first = spread(packed)
     mail = lax.ppermute(mail, "dp", [(g, g ^ 2) for g in range(groups)])
-    mail, onward, back = lax.optimization_barrier((mail, own_keys, queries))
-    rtl1 = passed_along(onward, "loop", 1)
-    net1 = passed_along(back, "loop", -1)
+    size = lax.axis_size("loop")
+    line = size // 2
+    spot = lax.axis_index("loop") % line
+    up = [(i, i + 1) for i in range(size) if i % line < line - 1]
+    down = [(i, i - 1) for i in range(size) if i % line > 0]
+    seam = [(i, (i + 1) % size) for i in range(line - 1, size, line)] + [(i, (i - 1) % size) for i in range(0, size, line)]
+    rtl1 = lax.ppermute(own_keys, "loop", up)
+    net1 = lax.ppermute(queries, "loop", down)
+    edge = jnp.where(spot == 0, queries, own_keys)
+    mail, rtl1, net1, edge = lax.optimization_barrier((mail, rtl1, net1, edge))
+    edge = lax.ppermute(edge, "loop", seam)
     second = spread(pack_far(at, mail, places, targets.shape[0]))
 
-    state = cycle_part(rate, scale, queries, own_keys)
+    state = cycle_part(rate, scale, queries, [own_keys])
     state = hard_part(rate, queries, [state], first, "hard_first")
-    rtl1, net1, state = lax.optimization_barrier((rtl1, net1, state))
+    edge, state = lax.optimization_barrier((edge, state))
+    rtl1 = jnp.where(spot == 0, edge, rtl1)
+    net1 = jnp.where(spot == line - 1, edge, net1)
     rtl2 = passed_along(rtl1, "loop", 1)
     net2 = passed_along(net1, "loop", -1)
-    state = cycle_part(rate, scale, queries, rtl1, state)
     others = hard_part(rate, queries, [], second, "hard_second")
-    grad, loss, stats = cycle_part(rate, scale, queries, rtl2, state, (others, own_keys))
+    grad, loss, stats = cycle_part(rate, scale, queries, [rtl1, rtl2], [state, others], own_keys)
     stats1 = passed_along(stats, "loop", -1)
     stats2 = passed_along(stats, "loop", -2)
     rtl_grad = rtl_part(rate, scale, own_keys, queries, net1, net2, stats, stats1, stats2)

time: 101 us -> 102 us (level)
  the two profiles are of different devices: /device:TPU:8 before, /device:TPU:32 now
where the time goes in v7:
time: 102 us; the launch traced here: 101 us
  starting transfers between devices  50.4 us (49%)
  Pallas kernels  22.7 us (22%)
  waiting for transfers between devices  21.6 us (21%)
  other arithmetic  3.37 us (3%)
  local copies, waits for them, and re-layouts  2.16 us (2%)
    ppermute x4, starting transfers between devices, passed_along(): return lax.ppermute(block, axis, route)  29.2 us
    ppermute x4, waiting for transfers between devices, passed_along(): return lax.ppermute(block, axis, route)  9.63 us
    all_to_all x2, starting transfers between devices, spread(): lax.all_to_all(packed, 'dp', split_axis=0, concat_axis=0, axis_index_grou...  8.97 us
    ppermute x1, waiting for transfers between devices, body(): net1 = lax.ppermute(queries, 'loop', down)  8.36 us
    pallas_call x2, Pallas kernels, hard_part(): pl.pallas_call(functools.partial(hard_kernel, rate, not states), out_shap...  7.33 us
    pallas_call x2, Pallas kernels, cycle_part(): pl.pallas_call(functools.partial(cycle_kernel, rate, scale, tiles, end),...  5.6 us
    ppermute x1, starting transfers between devices, body(): mail = lax.ppermute(mail, 'dp', [(g, g ^ 2) for g in range(groups)])  4.88 us
    pallas_call x1, Pallas kernels, rtl_part(): pl.pallas_call(functools.partial(rtl_kernel, rate, scale), grid=(n // row...  4.43 us
  transfers between devices with their start and end apart: 10, of which 4 were waited for; matrix products, arithmetic and copies ran while one was open for 3% of the time, Pallas kernels for 15%

profile of v7, /device:TPU:32, one launch (start us, length us, event | category | flops | bytes accessed | tf_op | source)
XLA Modules:
  0.0 101.0 jit_solution(15599535388265945228)
XLA Ops:
  0.6 2.6 %pack_own.1 = (bf16[16,128,512]{2,1,0:T(8,128)(2,1)}, bf16[528,512]{1,0:T(8,128)(2,1)}) custom-call(s32[1]{0:T(128)} %bitcast.1.me, s32[16]{0:T(128)} %bitcast.20, s32[16]{0:T(128)} %bitcast.21, bf16[512,512]{1,0:T(8,128)(2,1)} %bitcast.15), custom_call_target="tpu_custom_call" | custom-call | tf_op jit(solution)/shard_map/pack_own/pallas_call | solution.py:105
  3.3 0.0 copy-start
  3.3 4.6 %all-to-all-start = ((bf16[16,128,512]{2,1,0:T(8,128)(2,1)}), bf16[16,128,512]{2,1,0:T(8,128)(2,1)S(1)}, u32[]{:S(2)}, u32[]{:S(2)}) async-start(bf16[16,128,512]{2,1,0:T(8,128)(2,1)} %get-tuple-element.16), calls=%async_computation | async-start | bytes 4194304 | tf_op jit(solution)/shard_map/all_to_all | solution.py:368
  7.8 4.9 %collective-permute-start = (bf16[528,512]{1,0:T(8,128)(2,1)}, bf16[528,512]{1,0:T(8,128)(2,1)}, u32[]{:S(2)}, u32[]{:S(2)}) collective-permute-start(bf16[528,512]{1,0:T(8,128)(2,1)} %get-tuple-element.14), channel_id=1, source_target_pairs={{0,64},{32,96},{64,0},{96,32},{128,192},{160,224},{192,128},{224,1... | collective-permute-start | bytes 1622024 | tf_op jit(solution)/shard_map/ppermute | solution.py:373
  12.7 0.0 copy-done
  12.7 3.6 %collective-permute-start.2 = (bf16[512,512]{1,0:T(8,128)(2,1)S(1)}, bf16[512,512]{1,0:T(8,128)(2,1)}, u32[]{:S(2)}, u32[]{:S(2)}) collective-permute-start(bf16[512,512]{1,0:T(8,128)(2,1)S(1)} %bitcast.9), channel_id=1, source_target_pairs={{1,0},{2,1},{3,2},{4,3},{5,4},{6,5},{7,6},{8,7},{9,8},{10,9},{11,1... | collective-permute-start | bytes 1572872 | tf_op jit(solution)/shard_map/ppermute | solution.py:381
  16.4 2.2 %collective-permute-start.1 = (bf16[512,512]{1,0:T(8,128)(2,1)}, bf16[512,512]{1,0:T(8,128)(2,1)}, u32[]{:S(2)}, u32[]{:S(2)}) collective-permute-start(bf16[512,512]{1,0:T(8,128)(2,1)} %bitcast.16), channel_id=1, source_target_pairs={{0,1},{1,2},{2,3},{3,4},{4,5},{5,6},{6,7},{7,8},{8,9},{9,10},{10,1... | collective-permute-start | bytes 1572872 | tf_op jit(solution)/shard_map/ppermute | solution.py:380
  18.6 1.9 %broadcast_select_fusion.2 = bf16[512,512]{1,0:T(8,128)(2,1)} fusion(pred[]{:T(512)S(6)} %eq.9, bf16[1,512,512]{2,1,0:T(8,128)(2,1)} %param.5, bf16[1,512,512]{2,1,0:T(8,128)(2,1)S(1)} %copy-done), kind=kLoop, calls=%fused_computation.2 | loop fusion | flops 262144 | bytes 1572865 | tf_op jit(solution)/shard_map/jit(_where)/select_n | solution.py:382
  20.5 8.4 %collective-permute-done.2 = bf16[512,512]{1,0:T(8,128)(2,1)} collective-permute-done((bf16[512,512]{1,0:T(8,128)(2,1)S(1)}, bf16[512,512]{1,0:T(8,128)(2,1)}, u32[]{:S(2)}, u32[]{:S(2)}) %collective-permute-start.2) | collective-permute-done | bytes 524320 | tf_op jit(solution)/shard_map/ppermute | solution.py:381
  28.9 3.6 %collective-permute-done.1 = bf16[512,512]{1,0:T(8,128)(2,1)} collective-permute-done((bf16[512,512]{1,0:T(8,128)(2,1)}, bf16[512,512]{1,0:T(8,128)(2,1)}, u32[]{:S(2)}, u32[]{:S(2)}) %collective-permute-start.1) | collective-permute-done | bytes 524320 | tf_op jit(solution)/shard_map/ppermute | solution.py:380
  32.5 0.0 collective-permute-done.mail
  32.5 2.7 %pack_far.1 = bf16[16,128,512]{2,1,0:T(8,128)(2,1)} custom-call(s32[1]{0:T(128)} %bitcast.1.me, bf16[528,512]{1,0:T(8,128)(2,1)} %collective-permute-done.mail), custom_call_target="tpu_custom_call" | custom-call | tf_op jit(solution)/shard_map/pack_far/pallas_call | solution.py:149
  35.2 0.0 all-to-all-done.refs_1_
  35.2 4.4 %all-to-all-start.1 = ((bf16[16,128,512]{2,1,0:T(8,128)(2,1)}), bf16[16,128,512]{2,1,0:T(8,128)(2,1)}, u32[]{:S(2)}, u32[]{:S(2)}) async-start(bf16[16,128,512]{2,1,0:T(8,128)(2,1)} %pack_far.1), calls=%async_computation.1 | async-start | bytes 4194304 | tf_op jit(solution)/shard_map/all_to_all | solution.py:368
  39.6 1.5 %collective-permute-start.3 = (bf16[512,512]{1,0:T(8,128)(2,1)}, bf16[512,512]{1,0:T(8,128)(2,1)}, u32[]{:S(2)}, u32[]{:S(2)}) collective-permute-start(bf16[512,512]{1,0:T(8,128)(2,1)} %broadcast_select_fusion.2), channel_id=1, source_target_pairs={{15,16},{31,0},{0,31},{16,15},{47,48},{63,32},{32,63},{48,47},{79,... | collective-permute-start | bytes 1572872 | tf_op jit(solution)/shard_map/ppermute | solution.py:384
  41.1 0.0 copy-start.1
  41.1 1.0 %copy-done.1 = bf16[1,512,512]{2,1,0:T(8,128)(2,1)S(1)} copy-done((bf16[1,512,512]{2,1,0:T(8,128)(2,1)S(1)}, bf16[1,512,512]{2,1,0:T(8,128)(2,1)}, u32[]{:S(2)}) %copy-start.1) | copy-done | bytes 524312
  42.1 1.3 %cycle_own.1.refs_0_ = f32[512,640]{1,0:T(8,128)S(1)} custom-call(bf16[512,512]{1,0:T(8,128)(2,1)S(1)} %bitcast.10, bf16[512,512]{1,0:T(8,128)(2,1)S(1)} %bitcast.17), custom_call_target="tpu_custom_call" | custom-call | flops 536870912 | bytes 2097152 | tf_op jit(solution)/shard_map/cycle_own/pallas_call | solution.py:224
  43.4 3.3 %hard_first.1.refs_2_ = f32[512,640]{1,0:T(8,128)S(1)} custom-call(bf16[512,512]{1,0:T(8,128)(2,1)S(1)} %bitcast.11, f32[512,640]{1,0:T(8,128)S(1)} %cycle_own.1.refs_0_, bf16[16,128,512]{2,1,0:T(8,128)(2,1)S(1)} %all-to-all-done.refs_1_), custom_call_target="tpu_custom_call" | custom-call | flops 1073741824 | bytes 2097152 | tf_op jit(solution)/shard_map/hard_first/pallas_call | solution.py:308
  46.7 0.0 copy-start.3
  46.7 1.1 %copy-done.3 = f32[512,640]{1,0:T(8,128)} copy-done((f32[512,640]{1,0:T(8,128)}, f32[512,640]{1,0:T(8,128)S(1)}, u32[]{:S(2)}) %copy-start.3) | copy-done | bytes 1310744
  47.8 0.0 collective-permute-done.3
  47.8 1.4 %broadcast_select_fusion = (bf16[512,512]{1,0:T(8,128)(2,1)S(1)}, bf16[512,512]{1,0:T(8,128)(2,1)S(1)}) fusion(bf16[512,512]{1,0:T(8,128)(2,1)} %collective-permute-done.3, bf16[512,512]{1,0:T(8,128)(2,1)} %collective-permute-done.2, pred[]{:T(512)S(6)} %eq.10, bf16[512,512]{1,0:T(8,128)(2,1)} %collective-permute-done.1, pred[]{:T(512)S(6)} %eq.9), kind=kLoop, calls=%fused_computation | loop fusion | flops 524288 | bytes 2621442 | tf_op jit(solution)/shard_map/jit(_where)/select_n | solution.py:391
  49.2 0.0 copy-start.2
  49.3 0.0 copy-start.4
  49.3 3.8 %collective-permute-start.4 = (bf16[512,512]{1,0:T(8,128)(2,1)S(1)}, bf16[512,512]{1,0:T(8,128)(2,1)}, u32[]{:S(2)}, u32[]{:S(2)}) collective-permute-start(bf16[512,512]{1,0:T(8,128)(2,1)S(1)} %get-tuple-element.26.refs_0_), channel_id=1, source_target_pairs={{31,0},{0,1},{1,2},{2,3},{3,4},{4,5},{5,6},{6,7},{7,8},{8,9},{9,10... | collective-permute-start | bytes 1572872 | tf_op jit(solution)/shard_map/ppermute | solution.py:25
  53.1 16.9 %collective-permute-start.5 = (bf16[512,512]{1,0:T(8,128)(2,1)S(1)}, bf16[512,512]{1,0:T(8,128)(2,1)}, u32[]{:S(2)}, u32[]{:S(2)}) collective-permute-start(bf16[512,512]{1,0:T(8,128)(2,1)S(1)} %get-tuple-element.25.n1_ref), channel_id=1, source_target_pairs={{1,0},{2,1},{3,2},{4,3},{5,4},{6,5},{7,6},{8,7},{9,8},{10,9},{11,1... | collective-permute-start | bytes 1572872 | tf_op jit(solution)/shard_map/ppermute | solution.py:25
  69.9 0.0 all-to-all-done.1.refs_0_
  69.9 4.1 %hard_second.1.refs_3_ = f32[512,640]{1,0:T(8,128)S(1)} custom-call(bf16[512,512]{1,0:T(8,128)(2,1)S(1)} %bitcast.12, bf16[16,128,512]{2,1,0:T(8,128)(2,1)} %all-to-all-done.1.refs_0_), custom_call_target="tpu_custom_call" | custom-call | flops 1073741824 | bytes 2097152 | tf_op jit(solution)/shard_map/hard_second/pallas_call | solution.py:308
  74.0 5.9 %collective-permute-done.4.refs_1_ = bf16[512,512]{1,0:T(8,128)(2,1)} collective-permute-done((bf16[512,512]{1,0:T(8,128)(2,1)S(1)}, bf16[512,512]{1,0:T(8,128)(2,1)}, u32[]{:S(2)}, u32[]{:S(2)}) %collective-permute-start.4) | collective-permute-done | bytes 524320 | tf_op jit(solution)/shard_map/ppermute | solution.py:25
  80.0 0.0 copy-done.2
  80.0 0.0 copy-done.4
  80.0 4.3 %cycle_last.1 = (f32[512,512]{1,0:T(8,128)}, f32[1,512]{1,0:T(1,128)}, f32[8,512]{1,0:T(8,128)S(1)}) custom-call(bf16[512,512]{1,0:T(8,128)(2,1)S(1)} %bitcast.13, bf16[512,512]{1,0:T(8,128)(2,1)S(1)} %get-tuple-element.26.refs_0_, bf16[512,512]{1,0:T(8,128)(2,1)} %collective-permute-done.4.refs_1_, f32[512,640]{1,0:T(8,128)S(1)} %copy-done.4, ...), custom_call_target="tpu_custom_call" | custom-call | flops 1073741824 | bytes 2097152 | tf_op jit(solution)/shard_map/cycle_last/pallas_call | solution.py:224
  84.3 6.7 %collective-permute-start.7 = (f32[8,512]{1,0:T(8,128)S(1)}, f32[8,512]{1,0:T(8,128)S(1)}, u32[]{:S(2)}, u32[]{:S(2)}) collective-permute-start(f32[8,512]{1,0:T(8,128)S(1)} %get-tuple-element.24.s0_ref), channel_id=1, source_target_pairs={{2,0},{3,1},{4,2},{5,3},{6,4},{7,5},{8,6},{9,7},{10,8},{11,9},{12,... | collective-permute-start | bytes 49160 | tf_op jit(solution)/shard_map/ppermute | solution.py:25
  91.0 1.9 %collective-permute-start.6 = (f32[8,512]{1,0:T(8,128)S(1)}, f32[8,512]{1,0:T(8,128)S(1)}, u32[]{:S(2)}, u32[]{:S(2)}) collective-permute-start(f32[8,512]{1,0:T(8,128)S(1)} %get-tuple-element.24.s0_ref), channel_id=1, source_target_pairs={{1,0},{2,1},{3,2},{4,3},{5,4},{6,5},{7,6},{8,7},{9,8},{10,9},{11,1... | collective-permute-start | bytes 49160 | tf_op jit(solution)/shard_map/ppermute | solution.py:25
  92.9 0.0 collective-permute-done.5.n2_ref
  92.9 0.0 collective-permute-done.7.s2_ref
  92.9 3.7 %collective-permute-done.6.s1_ref = f32[8,512]{1,0:T(8,128)S(1)} collective-permute-done((f32[8,512]{1,0:T(8,128)S(1)}, f32[8,512]{1,0:T(8,128)S(1)}, u32[]{:S(2)}, u32[]{:S(2)}) %collective-permute-start.6) | collective-permute-done | bytes 16416 | tf_op jit(solution)/shard_map/ppermute | solution.py:25
  96.6 4.4 %rtl.1 = f32[512,512]{1,0:T(8,128)} custom-call(bf16[512,512]{1,0:T(8,128)(2,1)S(1)} %bitcast.19, bf16[512,512]{1,0:T(8,128)(2,1)S(1)} %bitcast.14, bf16[512,512]{1,0:T(8,128)(2,1)S(1)} %get-tuple-element.25.n1_ref, bf16[512,512]{1,0:T(8,128)(2,1)} %collective-permute-done.5.n2_ref, f32[8,512]{1,0:T(8,128)S(1)} %get-tuple-element.24.s0_ref, ...), custom_call_target="tpu_custom_call" | custom-call | flops 1610612736 | bytes 3145728 | tf_op jit(solution)/shard_map/rtl/pallas_call | solution.py:343
Async XLA Ops:
  3.3 9.5 %copy-start = (bf16[1,512,512]{2,1,0:T(8,128)(2,1)S(1)}, bf16[1,512,512]{2,1,0:T(8,128)(2,1)}, u32[]{:S(2)}) copy-start(bf16[1,512,512]{2,1,0:T(8,128)(2,1)} %param.4) | copy-start | bytes 1572868
  3.3 31.9 %all-to-all-start = ((bf16[16,128,512]{2,1,0:T(8,128)(2,1)}), bf16[16,128,512]{2,1,0:T(8,128)(2,1)S(1)}, u32[]{:S(2)}, u32[]{:S(2)}) async-start(bf16[16,128,512]{2,1,0:T(8,128)(2,1)} %get-tuple-element.16), calls=%async_computation | async-start | bytes 4194304 | tf_op jit(solution)/shard_map/all_to_all | solution.py:368
  7.8 24.6 %collective-permute-start = (bf16[528,512]{1,0:T(8,128)(2,1)}, bf16[528,512]{1,0:T(8,128)(2,1)}, u32[]{:S(2)}, u32[]{:S(2)}) collective-permute-start(bf16[528,512]{1,0:T(8,128)(2,1)} %get-tuple-element.14), channel_id=1, source_target_pairs={{0,64},{32,96},{64,0},{96,32},{128,192},{160,224},{192,128},{224,1... | collective-permute-start | bytes 1622024 | tf_op jit(solution)/shard_map/ppermute | solution.py:373
  12.7 16.2 %collective-permute-start.2 = (bf16[512,512]{1,0:T(8,128)(2,1)S(1)}, bf16[512,512]{1,0:T(8,128)(2,1)}, u32[]{:S(2)}, u32[]{:S(2)}) collective-permute-start(bf16[512,512]{1,0:T(8,128)(2,1)S(1)} %bitcast.9), channel_id=1, source_target_pairs={{1,0},{2,1},{3,2},{4,3},{5,4},{6,5},{7,6},{8,7},{9,8},{10,9},{11,1... | collective-permute-start | bytes 1572872 | tf_op jit(solution)/shard_map/ppermute | solution.py:381
  16.4 16.1 %collective-permute-start.1 = (bf16[512,512]{1,0:T(8,128)(2,1)}, bf16[512,512]{1,0:T(8,128)(2,1)}, u32[]{:S(2)}, u32[]{:S(2)}) collective-permute-start(bf16[512,512]{1,0:T(8,128)(2,1)} %bitcast.16), channel_id=1, source_target_pairs={{0,1},{1,2},{2,3},{3,4},{4,5},{5,6},{6,7},{7,8},{8,9},{9,10},{10,1... | collective-permute-start | bytes 1572872 | tf_op jit(solution)/shard_map/ppermute | solution.py:380
  35.2 34.7 %all-to-all-start.1 = ((bf16[16,128,512]{2,1,0:T(8,128)(2,1)}), bf16[16,128,512]{2,1,0:T(8,128)(2,1)}, u32[]{:S(2)}, u32[]{:S(2)}) async-start(bf16[16,128,512]{2,1,0:T(8,128)(2,1)} %pack_far.1), calls=%async_computation.1 | async-start | bytes 4194304 | tf_op jit(solution)/shard_map/all_to_all | solution.py:368
  39.6 8.2 %collective-permute-start.3 = (bf16[512,512]{1,0:T(8,128)(2,1)}, bf16[512,512]{1,0:T(8,128)(2,1)}, u32[]{:S(2)}, u32[]{:S(2)}) collective-permute-start(bf16[512,512]{1,0:T(8,128)(2,1)} %broadcast_select_fusion.2), channel_id=1, source_target_pairs={{15,16},{31,0},{0,31},{16,15},{47,48},{63,32},{32,63},{48,47},{79,... | collective-permute-start | bytes 1572872 | tf_op jit(solution)/shard_map/ppermute | solution.py:384
  41.1 1.0 %copy-start.1 = (bf16[1,512,512]{2,1,0:T(8,128)(2,1)S(1)}, bf16[1,512,512]{2,1,0:T(8,128)(2,1)}, u32[]{:S(2)}) copy-start(bf16[1,512,512]{2,1,0:T(8,128)(2,1)} %param.5) | copy-start | bytes 1572868
  46.7 1.1 %copy-start.3 = (f32[512,640]{1,0:T(8,128)}, f32[512,640]{1,0:T(8,128)S(1)}, u32[]{:S(2)}) copy-start(f32[512,640]{1,0:T(8,128)S(1)} %hard_first.1.refs_2_) | copy-start | bytes 3932164
  49.2 30.7 %copy-start.2 = (bf16[1,512,512]{2,1,0:T(8,128)(2,1)S(1)}, bf16[1,512,512]{2,1,0:T(8,128)(2,1)}, u32[]{:S(2)}) copy-start(bf16[1,512,512]{2,1,0:T(8,128)(2,1)} %param.5) | copy-start | bytes 1572868
  49.3 30.7 %copy-start.4 = (f32[512,640]{1,0:T(8,128)S(1)}, f32[512,640]{1,0:T(8,128)}, u32[]{:S(2)}) copy-start(f32[512,640]{1,0:T(8,128)} %copy-done.3) | copy-start | bytes 3932164
  49.3 30.7 %collective-permute-start.4 = (bf16[512,512]{1,0:T(8,128)(2,1)S(1)}, bf16[512,512]{1,0:T(8,128)(2,1)}, u32[]{:S(2)}, u32[]{:S(2)}) collective-permute-start(bf16[512,512]{1,0:T(8,128)(2,1)S(1)} %get-tuple-element.26.refs_0_), channel_id=1, source_target_pairs={{31,0},{0,1},{1,2},{2,3},{3,4},{4,5},{5,6},{6,7},{7,8},{8,9},{9,10... | collective-permute-start | bytes 1572872 | tf_op jit(solution)/shard_map/ppermute | solution.py:25
  53.1 39.8 %collective-permute-start.5 = (bf16[512,512]{1,0:T(8,128)(2,1)S(1)}, bf16[512,512]{1,0:T(8,128)(2,1)}, u32[]{:S(2)}, u32[]{:S(2)}) collective-permute-start(bf16[512,512]{1,0:T(8,128)(2,1)S(1)} %get-tuple-element.25.n1_ref), channel_id=1, source_target_pairs={{1,0},{2,1},{3,2},{4,3},{5,4},{6,5},{7,6},{8,7},{9,8},{10,9},{11,1... | collective-permute-start | bytes 1572872 | tf_op jit(solution)/shard_map/ppermute | solution.py:25
  84.3 8.6 %collective-permute-start.7 = (f32[8,512]{1,0:T(8,128)S(1)}, f32[8,512]{1,0:T(8,128)S(1)}, u32[]{:S(2)}, u32[]{:S(2)}) collective-permute-start(f32[8,512]{1,0:T(8,128)S(1)} %get-tuple-element.24.s0_ref), channel_id=1, source_target_pairs={{2,0},{3,1},{4,2},{5,3},{6,4},{7,5},{8,6},{9,7},{10,8},{11,9},{12,... | collective-permute-start | bytes 49160 | tf_op jit(solution)/shard_map/ppermute | solution.py:25
  91.0 5.6 %collective-permute-start.6 = (f32[8,512]{1,0:T(8,128)S(1)}, f32[8,512]{1,0:T(8,128)S(1)}, u32[]{:S(2)}, u32[]{:S(2)}) collective-permute-start(f32[8,512]{1,0:T(8,128)S(1)} %get-tuple-element.24.s0_ref), channel_id=1, source_target_pairs={{1,0},{2,1},{3,2},{4,3},{5,4},{6,5},{7,6},{8,7},{9,8},{10,9},{11,1... | collective-permute-start | bytes 49160 | tf_op jit(solution)/shard_map/ppermute | solution.py:25

commit v8 on v7

--- a/solution.py
+++ b/solution.py
@@ -371,28 +371,18 @@
     packed, mail = pack_own(at, targets, picks, own_keys, places)
     first = spread(packed)
     mail = lax.ppermute(mail, "dp", [(g, g ^ 2) for g in range(groups)])
-    size = lax.axis_size("loop")
-    line = size // 2
-    spot = lax.axis_index("loop") % line
-    up = [(i, i + 1) for i in range(size) if i % line < line - 1]
-    down = [(i, i - 1) for i in range(size) if i % line > 0]
-    seam = [(i, (i + 1) % size) for i in range(line - 1, size, line)] + [(i, (i - 1) % size) for i in range(0, size, line)]
-    rtl1 = lax.ppermute(own_keys, "loop", up)
-    net1 = lax.ppermute(queries, "loop", down)
-    edge = jnp.where(spot == 0, queries, own_keys)
-    mail, rtl1, net1, edge = lax.optimization_barrier((mail, rtl1, net1, edge))
-    edge = lax.ppermute(edge, "loop", seam)
+    rtl1 = passed_along(own_keys, "loop", 1)
+    mail, rtl1, back = lax.optimization_barrier((mail, rtl1, queries))
     second = spread(pack_far(at, mail, places, targets.shape[0]))
-
-    state = cycle_part(rate, scale, queries, [own_keys])
+    rtl2 = passed_along(rtl1, "loop", 1)
+    net1 = passed_along(back, "loop", -1)
+
+    state = cycle_part(rate, scale, queries, [own_keys, rtl1])
     state = hard_part(rate, queries, [state], first, "hard_first")
-    edge, state = lax.optimization_barrier((edge, state))
-    rtl1 = jnp.where(spot == 0, edge, rtl1)
-    net1 = jnp.where(spot == line - 1, edge, net1)
-    rtl2 = passed_along(rtl1, "loop", 1)
+    net1, state = lax.optimization_barrier((net1, state))
     net2 = passed_along(net1, "loop", -1)
     others = hard_part(rate, queries, [], second, "hard_second")
-    grad, loss, stats = cycle_part(rate, scale, queries, [rtl1, rtl2], [state, others], own_keys)
+    grad, loss, stats = cycle_part(rate, scale, queries, [rtl2], [state, others], own_keys)
     stats1 = passed_along(stats, "loop", -1)
     stats2 = passed_along(stats, "loop", -2)
     rtl_grad = rtl_part(rate, scale, own_keys, queries, net1, net2, stats, stats1, stats2)

time: 102 us -> 98.3 us (0.964)
  the two profiles are of different devices: /device:TPU:32 before, /device:TPU:1 now
where the time goes in v8:
time: 98.3 us; the launch traced here: 97.1 us
  waiting for transfers between devices  36.5 us (37%)
  starting transfers between devices  34.6 us (35%)
  Pallas kernels  22.9 us (23%)
  local copies, waits for them, and re-layouts  2.17 us (2%)
    ppermute x6, waiting for transfers between devices, passed_along(): return lax.ppermute(block, axis, route)  24.9 us
    ppermute x6, starting transfers between devices, passed_along(): return lax.ppermute(block, axis, route)  16.7 us
    all_to_all x2, starting transfers between devices, spread(): lax.all_to_all(packed, 'dp', split_axis=0, concat_axis=0, axis_index_grou...  16 us
    pallas_call x2, Pallas kernels, hard_part(): pl.pallas_call(functools.partial(hard_kernel, rate, not states), out_shap...  7.33 us
    all_to_all x2, waiting for transfers between devices, spread(): lax.all_to_all(packed, 'dp', split_axis=0, concat_axis=0, axis_index_grou...  6.61 us
    pallas_call x2, Pallas kernels, cycle_part(): pl.pallas_call(functools.partial(cycle_kernel, rate, scale, tiles, end),...  5.8 us
    ppermute x1, waiting for transfers between devices, body(): mail = lax.ppermute(mail, 'dp', [(g, g ^ 2) for g in range(groups)])  5.05 us
    pallas_call x1, Pallas kernels, rtl_part(): pl.pallas_call(functools.partial(rtl_kernel, rate, scale), grid=(n // row...  4.58 us
  transfers between devices with their start and end apart: 9, of which 5 were waited for; matrix products, arithmetic and copies ran while one was open for 0% of the time, Pallas kernels for 16%

profile of v8, /device:TPU:1, one launch (start us, length us, event | category | flops | bytes accessed | tf_op | source)
XLA Modules:
  0.0 97.1 jit_solution(11873165079413680586)
XLA Ops:
  0.6 2.5 %pack_own.1 = (bf16[16,128,512]{2,1,0:T(8,128)(2,1)}, bf16[528,512]{1,0:T(8,128)(2,1)}) custom-call(s32[1]{0:T(128)} %bitcast.1.me, s32[16]{0:T(128)} %bitcast.18, s32[16]{0:T(128)} %bitcast.19, bf16[512,512]{1,0:T(8,128)(2,1)} %bitcast.13), custom_call_target="tpu_custom_call" | custom-call | tf_op jit(solution)/shard_map/pack_own/pallas_call | solution.py:105
  3.2 0.0 copy-start.3
  3.2 10.5 %all-to-all-start = ((bf16[16,128,512]{2,1,0:T(8,128)(2,1)}), bf16[16,128,512]{2,1,0:T(8,128)(2,1)S(1)}, u32[]{:S(2)}, u32[]{:S(2)}) async-start(bf16[16,128,512]{2,1,0:T(8,128)(2,1)} %get-tuple-element.16), calls=%async_computation | async-start | bytes 4194304 | tf_op jit(solution)/shard_map/all_to_all | solution.py:368
  13.7 1.9 %collective-permute-start = (bf16[528,512]{1,0:T(8,128)(2,1)}, bf16[528,512]{1,0:T(8,128)(2,1)}, u32[]{:S(2)}, u32[]{:S(2)}) collective-permute-start(bf16[528,512]{1,0:T(8,128)(2,1)} %get-tuple-element.13), channel_id=1, source_target_pairs={{0,64},{32,96},{64,0},{96,32},{128,192},{160,224},{192,128},{224,1... | collective-permute-start | bytes 1622024 | tf_op jit(solution)/shard_map/ppermute | solution.py:373
  15.6 0.0 copy-done.3
  15.6 1.9 %collective-permute-start.1 = (bf16[512,512]{1,0:T(8,128)(2,1)S(1)}, bf16[512,512]{1,0:T(8,128)(2,1)S(1)}, u32[]{:S(2)}, u32[]{:S(2)}) collective-permute-start(bf16[512,512]{1,0:T(8,128)(2,1)S(1)} %bitcast.14), channel_id=1, source_target_pairs={{31,0},{0,1},{1,2},{2,3},{3,4},{4,5},{5,6},{6,7},{7,8},{8,9},{9,10... | collective-permute-start | bytes 1572872 | tf_op jit(solution)/shard_map/ppermute | solution.py:25
  17.6 19.8 %collective-permute-done.1.refs_1_ = bf16[512,512]{1,0:T(8,128)(2,1)S(1)} collective-permute-done((bf16[512,512]{1,0:T(8,128)(2,1)S(1)}, bf16[512,512]{1,0:T(8,128)(2,1)S(1)}, u32[]{:S(2)}, u32[]{:S(2)}) %collective-permute-start.1) | collective-permute-done | bytes 524320 | tf_op jit(solution)/shard_map/ppermute | solution.py:25
  37.4 5.0 %collective-permute-done.mail = bf16[528,512]{1,0:T(8,128)(2,1)} collective-permute-done((bf16[528,512]{1,0:T(8,128)(2,1)}, bf16[528,512]{1,0:T(8,128)(2,1)}, u32[]{:S(2)}, u32[]{:S(2)}) %collective-permute-start) | collective-permute-done | bytes 540704 | tf_op jit(solution)/shard_map/ppermute | solution.py:373
  42.4 2.6 %pack_far.1 = bf16[16,128,512]{2,1,0:T(8,128)(2,1)} custom-call(s32[1]{0:T(128)} %bitcast.1.me, bf16[528,512]{1,0:T(8,128)(2,1)} %collective-permute-done.mail), custom_call_target="tpu_custom_call" | custom-call | tf_op jit(solution)/shard_map/pack_far/pallas_call | solution.py:149
  45.0 0.0 copy-start.2
  45.1 0.0 all-to-all-done.refs_1_
  45.1 5.5 %all-to-all-start.1 = ((bf16[16,128,512]{2,1,0:T(8,128)(2,1)}), bf16[16,128,512]{2,1,0:T(8,128)(2,1)}, u32[]{:S(2)}, u32[]{:S(2)}) async-start(bf16[16,128,512]{2,1,0:T(8,128)(2,1)} %pack_far.1), calls=%async_computation.1 | async-start | bytes 4194304 | tf_op jit(solution)/shard_map/all_to_all | solution.py:368
  50.5 0.0 copy-done.2
  50.5 2.2 %collective-permute-start.3 = (bf16[512,512]{1,0:T(8,128)(2,1)S(1)}, bf16[512,512]{1,0:T(8,128)(2,1)}, u32[]{:S(2)}, u32[]{:S(2)}) collective-permute-start(bf16[512,512]{1,0:T(8,128)(2,1)S(1)} %bitcast.7), channel_id=1, source_target_pairs={{1,0},{2,1},{3,2},{4,3},{5,4},{6,5},{7,6},{8,7},{9,8},{10,9},{11,1... | collective-permute-start | bytes 1572872 | tf_op jit(solution)/shard_map/ppermute | solution.py:25
  52.8 3.1 %collective-permute-start.2 = (bf16[512,512]{1,0:T(8,128)(2,1)S(1)}, bf16[512,512]{1,0:T(8,128)(2,1)}, u32[]{:S(2)}, u32[]{:S(2)}) collective-permute-start(bf16[512,512]{1,0:T(8,128)(2,1)S(1)} %collective-permute-done.1.refs_1_), channel_id=1, source_target_pairs={{31,0},{0,1},{1,2},{2,3},{3,4},{4,5},{5,6},{6,7},{7,8},{8,9},{9,10... | collective-permute-start | bytes 1572872 | tf_op jit(solution)/shard_map/ppermute | solution.py:25
  55.8 0.0 copy-start.4
  55.8 1.0 %copy-done.4 = bf16[1,512,512]{2,1,0:T(8,128)(2,1)S(1)} copy-done((bf16[1,512,512]{2,1,0:T(8,128)(2,1)S(1)}, bf16[1,512,512]{2,1,0:T(8,128)(2,1)}, u32[]{:S(2)}) %copy-start.4) | copy-done | bytes 524312
  56.9 2.0 %cycle_own.1.refs_0_ = f32[512,640]{1,0:T(8,128)S(1)} custom-call(bf16[512,512]{1,0:T(8,128)(2,1)S(1)} %bitcast.8, bf16[512,512]{1,0:T(8,128)(2,1)S(1)} %bitcast.15, bf16[512,512]{1,0:T(8,128)(2,1)S(1)} %collective-permute-done.1.refs_1_), custom_call_target="tpu_custom_call" | custom-call | flops 1073741824 | bytes 2097152 | tf_op jit(solution)/shard_map/cycle_own/pallas_call | solution.py:224
  58.8 3.3 %hard_first.1.refs_1_ = f32[512,640]{1,0:T(8,128)S(1)} custom-call(bf16[512,512]{1,0:T(8,128)(2,1)S(1)} %bitcast.9, f32[512,640]{1,0:T(8,128)S(1)} %cycle_own.1.refs_0_, bf16[16,128,512]{2,1,0:T(8,128)(2,1)S(1)} %all-to-all-done.refs_1_), custom_call_target="tpu_custom_call" | custom-call | flops 1073741824 | bytes 2097152 | tf_op jit(solution)/shard_map/hard_first/pallas_call | solution.py:308
  62.1 0.0 copy-start
  62.1 1.1 %copy-done = f32[512,640]{1,0:T(8,128)} copy-done((f32[512,640]{1,0:T(8,128)}, f32[512,640]{1,0:T(8,128)S(1)}, u32[]{:S(2)}) %copy-start) | copy-done | bytes 1310744
  63.2 0.0 copy-start.5
  63.2 2.8 %collective-permute-done.3.n1_ref = bf16[512,512]{1,0:T(8,128)(2,1)} collective-permute-done((bf16[512,512]{1,0:T(8,128)(2,1)S(1)}, bf16[512,512]{1,0:T(8,128)(2,1)}, u32[]{:S(2)}, u32[]{:S(2)}) %collective-permute-start.3) | collective-permute-done | bytes 524320 | tf_op jit(solution)/shard_map/ppermute | solution.py:25
  66.1 0.0 copy-start.1
  66.1 4.3 %collective-permute-start.4 = (bf16[512,512]{1,0:T(8,128)(2,1)}, bf16[512,512]{1,0:T(8,128)(2,1)}, u32[]{:S(2)}, u32[]{:S(2)}) collective-permute-start(bf16[512,512]{1,0:T(8,128)(2,1)} %collective-permute-done.3.n1_ref), channel_id=1, source_target_pairs={{1,0},{2,1},{3,2},{4,3},{5,4},{6,5},{7,6},{8,7},{9,8},{10,9},{11,1... | collective-permute-start | bytes 1572872 | tf_op jit(solution)/shard_map/ppermute | solution.py:25
  70.4 6.6 %all-to-all-done.1.refs_0_ = bf16[16,128,512]{2,1,0:T(8,128)(2,1)} async-done(((bf16[16,128,512]{2,1,0:T(8,128)(2,1)}), bf16[16,128,512]{2,1,0:T(8,128)(2,1)}, u32[]{:S(2)}, u32[]{:S(2)}) %all-to-all-start.1) | async-done | bytes 2097184 | tf_op jit(solution)/shard_map/all_to_all | solution.py:368
  77.0 4.1 %hard_second.1.refs_2_ = f32[512,640]{1,0:T(8,128)S(1)} custom-call(bf16[512,512]{1,0:T(8,128)(2,1)S(1)} %bitcast.10, bf16[16,128,512]{2,1,0:T(8,128)(2,1)} %all-to-all-done.1.refs_0_), custom_call_target="tpu_custom_call" | custom-call | flops 1073741824 | bytes 2097152 | tf_op jit(solution)/shard_map/hard_second/pallas_call | solution.py:308
  81.0 0.0 collective-permute-done.2.refs_0_
  81.1 0.0 copy-done.5
  81.1 0.0 copy-done.1
  81.1 3.8 %cycle_last.1 = (f32[512,512]{1,0:T(8,128)}, f32[1,512]{1,0:T(1,128)}, f32[8,512]{1,0:T(8,128)S(1)}) custom-call(bf16[512,512]{1,0:T(8,128)(2,1)S(1)} %bitcast.11, bf16[512,512]{1,0:T(8,128)(2,1)} %collective-permute-done.2.refs_0_, f32[512,640]{1,0:T(8,128)S(1)} %copy-done.1, f32[512,640]{1,0:T(8,128)S(1)} %hard_second.1.refs_2_, bf16[512,512]{1,0:T(8,128)(2,1)S(1)} %bitcast.16), custom_call_target="tpu_custom_call" | custom-call | flops 536870912 | bytes 2097152 | tf_op jit(solution)/shard_map/cycle_last/pallas_call | solution.py:224
  84.9 2.2 %collective-permute-start.5 = (f32[8,512]{1,0:T(8,128)S(1)}, f32[8,512]{1,0:T(8,128)S(1)}, u32[]{:S(2)}, u32[]{:S(2)}) collective-permute-start(f32[8,512]{1,0:T(8,128)S(1)} %get-tuple-element.22.s0_ref), channel_id=1, source_target_pairs={{1,0},{2,1},{3,2},{4,3},{5,4},{6,5},{7,6},{8,7},{9,8},{10,9},{11,1... | collective-permute-start | bytes 49160 | tf_op jit(solution)/shard_map/ppermute | solution.py:25
  87.1 3.1 %collective-permute-start.6 = (f32[8,512]{1,0:T(8,128)S(1)}, f32[8,512]{1,0:T(8,128)S(1)}, u32[]{:S(2)}, u32[]{:S(2)}) collective-permute-start(f32[8,512]{1,0:T(8,128)S(1)} %get-tuple-element.22.s0_ref), channel_id=1, source_target_pairs={{2,0},{3,1},{4,2},{5,3},{6,4},{7,5},{8,6},{9,7},{10,8},{11,9},{12,... | collective-permute-start | bytes 49160 | tf_op jit(solution)/shard_map/ppermute | solution.py:25
  90.2 0.0 collective-permute-done.4.n2_ref
  90.2 0.0 collective-permute-done.5.s1_ref
  90.2 2.3 %collective-permute-done.6.s2_ref = f32[8,512]{1,0:T(8,128)S(1)} collective-permute-done((f32[8,512]{1,0:T(8,128)S(1)}, f32[8,512]{1,0:T(8,128)S(1)}, u32[]{:S(2)}, u32[]{:S(2)}) %collective-permute-start.6) | collective-permute-done | bytes 16416 | tf_op jit(solution)/shard_map/ppermute | solution.py:25
  92.5 4.6 %rtl.1 = f32[512,512]{1,0:T(8,128)} custom-call(bf16[512,512]{1,0:T(8,128)(2,1)S(1)} %bitcast.17, bf16[512,512]{1,0:T(8,128)(2,1)S(1)} %bitcast.12, bf16[512,512]{1,0:T(8,128)(2,1)} %collective-permute-done.3.n1_ref, bf16[512,512]{1,0:T(8,128)(2,1)} %collective-permute-done.4.n2_ref, f32[8,512]{1,0:T(8,128)S(1)} %get-tuple-element.22.s0_ref, ...), custom_call_target="tpu_custom_call" | custom-call | flops 1610612736 | bytes 3145728 | tf_op jit(solution)/shard_map/rtl/pallas_call | solution.py:343
Async XLA Ops:
  3.2 12.5 %copy-start.3 = (bf16[1,512,512]{2,1,0:T(8,128)(2,1)S(1)}, bf16[1,512,512]{2,1,0:T(8,128)(2,1)}, u32[]{:S(2)}) copy-start(bf16[1,512,512]{2,1,0:T(8,128)(2,1)} %param.5) | copy-start | bytes 1572868
  3.2 41.9 %all-to-all-start = ((bf16[16,128,512]{2,1,0:T(8,128)(2,1)}), bf16[16,128,512]{2,1,0:T(8,128)(2,1)S(1)}, u32[]{:S(2)}, u32[]{:S(2)}) async-start(bf16[16,128,512]{2,1,0:T(8,128)(2,1)} %get-tuple-element.16), calls=%async_computation | async-start | bytes 4194304 | tf_op jit(solution)/shard_map/all_to_all | solution.py:368
  13.7 28.7 %collective-permute-start = (bf16[528,512]{1,0:T(8,128)(2,1)}, bf16[528,512]{1,0:T(8,128)(2,1)}, u32[]{:S(2)}, u32[]{:S(2)}) collective-permute-start(bf16[528,512]{1,0:T(8,128)(2,1)} %get-tuple-element.13), channel_id=1, source_target_pairs={{0,64},{32,96},{64,0},{96,32},{128,192},{160,224},{192,128},{224,1... | collective-permute-start | bytes 1622024 | tf_op jit(solution)/shard_map/ppermute | solution.py:373
  15.6 21.7 %collective-permute-start.1 = (bf16[512,512]{1,0:T(8,128)(2,1)S(1)}, bf16[512,512]{1,0:T(8,128)(2,1)S(1)}, u32[]{:S(2)}, u32[]{:S(2)}) collective-permute-start(bf16[512,512]{1,0:T(8,128)(2,1)S(1)} %bitcast.14), channel_id=1, source_target_pairs={{31,0},{0,1},{1,2},{2,3},{3,4},{4,5},{5,6},{6,7},{7,8},{8,9},{9,10... | collective-permute-start | bytes 1572872 | tf_op jit(solution)/shard_map/ppermute | solution.py:25
  45.0 5.5 %copy-start.2 = (bf16[1,512,512]{2,1,0:T(8,128)(2,1)S(1)}, bf16[1,512,512]{2,1,0:T(8,128)(2,1)}, u32[]{:S(2)}) copy-start(bf16[1,512,512]{2,1,0:T(8,128)(2,1)} %param.4) | copy-start | bytes 1572868
  45.1 31.9 %all-to-all-start.1 = ((bf16[16,128,512]{2,1,0:T(8,128)(2,1)}), bf16[16,128,512]{2,1,0:T(8,128)(2,1)}, u32[]{:S(2)}, u32[]{:S(2)}) async-start(bf16[16,128,512]{2,1,0:T(8,128)(2,1)} %pack_far.1), calls=%async_computation.1 | async-start | bytes 4194304 | tf_op jit(solution)/shard_map/all_to_all | solution.py:368
  50.5 15.5 %collective-permute-start.3 = (bf16[512,512]{1,0:T(8,128)(2,1)S(1)}, bf16[512,512]{1,0:T(8,128)(2,1)}, u32[]{:S(2)}, u32[]{:S(2)}) collective-permute-start(bf16[512,512]{1,0:T(8,128)(2,1)S(1)} %bitcast.7), channel_id=1, source_target_pairs={{1,0},{2,1},{3,2},{4,3},{5,4},{6,5},{7,6},{8,7},{9,8},{10,9},{11,1... | collective-permute-start | bytes 1572872 | tf_op jit(solution)/shard_map/ppermute | solution.py:25
  52.8 28.3 %collective-permute-start.2 = (bf16[512,512]{1,0:T(8,128)(2,1)S(1)}, bf16[512,512]{1,0:T(8,128)(2,1)}, u32[]{:S(2)}, u32[]{:S(2)}) collective-permute-start(bf16[512,512]{1,0:T(8,128)(2,1)S(1)} %collective-permute-done.1.refs_1_), channel_id=1, source_target_pairs={{31,0},{0,1},{1,2},{2,3},{3,4},{4,5},{5,6},{6,7},{7,8},{8,9},{9,10... | collective-permute-start | bytes 1572872 | tf_op jit(solution)/shard_map/ppermute | solution.py:25
  55.8 1.0 %copy-start.4 = (bf16[1,512,512]{2,1,0:T(8,128)(2,1)S(1)}, bf16[1,512,512]{2,1,0:T(8,128)(2,1)}, u32[]{:S(2)}) copy-start(bf16[1,512,512]{2,1,0:T(8,128)(2,1)} %param.5) | copy-start | bytes 1572868
  62.1 1.1 %copy-start = (f32[512,640]{1,0:T(8,128)}, f32[512,640]{1,0:T(8,128)S(1)}, u32[]{:S(2)}) copy-start(f32[512,640]{1,0:T(8,128)S(1)} %hard_first.1.refs_1_) | copy-start | bytes 3932164
  63.2 17.8 %copy-start.5 = (bf16[1,512,512]{2,1,0:T(8,128)(2,1)S(1)}, bf16[1,512,512]{2,1,0:T(8,128)(2,1)}, u32[]{:S(2)}) copy-start(bf16[1,512,512]{2,1,0:T(8,128)(2,1)} %param.5) | copy-start | bytes 1572868
  66.1 15.0 %copy-start.1 = (f32[512,640]{1,0:T(8,128)S(1)}, f32[512,640]{1,0:T(8,128)}, u32[]{:S(2)}) copy-start(f32[512,640]{1,0:T(8,128)} %copy-done) | copy-start | bytes 3932164
  66.1 24.1 %collective-permute-start.4 = (bf16[512,512]{1,0:T(8,128)(2,1)}, bf16[512,512]{1,0:T(8,128)(2,1)}, u32[]{:S(2)}, u32[]{:S(2)}) collective-permute-start(bf16[512,512]{1,0:T(8,128)(2,1)} %collective-permute-done.3.n1_ref), channel_id=1, source_target_pairs={{1,0},{2,1},{3,2},{4,3},{5,4},{6,5},{7,6},{8,7},{9,8},{10,9},{11,1... | collective-permute-start | bytes 1572872 | tf_op jit(solution)/shard_map/ppermute | solution.py:25
  84.9 5.3 %collective-permute-start.5 = (f32[8,512]{1,0:T(8,128)S(1)}, f32[8,512]{1,0:T(8,128)S(1)}, u32[]{:S(2)}, u32[]{:S(2)}) collective-permute-start(f32[8,512]{1,0:T(8,128)S(1)} %get-tuple-element.22.s0_ref), channel_id=1, source_target_pairs={{1,0},{2,1},{3,2},{4,3},{5,4},{6,5},{7,6},{8,7},{9,8},{10,9},{11,1... | collective-permute-start | bytes 49160 | tf_op jit(solution)/shard_map/ppermute | solution.py:25
  87.1 5.4 %collective-permute-start.6 = (f32[8,512]{1,0:T(8,128)S(1)}, f32[8,512]{1,0:T(8,128)S(1)}, u32[]{:S(2)}, u32[]{:S(2)}) collective-permute-start(f32[8,512]{1,0:T(8,128)S(1)} %get-tuple-element.22.s0_ref), channel_id=1, source_target_pairs={{2,0},{3,1},{4,2},{5,3},{6,4},{7,5},{8,6},{9,7},{10,8},{11,9},{12,... | collective-permute-start | bytes 49160 | tf_op jit(solution)/shard_map/ppermute | solution.py:25

commit v9 on v8

--- a/solution.py
+++ b/solution.py
@@ -169,20 +169,20 @@
     )(me, mail)
 
 
-def cycle_kernel(rate, scale, tiles, end, q_ref, *refs):
+def cycle_kernel(rate, scale, tiles, given, end, q_ref, *refs):
     q = q_ref[...]
     rows, feature = q.shape
     first = pl.multiple_of(pl.program_id(0) * rows, rows)
     keys = [ref[...] for ref in refs[:tiles]]
     scores = [nt_dot(q, k) for k in keys]
-    m = jnp.max(functools.reduce(jnp.maximum, scores), axis=1, keepdims=True)
-    states = refs[tiles : tiles + 2] if end else ()
-    for state in states:
-        m = jnp.maximum(m, state[:, feature : feature + 1])
-    exps = [jnp.exp2((s - m) * rate) for s in scores]
-    l = jnp.sum(functools.reduce(jnp.add, exps), axis=1, keepdims=True)
-    num = jnp.dot(exps[0].astype(jnp.bfloat16), keys[0], preferred_element_type=jnp.float32)
-    for e, k in zip(exps[1:], keys[1:]):
+    states = refs[tiles : tiles + given]
+    peaks = [jnp.max(s, axis=1, keepdims=True) for s in scores] + [state[:, feature : feature + 1] for state in states]
+    m = functools.reduce(jnp.maximum, peaks)
+    l = jnp.zeros((rows, 1), jnp.float32)
+    num = jnp.zeros((rows, feature), jnp.float32)
+    for s, k in zip(scores, keys):
+        e = jnp.exp2((s - m) * rate)
+        l += jnp.sum(e, axis=1, keepdims=True)
         num += jnp.dot(e.astype(jnp.bfloat16), k, preferred_element_type=jnp.float32)
     for state in states:
         shrink = jnp.exp2((state[:, feature : feature + 1] - m) * rate)
@@ -191,13 +191,16 @@
     lane = lax.broadcasted_iota(jnp.int32, (rows, LANES), 1)
     if not end:
         state_ref = refs[-1]
-        own = refs[0][pl.ds(first, rows), :].astype(jnp.float32)
-        positive = jnp.sum(q.astype(jnp.float32) * own, axis=1, keepdims=True)
+        if given:
+            positive = states[0][:, feature + 2 : feature + 3]
+        else:
+            own = refs[0][pl.ds(first, rows), :].astype(jnp.float32)
+            positive = jnp.sum(q.astype(jnp.float32) * own, axis=1, keepdims=True)
         state_ref[:, :feature] = num
         state_ref[:, feature:] = jnp.where(lane == 0, m, jnp.where(lane == 1, l, positive))
         return
     positive = states[0][:, feature + 2 : feature + 3]
-    own_ref, grad_ref, loss_ref, stats_ref = refs[tiles + 2 :]
+    own_ref, grad_ref, loss_ref, stats_ref = refs[tiles + given :]
     inverse = 1.0 / l
     grad_ref[...] = (num * inverse - own_ref[...].astype(jnp.float32)) * scale
     loss = (m - positive) * scale + jnp.log(l)
@@ -222,14 +225,14 @@
         shapes = (jax.ShapeDtypeStruct((n, feature), f32), jax.ShapeDtypeStruct((1, n), f32), jax.ShapeDtypeStruct((8, n), f32))
         outs = (block, pl.BlockSpec((1, rows), lambda i: (0, i)), pl.BlockSpec((8, rows), lambda i: (0, i)))
     return pl.pallas_call(
-        functools.partial(cycle_kernel, rate, scale, tiles, end),
+        functools.partial(cycle_kernel, rate, scale, tiles, len(states), end),
         grid=(n // rows,),
         out_shape=shapes,
         in_specs=specs,
         out_specs=outs,
         compiler_params=pltpu.CompilerParams(vmem_limit_bytes=VMEM_LIMIT),
         cost_estimate=pl.CostEstimate(flops=4 * n * tiles * n * feature, bytes_accessed=8 * n * feature, transcendentals=tiles * n * n),
-        name="cycle_last" if end else "cycle_own",
+        name="cycle_last" if end else "cycle_more" if states else "cycle_own",
     )(*args)
 
 
@@ -323,33 +326,35 @@
     )(q, *states, blocks)
 
 
-def rtl_kernel(rate, scale, k_ref, n0_ref, n1_ref, n2_ref, s0_ref, s1_ref, s2_ref, out_ref):
+def rtl_kernel(rate, scale, tiles, k_ref, *refs):
+    n_refs, s_refs = refs[:tiles], refs[tiles : 2 * tiles]
+    base_ref, out_ref = refs[2 * tiles :]
     k = k_ref[...]
-    first = pl.multiple_of(pl.program_id(0) * k.shape[0], k.shape[0])
-    total = -n0_ref[pl.ds(first, k.shape[0]), :].astype(jnp.float32)
-    for n_ref, s_ref in ((n0_ref, s0_ref), (n1_ref, s1_ref), (n2_ref, s2_ref)):
+    total = -base_ref[...].astype(jnp.float32) if tiles == 1 else base_ref[...]
+    for n_ref, s_ref in zip(n_refs, s_refs):
         rows = n_ref[...]
         s = nt_dot(k, rows)
         w = jnp.exp2((s - s_ref[0:1, :]) * rate) * s_ref[1:2, :]
         total += jnp.dot(w.astype(jnp.bfloat16), rows, preferred_element_type=jnp.float32)
-    out_ref[...] = total * scale
-
-
-def rtl_part(rate, scale, k, n0, n1, n2, s0, s1, s2, rows=256):
+    out_ref[...] = total if tiles == 1 else total * scale
+
+
+def rtl_part(rate, scale, k, nets, stats, base, rows=256):
     n, feature = k.shape
+    tiles = len(nets)
     block = pl.BlockSpec((rows, feature), lambda i: (i, 0))
     full = pl.BlockSpec((n, feature), lambda i: (0, 0), pipeline_mode=pl.Buffered(1))
     stat = pl.BlockSpec((8, n), lambda i: (0, 0), pipeline_mode=pl.Buffered(1))
     return pl.pallas_call(
-        functools.partial(rtl_kernel, rate, scale),
+        functools.partial(rtl_kernel, rate, scale, tiles),
         grid=(n // rows,),
         out_shape=jax.ShapeDtypeStruct((n, feature), jnp.float32),
-        in_specs=[block, full, full, full, stat, stat, stat],
+        in_specs=[block] + [full] * tiles + [stat] * tiles + [block],
         out_specs=block,
         compiler_params=pltpu.CompilerParams(vmem_limit_bytes=VMEM_LIMIT),
-        cost_estimate=pl.CostEstimate(flops=4 * n * 3 * n * feature, bytes_accessed=6 * n * feature * 2, transcendentals=3 * n * n),
-        name="rtl",
-    )(k, n0, n1, n2, s0, s1, s2)
+        cost_estimate=pl.CostEstimate(flops=4 * n * tiles * n * feature, bytes_accessed=(tiles + 3) * n * feature * 2, transcendentals=tiles * n * n),
+        name="rtl_own" if tiles == 1 else "rtl_others",
+    )(k, *nets, *stats, base)
 
 
 def body(netlist, rtl, hard_target, hard_block):
@@ -381,11 +386,13 @@
     state = hard_part(rate, queries, [state], first, "hard_first")
     net1, state = lax.optimization_barrier((net1, state))
     net2 = passed_along(net1, "loop", -1)
+    state = cycle_part(rate, scale, queries, [rtl2], [state])
     others = hard_part(rate, queries, [], second, "hard_second")
-    grad, loss, stats = cycle_part(rate, scale, queries, [rtl2], [state, others], own_keys)
+    grad, loss, stats = cycle_part(rate, scale, queries, [], [state, others], own_keys)
     stats1 = passed_along(stats, "loop", -1)
     stats2 = passed_along(stats, "loop", -2)
-    rtl_grad = rtl_part(rate, scale, own_keys, queries, net1, net2, stats, stats1, stats2)
+    begun = rtl_part(rate, scale, own_keys, [queries], [stats], queries)
+    rtl_grad = rtl_part(rate, scale, own_keys, [net1, net2], [stats1, stats2], begun)
     return (loss, grad[None], rtl_grad[None])
 
 

time: 98.3 us -> 96.6 us (0.983)
  waiting for transfers between devices: 36.5 us -> 31.6 us
  Pallas kernels: 22.9 us -> 26.5 us
    pallas_call x2, Pallas kernels: 7.33 us -> 11.2 us  [hard_part(): pl.pallas_call(functools.partial(hard_kernel, rate, not states), out_shap...]
    ppermute x6, waiting for transfers between devices: 24.9 us -> 22.2 us  [passed_along(): return lax.ppermute(block, axis, route)]
    all_to_all x2, waiting for transfers between devices: 6.61 us -> 5.12 us  [spread(): lax.all_to_all(packed, 'dp', split_axis=0, concat_axis=0, axis_index_grou...]
    unnamed x12 -> x10, local copies, waits for them, and re-layouts: 2.17 us -> 2.65 us
    pallas_call x3 -> x5, Pallas kernels: 10.4 us -> 10.1 us  [the longest x3 5.27 us: cycle_part(): pl.pallas_call(functools.partial(cycle_kernel, rate, scale, tiles, len(st...]
  transfers between devices with their start and end apart: 9 -> 9, of which waited for: 5 -> 5; matrix products, arithmetic and copies ran while one was open for 0% -> 0% of each run, Pallas kernels for 16% -> 21%
where the time goes in v9:
time: 96.6 us; the launch traced here: 95.6 us
  starting transfers between devices  33.9 us (35%)
  waiting for transfers between devices  31.6 us (33%)
  Pallas kernels  26.5 us (27%)
  local copies, waits for them, and re-layouts  2.65 us (3%)
    ppermute x6, waiting for transfers between devices, passed_along(): return lax.ppermute(block, axis, route)  22.2 us
    ppermute x6, starting transfers between devices, passed_along(): return lax.ppermute(block, axis, route)  16 us
    all_to_all x2, starting transfers between devices, spread(): lax.all_to_all(packed, 'dp', split_axis=0, concat_axis=0, axis_index_grou...  16 us
    pallas_call x2, Pallas kernels, hard_part(): pl.pallas_call(functools.partial(hard_kernel, rate, not states), out_shap...  11.2 us
    pallas_call x3, Pallas kernels, cycle_part(): pl.pallas_call(functools.partial(cycle_kernel, rate, scale, tiles, len(st...  5.27 us
    all_to_all x2, waiting for transfers between devices, spread(): lax.all_to_all(packed, 'dp', split_axis=0, concat_axis=0, axis_index_grou...  5.12 us
    pallas_call x2, Pallas kernels, rtl_part(): pl.pallas_call(functools.partial(rtl_kernel, rate, scale, tiles), grid=(n...  4.84 us
    ppermute x1, waiting for transfers between devices, body(): mail = lax.ppermute(mail, 'dp', [(g, g ^ 2) for g in range(groups)])  4.29 us
  transfers between devices with their start and end apart: 9, of which 5 were waited for; matrix products, arithmetic and copies ran while one was open for 0% of the time, Pallas kernels for 21%

profile of v9, /device:TPU:1, one launch (start us, length us, event | category | flops | bytes accessed | tf_op | source)
XLA Modules:
  0.0 95.6 jit_solution(626491676663838078)
XLA Ops:
  0.6 2.5 %pack_own.1 = (bf16[16,128,512]{2,1,0:T(8,128)(2,1)}, bf16[528,512]{1,0:T(8,128)(2,1)}) custom-call(s32[1]{0:T(128)} %bitcast.1.me, s32[16]{0:T(128)} %bitcast.21, s32[16]{0:T(128)} %bitcast.22, bf16[512,512]{1,0:T(8,128)(2,1)} %bitcast.15), custom_call_target="tpu_custom_call" | custom-call | tf_op jit(solution)/shard_map/pack_own/pallas_call | solution.py:105
  3.2 0.0 copy-start.1
  3.2 10.5 %all-to-all-start = ((bf16[16,128,512]{2,1,0:T(8,128)(2,1)}), bf16[16,128,512]{2,1,0:T(8,128)(2,1)S(1)}, u32[]{:S(2)}, u32[]{:S(2)}) async-start(bf16[16,128,512]{2,1,0:T(8,128)(2,1)} %get-tuple-element.16), calls=%async_computation | async-start | bytes 4194304 | tf_op jit(solution)/shard_map/all_to_all | solution.py:373
  13.7 1.9 %collective-permute-start = (bf16[528,512]{1,0:T(8,128)(2,1)}, bf16[528,512]{1,0:T(8,128)(2,1)S(1)}, u32[]{:S(2)}, u32[]{:S(2)}) collective-permute-start(bf16[528,512]{1,0:T(8,128)(2,1)} %get-tuple-element.13), channel_id=1, source_target_pairs={{0,64},{32,96},{64,0},{96,32},{128,192},{160,224},{192,128},{224,1... | collective-permute-start | bytes 1622024 | tf_op jit(solution)/shard_map/ppermute | solution.py:378
  15.6 0.0 copy-done.1
  15.6 1.9 %collective-permute-start.1 = (bf16[512,512]{1,0:T(8,128)(2,1)S(1)}, bf16[512,512]{1,0:T(8,128)(2,1)S(1)}, u32[]{:S(2)}, u32[]{:S(2)}) collective-permute-start(bf16[512,512]{1,0:T(8,128)(2,1)S(1)} %bitcast.16), channel_id=1, source_target_pairs={{31,0},{0,1},{1,2},{2,3},{3,4},{4,5},{5,6},{6,7},{7,8},{8,9},{9,10... | collective-permute-start | bytes 1572872 | tf_op jit(solution)/shard_map/ppermute | solution.py:25
  17.6 19.6 %collective-permute-done.1.refs_1_ = bf16[512,512]{1,0:T(8,128)(2,1)S(1)} collective-permute-done((bf16[512,512]{1,0:T(8,128)(2,1)S(1)}, bf16[512,512]{1,0:T(8,128)(2,1)S(1)}, u32[]{:S(2)}, u32[]{:S(2)}) %collective-permute-start.1) | collective-permute-done | bytes 524320 | tf_op jit(solution)/shard_map/ppermute | solution.py:25
  37.2 0.0 copy-start.2
  37.2 0.8 copy-done.2
  38.0 4.3 %collective-permute-done.mail = bf16[528,512]{1,0:T(8,128)(2,1)S(1)} collective-permute-done((bf16[528,512]{1,0:T(8,128)(2,1)}, bf16[528,512]{1,0:T(8,128)(2,1)S(1)}, u32[]{:S(2)}, u32[]{:S(2)}) %collective-permute-start) | collective-permute-done | bytes 540704 | tf_op jit(solution)/shard_map/ppermute | solution.py:378
  42.3 0.0 copy-start.4
  42.3 0.8 copy-done.4
  43.1 2.7 %pack_far.1 = bf16[16,128,512]{2,1,0:T(8,128)(2,1)} custom-call(s32[1]{0:T(128)} %bitcast.1.me, bf16[528,512]{1,0:T(8,128)(2,1)} %copy-done.4), custom_call_target="tpu_custom_call" | custom-call | tf_op jit(solution)/shard_map/pack_far/pallas_call | solution.py:149
  45.8 0.0 copy-start
  45.8 0.0 all-to-all-done.refs_1_
  45.8 5.5 %all-to-all-start.1 = ((bf16[16,128,512]{2,1,0:T(8,128)(2,1)}), bf16[16,128,512]{2,1,0:T(8,128)(2,1)}, u32[]{:S(2)}, u32[]{:S(2)}) async-start(bf16[16,128,512]{2,1,0:T(8,128)(2,1)} %pack_far.1), calls=%async_computation.1 | async-start | bytes 4194304 | tf_op jit(solution)/shard_map/all_to_all | solution.py:373
  51.2 0.0 copy-done
  51.2 1.9 %collective-permute-start.3 = (bf16[512,512]{1,0:T(8,128)(2,1)S(1)}, bf16[512,512]{1,0:T(8,128)(2,1)}, u32[]{:S(2)}, u32[]{:S(2)}) collective-permute-start(bf16[512,512]{1,0:T(8,128)(2,1)S(1)} %bitcast.7), channel_id=1, source_target_pairs={{1,0},{2,1},{3,2},{4,3},{5,4},{6,5},{7,6},{8,7},{9,8},{10,9},{11,1... | collective-permute-start | bytes 1572872 | tf_op jit(solution)/shard_map/ppermute | solution.py:25
  53.2 3.4 %collective-permute-start.2 = (bf16[512,512]{1,0:T(8,128)(2,1)}, bf16[512,512]{1,0:T(8,128)(2,1)S(1)}, u32[]{:S(2)}, u32[]{:S(2)}) collective-permute-start(bf16[512,512]{1,0:T(8,128)(2,1)} %copy-done.2), channel_id=1, source_target_pairs={{31,0},{0,1},{1,2},{2,3},{3,4},{4,5},{5,6},{6,7},{7,8},{8,9},{9,10... | collective-permute-start | bytes 1572872 | tf_op jit(solution)/shard_map/ppermute | solution.py:25
  56.5 0.0 copy-start.3
  56.5 1.0 %copy-done.3 = bf16[512,512]{1,0:T(8,128)(2,1)S(1)} copy-done((bf16[512,512]{1,0:T(8,128)(2,1)S(1)}, bf16[512,512]{1,0:T(8,128)(2,1)}, u32[]{:S(2)}) %copy-start.3) | copy-done | bytes 524312
  57.6 1.9 %cycle_own.1.refs_0_ = f32[512,640]{1,0:T(8,128)S(1)} custom-call(bf16[512,512]{1,0:T(8,128)(2,1)S(1)} %bitcast.8, bf16[512,512]{1,0:T(8,128)(2,1)S(1)} %bitcast.17, bf16[512,512]{1,0:T(8,128)(2,1)S(1)} %copy-done.3), custom_call_target="tpu_custom_call" | custom-call | flops 1073741824 | bytes 2097152 | tf_op jit(solution)/shard_map/cycle_own/pallas_call | solution.py:227
  59.5 5.3 %hard_first.1.refs_1_ = f32[512,640]{1,0:T(8,128)S(1)} custom-call(bf16[512,512]{1,0:T(8,128)(2,1)S(1)} %bitcast.9, f32[512,640]{1,0:T(8,128)S(1)} %cycle_own.1.refs_0_, bf16[16,128,512]{2,1,0:T(8,128)(2,1)S(1)} %all-to-all-done.refs_1_), custom_call_target="tpu_custom_call" | custom-call | flops 1073741824 | bytes 2097152 | tf_op jit(solution)/shard_map/hard_first/pallas_call | solution.py:311
  64.8 1.9 %collective-permute-done.3.refs_0_ = bf16[512,512]{1,0:T(8,128)(2,1)} collective-permute-done((bf16[512,512]{1,0:T(8,128)(2,1)S(1)}, bf16[512,512]{1,0:T(8,128)(2,1)}, u32[]{:S(2)}, u32[]{:S(2)}) %collective-permute-start.3) | collective-permute-done | bytes 524320 | tf_op jit(solution)/shard_map/ppermute | solution.py:25
  66.7 4.2 %collective-permute-start.4 = (bf16[512,512]{1,0:T(8,128)(2,1)}, bf16[512,512]{1,0:T(8,128)(2,1)S(1)}, u32[]{:S(2)}, u32[]{:S(2)}) collective-permute-start(bf16[512,512]{1,0:T(8,128)(2,1)} %collective-permute-done.3.refs_0_), channel_id=1, source_target_pairs={{1,0},{2,1},{3,2},{4,3},{5,4},{6,5},{7,6},{8,7},{9,8},{10,9},{11,1... | collective-permute-start | bytes 1572872 | tf_op jit(solution)/shard_map/ppermute | solution.py:25
  70.9 0.0 collective-permute-done.2.refs_0_
  70.9 1.6 %cycle_more.1.refs_0_ = f32[512,640]{1,0:T(8,128)S(1)} custom-call(bf16[512,512]{1,0:T(8,128)(2,1)S(1)} %bitcast.10, bf16[512,512]{1,0:T(8,128)(2,1)S(1)} %collective-permute-done.2.refs_0_, f32[512,640]{1,0:T(8,128)S(1)} %hard_first.1.refs_1_), custom_call_target="tpu_custom_call" | custom-call | flops 536870912 | bytes 2097152 | tf_op jit(solution)/shard_map/cycle_more/pallas_call | solution.py:227
  72.6 5.1 %all-to-all-done.1.refs_0_ = bf16[16,128,512]{2,1,0:T(8,128)(2,1)} async-done(((bf16[16,128,512]{2,1,0:T(8,128)(2,1)}), bf16[16,128,512]{2,1,0:T(8,128)(2,1)}, u32[]{:S(2)}, u32[]{:S(2)}) %all-to-all-start.1) | async-done | bytes 2097184 | tf_op jit(solution)/shard_map/all_to_all | solution.py:373
  77.7 5.9 %hard_second.1.refs_1_ = f32[512,640]{1,0:T(8,128)S(1)} custom-call(bf16[512,512]{1,0:T(8,128)(2,1)S(1)} %bitcast.11, bf16[16,128,512]{2,1,0:T(8,128)(2,1)} %all-to-all-done.1.refs_0_), custom_call_target="tpu_custom_call" | custom-call | flops 1073741824 | bytes 2097152 | tf_op jit(solution)/shard_map/hard_second/pallas_call | solution.py:311
  83.6 1.8 %cycle_last.1 = (f32[512,512]{1,0:T(8,128)}, f32[1,512]{1,0:T(1,128)}, f32[8,512]{1,0:T(8,128)S(1)}) custom-call(bf16[512,512]{1,0:T(8,128)(2,1)S(1)} %bitcast.12, f32[512,640]{1,0:T(8,128)S(1)} %cycle_more.1.refs_0_, f32[512,640]{1,0:T(8,128)S(1)} %hard_second.1.refs_1_, bf16[512,512]{1,0:T(8,128)(2,1)S(1)} %bitcast.18), custom_call_target="tpu_custom_call" | custom-call | bytes 2097152 | tf_op jit(solution)/shard_map/cycle_last/pallas_call | solution.py:227
  85.4 2.0 %collective-permute-start.6 = (f32[8,512]{1,0:T(8,128)S(1)}, f32[8,512]{1,0:T(8,128)S(1)}, u32[]{:S(2)}, u32[]{:S(2)}) collective-permute-start(f32[8,512]{1,0:T(8,128)S(1)} %get-tuple-element.22.refs_1_), channel_id=1, source_target_pairs={{2,0},{3,1},{4,2},{5,3},{6,4},{7,5},{8,6},{9,7},{10,8},{11,9},{12,... | collective-permute-start | bytes 49160 | tf_op jit(solution)/shard_map/ppermute | solution.py:25
  87.4 2.6 %collective-permute-start.5 = (f32[8,512]{1,0:T(8,128)S(1)}, f32[8,512]{1,0:T(8,128)S(1)}, u32[]{:S(2)}, u32[]{:S(2)}) collective-permute-start(f32[8,512]{1,0:T(8,128)S(1)} %get-tuple-element.22.refs_1_), channel_id=1, source_target_pairs={{1,0},{2,1},{3,2},{4,3},{5,4},{6,5},{7,6},{8,7},{9,8},{10,9},{11,1... | collective-permute-start | bytes 49160 | tf_op jit(solution)/shard_map/ppermute | solution.py:25
  90.0 1.1 %rtl_own.1.refs_4_ = f32[512,512]{1,0:T(8,128)S(1)} custom-call(bf16[512,512]{1,0:T(8,128)(2,1)S(1)} %bitcast.19, bf16[512,512]{1,0:T(8,128)(2,1)S(1)} %bitcast.13, f32[8,512]{1,0:T(8,128)S(1)} %get-tuple-element.22.refs_1_, bf16[512,512]{1,0:T(8,128)(2,1)S(1)} %bitcast.14), custom_call_target="tpu_custom_call" | custom-call | flops 536870912 | bytes 2097152 | tf_op jit(solution)/shard_map/rtl_own/pallas_call | solution.py:348
  91.2 0.0 collective-permute-done.4.refs_1_
  91.2 0.0 collective-permute-done.6.refs_3_
  91.2 0.7 collective-permute-done.5.refs_2_
  91.9 3.7 %rtl_others.1 = f32[512,512]{1,0:T(8,128)} custom-call(bf16[512,512]{1,0:T(8,128)(2,1)S(1)} %bitcast.20, bf16[512,512]{1,0:T(8,128)(2,1)} %collective-permute-done.3.refs_0_, bf16[512,512]{1,0:T(8,128)(2,1)S(1)} %collective-permute-done.4.refs_1_, f32[8,512]{1,0:T(8,128)S(1)} %collective-permute-done.5.refs_2_, f32[8,512]{1,0:T(8,128)S(1)} %collective-permute-done.6.refs_3_, ...), custom_call_target="tpu_custom_call" | custom-call | flops 1073741824 | bytes 2621440 | tf_op jit(solution)/shard_map/rtl_others/pallas_call | solution.py:348
Async XLA Ops:
  3.2 12.5 %copy-start.1 = (bf16[1,512,512]{2,1,0:T(8,128)(2,1)S(1)}, bf16[1,512,512]{2,1,0:T(8,128)(2,1)}, u32[]{:S(2)}) copy-start(bf16[1,512,512]{2,1,0:T(8,128)(2,1)} %param.5) | copy-start | bytes 1572868
  3.2 42.6 %all-to-all-start = ((bf16[16,128,512]{2,1,0:T(8,128)(2,1)}), bf16[16,128,512]{2,1,0:T(8,128)(2,1)S(1)}, u32[]{:S(2)}, u32[]{:S(2)}) async-start(bf16[16,128,512]{2,1,0:T(8,128)(2,1)} %get-tuple-element.16), calls=%async_computation | async-start | bytes 4194304 | tf_op jit(solution)/shard_map/all_to_all | solution.py:373
  13.7 28.6 %collective-permute-start = (bf16[528,512]{1,0:T(8,128)(2,1)}, bf16[528,512]{1,0:T(8,128)(2,1)S(1)}, u32[]{:S(2)}, u32[]{:S(2)}) collective-permute-start(bf16[528,512]{1,0:T(8,128)(2,1)} %get-tuple-element.13), channel_id=1, source_target_pairs={{0,64},{32,96},{64,0},{96,32},{128,192},{160,224},{192,128},{224,1... | collective-permute-start | bytes 1622024 | tf_op jit(solution)/shard_map/ppermute | solution.py:378
  15.6 21.6 %collective-permute-start.1 = (bf16[512,512]{1,0:T(8,128)(2,1)S(1)}, bf16[512,512]{1,0:T(8,128)(2,1)S(1)}, u32[]{:S(2)}, u32[]{:S(2)}) collective-permute-start(bf16[512,512]{1,0:T(8,128)(2,1)S(1)} %bitcast.16), channel_id=1, source_target_pairs={{31,0},{0,1},{1,2},{2,3},{3,4},{4,5},{5,6},{6,7},{7,8},{8,9},{9,10... | collective-permute-start | bytes 1572872 | tf_op jit(solution)/shard_map/ppermute | solution.py:25
  37.2 0.8 copy-start.2
  42.3 0.8 copy-start.4
  45.8 5.5 %copy-start = (bf16[1,512,512]{2,1,0:T(8,128)(2,1)S(1)}, bf16[1,512,512]{2,1,0:T(8,128)(2,1)}, u32[]{:S(2)}) copy-start(bf16[1,512,512]{2,1,0:T(8,128)(2,1)} %param.4) | copy-start | bytes 1572868
  45.8 31.9 %all-to-all-start.1 = ((bf16[16,128,512]{2,1,0:T(8,128)(2,1)}), bf16[16,128,512]{2,1,0:T(8,128)(2,1)}, u32[]{:S(2)}, u32[]{:S(2)}) async-start(bf16[16,128,512]{2,1,0:T(8,128)(2,1)} %pack_far.1), calls=%async_computation.1 | async-start | bytes 4194304 | tf_op jit(solution)/shard_map/all_to_all | solution.py:373
  51.2 15.5 %collective-permute-start.3 = (bf16[512,512]{1,0:T(8,128)(2,1)S(1)}, bf16[512,512]{1,0:T(8,128)(2,1)}, u32[]{:S(2)}, u32[]{:S(2)}) collective-permute-start(bf16[512,512]{1,0:T(8,128)(2,1)S(1)} %bitcast.7), channel_id=1, source_target_pairs={{1,0},{2,1},{3,2},{4,3},{5,4},{6,5},{7,6},{8,7},{9,8},{10,9},{11,1... | collective-permute-start | bytes 1572872 | tf_op jit(solution)/shard_map/ppermute | solution.py:25
  53.2 17.8 %collective-permute-start.2 = (bf16[512,512]{1,0:T(8,128)(2,1)}, bf16[512,512]{1,0:T(8,128)(2,1)S(1)}, u32[]{:S(2)}, u32[]{:S(2)}) collective-permute-start(bf16[512,512]{1,0:T(8,128)(2,1)} %copy-done.2), channel_id=1, source_target_pairs={{31,0},{0,1},{1,2},{2,3},{3,4},{4,5},{5,6},{6,7},{7,8},{8,9},{9,10... | collective-permute-start | bytes 1572872 | tf_op jit(solution)/shard_map/ppermute | solution.py:25
  56.5 1.1 %copy-start.3 = (bf16[512,512]{1,0:T(8,128)(2,1)S(1)}, bf16[512,512]{1,0:T(8,128)(2,1)}, u32[]{:S(2)}) copy-start(bf16[512,512]{1,0:T(8,128)(2,1)} %copy-done.2) | copy-start | bytes 1572868
  66.7 24.4 %collective-permute-start.4 = (bf16[512,512]{1,0:T(8,128)(2,1)}, bf16[512,512]{1,0:T(8,128)(2,1)S(1)}, u32[]{:S(2)}, u32[]{:S(2)}) collective-permute-start(bf16[512,512]{1,0:T(8,128)(2,1)} %collective-permute-done.3.refs_0_), channel_id=1, source_target_pairs={{1,0},{2,1},{3,2},{4,3},{5,4},{6,5},{7,6},{8,7},{9,8},{10,9},{11,1... | collective-permute-start | bytes 1572872 | tf_op jit(solution)/shard_map/ppermute | solution.py:25
  85.4 5.8 %collective-permute-start.6 = (f32[8,512]{1,0:T(8,128)S(1)}, f32[8,512]{1,0:T(8,128)S(1)}, u32[]{:S(2)}, u32[]{:S(2)}) collective-permute-start(f32[8,512]{1,0:T(8,128)S(1)} %get-tuple-element.22.refs_1_), channel_id=1, source_target_pairs={{2,0},{3,1},{4,2},{5,3},{6,4},{7,5},{8,6},{9,7},{10,8},{11,9},{12,... | collective-permute-start | bytes 49160 | tf_op jit(solution)/shard_map/ppermute | solution.py:25
  87.4 4.5 %collective-permute-start.5 = (f32[8,512]{1,0:T(8,128)S(1)}, f32[8,512]{1,0:T(8,128)S(1)}, u32[]{:S(2)}, u32[]{:S(2)}) collective-permute-start(f32[8,512]{1,0:T(8,128)S(1)} %get-tuple-element.22.refs_1_), channel_id=1, source_target_pairs={{1,0},{2,1},{3,2},{4,3},{5,4},{6,5},{7,6},{8,7},{9,8},{10,9},{11,1... | collective-permute-start | bytes 49160 | tf_op jit(solution)/shard_map/ppermute | solution.py:25

commit v10 on v9

--- a/solution.py
+++ b/solution.py
@@ -326,6 +326,108 @@
     )(q, *states, blocks)
 
 
+def final_kernel(rate, scale, q_hbm, own_hbm, state_ref, blocks, grad, loss_ref, stats_ref, q_ref, own_ref, num, keys, scores, order, sems, out_sems):
+    n, feature = q_ref.shape
+    slots = blocks.shape[0]
+    per = CHUNK // BLOCK
+    load_keys = pltpu.make_async_copy(blocks, keys, sems.at[0])
+    load_q = pltpu.make_async_copy(q_hbm, q_ref, sems.at[1])
+    load_own = pltpu.make_async_copy(own_hbm, own_ref, sems.at[2])
+    load_keys.start()
+    load_q.start()
+    load_own.start()
+    old = state_ref[:, feature : feature + 1]
+    load_keys.wait()
+    there = [(jnp.max(keys[s, :16, :128].astype(jnp.float32)) < ABSENT / 2).astype(jnp.int32) for s in range(slots)]
+    live = jnp.int32(0)
+    for s in range(slots):
+        order[live] = s
+        live += there[s]
+    chunks = (live + per - 1) // per
+    tail = order[jnp.maximum(live - 1, 0)]
+    for p in range(per - 1):
+        order[live + p] = tail
+
+    def chunk_keys(i):
+        return jnp.concatenate([keys[order[i * per + p]] for p in range(per)], axis=0)
+
+    load_q.wait()
+    q = q_ref[...]
+
+    def score(i, m):
+        s = nt_dot(q, chunk_keys(i))
+        scores[i] = s
+        for c in range(per):
+            m = jnp.maximum(m, s[:, c * BLOCK : (c + 1) * BLOCK])
+        return m
+
+    wide = lax.fori_loop(0, chunks, score, jnp.full((n, BLOCK), -jnp.inf, jnp.float32))
+    m = jnp.maximum(jnp.max(wide, axis=1, keepdims=True), old)
+    shrink = jnp.exp2((old - m) * rate)
+    kept = state_ref[:, feature + 1 : feature + 2] * shrink
+    num[...] = state_ref[:, :feature] * shrink
+    for p in range(1, per):
+        @pl.when(((chunks - 1) * per + p >= live) & (chunks > 0))
+        def _(p=p):
+            scores[chunks - 1, :, p * BLOCK : (p + 1) * BLOCK] = jnp.full((n, BLOCK), -jnp.inf, jnp.float32)
+
+    def weigh(i, l):
+        e = jnp.exp2((scores[i] - m) * rate)
+        num[...] += jnp.dot(e.astype(jnp.bfloat16), chunk_keys(i), preferred_element_type=jnp.float32)
+        for c in range(per):
+            l = l + e[:, c * BLOCK : (c + 1) * BLOCK]
+        return l
+
+    l = lax.fori_loop(0, chunks, weigh, jnp.zeros((n, BLOCK), jnp.float32))
+    total = jnp.sum(l, axis=1, keepdims=True) + kept
+    inverse = 1.0 / total
+    load_own.wait()
+    pieces = out_sems.shape[0]
+    piece = n // pieces
+    saves = []
+    for r in range(pieces):
+        part = pl.ds(r * piece, piece)
+        gain = inverse[r * piece : (r + 1) * piece]
+        num[part, :] = (num[part, :] * gain - own_ref[part, :].astype(jnp.float32)) * scale
+        saves.append(pltpu.make_async_copy(num.at[part], grad.at[part], out_sems.at[r]))
+        saves[-1].start()
+    positive = state_ref[:, feature + 2 : feature + 3]
+    loss = (m - positive) * scale + jnp.log(total)
+    lane = lax.broadcasted_iota(jnp.int32, (n, LANES), 1)
+    table = jnp.where(lane == 0, m, jnp.where(lane == 1, inverse, loss))
+    flipped = table.T
+    stats_ref[...] = flipped[:8]
+    loss_ref[...] = flipped[2:3]
+    for save in saves:
+        save.wait()
+
+
+def final_part(rate, scale, q, own, state, blocks):
+    n, feature = q.shape
+    slots = blocks.shape[0]
+    f32 = jnp.float32
+    keys = slots * BLOCK
+    return pl.pallas_call(
+        functools.partial(final_kernel, rate, scale),
+        out_shape=(jax.ShapeDtypeStruct((n, feature), f32), jax.ShapeDtypeStruct((1, n), f32), jax.ShapeDtypeStruct((8, n), f32)),
+        in_specs=[whole(pl.ANY), whole(pl.ANY), whole(), whole(pl.ANY)],
+        out_specs=(whole(pl.ANY), whole(), whole()),
+        scratch_shapes=[
+            pltpu.VMEM(q.shape, q.dtype),
+            pltpu.VMEM(own.shape, own.dtype),
+            pltpu.VMEM((n, feature), f32),
+            pltpu.VMEM(blocks.shape, blocks.dtype),
+            pltpu.VMEM((keys // CHUNK, n, CHUNK), f32),
+            pltpu.SMEM((slots + CHUNK // BLOCK,), jnp.int32),
+            pltpu.SemaphoreType.DMA((3,)),
+            pltpu.SemaphoreType.DMA((4,)),
+        ],
+        compiler_params=pltpu.CompilerParams(vmem_limit_bytes=HARD_GRANT),
+        cost_estimate=pl.CostEstimate(flops=2 * n * keys * feature, bytes_accessed=2 * keys * feature, transcendentals=n * keys // 2),
+        name="hard_last",
+    )(q, own, state, blocks)
+
+
 def rtl_kernel(rate, scale, tiles, k_ref, *refs):
     n_refs, s_refs = refs[:tiles], refs[tiles : 2 * tiles]
     base_ref, out_ref = refs[2 * tiles :]
@@ -387,8 +489,7 @@
     net1, state = lax.optimization_barrier((net1, state))
     net2 = passed_along(net1, "loop", -1)
     state = cycle_part(rate, scale, queries, [rtl2], [state])
-    others = hard_part(rate, queries, [], second, "hard_second")
-    grad, loss, stats = cycle_part(rate, scale, queries, [], [state, others], own_keys)
+    grad, loss, stats = final_part(rate, scale, queries, own_keys, state, second)
     stats1 = passed_along(stats, "loop", -1)
     stats2 = passed_along(stats, "loop", -2)
     begun = rtl_part(rate, scale, own_keys, [queries], [stats], queries)

time: 96.6 us -> 95 us (0.983)
  Pallas kernels: 26.5 us -> 22.9 us
  waiting for transfers between devices: 31.6 us -> 34 us
    pallas_call x2 -> x1, Pallas kernels: 11.2 us -> 3.26 us  [hard_part(): pl.pallas_call(functools.partial(hard_kernel, rate, not states), out_shap...]
    pallas_call x0 -> x1, Pallas kernels: none -> 6.09 us  [final_part(): pl.pallas_call(functools.partial(final_kernel, rate, scale), out_shape=(j...]
    ppermute x6, waiting for transfers between devices: 22.2 us -> 24.7 us  [passed_along(): return lax.ppermute(block, axis, route)]
    pallas_call x3 -> x2, Pallas kernels: 5.27 us -> 3.51 us  [cycle_part(): pl.pallas_call(functools.partial(cycle_kernel, rate, scale, tiles, len(st...]
  transfers between devices with their start and end apart: 9 -> 9, of which waited for: 5 -> 5; matrix products, arithmetic and copies ran while one was open for 0% -> 0% of each run, Pallas kernels for 21% -> 18%
where the time goes in v10:
time: 95 us; the launch traced here: 94.3 us
  starting transfers between devices  34 us (36%)
  waiting for transfers between devices  34 us (36%)
  Pallas kernels  22.9 us (24%)
  local copies, waits for them, and re-layouts  2.65 us (3%)
    ppermute x6, waiting for transfers between devices, passed_along(): return lax.ppermute(block, axis, route)  24.7 us
    all_to_all x2, starting transfers between devices, spread(): lax.all_to_all(packed, 'dp', split_axis=0, concat_axis=0, axis_index_grou...  16.1 us
    ppermute x6, starting transfers between devices, passed_along(): return lax.ppermute(block, axis, route)  16 us
    pallas_call x1, Pallas kernels, final_part(): pl.pallas_call(functools.partial(final_kernel, rate, scale), out_shape=(j...  6.09 us
    all_to_all x2, waiting for transfers between devices, spread(): lax.all_to_all(packed, 'dp', split_axis=0, concat_axis=0, axis_index_grou...  5.06 us
    pallas_call x2, Pallas kernels, rtl_part(): pl.pallas_call(functools.partial(rtl_kernel, rate, scale, tiles), grid=(n...  4.85 us
    ppermute x1, waiting for transfers between devices, body(): mail = lax.ppermute(mail, 'dp', [(g, g ^ 2) for g in range(groups)])  4.25 us
    pallas_call x2, Pallas kernels, cycle_part(): pl.pallas_call(functools.partial(cycle_kernel, rate, scale, tiles, len(st...  3.51 us
  transfers between devices with their start and end apart: 9, of which 5 were waited for; matrix products, arithmetic and copies ran while one was open for 0% of the time, Pallas kernels for 18%

profile of v10, /device:TPU:1, one launch (start us, length us, event | category | flops | bytes accessed | tf_op | source)
XLA Modules:
  0.0 94.3 jit_solution(5484061494048787481)
XLA Ops:
  0.6 2.5 %pack_own.1 = (bf16[16,128,512]{2,1,0:T(8,128)(2,1)}, bf16[528,512]{1,0:T(8,128)(2,1)}) custom-call(s32[1]{0:T(128)} %bitcast.2.me, s32[16]{0:T(128)} %bitcast.20, s32[16]{0:T(128)} %bitcast.21, bf16[512,512]{1,0:T(8,128)(2,1)} %bitcast.14), custom_call_target="tpu_custom_call" | custom-call | tf_op jit(solution)/shard_map/pack_own/pallas_call | solution.py:105
  3.2 0.0 copy-start.1
  3.2 10.6 %all-to-all-start = ((bf16[16,128,512]{2,1,0:T(8,128)(2,1)}), bf16[16,128,512]{2,1,0:T(8,128)(2,1)S(1)}, u32[]{:S(2)}, u32[]{:S(2)}) async-start(bf16[16,128,512]{2,1,0:T(8,128)(2,1)} %get-tuple-element.16), calls=%async_computation | async-start | bytes 4194304 | tf_op jit(solution)/shard_map/all_to_all | solution.py:475
  13.8 1.9 %collective-permute-start = (bf16[528,512]{1,0:T(8,128)(2,1)}, bf16[528,512]{1,0:T(8,128)(2,1)S(1)}, u32[]{:S(2)}, u32[]{:S(2)}) collective-permute-start(bf16[528,512]{1,0:T(8,128)(2,1)} %get-tuple-element.13), channel_id=1, source_target_pairs={{0,64},{32,96},{64,0},{96,32},{128,192},{160,224},{192,128},{224,1... | collective-permute-start | bytes 1622024 | tf_op jit(solution)/shard_map/ppermute | solution.py:480
  15.7 0.0 copy-done.1
  15.7 1.9 %collective-permute-start.1 = (bf16[512,512]{1,0:T(8,128)(2,1)S(1)}, bf16[512,512]{1,0:T(8,128)(2,1)S(1)}, u32[]{:S(2)}, u32[]{:S(2)}) collective-permute-start(bf16[512,512]{1,0:T(8,128)(2,1)S(1)} %bitcast.15), channel_id=1, source_target_pairs={{31,0},{0,1},{1,2},{2,3},{3,4},{4,5},{5,6},{6,7},{7,8},{8,9},{9,10... | collective-permute-start | bytes 1572872 | tf_op jit(solution)/shard_map/ppermute | solution.py:25
  17.6 19.7 %collective-permute-done.1.refs_1_ = bf16[512,512]{1,0:T(8,128)(2,1)S(1)} collective-permute-done((bf16[512,512]{1,0:T(8,128)(2,1)S(1)}, bf16[512,512]{1,0:T(8,128)(2,1)S(1)}, u32[]{:S(2)}, u32[]{:S(2)}) %collective-permute-start.1) | collective-permute-done | bytes 524320 | tf_op jit(solution)/shard_map/ppermute | solution.py:25
  37.3 0.0 copy-start.2
  37.3 0.8 copy-done.2
  38.1 4.3 %collective-permute-done.mail = bf16[528,512]{1,0:T(8,128)(2,1)S(1)} collective-permute-done((bf16[528,512]{1,0:T(8,128)(2,1)}, bf16[528,512]{1,0:T(8,128)(2,1)S(1)}, u32[]{:S(2)}, u32[]{:S(2)}) %collective-permute-start) | collective-permute-done | bytes 540704 | tf_op jit(solution)/shard_map/ppermute | solution.py:480
  42.3 0.0 copy-start.4
  42.3 0.8 copy-done.4
  43.1 2.6 %pack_far.1 = bf16[16,128,512]{2,1,0:T(8,128)(2,1)} custom-call(s32[1]{0:T(128)} %bitcast.2.me, bf16[528,512]{1,0:T(8,128)(2,1)} %copy-done.4), custom_call_target="tpu_custom_call" | custom-call | tf_op jit(solution)/shard_map/pack_far/pallas_call | solution.py:149
  45.8 0.0 copy-start
  45.8 0.0 all-to-all-done.refs_1_
  45.8 5.6 %all-to-all-start.1 = ((bf16[16,128,512]{2,1,0:T(8,128)(2,1)}), bf16[16,128,512]{2,1,0:T(8,128)(2,1)}, u32[]{:S(2)}, u32[]{:S(2)}) async-start(bf16[16,128,512]{2,1,0:T(8,128)(2,1)} %pack_far.1), calls=%async_computation.1 | async-start | bytes 4194304 | tf_op jit(solution)/shard_map/all_to_all | solution.py:475
  51.4 0.0 copy-done
  51.4 1.9 %collective-permute-start.3 = (bf16[512,512]{1,0:T(8,128)(2,1)S(1)}, bf16[512,512]{1,0:T(8,128)(2,1)}, u32[]{:S(2)}, u32[]{:S(2)}) collective-permute-start(bf16[512,512]{1,0:T(8,128)(2,1)S(1)} %bitcast.7), channel_id=1, source_target_pairs={{1,0},{2,1},{3,2},{4,3},{5,4},{6,5},{7,6},{8,7},{9,8},{10,9},{11,1... | collective-permute-start | bytes 1572872 | tf_op jit(solution)/shard_map/ppermute | solution.py:25
  53.3 3.4 %collective-permute-start.2 = (bf16[512,512]{1,0:T(8,128)(2,1)}, bf16[512,512]{1,0:T(8,128)(2,1)S(1)}, u32[]{:S(2)}, u32[]{:S(2)}) collective-permute-start(bf16[512,512]{1,0:T(8,128)(2,1)} %copy-done.2), channel_id=1, source_target_pairs={{31,0},{0,1},{1,2},{2,3},{3,4},{4,5},{5,6},{6,7},{7,8},{8,9},{9,10... | collective-permute-start | bytes 1572872 | tf_op jit(solution)/shard_map/ppermute | solution.py:25
  56.6 0.0 copy-start.3
  56.7 1.0 %copy-done.3 = bf16[512,512]{1,0:T(8,128)(2,1)S(1)} copy-done((bf16[512,512]{1,0:T(8,128)(2,1)S(1)}, bf16[512,512]{1,0:T(8,128)(2,1)}, u32[]{:S(2)}) %copy-start.3) | copy-done | bytes 524312
  57.7 1.9 %cycle_own.1.refs_0_ = f32[512,640]{1,0:T(8,128)S(1)} custom-call(bf16[512,512]{1,0:T(8,128)(2,1)S(1)} %bitcast.8, bf16[512,512]{1,0:T(8,128)(2,1)S(1)} %bitcast.16, bf16[512,512]{1,0:T(8,128)(2,1)S(1)} %copy-done.3), custom_call_target="tpu_custom_call" | custom-call | flops 1073741824 | bytes 2097152 | tf_op jit(solution)/shard_map/cycle_own/pallas_call | solution.py:227
  59.6 3.3 %hard_first.1.refs_1_ = f32[512,640]{1,0:T(8,128)S(1)} custom-call(bf16[512,512]{1,0:T(8,128)(2,1)S(1)} %bitcast.9, f32[512,640]{1,0:T(8,128)S(1)} %cycle_own.1.refs_0_, bf16[16,128,512]{2,1,0:T(8,128)(2,1)S(1)} %all-to-all-done.refs_1_), custom_call_target="tpu_custom_call" | custom-call | flops 1073741824 | bytes 2097152 | tf_op jit(solution)/shard_map/hard_first/pallas_call | solution.py:311
  62.9 4.0 %collective-permute-done.3.refs_0_ = bf16[512,512]{1,0:T(8,128)(2,1)} collective-permute-done((bf16[512,512]{1,0:T(8,128)(2,1)S(1)}, bf16[512,512]{1,0:T(8,128)(2,1)}, u32[]{:S(2)}, u32[]{:S(2)}) %collective-permute-start.3) | collective-permute-done | bytes 524320 | tf_op jit(solution)/shard_map/ppermute | solution.py:25
  66.9 4.2 %collective-permute-start.4 = (bf16[512,512]{1,0:T(8,128)(2,1)}, bf16[512,512]{1,0:T(8,128)(2,1)S(1)}, u32[]{:S(2)}, u32[]{:S(2)}) collective-permute-start(bf16[512,512]{1,0:T(8,128)(2,1)} %collective-permute-done.3.refs_0_), channel_id=1, source_target_pairs={{1,0},{2,1},{3,2},{4,3},{5,4},{6,5},{7,6},{8,7},{9,8},{10,9},{11,1... | collective-permute-start | bytes 1572872 | tf_op jit(solution)/shard_map/ppermute | solution.py:25
  71.1 0.0 collective-permute-done.2.refs_0_
  71.1 1.6 %cycle_more.1.state_ref = f32[512,640]{1,0:T(8,128)S(1)} custom-call(bf16[512,512]{1,0:T(8,128)(2,1)S(1)} %bitcast.10, bf16[512,512]{1,0:T(8,128)(2,1)S(1)} %collective-permute-done.2.refs_0_, f32[512,640]{1,0:T(8,128)S(1)} %hard_first.1.refs_1_), custom_call_target="tpu_custom_call" | custom-call | flops 536870912 | bytes 2097152 | tf_op jit(solution)/shard_map/cycle_more/pallas_call | solution.py:227
  72.7 5.1 %all-to-all-done.1.blocks = bf16[16,128,512]{2,1,0:T(8,128)(2,1)} async-done(((bf16[16,128,512]{2,1,0:T(8,128)(2,1)}), bf16[16,128,512]{2,1,0:T(8,128)(2,1)}, u32[]{:S(2)}, u32[]{:S(2)}) %all-to-all-start.1) | async-done | bytes 2097184 | tf_op jit(solution)/shard_map/all_to_all | solution.py:475
  77.8 6.1 %hard_last.1 = (f32[512,512]{1,0:T(8,128)}, f32[1,512]{1,0:T(1,128)}, f32[8,512]{1,0:T(8,128)S(1)}) custom-call(bf16[512,512]{1,0:T(8,128)(2,1)S(1)} %bitcast.11, bf16[512,512]{1,0:T(8,128)(2,1)S(1)} %bitcast.17, f32[512,640]{1,0:T(8,128)S(1)} %cycle_more.1.state_ref, bf16[16,128,512]{2,1,0:T(8,128)(2,1)} %all-to-all-done.1.blocks), custom_call_target="tpu_custom_call" | custom-call | flops 1073741824 | bytes 2097152 | tf_op jit(solution)/shard_map/hard_last/pallas_call | solution.py:410
  83.9 1.9 %collective-permute-start.6 = (f32[8,512]{1,0:T(8,128)S(1)}, f32[8,512]{1,0:T(8,128)S(1)}, u32[]{:S(2)}, u32[]{:S(2)}) collective-permute-start(f32[8,512]{1,0:T(8,128)S(1)} %get-tuple-element.22.refs_1_), channel_id=1, source_target_pairs={{2,0},{3,1},{4,2},{5,3},{6,4},{7,5},{8,6},{9,7},{10,8},{11,9},{12,... | collective-permute-start | bytes 49160 | tf_op jit(solution)/shard_map/ppermute | solution.py:25
  85.8 2.6 %collective-permute-start.5 = (f32[8,512]{1,0:T(8,128)S(1)}, f32[8,512]{1,0:T(8,128)S(1)}, u32[]{:S(2)}, u32[]{:S(2)}) collective-permute-start(f32[8,512]{1,0:T(8,128)S(1)} %get-tuple-element.22.refs_1_), channel_id=1, source_target_pairs={{1,0},{2,1},{3,2},{4,3},{5,4},{6,5},{7,6},{8,7},{9,8},{10,9},{11,1... | collective-permute-start | bytes 49160 | tf_op jit(solution)/shard_map/ppermute | solution.py:25
  88.5 1.1 %rtl_own.1.refs_4_ = f32[512,512]{1,0:T(8,128)S(1)} custom-call(bf16[512,512]{1,0:T(8,128)(2,1)S(1)} %bitcast.18, bf16[512,512]{1,0:T(8,128)(2,1)S(1)} %bitcast.12, f32[8,512]{1,0:T(8,128)S(1)} %get-tuple-element.22.refs_1_, bf16[512,512]{1,0:T(8,128)(2,1)S(1)} %bitcast.13), custom_call_target="tpu_custom_call" | custom-call | flops 536870912 | bytes 2097152 | tf_op jit(solution)/shard_map/rtl_own/pallas_call | solution.py:450
  89.6 0.0 collective-permute-done.4.refs_1_
  89.6 0.0 collective-permute-done.6.refs_3_
  89.6 1.0 %collective-permute-done.5.refs_2_ = f32[8,512]{1,0:T(8,128)S(1)} collective-permute-done((f32[8,512]{1,0:T(8,128)S(1)}, f32[8,512]{1,0:T(8,128)S(1)}, u32[]{:S(2)}, u32[]{:S(2)}) %collective-permute-start.5) | collective-permute-done | bytes 16416 | tf_op jit(solution)/shard_map/ppermute | solution.py:25
  90.6 3.7 %rtl_others.1 = f32[512,512]{1,0:T(8,128)} custom-call(bf16[512,512]{1,0:T(8,128)(2,1)S(1)} %bitcast.19, bf16[512,512]{1,0:T(8,128)(2,1)} %collective-permute-done.3.refs_0_, bf16[512,512]{1,0:T(8,128)(2,1)S(1)} %collective-permute-done.4.refs_1_, f32[8,512]{1,0:T(8,128)S(1)} %collective-permute-done.5.refs_2_, f32[8,512]{1,0:T(8,128)S(1)} %collective-permute-done.6.refs_3_, ...), custom_call_target="tpu_custom_call" | custom-call | flops 1073741824 | bytes 2621440 | tf_op jit(solution)/shard_map/rtl_others/pallas_call | solution.py:450
Async XLA Ops:
  3.2 12.5 %copy-start.1 = (bf16[1,512,512]{2,1,0:T(8,128)(2,1)S(1)}, bf16[1,512,512]{2,1,0:T(8,128)(2,1)}, u32[]{:S(2)}) copy-start(bf16[1,512,512]{2,1,0:T(8,128)(2,1)} %param.5) | copy-start | bytes 1572868
  3.2 42.6 %all-to-all-start = ((bf16[16,128,512]{2,1,0:T(8,128)(2,1)}), bf16[16,128,512]{2,1,0:T(8,128)(2,1)S(1)}, u32[]{:S(2)}, u32[]{:S(2)}) async-start(bf16[16,128,512]{2,1,0:T(8,128)(2,1)} %get-tuple-element.16), calls=%async_computation | async-start | bytes 4194304 | tf_op jit(solution)/shard_map/all_to_all | solution.py:475
  13.8 28.6 %collective-permute-start = (bf16[528,512]{1,0:T(8,128)(2,1)}, bf16[528,512]{1,0:T(8,128)(2,1)S(1)}, u32[]{:S(2)}, u32[]{:S(2)}) collective-permute-start(bf16[528,512]{1,0:T(8,128)(2,1)} %get-tuple-element.13), channel_id=1, source_target_pairs={{0,64},{32,96},{64,0},{96,32},{128,192},{160,224},{192,128},{224,1... | collective-permute-start | bytes 1622024 | tf_op jit(solution)/shard_map/ppermute | solution.py:480
  15.7 21.6 %collective-permute-start.1 = (bf16[512,512]{1,0:T(8,128)(2,1)S(1)}, bf16[512,512]{1,0:T(8,128)(2,1)S(1)}, u32[]{:S(2)}, u32[]{:S(2)}) collective-permute-start(bf16[512,512]{1,0:T(8,128)(2,1)S(1)} %bitcast.15), channel_id=1, source_target_pairs={{31,0},{0,1},{1,2},{2,3},{3,4},{4,5},{5,6},{6,7},{7,8},{8,9},{9,10... | collective-permute-start | bytes 1572872 | tf_op jit(solution)/shard_map/ppermute | solution.py:25
  37.3 0.8 copy-start.2
  42.3 0.8 copy-start.4
  45.8 5.6 %copy-start = (bf16[1,512,512]{2,1,0:T(8,128)(2,1)S(1)}, bf16[1,512,512]{2,1,0:T(8,128)(2,1)}, u32[]{:S(2)}) copy-start(bf16[1,512,512]{2,1,0:T(8,128)(2,1)} %param.4) | copy-start | bytes 1572868
  45.8 32.0 %all-to-all-start.1 = ((bf16[16,128,512]{2,1,0:T(8,128)(2,1)}), bf16[16,128,512]{2,1,0:T(8,128)(2,1)}, u32[]{:S(2)}, u32[]{:S(2)}) async-start(bf16[16,128,512]{2,1,0:T(8,128)(2,1)} %pack_far.1), calls=%async_computation.1 | async-start | bytes 4194304 | tf_op jit(solution)/shard_map/all_to_all | solution.py:475
  51.4 15.5 %collective-permute-start.3 = (bf16[512,512]{1,0:T(8,128)(2,1)S(1)}, bf16[512,512]{1,0:T(8,128)(2,1)}, u32[]{:S(2)}, u32[]{:S(2)}) collective-permute-start(bf16[512,512]{1,0:T(8,128)(2,1)S(1)} %bitcast.7), channel_id=1, source_target_pairs={{1,0},{2,1},{3,2},{4,3},{5,4},{6,5},{7,6},{8,7},{9,8},{10,9},{11,1... | collective-permute-start | bytes 1572872 | tf_op jit(solution)/shard_map/ppermute | solution.py:25
  53.3 17.8 %collective-permute-start.2 = (bf16[512,512]{1,0:T(8,128)(2,1)}, bf16[512,512]{1,0:T(8,128)(2,1)S(1)}, u32[]{:S(2)}, u32[]{:S(2)}) collective-permute-start(bf16[512,512]{1,0:T(8,128)(2,1)} %copy-done.2), channel_id=1, source_target_pairs={{31,0},{0,1},{1,2},{2,3},{3,4},{4,5},{5,6},{6,7},{7,8},{8,9},{9,10... | collective-permute-start | bytes 1572872 | tf_op jit(solution)/shard_map/ppermute | solution.py:25
  56.6 1.1 %copy-start.3 = (bf16[512,512]{1,0:T(8,128)(2,1)S(1)}, bf16[512,512]{1,0:T(8,128)(2,1)}, u32[]{:S(2)}) copy-start(bf16[512,512]{1,0:T(8,128)(2,1)} %copy-done.2) | copy-start | bytes 1572868
  66.9 22.7 %collective-permute-start.4 = (bf16[512,512]{1,0:T(8,128)(2,1)}, bf16[512,512]{1,0:T(8,128)(2,1)S(1)}, u32[]{:S(2)}, u32[]{:S(2)}) collective-permute-start(bf16[512,512]{1,0:T(8,128)(2,1)} %collective-permute-done.3.refs_0_), channel_id=1, source_target_pairs={{1,0},{2,1},{3,2},{4,3},{5,4},{6,5},{7,6},{8,7},{9,8},{10,9},{11,1... | collective-permute-start | bytes 1572872 | tf_op jit(solution)/shard_map/ppermute | solution.py:25
  83.9 5.7 %collective-permute-start.6 = (f32[8,512]{1,0:T(8,128)S(1)}, f32[8,512]{1,0:T(8,128)S(1)}, u32[]{:S(2)}, u32[]{:S(2)}) collective-permute-start(f32[8,512]{1,0:T(8,128)S(1)} %get-tuple-element.22.refs_1_), channel_id=1, source_target_pairs={{2,0},{3,1},{4,2},{5,3},{6,4},{7,5},{8,6},{9,7},{10,8},{11,9},{12,... | collective-permute-start | bytes 49160 | tf_op jit(solution)/shard_map/ppermute | solution.py:25
  85.8 4.8 %collective-permute-start.5 = (f32[8,512]{1,0:T(8,128)S(1)}, f32[8,512]{1,0:T(8,128)S(1)}, u32[]{:S(2)}, u32[]{:S(2)}) collective-permute-start(f32[8,512]{1,0:T(8,128)S(1)} %get-tuple-element.22.refs_1_), channel_id=1, source_target_pairs={{1,0},{2,1},{3,2},{4,3},{5,4},{6,5},{7,6},{8,7},{9,8},{10,9},{11,1... | collective-permute-start | bytes 49160 | tf_op jit(solution)/shard_map/ppermute | solution.py:25

commit v11 on v9

--- a/solution.py
+++ b/solution.py
@@ -392,6 +392,8 @@
     stats1 = passed_along(stats, "loop", -1)
     stats2 = passed_along(stats, "loop", -2)
     begun = rtl_part(rate, scale, own_keys, [queries], [stats], queries)
+    net1, begun = lax.optimization_barrier((net1, begun))
+    net1 = jnp.where(at < 0, queries, net1)
     rtl_grad = rtl_part(rate, scale, own_keys, [net1, net2], [stats1, stats2], begun)
     return (loss, grad[None], rtl_grad[None])
 

time: 96.6 us -> 94.2 us (0.975)
  Pallas kernels: 26.5 us -> 20.6 us
  waiting for transfers between devices: 31.6 us -> 33 us
  other arithmetic: 0 us -> 1.1 us
  starting transfers between devices: 33.9 us -> 34.9 us
    pallas_call x2, Pallas kernels: 11.2 us -> 6.38 us  [hard_part(): pl.pallas_call(functools.partial(hard_kernel, rate, not states), out_shap...]
    ppermute x6, waiting for transfers between devices: 22.2 us -> 23.7 us  [passed_along(): return lax.ppermute(block, axis, route)]
    select_n x0 -> x1, other arithmetic: none -> 1.1 us  [body(): net1 = jnp.where(at < 0, queries, net1)]
    ppermute x6, starting transfers between devices: 16 us -> 17.1 us  [passed_along(): return lax.ppermute(block, axis, route)]
    pallas_call x2, Pallas kernels: 4.84 us -> 3.82 us  [rtl_part(): pl.pallas_call(functools.partial(rtl_kernel, rate, scale, tiles), grid=(n...]
  transfers between devices with their start and end apart: 9 -> 9, of which waited for: 5 -> 4; matrix products, arithmetic and copies ran while one was open for 0% -> 1% of each run, Pallas kernels for 21% -> 17%
where the time goes in v11:
time: 94.2 us; the launch traced here: 93.1 us
  starting transfers between devices  34.9 us (37%)
  waiting for transfers between devices  33 us (35%)
  Pallas kernels  20.6 us (22%)
  local copies, waits for them, and re-layouts  2.65 us (3%)
  other arithmetic  1.1 us (1%)
    ppermute x6, waiting for transfers between devices, passed_along(): return lax.ppermute(block, axis, route)  23.7 us
    ppermute x6, starting transfers between devices, passed_along(): return lax.ppermute(block, axis, route)  17.1 us
    all_to_all x2, starting transfers between devices, spread(): lax.all_to_all(packed, 'dp', split_axis=0, concat_axis=0, axis_index_grou...  15.9 us
    pallas_call x2, Pallas kernels, hard_part(): pl.pallas_call(functools.partial(hard_kernel, rate, not states), out_shap...  6.38 us
    pallas_call x3, Pallas kernels, cycle_part(): pl.pallas_call(functools.partial(cycle_kernel, rate, scale, tiles, len(st...  5.27 us
    all_to_all x2, waiting for transfers between devices, spread(): lax.all_to_all(packed, 'dp', split_axis=0, concat_axis=0, axis_index_grou...  5.13 us
    ppermute x1, waiting for transfers between devices, body(): mail = lax.ppermute(mail, 'dp', [(g, g ^ 2) for g in range(groups)])  4.17 us
    pallas_call x2, Pallas kernels, rtl_part(): pl.pallas_call(functools.partial(rtl_kernel, rate, scale, tiles), grid=(n...  3.82 us
  transfers between devices with their start and end apart: 9, of which 4 were waited for; matrix products, arithmetic and copies ran while one was open for 1% of the time, Pallas kernels for 17%

profile of v11, /device:TPU:1, one launch (start us, length us, event | category | flops | bytes accessed | tf_op | source)
XLA Modules:
  0.0 93.1 jit_solution(12352515750011155661)
XLA Ops:
  0.6 2.5 %pack_own.1 = (bf16[16,128,512]{2,1,0:T(8,128)(2,1)}, bf16[528,512]{1,0:T(8,128)(2,1)}) custom-call(s32[1]{0:T(128)} %bitcast.1.me, s32[16]{0:T(128)} %bitcast.23, s32[16]{0:T(128)} %bitcast.24, bf16[512,512]{1,0:T(8,128)(2,1)} %bitcast.17), custom_call_target="tpu_custom_call" | custom-call | tf_op jit(solution)/shard_map/pack_own/pallas_call | solution.py:105
  3.2 0.0 copy-start.1
  3.2 10.4 %all-to-all-start = ((bf16[16,128,512]{2,1,0:T(8,128)(2,1)}), bf16[16,128,512]{2,1,0:T(8,128)(2,1)S(1)}, u32[]{:S(2)}, u32[]{:S(2)}) async-start(bf16[16,128,512]{2,1,0:T(8,128)(2,1)} %get-tuple-element.18), calls=%async_computation | async-start | bytes 4194304 | tf_op jit(solution)/shard_map/all_to_all | solution.py:373
  13.6 1.9 %collective-permute-start = (bf16[528,512]{1,0:T(8,128)(2,1)}, bf16[528,512]{1,0:T(8,128)(2,1)S(1)}, u32[]{:S(2)}, u32[]{:S(2)}) collective-permute-start(bf16[528,512]{1,0:T(8,128)(2,1)} %get-tuple-element.15), channel_id=1, source_target_pairs={{0,64},{32,96},{64,0},{96,32},{128,192},{160,224},{192,128},{224,1... | collective-permute-start | bytes 1622024 | tf_op jit(solution)/shard_map/ppermute | solution.py:378
  15.6 0.0 copy-done.1
  15.6 2.0 %collective-permute-start.1 = (bf16[512,512]{1,0:T(8,128)(2,1)S(1)}, bf16[512,512]{1,0:T(8,128)(2,1)S(1)}, u32[]{:S(2)}, u32[]{:S(2)}) collective-permute-start(bf16[512,512]{1,0:T(8,128)(2,1)S(1)} %bitcast.18), channel_id=1, source_target_pairs={{31,0},{0,1},{1,2},{2,3},{3,4},{4,5},{5,6},{6,7},{7,8},{8,9},{9,10... | collective-permute-start | bytes 1572872 | tf_op jit(solution)/shard_map/ppermute | solution.py:25
  17.6 19.7 %collective-permute-done.1.refs_1_ = bf16[512,512]{1,0:T(8,128)(2,1)S(1)} collective-permute-done((bf16[512,512]{1,0:T(8,128)(2,1)S(1)}, bf16[512,512]{1,0:T(8,128)(2,1)S(1)}, u32[]{:S(2)}, u32[]{:S(2)}) %collective-permute-start.1) | collective-permute-done | bytes 524320 | tf_op jit(solution)/shard_map/ppermute | solution.py:25
  37.2 0.0 copy-start.2
  37.2 0.8 copy-done.2
  38.0 4.2 %collective-permute-done.mail = bf16[528,512]{1,0:T(8,128)(2,1)S(1)} collective-permute-done((bf16[528,512]{1,0:T(8,128)(2,1)}, bf16[528,512]{1,0:T(8,128)(2,1)S(1)}, u32[]{:S(2)}, u32[]{:S(2)}) %collective-permute-start) | collective-permute-done | bytes 540704 | tf_op jit(solution)/shard_map/ppermute | solution.py:378
  42.2 0.0 copy-start.4
  42.2 0.8 copy-done.4
  43.0 2.6 %pack_far.1 = bf16[16,128,512]{2,1,0:T(8,128)(2,1)} custom-call(s32[1]{0:T(128)} %bitcast.1.me, bf16[528,512]{1,0:T(8,128)(2,1)} %copy-done.4), custom_call_target="tpu_custom_call" | custom-call | tf_op jit(solution)/shard_map/pack_far/pallas_call | solution.py:149
  45.6 0.0 copy-start
  45.7 0.0 all-to-all-done.refs_1_
  45.7 5.5 %all-to-all-start.1 = ((bf16[16,128,512]{2,1,0:T(8,128)(2,1)}), bf16[16,128,512]{2,1,0:T(8,128)(2,1)}, u32[]{:S(2)}, u32[]{:S(2)}) async-start(bf16[16,128,512]{2,1,0:T(8,128)(2,1)} %pack_far.1), calls=%async_computation.1 | async-start | bytes 4194304 | tf_op jit(solution)/shard_map/all_to_all | solution.py:373
  51.1 0.0 copy-done
  51.1 1.9 %collective-permute-start.3 = (bf16[512,512]{1,0:T(8,128)(2,1)S(1)}, bf16[512,512]{1,0:T(8,128)(2,1)}, u32[]{:S(2)}, u32[]{:S(2)}) collective-permute-start(bf16[512,512]{1,0:T(8,128)(2,1)S(1)} %bitcast.9), channel_id=1, source_target_pairs={{1,0},{2,1},{3,2},{4,3},{5,4},{6,5},{7,6},{8,7},{9,8},{10,9},{11,1... | collective-permute-start | bytes 1572872 | tf_op jit(solution)/shard_map/ppermute | solution.py:25
  53.1 3.4 %collective-permute-start.2 = (bf16[512,512]{1,0:T(8,128)(2,1)}, bf16[512,512]{1,0:T(8,128)(2,1)S(1)}, u32[]{:S(2)}, u32[]{:S(2)}) collective-permute-start(bf16[512,512]{1,0:T(8,128)(2,1)} %copy-done.2), channel_id=1, source_target_pairs={{31,0},{0,1},{1,2},{2,3},{3,4},{4,5},{5,6},{6,7},{7,8},{8,9},{9,10... | collective-permute-start | bytes 1572872 | tf_op jit(solution)/shard_map/ppermute | solution.py:25
  56.4 0.0 copy-start.3
  56.4 1.0 %copy-done.3 = bf16[512,512]{1,0:T(8,128)(2,1)S(1)} copy-done((bf16[512,512]{1,0:T(8,128)(2,1)S(1)}, bf16[512,512]{1,0:T(8,128)(2,1)}, u32[]{:S(2)}) %copy-start.3) | copy-done | bytes 524312
  57.5 1.9 %cycle_own.1.refs_0_ = f32[512,640]{1,0:T(8,128)S(1)} custom-call(bf16[512,512]{1,0:T(8,128)(2,1)S(1)} %bitcast.10, bf16[512,512]{1,0:T(8,128)(2,1)S(1)} %bitcast.19, bf16[512,512]{1,0:T(8,128)(2,1)S(1)} %copy-done.3), custom_call_target="tpu_custom_call" | custom-call | flops 1073741824 | bytes 2097152 | tf_op jit(solution)/shard_map/cycle_own/pallas_call | solution.py:227
  59.4 3.3 %hard_first.1.refs_1_ = f32[512,640]{1,0:T(8,128)S(1)} custom-call(bf16[512,512]{1,0:T(8,128)(2,1)S(1)} %bitcast.11, f32[512,640]{1,0:T(8,128)S(1)} %cycle_own.1.refs_0_, bf16[16,128,512]{2,1,0:T(8,128)(2,1)S(1)} %all-to-all-done.refs_1_), custom_call_target="tpu_custom_call" | custom-call | flops 1073741824 | bytes 2097152 | tf_op jit(solution)/shard_map/hard_first/pallas_call | solution.py:311
  62.7 4.0 %collective-permute-done.3 = bf16[512,512]{1,0:T(8,128)(2,1)} collective-permute-done((bf16[512,512]{1,0:T(8,128)(2,1)S(1)}, bf16[512,512]{1,0:T(8,128)(2,1)}, u32[]{:S(2)}, u32[]{:S(2)}) %collective-permute-start.3) | collective-permute-done | bytes 524320 | tf_op jit(solution)/shard_map/ppermute | solution.py:25
  66.7 4.1 %collective-permute-start.4 = (bf16[512,512]{1,0:T(8,128)(2,1)}, bf16[512,512]{1,0:T(8,128)(2,1)S(1)}, u32[]{:S(2)}, u32[]{:S(2)}) collective-permute-start(bf16[512,512]{1,0:T(8,128)(2,1)} %collective-permute-done.3), channel_id=1, source_target_pairs={{1,0},{2,1},{3,2},{4,3},{5,4},{6,5},{7,6},{8,7},{9,8},{10,9},{11,1... | collective-permute-start | bytes 1572872 | tf_op jit(solution)/shard_map/ppermute | solution.py:25
  70.8 0.0 collective-permute-done.2.refs_0_
  70.8 1.6 %cycle_more.1.refs_0_ = f32[512,640]{1,0:T(8,128)S(1)} custom-call(bf16[512,512]{1,0:T(8,128)(2,1)S(1)} %bitcast.12, bf16[512,512]{1,0:T(8,128)(2,1)S(1)} %collective-permute-done.2.refs_0_, f32[512,640]{1,0:T(8,128)S(1)} %hard_first.1.refs_1_), custom_call_target="tpu_custom_call" | custom-call | flops 536870912 | bytes 2097152 | tf_op jit(solution)/shard_map/cycle_more/pallas_call | solution.py:227
  72.5 5.1 %all-to-all-done.1.refs_0_ = bf16[16,128,512]{2,1,0:T(8,128)(2,1)} async-done(((bf16[16,128,512]{2,1,0:T(8,128)(2,1)}), bf16[16,128,512]{2,1,0:T(8,128)(2,1)}, u32[]{:S(2)}, u32[]{:S(2)}) %all-to-all-start.1) | async-done | bytes 2097184 | tf_op jit(solution)/shard_map/all_to_all | solution.py:373
  77.6 3.1 %hard_second.1.refs_1_ = f32[512,640]{1,0:T(8,128)S(1)} custom-call(bf16[512,512]{1,0:T(8,128)(2,1)S(1)} %bitcast.13, bf16[16,128,512]{2,1,0:T(8,128)(2,1)} %all-to-all-done.1.refs_0_), custom_call_target="tpu_custom_call" | custom-call | flops 1073741824 | bytes 2097152 | tf_op jit(solution)/shard_map/hard_second/pallas_call | solution.py:311
  80.7 1.8 %cycle_last.1 = (f32[512,512]{1,0:T(8,128)}, f32[1,512]{1,0:T(1,128)}, f32[8,512]{1,0:T(8,128)S(1)}) custom-call(bf16[512,512]{1,0:T(8,128)(2,1)S(1)} %bitcast.14, f32[512,640]{1,0:T(8,128)S(1)} %cycle_more.1.refs_0_, f32[512,640]{1,0:T(8,128)S(1)} %hard_second.1.refs_1_, bf16[512,512]{1,0:T(8,128)(2,1)S(1)} %bitcast.20), custom_call_target="tpu_custom_call" | custom-call | bytes 2097152 | tf_op jit(solution)/shard_map/cycle_last/pallas_call | solution.py:227
  82.4 3.1 %collective-permute-start.6 = (f32[8,512]{1,0:T(8,128)S(1)}, f32[8,512]{1,0:T(8,128)S(1)}, u32[]{:S(2)}, u32[]{:S(2)}) collective-permute-start(f32[8,512]{1,0:T(8,128)S(1)} %get-tuple-element.24.refs_1_), channel_id=1, source_target_pairs={{2,0},{3,1},{4,2},{5,3},{6,4},{7,5},{8,6},{9,7},{10,8},{11,9},{12,... | collective-permute-start | bytes 49160 | tf_op jit(solution)/shard_map/ppermute | solution.py:25
  85.5 2.6 %collective-permute-start.5 = (f32[8,512]{1,0:T(8,128)S(1)}, f32[8,512]{1,0:T(8,128)S(1)}, u32[]{:S(2)}, u32[]{:S(2)}) collective-permute-start(f32[8,512]{1,0:T(8,128)S(1)} %get-tuple-element.24.refs_1_), channel_id=1, source_target_pairs={{1,0},{2,1},{3,2},{4,3},{5,4},{6,5},{7,6},{8,7},{9,8},{10,9},{11,1... | collective-permute-start | bytes 49160 | tf_op jit(solution)/shard_map/ppermute | solution.py:25
  88.1 1.1 %rtl_own.1.refs_4_ = f32[512,512]{1,0:T(8,128)S(1)} custom-call(bf16[512,512]{1,0:T(8,128)(2,1)S(1)} %bitcast.21, bf16[512,512]{1,0:T(8,128)(2,1)S(1)} %bitcast.15, f32[8,512]{1,0:T(8,128)S(1)} %get-tuple-element.24.refs_1_, bf16[512,512]{1,0:T(8,128)(2,1)S(1)} %bitcast.16), custom_call_target="tpu_custom_call" | custom-call | flops 536870912 | bytes 2097152 | tf_op jit(solution)/shard_map/rtl_own/pallas_call | solution.py:348
  89.3 1.1 %broadcast_select_fusion.refs_0_ = bf16[512,512]{1,0:T(8,128)(2,1)S(1)} fusion(bf16[512,512]{1,0:T(8,128)(2,1)} %collective-permute-done.3, pred[]{:T(512)} %bitcast.6, bf16[1,512,512]{2,1,0:T(8,128)(2,1)S(1)} %copy-done), kind=kLoop, calls=%fused_computation | loop fusion | flops 262144 | bytes 1572865 | tf_op jit(solution)/shard_map/jit(_where)/select_n | solution.py:396
  90.4 0.0 collective-permute-done.4.refs_1_
  90.4 0.0 collective-permute-done.6.refs_3_
  90.4 0.0 collective-permute-done.5.refs_2_
  90.4 2.7 %rtl_others.1 = f32[512,512]{1,0:T(8,128)} custom-call(bf16[512,512]{1,0:T(8,128)(2,1)S(1)} %bitcast.22, bf16[512,512]{1,0:T(8,128)(2,1)S(1)} %broadcast_select_fusion.refs_0_, bf16[512,512]{1,0:T(8,128)(2,1)S(1)} %collective-permute-done.4.refs_1_, f32[8,512]{1,0:T(8,128)S(1)} %collective-permute-done.5.refs_2_, ...), custom_call_target="tpu_custom_call" | custom-call | flops 1073741824 | bytes 2621440 | tf_op jit(solution)/shard_map/rtl_others/pallas_call | solution.py:348
Async XLA Ops:
  3.2 12.4 %copy-start.1 = (bf16[1,512,512]{2,1,0:T(8,128)(2,1)S(1)}, bf16[1,512,512]{2,1,0:T(8,128)(2,1)}, u32[]{:S(2)}) copy-start(bf16[1,512,512]{2,1,0:T(8,128)(2,1)} %param.5) | copy-start | bytes 1572868
  3.2 42.5 %all-to-all-start = ((bf16[16,128,512]{2,1,0:T(8,128)(2,1)}), bf16[16,128,512]{2,1,0:T(8,128)(2,1)S(1)}, u32[]{:S(2)}, u32[]{:S(2)}) async-start(bf16[16,128,512]{2,1,0:T(8,128)(2,1)} %get-tuple-element.18), calls=%async_computation | async-start | bytes 4194304 | tf_op jit(solution)/shard_map/all_to_all | solution.py:373
  13.6 28.6 %collective-permute-start = (bf16[528,512]{1,0:T(8,128)(2,1)}, bf16[528,512]{1,0:T(8,128)(2,1)S(1)}, u32[]{:S(2)}, u32[]{:S(2)}) collective-permute-start(bf16[528,512]{1,0:T(8,128)(2,1)} %get-tuple-element.15), channel_id=1, source_target_pairs={{0,64},{32,96},{64,0},{96,32},{128,192},{160,224},{192,128},{224,1... | collective-permute-start | bytes 1622024 | tf_op jit(solution)/shard_map/ppermute | solution.py:378
  15.6 21.7 %collective-permute-start.1 = (bf16[512,512]{1,0:T(8,128)(2,1)S(1)}, bf16[512,512]{1,0:T(8,128)(2,1)S(1)}, u32[]{:S(2)}, u32[]{:S(2)}) collective-permute-start(bf16[512,512]{1,0:T(8,128)(2,1)S(1)} %bitcast.18), channel_id=1, source_target_pairs={{31,0},{0,1},{1,2},{2,3},{3,4},{4,5},{5,6},{6,7},{7,8},{8,9},{9,10... | collective-permute-start | bytes 1572872 | tf_op jit(solution)/shard_map/ppermute | solution.py:25
  37.2 0.8 copy-start.2
  42.2 0.8 copy-start.4
  45.6 5.5 %copy-start = (bf16[1,512,512]{2,1,0:T(8,128)(2,1)S(1)}, bf16[1,512,512]{2,1,0:T(8,128)(2,1)}, u32[]{:S(2)}) copy-start(bf16[1,512,512]{2,1,0:T(8,128)(2,1)} %param.4) | copy-start | bytes 1572868
  45.7 31.9 %all-to-all-start.1 = ((bf16[16,128,512]{2,1,0:T(8,128)(2,1)}), bf16[16,128,512]{2,1,0:T(8,128)(2,1)}, u32[]{:S(2)}, u32[]{:S(2)}) async-start(bf16[16,128,512]{2,1,0:T(8,128)(2,1)} %pack_far.1), calls=%async_computation.1 | async-start | bytes 4194304 | tf_op jit(solution)/shard_map/all_to_all | solution.py:373
  51.1 15.5 %collective-permute-start.3 = (bf16[512,512]{1,0:T(8,128)(2,1)S(1)}, bf16[512,512]{1,0:T(8,128)(2,1)}, u32[]{:S(2)}, u32[]{:S(2)}) collective-permute-start(bf16[512,512]{1,0:T(8,128)(2,1)S(1)} %bitcast.9), channel_id=1, source_target_pairs={{1,0},{2,1},{3,2},{4,3},{5,4},{6,5},{7,6},{8,7},{9,8},{10,9},{11,1... | collective-permute-start | bytes 1572872 | tf_op jit(solution)/shard_map/ppermute | solution.py:25
  53.1 17.8 %collective-permute-start.2 = (bf16[512,512]{1,0:T(8,128)(2,1)}, bf16[512,512]{1,0:T(8,128)(2,1)S(1)}, u32[]{:S(2)}, u32[]{:S(2)}) collective-permute-start(bf16[512,512]{1,0:T(8,128)(2,1)} %copy-done.2), channel_id=1, source_target_pairs={{31,0},{0,1},{1,2},{2,3},{3,4},{4,5},{5,6},{6,7},{7,8},{8,9},{9,10... | collective-permute-start | bytes 1572872 | tf_op jit(solution)/shard_map/ppermute | solution.py:25
  56.4 1.1 %copy-start.3 = (bf16[512,512]{1,0:T(8,128)(2,1)S(1)}, bf16[512,512]{1,0:T(8,128)(2,1)}, u32[]{:S(2)}) copy-start(bf16[512,512]{1,0:T(8,128)(2,1)} %copy-done.2) | copy-start | bytes 1572868
  66.7 23.7 %collective-permute-start.4 = (bf16[512,512]{1,0:T(8,128)(2,1)}, bf16[512,512]{1,0:T(8,128)(2,1)S(1)}, u32[]{:S(2)}, u32[]{:S(2)}) collective-permute-start(bf16[512,512]{1,0:T(8,128)(2,1)} %collective-permute-done.3), channel_id=1, source_target_pairs={{1,0},{2,1},{3,2},{4,3},{5,4},{6,5},{7,6},{8,7},{9,8},{10,9},{11,1... | collective-permute-start | bytes 1572872 | tf_op jit(solution)/shard_map/ppermute | solution.py:25
  82.4 8.0 %collective-permute-start.6 = (f32[8,512]{1,0:T(8,128)S(1)}, f32[8,512]{1,0:T(8,128)S(1)}, u32[]{:S(2)}, u32[]{:S(2)}) collective-permute-start(f32[8,512]{1,0:T(8,128)S(1)} %get-tuple-element.24.refs_1_), channel_id=1, source_target_pairs={{2,0},{3,1},{4,2},{5,3},{6,4},{7,5},{8,6},{9,7},{10,8},{11,9},{12,... | collective-permute-start | bytes 49160 | tf_op jit(solution)/shard_map/ppermute | solution.py:25
  85.5 4.9 %collective-permute-start.5 = (f32[8,512]{1,0:T(8,128)S(1)}, f32[8,512]{1,0:T(8,128)S(1)}, u32[]{:S(2)}, u32[]{:S(2)}) collective-permute-start(f32[8,512]{1,0:T(8,128)S(1)} %get-tuple-element.24.refs_1_), channel_id=1, source_target_pairs={{1,0},{2,1},{3,2},{4,3},{5,4},{6,5},{7,6},{8,7},{9,8},{10,9},{11,1... | collective-permute-start | bytes 49160 | tf_op jit(solution)/shard_map/ppermute | solution.py:25

commit v12 on v11

--- a/solution.py
+++ b/solution.py
@@ -13,7 +13,7 @@
 CHUNK = 512
 VMEM_LIMIT = 20 * 1024 * 1024
 BIG_GRANT = 60 * 1024 * 1024
-FAR_GRANT = 64_000_000
+FAR_GRANT = 40_000_000
 HARD_GRANT = 32 * 1024 * 1024
 ABSENT = 1024.0
 LANES = 128
@@ -125,44 +125,34 @@
     )(me, targets, picks, tile)
 
 
-def far_kernel(entries, me, mail, out, list_v, list_s, tile, head, place, used, seen, mark, sems, mark_sems, in_sems):
-    size = tile.shape[0]
-    rows, lanes = head.shape
-    note = pltpu.make_async_copy(mail.at[pl.ds(size, rows), pl.ds(0, lanes)], head, in_sems.at[0])
-    load = pltpu.make_async_copy(mail.at[pl.ds(0, size)], tile, in_sems.at[1])
-    note.start()
-    load.start()
-    note.wait()
-    list_v[...] = head[...].astype(jnp.float32)[:8].astype(jnp.int32)
-    down = pltpu.make_async_copy(list_v, list_s, in_sems.at[2])
+def far_kernel(entries, me, mail, out, list_v, list_s, place, used, seen, mark, sems, mark_sems, in_sems):
+    size = mail.shape[0] - 16
+    list_v[...] = mail[size : size + 8, :128].astype(jnp.float32).astype(jnp.int32)
+    down = pltpu.make_async_copy(list_v, list_s, in_sems.at[0])
     down.start()
     down.wait()
-    load.wait()
     column = (me[0] >> 1) & 1
-    shared(out.shape[0], entries, out, tile, place, used, seen, mark, sems, mark_sems, column, lambda j: list_s[0, j], lambda j: list_s[0, entries + j])()
+    shared(out.shape[0], entries, out, mail, place, used, seen, mark, sems, mark_sems, column, lambda j: list_s[0, j], lambda j: list_s[0, entries + j])()
 
 
 def pack_far(me, mail, places, entries):
     rows, feature = mail.shape
     slots = places * CAP
-    hbm = whole(pltpu.HBM)
     return pl.pallas_call(
         functools.partial(far_kernel, entries),
         out_shape=jax.ShapeDtypeStruct((slots, BLOCK, feature), mail.dtype),
-        in_specs=[whole(pltpu.SMEM), hbm],
-        out_specs=hbm,
+        in_specs=[whole(pltpu.SMEM), whole()],
+        out_specs=whole(pltpu.HBM),
         scratch_shapes=[
             pltpu.VMEM((8, 128), jnp.int32),
             pltpu.SMEM((8, 128), jnp.int32),
-            pltpu.VMEM((rows - 16, feature), mail.dtype),
-            pltpu.VMEM((16, 128), mail.dtype),
             pltpu.SMEM((entries,), jnp.int32),
             pltpu.SMEM((slots,), jnp.int32),
             pltpu.SMEM((slots,), jnp.int32),
             pltpu.VMEM((16, 128), mail.dtype),
             pltpu.SemaphoreType.DMA((entries,)),
             pltpu.SemaphoreType.DMA((slots,)),
-            pltpu.SemaphoreType.DMA((3,)),
+            pltpu.SemaphoreType.DMA((1,)),
         ],
         compiler_params=pltpu.CompilerParams(vmem_limit_bytes=FAR_GRANT),
         name="pack_far",

time: 94.2 us -> 94.6 us (level)
  starting transfers between devices: 34.9 us -> 33.7 us
    ppermute x6, starting transfers between devices: 17.1 us -> 15.6 us  [passed_along(): return lax.ppermute(block, axis, route)]
    pallas_call x2, Pallas kernels: 6.38 us -> 7.39 us  [hard_part(): pl.pallas_call(functools.partial(hard_kernel, rate, not states), out_shap...]
  transfers between devices with their start and end apart: 9 -> 9, of which waited for: 4 -> 5; matrix products, arithmetic and copies ran while one was open for 1% -> 1% of each run, Pallas kernels for 17% -> 17%
where the time goes in v12:
time: 94.6 us; the launch traced here: 93.3 us
  waiting for transfers between devices  33.9 us (36%)
  starting transfers between devices  33.7 us (36%)
  Pallas kernels  21.3 us (23%)
  local copies, waits for them, and re-layouts  2.39 us (3%)
  other arithmetic  1.1 us (1%)
    ppermute x6, waiting for transfers between devices, passed_along(): return lax.ppermute(block, axis, route)  23.8 us
    all_to_all x2, starting transfers between devices, spread(): lax.all_to_all(packed, 'dp', split_axis=0, concat_axis=0, axis_index_grou...  16.2 us
    ppermute x6, starting transfers between devices, passed_along(): return lax.ppermute(block, axis, route)  15.6 us
    pallas_call x2, Pallas kernels, hard_part(): pl.pallas_call(functools.partial(hard_kernel, rate, not states), out_shap...  7.39 us
    pallas_call x3, Pallas kernels, cycle_part(): pl.pallas_call(functools.partial(cycle_kernel, rate, scale, tiles, len(st...  5.28 us
    all_to_all x2, waiting for transfers between devices, spread(): lax.all_to_all(packed, 'dp', split_axis=0, concat_axis=0, axis_index_grou...  5.2 us
    ppermute x1, waiting for transfers between devices, body(): mail = lax.ppermute(mail, 'dp', [(g, g ^ 2) for g in range(groups)])  4.93 us
    pallas_call x2, Pallas kernels, rtl_part(): pl.pallas_call(functools.partial(rtl_kernel, rate, scale, tiles), grid=(n...  3.8 us
  transfers between devices with their start and end apart: 9, of which 5 were waited for; matrix products, arithmetic and copies ran while one was open for 1% of the time, Pallas kernels for 17%

profile of v12, /device:TPU:1, one launch (start us, length us, event | category | flops | bytes accessed | tf_op | source)
XLA Modules:
  0.0 93.3 jit_solution(2862391985643499232)
XLA Ops:
  0.6 2.5 %pack_own.1 = (bf16[16,128,512]{2,1,0:T(8,128)(2,1)}, bf16[528,512]{1,0:T(8,128)(2,1)}) custom-call(s32[1]{0:T(128)} %bitcast.1.me, s32[16]{0:T(128)} %bitcast.23, s32[16]{0:T(128)} %bitcast.24, bf16[512,512]{1,0:T(8,128)(2,1)} %bitcast.17), custom_call_target="tpu_custom_call" | custom-call | tf_op jit(solution)/shard_map/pack_own/pallas_call | solution.py:105
  3.1 0.0 copy-start.2
  3.1 10.6 %all-to-all-start = ((bf16[16,128,512]{2,1,0:T(8,128)(2,1)}), bf16[16,128,512]{2,1,0:T(8,128)(2,1)S(1)}, u32[]{:S(2)}, u32[]{:S(2)}) async-start(bf16[16,128,512]{2,1,0:T(8,128)(2,1)} %get-tuple-element.18), calls=%async_computation | async-start | bytes 4194304 | tf_op jit(solution)/shard_map/all_to_all | solution.py:363
  13.7 1.9 %collective-permute-start = (bf16[528,512]{1,0:T(8,128)(2,1)}, bf16[528,512]{1,0:T(8,128)(2,1)S(1)}, u32[]{:S(2)}, u32[]{:S(2)}) collective-permute-start(bf16[528,512]{1,0:T(8,128)(2,1)} %get-tuple-element.15), channel_id=1, source_target_pairs={{0,64},{32,96},{64,0},{96,32},{128,192},{160,224},{192,128},{224,1... | collective-permute-start | bytes 1622024 | tf_op jit(solution)/shard_map/ppermute | solution.py:368
  15.6 0.0 copy-done.2
  15.6 2.0 %collective-permute-start.1 = (bf16[512,512]{1,0:T(8,128)(2,1)S(1)}, bf16[512,512]{1,0:T(8,128)(2,1)S(1)}, u32[]{:S(2)}, u32[]{:S(2)}) collective-permute-start(bf16[512,512]{1,0:T(8,128)(2,1)S(1)} %bitcast.18), channel_id=1, source_target_pairs={{31,0},{0,1},{1,2},{2,3},{3,4},{4,5},{5,6},{6,7},{7,8},{8,9},{9,10... | collective-permute-start | bytes 1572872 | tf_op jit(solution)/shard_map/ppermute | solution.py:25
  17.6 19.7 %collective-permute-done.1.refs_1_ = bf16[512,512]{1,0:T(8,128)(2,1)S(1)} collective-permute-done((bf16[512,512]{1,0:T(8,128)(2,1)S(1)}, bf16[512,512]{1,0:T(8,128)(2,1)S(1)}, u32[]{:S(2)}, u32[]{:S(2)}) %collective-permute-start.1) | collective-permute-done | bytes 524320 | tf_op jit(solution)/shard_map/ppermute | solution.py:25
  37.3 0.0 copy-start.3
  37.3 4.9 %collective-permute-done.mail = bf16[528,512]{1,0:T(8,128)(2,1)S(1)} collective-permute-done((bf16[528,512]{1,0:T(8,128)(2,1)}, bf16[528,512]{1,0:T(8,128)(2,1)S(1)}, u32[]{:S(2)}, u32[]{:S(2)}) %collective-permute-start) | collective-permute-done | bytes 540704 | tf_op jit(solution)/shard_map/ppermute | solution.py:368
  42.3 0.0 copy-done.3
  42.3 2.4 %pack_far.1 = bf16[16,128,512]{2,1,0:T(8,128)(2,1)S(1)} custom-call(s32[1]{0:T(128)} %bitcast.1.me, bf16[528,512]{1,0:T(8,128)(2,1)S(1)} %collective-permute-done.mail), custom_call_target="tpu_custom_call" | custom-call | tf_op jit(solution)/shard_map/pack_far/pallas_call | solution.py:141
  44.7 0.0 copy-start.1
  44.7 1.3 %copy-done.1 = bf16[16,128,512]{2,1,0:T(8,128)(2,1)} copy-done((bf16[16,128,512]{2,1,0:T(8,128)(2,1)}, bf16[16,128,512]{2,1,0:T(8,128)(2,1)S(1)}, u32[]{:S(2)}) %copy-start.1) | copy-done | bytes 2097176
  46.0 0.0 copy-start
  46.0 0.0 all-to-all-done.refs_1_
  46.0 5.7 %all-to-all-start.1 = ((bf16[16,128,512]{2,1,0:T(8,128)(2,1)}), bf16[16,128,512]{2,1,0:T(8,128)(2,1)}, u32[]{:S(2)}, u32[]{:S(2)}) async-start(bf16[16,128,512]{2,1,0:T(8,128)(2,1)} %copy-done.1), calls=%async_computation.1 | async-start | bytes 4194304 | tf_op jit(solution)/shard_map/all_to_all | solution.py:363
  51.7 0.0 copy-done
  51.7 1.9 %collective-permute-start.3 = (bf16[512,512]{1,0:T(8,128)(2,1)S(1)}, bf16[512,512]{1,0:T(8,128)(2,1)}, u32[]{:S(2)}, u32[]{:S(2)}) collective-permute-start(bf16[512,512]{1,0:T(8,128)(2,1)S(1)} %bitcast.9), channel_id=1, source_target_pairs={{1,0},{2,1},{3,2},{4,3},{5,4},{6,5},{7,6},{8,7},{9,8},{10,9},{11,1... | collective-permute-start | bytes 1572872 | tf_op jit(solution)/shard_map/ppermute | solution.py:25
  53.6 3.4 %collective-permute-start.2 = (bf16[512,512]{1,0:T(8,128)(2,1)}, bf16[512,512]{1,0:T(8,128)(2,1)S(1)}, u32[]{:S(2)}, u32[]{:S(2)}) collective-permute-start(bf16[512,512]{1,0:T(8,128)(2,1)} %copy-done.3), channel_id=1, source_target_pairs={{31,0},{0,1},{1,2},{2,3},{3,4},{4,5},{5,6},{6,7},{7,8},{8,9},{9,10... | collective-permute-start | bytes 1572872 | tf_op jit(solution)/shard_map/ppermute | solution.py:25
  57.0 0.0 copy-start.4
  57.0 1.0 %copy-done.4 = bf16[512,512]{1,0:T(8,128)(2,1)S(1)} copy-done((bf16[512,512]{1,0:T(8,128)(2,1)S(1)}, bf16[512,512]{1,0:T(8,128)(2,1)}, u32[]{:S(2)}) %copy-start.4) | copy-done | bytes 524312
  58.0 1.9 %cycle_own.1.refs_0_ = f32[512,640]{1,0:T(8,128)S(1)} custom-call(bf16[512,512]{1,0:T(8,128)(2,1)S(1)} %bitcast.10, bf16[512,512]{1,0:T(8,128)(2,1)S(1)} %bitcast.19, bf16[512,512]{1,0:T(8,128)(2,1)S(1)} %copy-done.4), custom_call_target="tpu_custom_call" | custom-call | flops 1073741824 | bytes 2097152 | tf_op jit(solution)/shard_map/cycle_own/pallas_call | solution.py:217
  59.9 3.3 %hard_first.1.refs_1_ = f32[512,640]{1,0:T(8,128)S(1)} custom-call(bf16[512,512]{1,0:T(8,128)(2,1)S(1)} %bitcast.11, f32[512,640]{1,0:T(8,128)S(1)} %cycle_own.1.refs_0_, bf16[16,128,512]{2,1,0:T(8,128)(2,1)S(1)} %all-to-all-done.refs_1_), custom_call_target="tpu_custom_call" | custom-call | flops 1073741824 | bytes 2097152 | tf_op jit(solution)/shard_map/hard_first/pallas_call | solution.py:301
  63.3 3.8 %collective-permute-done.3 = bf16[512,512]{1,0:T(8,128)(2,1)} collective-permute-done((bf16[512,512]{1,0:T(8,128)(2,1)S(1)}, bf16[512,512]{1,0:T(8,128)(2,1)}, u32[]{:S(2)}, u32[]{:S(2)}) %collective-permute-start.3) | collective-permute-done | bytes 524320 | tf_op jit(solution)/shard_map/ppermute | solution.py:25
  67.0 4.3 %collective-permute-start.4 = (bf16[512,512]{1,0:T(8,128)(2,1)}, bf16[512,512]{1,0:T(8,128)(2,1)S(1)}, u32[]{:S(2)}, u32[]{:S(2)}) collective-permute-start(bf16[512,512]{1,0:T(8,128)(2,1)} %collective-permute-done.3), channel_id=1, source_target_pairs={{1,0},{2,1},{3,2},{4,3},{5,4},{6,5},{7,6},{8,7},{9,8},{10,9},{11,1... | collective-permute-start | bytes 1572872 | tf_op jit(solution)/shard_map/ppermute | solution.py:25
  71.3 0.0 collective-permute-done.2.refs_0_
  71.3 1.6 %cycle_more.1.refs_0_ = f32[512,640]{1,0:T(8,128)S(1)} custom-call(bf16[512,512]{1,0:T(8,128)(2,1)S(1)} %bitcast.12, bf16[512,512]{1,0:T(8,128)(2,1)S(1)} %collective-permute-done.2.refs_0_, f32[512,640]{1,0:T(8,128)S(1)} %hard_first.1.refs_1_), custom_call_target="tpu_custom_call" | custom-call | flops 536870912 | bytes 2097152 | tf_op jit(solution)/shard_map/cycle_more/pallas_call | solution.py:217
  72.9 5.2 %all-to-all-done.1.refs_0_ = bf16[16,128,512]{2,1,0:T(8,128)(2,1)} async-done(((bf16[16,128,512]{2,1,0:T(8,128)(2,1)}), bf16[16,128,512]{2,1,0:T(8,128)(2,1)}, u32[]{:S(2)}, u32[]{:S(2)}) %all-to-all-start.1) | async-done | bytes 2097184 | tf_op jit(solution)/shard_map/all_to_all | solution.py:363
  78.1 4.0 %hard_second.1.refs_1_ = f32[512,640]{1,0:T(8,128)S(1)} custom-call(bf16[512,512]{1,0:T(8,128)(2,1)S(1)} %bitcast.13, bf16[16,128,512]{2,1,0:T(8,128)(2,1)} %all-to-all-done.1.refs_0_), custom_call_target="tpu_custom_call" | custom-call | flops 1073741824 | bytes 2097152 | tf_op jit(solution)/shard_map/hard_second/pallas_call | solution.py:301
  82.2 1.8 %cycle_last.1 = (f32[512,512]{1,0:T(8,128)}, f32[1,512]{1,0:T(1,128)}, f32[8,512]{1,0:T(8,128)S(1)}) custom-call(bf16[512,512]{1,0:T(8,128)(2,1)S(1)} %bitcast.14, f32[512,640]{1,0:T(8,128)S(1)} %cycle_more.1.refs_0_, f32[512,640]{1,0:T(8,128)S(1)} %hard_second.1.refs_1_, bf16[512,512]{1,0:T(8,128)(2,1)S(1)} %bitcast.20), custom_call_target="tpu_custom_call" | custom-call | bytes 2097152 | tf_op jit(solution)/shard_map/cycle_last/pallas_call | solution.py:217
  83.9 1.9 %collective-permute-start.6 = (f32[8,512]{1,0:T(8,128)S(1)}, f32[8,512]{1,0:T(8,128)S(1)}, u32[]{:S(2)}, u32[]{:S(2)}) collective-permute-start(f32[8,512]{1,0:T(8,128)S(1)} %get-tuple-element.24.refs_1_), channel_id=1, source_target_pairs={{2,0},{3,1},{4,2},{5,3},{6,4},{7,5},{8,6},{9,7},{10,8},{11,9},{12,... | collective-permute-start | bytes 49160 | tf_op jit(solution)/shard_map/ppermute | solution.py:25
  85.9 2.2 %collective-permute-start.5 = (f32[8,512]{1,0:T(8,128)S(1)}, f32[8,512]{1,0:T(8,128)S(1)}, u32[]{:S(2)}, u32[]{:S(2)}) collective-permute-start(f32[8,512]{1,0:T(8,128)S(1)} %get-tuple-element.24.refs_1_), channel_id=1, source_target_pairs={{1,0},{2,1},{3,2},{4,3},{5,4},{6,5},{7,6},{8,7},{9,8},{10,9},{11,1... | collective-permute-start | bytes 49160 | tf_op jit(solution)/shard_map/ppermute | solution.py:25
  88.0 1.1 %rtl_own.1.refs_4_ = f32[512,512]{1,0:T(8,128)S(1)} custom-call(bf16[512,512]{1,0:T(8,128)(2,1)S(1)} %bitcast.21, bf16[512,512]{1,0:T(8,128)(2,1)S(1)} %bitcast.15, f32[8,512]{1,0:T(8,128)S(1)} %get-tuple-element.24.refs_1_, bf16[512,512]{1,0:T(8,128)(2,1)S(1)} %bitcast.16), custom_call_target="tpu_custom_call" | custom-call | flops 536870912 | bytes 2097152 | tf_op jit(solution)/shard_map/rtl_own/pallas_call | solution.py:338
  89.2 1.1 %broadcast_select_fusion.refs_0_ = bf16[512,512]{1,0:T(8,128)(2,1)S(1)} fusion(bf16[512,512]{1,0:T(8,128)(2,1)} %collective-permute-done.3, pred[]{:T(512)} %bitcast.6, bf16[1,512,512]{2,1,0:T(8,128)(2,1)S(1)} %copy-done), kind=kLoop, calls=%fused_computation | loop fusion | flops 262144 | bytes 1572865 | tf_op jit(solution)/shard_map/jit(_where)/select_n | solution.py:386
  90.3 0.0 collective-permute-done.4.refs_1_
  90.3 0.0 collective-permute-done.6.refs_3_
  90.3 0.3 collective-permute-done.5.refs_2_
  90.6 2.7 %rtl_others.1 = f32[512,512]{1,0:T(8,128)} custom-call(bf16[512,512]{1,0:T(8,128)(2,1)S(1)} %bitcast.22, bf16[512,512]{1,0:T(8,128)(2,1)S(1)} %broadcast_select_fusion.refs_0_, bf16[512,512]{1,0:T(8,128)(2,1)S(1)} %collective-permute-done.4.refs_1_, f32[8,512]{1,0:T(8,128)S(1)} %collective-permute-done.5.refs_2_, ...), custom_call_target="tpu_custom_call" | custom-call | flops 1073741824 | bytes 2621440 | tf_op jit(solution)/shard_map/rtl_others/pallas_call | solution.py:338
Async XLA Ops:
  3.1 12.5 %copy-start.2 = (bf16[1,512,512]{2,1,0:T(8,128)(2,1)S(1)}, bf16[1,512,512]{2,1,0:T(8,128)(2,1)}, u32[]{:S(2)}) copy-start(bf16[1,512,512]{2,1,0:T(8,128)(2,1)} %param.5) | copy-start | bytes 1572868
  3.1 42.9 %all-to-all-start = ((bf16[16,128,512]{2,1,0:T(8,128)(2,1)}), bf16[16,128,512]{2,1,0:T(8,128)(2,1)S(1)}, u32[]{:S(2)}, u32[]{:S(2)}) async-start(bf16[16,128,512]{2,1,0:T(8,128)(2,1)} %get-tuple-element.18), calls=%async_computation | async-start | bytes 4194304 | tf_op jit(solution)/shard_map/all_to_all | solution.py:363
  13.7 28.6 %collective-permute-start = (bf16[528,512]{1,0:T(8,128)(2,1)}, bf16[528,512]{1,0:T(8,128)(2,1)S(1)}, u32[]{:S(2)}, u32[]{:S(2)}) collective-permute-start(bf16[528,512]{1,0:T(8,128)(2,1)} %get-tuple-element.15), channel_id=1, source_target_pairs={{0,64},{32,96},{64,0},{96,32},{128,192},{160,224},{192,128},{224,1... | collective-permute-start | bytes 1622024 | tf_op jit(solution)/shard_map/ppermute | solution.py:368
  15.6 21.7 %collective-permute-start.1 = (bf16[512,512]{1,0:T(8,128)(2,1)S(1)}, bf16[512,512]{1,0:T(8,128)(2,1)S(1)}, u32[]{:S(2)}, u32[]{:S(2)}) collective-permute-start(bf16[512,512]{1,0:T(8,128)(2,1)S(1)} %bitcast.18), channel_id=1, source_target_pairs={{31,0},{0,1},{1,2},{2,3},{3,4},{4,5},{5,6},{6,7},{7,8},{8,9},{9,10... | collective-permute-start | bytes 1572872 | tf_op jit(solution)/shard_map/ppermute | solution.py:25
  37.3 4.9 %copy-start.3 = (bf16[512,512]{1,0:T(8,128)(2,1)}, bf16[512,512]{1,0:T(8,128)(2,1)S(1)}, u32[]{:S(2)}) copy-start(bf16[512,512]{1,0:T(8,128)(2,1)S(1)} %collective-permute-done.1.refs_1_) | copy-start | bytes 1572868
  44.7 1.3 %copy-start.1 = (bf16[16,128,512]{2,1,0:T(8,128)(2,1)}, bf16[16,128,512]{2,1,0:T(8,128)(2,1)S(1)}, u32[]{:S(2)}) copy-start(bf16[16,128,512]{2,1,0:T(8,128)(2,1)S(1)} %pack_far.1) | copy-start | bytes 6291460
  46.0 5.7 %copy-start = (bf16[1,512,512]{2,1,0:T(8,128)(2,1)S(1)}, bf16[1,512,512]{2,1,0:T(8,128)(2,1)}, u32[]{:S(2)}) copy-start(bf16[1,512,512]{2,1,0:T(8,128)(2,1)} %param.4) | copy-start | bytes 1572868
  46.0 32.1 %all-to-all-start.1 = ((bf16[16,128,512]{2,1,0:T(8,128)(2,1)}), bf16[16,128,512]{2,1,0:T(8,128)(2,1)}, u32[]{:S(2)}, u32[]{:S(2)}) async-start(bf16[16,128,512]{2,1,0:T(8,128)(2,1)} %copy-done.1), calls=%async_computation.1 | async-start | bytes 4194304 | tf_op jit(solution)/shard_map/all_to_all | solution.py:363
  51.7 15.4 %collective-permute-start.3 = (bf16[512,512]{1,0:T(8,128)(2,1)S(1)}, bf16[512,512]{1,0:T(8,128)(2,1)}, u32[]{:S(2)}, u32[]{:S(2)}) collective-permute-start(bf16[512,512]{1,0:T(8,128)(2,1)S(1)} %bitcast.9), channel_id=1, source_target_pairs={{1,0},{2,1},{3,2},{4,3},{5,4},{6,5},{7,6},{8,7},{9,8},{10,9},{11,1... | collective-permute-start | bytes 1572872 | tf_op jit(solution)/shard_map/ppermute | solution.py:25
  53.6 17.7 %collective-permute-start.2 = (bf16[512,512]{1,0:T(8,128)(2,1)}, bf16[512,512]{1,0:T(8,128)(2,1)S(1)}, u32[]{:S(2)}, u32[]{:S(2)}) collective-permute-start(bf16[512,512]{1,0:T(8,128)(2,1)} %copy-done.3), channel_id=1, source_target_pairs={{31,0},{0,1},{1,2},{2,3},{3,4},{4,5},{5,6},{6,7},{7,8},{8,9},{9,10... | collective-permute-start | bytes 1572872 | tf_op jit(solution)/shard_map/ppermute | solution.py:25
  57.0 1.1 %copy-start.4 = (bf16[512,512]{1,0:T(8,128)(2,1)S(1)}, bf16[512,512]{1,0:T(8,128)(2,1)}, u32[]{:S(2)}) copy-start(bf16[512,512]{1,0:T(8,128)(2,1)} %copy-done.3) | copy-start | bytes 1572868
  67.0 23.3 %collective-permute-start.4 = (bf16[512,512]{1,0:T(8,128)(2,1)}, bf16[512,512]{1,0:T(8,128)(2,1)S(1)}, u32[]{:S(2)}, u32[]{:S(2)}) collective-permute-start(bf16[512,512]{1,0:T(8,128)(2,1)} %collective-permute-done.3), channel_id=1, source_target_pairs={{1,0},{2,1},{3,2},{4,3},{5,4},{6,5},{7,6},{8,7},{9,8},{10,9},{11,1... | collective-permute-start | bytes 1572872 | tf_op jit(solution)/shard_map/ppermute | solution.py:25
  83.9 6.4 %collective-permute-start.6 = (f32[8,512]{1,0:T(8,128)S(1)}, f32[8,512]{1,0:T(8,128)S(1)}, u32[]{:S(2)}, u32[]{:S(2)}) collective-permute-start(f32[8,512]{1,0:T(8,128)S(1)} %get-tuple-element.24.refs_1_), channel_id=1, source_target_pairs={{2,0},{3,1},{4,2},{5,3},{6,4},{7,5},{8,6},{9,7},{10,8},{11,9},{12,... | collective-permute-start | bytes 49160 | tf_op jit(solution)/shard_map/ppermute | solution.py:25
  85.9 4.8 %collective-permute-start.5 = (f32[8,512]{1,0:T(8,128)S(1)}, f32[8,512]{1,0:T(8,128)S(1)}, u32[]{:S(2)}, u32[]{:S(2)}) collective-permute-start(f32[8,512]{1,0:T(8,128)S(1)} %get-tuple-element.24.refs_1_), channel_id=1, source_target_pairs={{1,0},{2,1},{3,2},{4,3},{5,4},{6,5},{7,6},{8,7},{9,8},{10,9},{11,1... | collective-permute-start | bytes 49160 | tf_op jit(solution)/shard_map/ppermute | solution.py:25
